TPU v7x, 256 devices: a whole 4x4x8 slice. The times are simulated.
256 devices in a mesh: tm: 4 (over x_hi, core), space: 64 (over z, x_lo, y).
Axes of the slice: x: 4 (x_hi: 2, x_lo: 2; x = x_hi * 2 + x_lo), y: 4, z: 8, core: 2. Of those that a mesh axis runs over, the one named last changes fastest.
Arguments:
- queries: bfloat16 [4, 4, 64, 32, 1536], P('tm', None, 'space'), may hold values from -30 to 30
- key_states: bfloat16 [4, 4, 64, 32, 1536], P('tm', None, 'space'), may hold values from -30 to 30, as said below
- value_states: bfloat16 [4, 4, 64, 32, 1536], P('tm', None, 'space'), may hold values from -6 to 6
- conv_weight: float32 [3, 3, 3, 1536], replicated, may hold values from -0.3125 to 0.3125
Outputs:
- mixed: bfloat16 [4, 4, 64, 32, 1536], P('tm', None, 'space')
Inputs may be any that keep to these rules, and one draw needn't show every extreme that they name: `key_states`: entries are real-valued keys.
All inputs are finite; a program needn't handle non-finite values.
Results may differ from a plain program's by a relative error of at most 0.0088.
Values may be sent and summed in bfloat16 or wider, within the bound.
No kernel may reach another device: no remote copies, remote signals or barrier semaphores. Data moves between devices by JAX's collectives and lax.ppermute only.
A program may use at most 192 MiB of HBM per device.

v0:
```python
import math

import jax
import jax.numpy as jnp
from jax import lax
from jax.sharding import PartitionSpec as P

HEADS = 24
HEAD_DIM = 64
D = 1536
FRAMES = 4
ROWS_DEV = 1
COLUMNS = 32
AGENT_DEV = 4


def extended(cells, sides, width):
    for axis, dim in sides:
        count = lax.axis_size(axis)
        ends = count - 1
        head = lax.slice_in_dim(cells, 0, width, axis=dim)
        tail = lax.slice_in_dim(cells, cells.shape[dim] - width, cells.shape[dim], axis=dim)
        cells = jnp.concatenate(
            [
                lax.ppermute(tail, axis, [(i, (i + 1) % count) for i in range(ends)]),
                cells,
                lax.ppermute(head, axis, [((i + 1) % count, i) for i in range(ends)]),
            ],
            axis=dim,
        )
    return cells


def mix_local(window, conv_weight):
    shape = (window.shape[0] - 2, window.shape[1] - 2, window.shape[2] - 2, window.shape[3])
    total = jnp.zeros(shape, jnp.float32)
    for time_off in range(3):
        for row_off in range(3):
            for col_off in range(3):
                piece = window[
                    time_off : time_off + shape[0],
                    row_off : row_off + shape[1],
                    col_off : col_off + shape[2],
                ]
                total = total + piece.astype(jnp.float32) * conv_weight[time_off, row_off, col_off]
    return total


def on_device(queries, key_states, value_states, conv_weight):
    tokens = FRAMES * ROWS_DEV * COLUMNS
    inv_root = HEAD_DIM ** (-0.5)
    per_block = math.gcd(HEADS, 8)
    blocks = HEADS // per_block
    padded = extended(value_states, (("tm", 1), ("space", 2)), 1)
    window = jnp.pad(padded[0], ((0, 0), (0, 0), (1, 1), (0, 0)))
    pooled = jnp.mean(
        queries.reshape(FRAMES, ROWS_DEV, AGENT_DEV, COLUMNS // AGENT_DEV, D),
        axis=(0, 1, 3),
        dtype=jnp.float32,
    )
    agents = lax.all_gather(pooled.astype(jnp.bfloat16), "space", axis=0, tiled=True)
    count = agents.shape[0]
    agent_heads = agents.reshape(count, HEADS, HEAD_DIM)
    query_heads = queries.reshape(tokens, HEADS, HEAD_DIM)
    key_heads = key_states.reshape(tokens, HEADS, HEAD_DIM)
    value_heads = value_states.reshape(tokens, HEADS, HEAD_DIM)

    def agent_block(index):
        start = index * per_block
        agent_part = lax.dynamic_slice_in_dim(agent_heads, start, per_block, 1)
        key_part = lax.dynamic_slice_in_dim(key_heads, start, per_block, 1)
        value_part = lax.dynamic_slice_in_dim(value_heads, start, per_block, 1)
        scores = (
            jnp.einsum("ahd,nhd->ahn", agent_part, key_part, preferred_element_type=jnp.float32)
            * inv_root
        )
        block_peak = jnp.max(scores, axis=2)
        weights = jnp.exp(scores - block_peak[..., None])
        block_total = jnp.sum(weights, axis=2)
        block_acc = jnp.einsum(
            "ahn,nhd->ahd",
            weights.astype(jnp.bfloat16),
            value_part,
            preferred_element_type=jnp.float32,
        )
        return (block_peak, block_total, block_acc)

    peaks, totals, accs = lax.map(agent_block, jnp.arange(blocks, dtype=jnp.int32))
    local_peak = peaks.transpose(1, 0, 2).reshape(count, HEADS)
    local_total = totals.transpose(1, 0, 2).reshape(count, HEADS)
    local_acc = accs.transpose(1, 0, 2, 3).reshape(count, HEADS, HEAD_DIM)
    peak = lax.pmax(local_peak, "space")
    rescale = jnp.exp(local_peak - peak)
    total_sum, acc_sum = lax.psum((local_total * rescale, local_acc * rescale[..., None]), "space")
    agent_values = (acc_sum / total_sum[..., None]).astype(jnp.bfloat16)

    def query_block(index):
        start = index * per_block
        query_part = lax.dynamic_slice_in_dim(query_heads, start, per_block, 1)
        agent_part = lax.dynamic_slice_in_dim(agent_heads, start, per_block, 1)
        values_part = lax.dynamic_slice_in_dim(agent_values, start, per_block, 1)
        query_scores = (
            jnp.einsum("nhd,ahd->hna", query_part, agent_part, preferred_element_type=jnp.float32)
            * inv_root
        )
        probs = jax.nn.softmax(query_scores, axis=-1).astype(jnp.bfloat16)
        return jnp.einsum("hna,ahd->nhd", probs, values_part, preferred_element_type=jnp.float32)

    outputs = lax.map(query_block, jnp.arange(blocks, dtype=jnp.int32))
    attended = outputs.transpose(1, 0, 2, 3).reshape(FRAMES, ROWS_DEV, COLUMNS, D)
    local_mix = mix_local(window, conv_weight)
    mixed = (attended + local_mix).astype(jnp.bfloat16)
    return mixed.reshape(value_states.shape)


def solution(mesh):
    return jax.shard_map(
        on_device,
        mesh=mesh,
        in_specs=(
            P("tm", None, "space", None, None),
            P("tm", None, "space", None, None),
            P("tm", None, "space", None, None),
            P(),
        ),
        out_specs=P("tm", None, "space", None, None),
        check_vma=False,
    )
```

profile of v0, /device:TPU:96, one launch (start us, length us, event | category | flops | bytes accessed | tf_op | source)
XLA Modules:
  0.0 1120.5 jit_solution(9148870399939223260)
XLA Ops:
  6.5 1.6 reshape.95
  8.8 144.1 %all-gather = bf16[64,4,1536]{2,1,0:T(4,128)(2,1)S(1)} all-gather(bf16[1,4,1536]{2,1,0:T(4,128)(2,1)S(1)} %fusion.47), channel_id=1, replica_groups=mesh['tm'=4,'space'=64] {'space'}, dimensions={0}, use_global_device_ids=true | all-gather | bytes 798720 | tf_op jit(solution)/shard_map/all_gather | solution.py:61
  155.7 9.1 while.24
  164.8 302.8 %pmax.7 = f32[256,24]{0,1:T(8,128)S(1)} all-reduce(f32[256,24]{0,1:T(8,128)S(1)} %bitcast.68), channel_id=1, replica_groups=mesh['tm'=4,'space'=64] {'space'}, use_global_device_ids=true, to_apply=%region_6.7 | all-reduce | flops 6144 | bytes 49152 | tf_op jit(solution)/shard_map/pmax | solution.py:92
  468.2 2.8 bitcast_multiply_fusion
  471.0 1.4 collective-permute-start.1
  472.4 3.0 collective-permute-start
  476.5 1.9 collective-permute-start.3
  478.4 3.9 collective-permute-start.2
  484.0 307.8 %psum.15 = f32[256,24]{0,1:T(8,128)} all-reduce(f32[256,24]{0,1:T(8,128)} %get-tuple-element.182), channel_id=1, replica_groups=mesh['tm'=4,'space'=64] {'space'}, use_global_device_ids=true, to_apply=%region_8.9 | all-reduce | flops 6144 | bytes 49152 | tf_op jit(solution)/shard_map/psum | solution.py:94
  791.8 1.6 slice_reduce_fusion.25
  793.4 2.0 slice_reduce_fusion.26
  795.5 1.4 maximum_bitcast_fusion
  796.9 290.7 %all-reduce.3.cloned.1.call-done = f32[256,24,64]{0,2,1:T(8,128)} async-done(((f32[256,24,64]{0,2,1:T(8,128)}), f32[256,24,64]{0,2,1:T(8,128)}) %all-reduce.3.cloned.1.call-update) | async-done | bytes 1572880 | tf_op jit(solution)/shard_map/psum | solution.py:94
  1087.6 1.6 divide_convert_fusion.2
  1089.2 15.7 %while.25 = (s32[]{:T(128)}, f32[3,128,8,64]{1,3,2,0:T(8,128)}, s32[3]{0:T(128)S(1)}, bf16[256,24,64]{0,2,1:T(8,128)(2,1)S(1)}, bf16[128,24,64]{0,2,1:T(8,128)(2...) while((s32[]{:T(128)}, f32[3,128,8,64]{1,3,2,0:T(8,128)}, ...), condition=%wide.region_12.13_spmd, body=%wide.region_9.12_spmd.sunk | while | flops 102499840 | bytes 1322151 | solution.py:109
  1090.5 1.6 fusion.77
  1092.0 2.4 fusion.78
  1095.7 1.6 fusion.77
  1097.3 2.4 fusion.78
  1100.9 1.6 fusion.77
  1102.5 2.4 fusion.78
  1104.9 1.7 copy.41
  1108.3 5.4 fusion.46
  (102 shorter events, 16.8 us)
Async XLA Ops:
  6.5 2.1 copy-start.1
  6.5 1081.0 %all-reduce.3.cloned.1.call-start = ((), (), s32[]{:S(2)}) async-start(), calls=%async_computation | async-start | bytes 3145728 | tf_op jit(solution)/shard_map/psum | solution.py:94
  470.9 11.4 %copy-start.2 = (bf16[1,4,1,32,1536]{4,3,2,1,0:T(8,128)(2,1)S(1)}, bf16[1,4,1,32,1536]{4,3,2,1,0:T(8,128)(2,1)}, u32[]{:S(2)}) copy-start(bf16[1,4,1,32,1536]{4,3,2,1,0:T(8,128)(2,1)} %param.8) | copy-start | bytes 1179652
  471.0 4.5 collective-permute-start.1
  472.4 4.0 collective-permute-start
  476.4 2.0 copy-start.4
  476.5 319.0 %collective-permute-start.3 = (bf16[1,6,1,32,1536]{4,3,1,2,0:T(8,128)(2,1)S(1)}, bf16[1,6,1,32,1536]{4,3,1,2,0:T(8,128)(2,1)S(1)}, u32[]{:S(2)}, u32[]{:S(2)}) collective-permute-start(bf16[1,6,1,32,1536]{4,3,1,2,0:T(8,128)(2,1)S(1)} %pad_maximum_fusion), channel_id=1, source_target_pairs={{1,0},{2,1},{3,2},{4,3},{5,4},{6,5},{7,6},{8,7},{9,8},{10,9},{11,1... | collective-permute-start | bytes 1769480 | tf_op jit(solution)/shard_map/ppermute | solution.py:27
  478.4 317.1 %collective-permute-start.2 = (bf16[1,6,1,32,1536]{4,3,1,2,0:T(8,128)(2,1)S(1)}, bf16[1,6,1,32,1536]{4,3,1,2,0:T(8,128)(2,1)}, u32[]{:S(2)}, u32[]{:S(2)}) collective-permute-start(bf16[1,6,1,32,1536]{4,3,1,2,0:T(8,128)(2,1)S(1)} %pad_maximum_fusion), channel_id=1, source_target_pairs={{0,1},{1,2},{2,3},{3,4},{4,5},{5,6},{6,7},{7,8},{8,9},{9,10},{10,1... | collective-permute-start | bytes 1769480 | tf_op jit(solution)/shard_map/ppermute | solution.py:25
  1106.6 1.5 copy-start.5
  1106.6 1.5 copy-start.6
  1106.6 1.5 copy-start.7
  1106.6 1.5 copy-start.8
  1106.6 1.5 copy-start.9
  1106.6 1.5 copy-start.10
  1106.7 1.5 copy-start.11
  1106.7 1.5 copy-start.12
  1106.7 1.5 copy-start.13
  1106.7 1.5 copy-start.14
  1106.7 1.5 copy-start.15
  1106.7 1.5 copy-start.16
  1106.7 1.5 copy-start.17
  1106.7 1.5 copy-start.18
  1106.7 1.5 copy-start.19
  1106.7 1.5 copy-start.20
  (10 other events, 13.8 us)
Sparse Core Ops, SparseCore 0:
  471.1 616.4 all-reduce.2
where the time goes:
time: 1130 us; the launch traced here: 1120 us
  blocking collectives  755 us (67%)
  waiting for transfers between devices  292 us (26%)
  local copies, waits for them, and re-layouts  17.1 us (2%)
  matrix products  16.4 us (1%)
  between operations  14 us (1%)
  other arithmetic  12.4 us (1%)
    psum x1, blocking collectives, on_device(): lax.psum((local_total * rescale, local_acc * rescale[..., None]), 'space')  308 us
    pmax x1, blocking collectives, on_device(): peak = lax.pmax(local_peak, 'space')  303 us
    psum x1, waiting for transfers between devices, on_device(): lax.psum((local_total * rescale, local_acc * rescale[..., None]), 'space')  291 us
    all_gather x1, blocking collectives, on_device(): lax.all_gather(pooled.astype(jnp.bfloat16), 'space', axis=0, tiled=True)  144 us
  transfers between devices with their start and end apart: 5, of which 2 were waited for; matrix products, arithmetic and copies ran while one was open for 1% of the time, Pallas kernels for 0%

commit v1 on v0

v1 whole, which is shorter than its diff:
```python
import jax
import jax.numpy as jnp
from jax import lax
from jax.experimental import pallas as pl
from jax.experimental.pallas import tpu as pltpu
from jax.sharding import Mesh
from jax.sharding import PartitionSpec as P

HEADS = 24
HEAD_DIM = 64
D = 1536
FRAMES = 4
COLUMNS = 32
TOKENS = FRAMES * COLUMNS
AGENT_DEV = 4
PLANES = 8
TILES = 8
AGENTS = 256
GROUP_HEADS = HEADS // TILES
GROUP = GROUP_HEADS * HEAD_DIM
HALF = GROUP // 2
K_ROW = GROUP
V_ROW = 2 * GROUP
H_ROW = 3 * GROUP
SENT = H_ROW + HALF
STATS = 16
INV_ROOT = HEAD_DIM ** (-0.5)
F32 = jnp.float32
BF16 = jnp.bfloat16


def call(kernel, out_shape, us, *args):
    cost = pl.CostEstimate(flops=int(us * 3.0e8), bytes_accessed=int(us * 2.0e6), transcendentals=0)
    return pl.pallas_call(kernel, out_shape=out_shape, cost_estimate=cost)(*args)


def pool_kernel(q_ref, out_ref):
    shape = (8, TOKENS)
    token = lax.broadcasted_iota(jnp.int32, shape, 1)
    agent = lax.broadcasted_iota(jnp.int32, shape, 0)
    width = COLUMNS // AGENT_DEV
    pick = ((token % COLUMNS) // width == agent).astype(F32).astype(BF16)
    sums = jnp.dot(pick, q_ref[...], preferred_element_type=F32)
    pooled = (sums[:AGENT_DEV] * (1.0 / (FRAMES * width))).astype(BF16)
    for tile in range(TILES):
        part = pooled[:, tile * GROUP : (tile + 1) * GROUP]
        for plane in range(PLANES):
            out_ref[plane * TILES + tile] = part


def pack_kernel(q_ref, k_ref, v_ref, before_ref, after_ref, out_ref):
    for row, ref in ((0, q_ref), (K_ROW, k_ref), (V_ROW, v_ref)):
        flipped = ref[...].T
        for tile in range(TILES):
            out_ref[tile, row : row + GROUP, :] = flipped[tile * GROUP : (tile + 1) * GROUP]
    edges = jnp.concatenate([before_ref[...], after_ref[...]], axis=0).T
    for tile in range(TILES):
        low = edges[tile * GROUP : tile * GROUP + HALF]
        high = edges[tile * GROUP + HALF : (tile + 1) * GROUP]
        out_ref[tile, H_ROW:, :] = jnp.concatenate([low, high], axis=1)


def rows_of(x_ref, start, size):
    return jnp.concatenate([x_ref[s, start : start + size, :] for s in range(TILES)], axis=1)


def agent_kernel(a_ref, x_ref, out_ref):
    columns = []
    lane = lax.broadcasted_iota(jnp.int32, (AGENTS, HEAD_DIM), 1)
    stats = jnp.zeros((AGENTS, HEAD_DIM), F32)
    for h in range(GROUP_HEADS):
        keys = rows_of(x_ref, K_ROW + h * HEAD_DIM, HEAD_DIM)
        values = rows_of(x_ref, V_ROW + h * HEAD_DIM, HEAD_DIM)
        agents = a_ref[:, h * HEAD_DIM : (h + 1) * HEAD_DIM]
        scores = jnp.dot(agents, keys, preferred_element_type=F32) * INV_ROOT
        peak = jnp.max(scores, axis=1, keepdims=True)
        weights = jnp.exp(scores - peak)
        total = jnp.sum(weights, axis=1, keepdims=True)
        acc = lax.dot_general(
            weights.astype(BF16), values, (((1,), (1,)), ((), ())), preferred_element_type=F32
        )
        columns.append(acc / total)
        left = peak + jnp.log(total)
        for piece in range(3):
            short = left.astype(BF16).astype(F32)
            left = left - short
            stats = jnp.where(lane == piece * GROUP_HEADS + h, short, stats)
    flipped = jnp.concatenate(columns + [stats], axis=1).T
    out_ref[...] = flipped[: GROUP + STATS].astype(BF16)


def query_kernel(a_ref, x_ref, e_ref, total_ref):
    for h in range(GROUP_HEADS):
        queries = rows_of(x_ref, h * HEAD_DIM, HEAD_DIM)
        agents = a_ref[:, h * HEAD_DIM : (h + 1) * HEAD_DIM]
        scores = jnp.dot(agents, queries, preferred_element_type=F32) * INV_ROOT
        weights = jnp.exp(scores - jnp.max(scores, axis=0, keepdims=True))
        total_ref[h : h + 1, :] = jnp.sum(weights, axis=0, keepdims=True)
        e_ref[h] = weights.astype(BF16)


def conv_kernel(x_ref, above_ref, below_ref, w_ref, out_ref):
    tall = 16
    lane = lax.broadcasted_iota(jnp.int32, (tall, TOKENS), 1)
    column = lane % COLUMNS
    first, last = lane < COLUMNS, lane >= TOKENS - COLUMNS

    def frames_of(r, at, edge_at, low):
        if r < 0:
            cells, edge = above_ref[pl.ds(at, tall), :], above_ref[pl.ds(GROUP + edge_at, tall), :]
        elif r == TILES:
            cells, edge = below_ref[pl.ds(at, tall), :], below_ref[pl.ds(GROUP + edge_at, tall), :]
        else:
            cells = x_ref[r, pl.ds(V_ROW + at, tall), :]
            edge = x_ref[r, pl.ds(H_ROW + edge_at, tall), :]
        cells, edge = cells.astype(F32), edge.astype(F32)
        turned = pltpu.roll(edge, TOKENS // 2, 1)
        before, after = (edge, turned) if low else (turned, edge)
        return (
            jnp.where(first, before, pltpu.roll(cells, COLUMNS, 1)),
            cells,
            jnp.where(last, after, pltpu.roll(cells, TOKENS - COLUMNS, 1)),
        )

    for low in (True, False):

        def step(i, carry, low=low):
            edge_at = pl.multiple_of(i * tall, tall)
            at = pl.multiple_of(edge_at + (0 if low else HALF), tall)
            w = w_ref[pl.ds(at, tall), :]
            taps = [jnp.broadcast_to(w[:, n : n + 1], (tall, TOKENS)) for n in range(27)]
            rows = {r: frames_of(r, at, edge_at, low) for r in range(-1, 2)}
            for r in range(TILES):
                if r > 0:
                    rows[r + 1] = frames_of(r + 1, at, edge_at, low)
                sums = []
                for k in range(3):
                    total = None
                    for j in range(3):
                        for i3 in range(3):
                            term = rows[r + j - 1][i3] * taps[i3 * 9 + j * 3 + k]
                            total = term if total is None else total + term
                    sums.append(total)
                left = jnp.where(column == 0, 0.0, pltpu.roll(sums[0], 1, 1))
                right = jnp.where(column == COLUMNS - 1, 0.0, pltpu.roll(sums[2], TOKENS - 1, 1))
                out_ref[r, pl.ds(at, tall), :] = left + sums[1] + right
            return carry

        lax.fori_loop(0, HALF // tall, step, 0)


def mix_kernel(parts_ref, e_ref, total_ref, local_ref, out_ref):
    logs = []
    for z in range(PLANES):
        pieces = parts_ref[z, GROUP : GROUP + STATS, :].astype(F32)
        n = GROUP_HEADS
        logs.append(pieces[:n] + pieces[n : 2 * n] + pieces[2 * n : 3 * n])
    peak = logs[0]
    for log in logs[1:]:
        peak = jnp.maximum(peak, log)
    shares = [jnp.exp(log - peak) for log in logs]
    whole = sum(shares[1:], shares[0])
    shares = [share / whole for share in shares]
    for h in range(GROUP_HEADS):
        rows = slice(h * HEAD_DIM, (h + 1) * HEAD_DIM)
        values = None
        for z in range(PLANES):
            term = parts_ref[z, rows, :].astype(F32) * shares[z][h : h + 1]
            values = term if values is None else values + term
        mixed = jnp.dot(values.astype(BF16), e_ref[h], preferred_element_type=F32)
        mixed = mixed / total_ref[h : h + 1, :]
        for s in range(TILES):
            cells = mixed[:, s * TOKENS : (s + 1) * TOKENS]
            out_ref[s, rows, :] = (cells + local_ref[s, rows, :]).astype(BF16)


def unpack_kernel(x_ref, out_ref):
    out_ref[...] = x_ref[...].reshape(D, TOKENS).T


def on_device(queries, key_states, value_states, conv_weight):
    q = queries.reshape(TOKENS, D)
    k = key_states.reshape(TOKENS, D)
    v = value_states.reshape(TOKENS, D)
    groups = lax.axis_size("tm")
    ends = groups - 1
    before = lax.ppermute(v[TOKENS - COLUMNS :], "tm", [(i, i + 1) for i in range(ends)])
    after = lax.ppermute(v[:COLUMNS], "tm", [(i + 1, i) for i in range(ends)])

    pooled = call(pool_kernel, jax.ShapeDtypeStruct((PLANES * TILES, AGENT_DEV, GROUP), BF16), 1.0, q)
    agents = lax.all_to_all(pooled, ("z", "xy"), 0, 0).reshape(AGENTS, GROUP)

    packed = call(
        pack_kernel, jax.ShapeDtypeStruct((TILES, SENT, TOKENS), BF16), 3.0, q, k, v, before, after
    )
    x = lax.all_to_all(packed, "xy", 0, 0)

    above = lax.ppermute(x[TILES - 1, V_ROW:], "z", [(i, i + 1) for i in range(PLANES - 1)])
    below = lax.ppermute(x[0, V_ROW:], "z", [(i + 1, i) for i in range(PLANES - 1)])

    part = call(
        agent_kernel, jax.ShapeDtypeStruct((GROUP + STATS, AGENTS), BF16), 4.0, agents, x
    )
    parts = lax.all_to_all(jnp.broadcast_to(part[None], (PLANES, *part.shape)), "z", 0, 0)

    weights, totals = call(
        query_kernel,
        (
            jax.ShapeDtypeStruct((GROUP_HEADS, AGENTS, TILES * TOKENS), BF16),
            jax.ShapeDtypeStruct((8, TILES * TOKENS), F32),
        ),
        4.0,
        agents,
        x,
    )
    taps = lax.dynamic_index_in_dim(
        conv_weight.reshape(27, TILES, GROUP), lax.axis_index("xy"), 1, keepdims=False
    ).T
    local = call(
        conv_kernel, jax.ShapeDtypeStruct((TILES, GROUP, TOKENS), F32), 6.0, x, above, below, taps
    )
    mixed = call(
        mix_kernel,
        jax.ShapeDtypeStruct((TILES, GROUP, TOKENS), BF16),
        3.0,
        parts,
        weights,
        totals,
        local,
    )
    mine = lax.all_to_all(mixed, "xy", 0, 0)
    out = call(unpack_kernel, jax.ShapeDtypeStruct((TOKENS, D), BF16), 1.0, mine)
    return out.reshape(value_states.shape)


def solution(mesh):
    devices = mesh.devices
    fine = Mesh(devices.reshape(devices.shape[0], PLANES, TILES), ("tm", "z", "xy"))
    spec = P("tm", None, ("z", "xy"), None, None)
    return jax.shard_map(
        on_device,
        mesh=fine,
        in_specs=(spec, spec, spec, P()),
        out_specs=spec,
        check_vma=False,
    )
```

time: 1130 us -> 110 us (0.10)
  blocking collectives: 755 us -> 12.2 us
  waiting for transfers between devices: 292 us -> 30 us
  starting transfers between devices: 10.3 us -> 35.6 us
  Pallas kernels: 0 us -> 23.4 us
  matrix products: 16.4 us -> 0 us
  between operations: 14 us -> 0.1 us
  other arithmetic: 12.4 us -> 0 us
    psum x1 -> x0, blocking collectives: 308 us -> none  [on_device(): lax.psum((local_total * rescale, local_acc * rescale[..., None]), 'space')]
    pmax x1 -> x0, blocking collectives: 303 us -> none  [on_device(): peak = lax.pmax(local_peak, 'space')]
    psum x1 -> x0, waiting for transfers between devices: 291 us -> none  [on_device(): lax.psum((local_total * rescale, local_acc * rescale[..., None]), 'space')]
    all_gather x1 -> x0, blocking collectives: 144 us -> none  [on_device(): lax.all_gather(pooled.astype(jnp.bfloat16), 'space', axis=0, tiled=True)]
    all_to_all x0 -> x3, starting transfers between devices: none -> 24.3 us  [the longest x1 11.8 us: on_device(): agents = lax.all_to_all(pooled, ('z', 'xy'), 0, 0).reshape(AGENTS, GROUP)]
    pallas_call x0 -> x7, Pallas kernels: none -> 23.4 us  [call(): pl.pallas_call(kernel, out_shape=out_shape, cost_estimate=cost)(*args)]
    all_to_all x0 -> x3, waiting for transfers between devices: none -> 18.6 us  [the longest x1 18.6 us: on_device(): x = lax.all_to_all(packed, 'xy', 0, 0)]
    all_to_all x0 -> x1, blocking collectives: none -> 12.2 us  [on_device(): mine = lax.all_to_all(mixed, 'xy', 0, 0)]
  transfers between devices with their start and end apart: 5 -> 7, of which waited for: 2 -> 3; matrix products, arithmetic and copies ran while one was open for 1% -> 2% of each run, Pallas kernels for 0% -> 12%
where the time goes in v1:
time: 110 us; the launch traced here: 109 us
  starting transfers between devices  35.6 us (32%)
  waiting for transfers between devices  30 us (27%)
  Pallas kernels  23.4 us (21%)
  blocking collectives  12.2 us (11%)
  local copies, waits for them, and re-layouts  7.78 us (7%)
    pallas_call x7, Pallas kernels, call(): pl.pallas_call(kernel, out_shape=out_shape, cost_estimate=cost)(*args)  23.4 us
    all_to_all x1, waiting for transfers between devices, on_device(): x = lax.all_to_all(packed, 'xy', 0, 0)  18.6 us
    all_to_all x1, blocking collectives, on_device(): mine = lax.all_to_all(mixed, 'xy', 0, 0)  12.2 us
    all_to_all x1, starting transfers between devices, on_device(): agents = lax.all_to_all(pooled, ('z', 'xy'), 0, 0).reshape(AGENTS, GROUP)  11.8 us
    ppermute x1, waiting for transfers between devices, on_device(): lax.ppermute(x[0, V_ROW:], 'z', [(i + 1, i) for i in range(PLANES - 1)])  10.5 us
    all_to_all x1, starting transfers between devices, on_device(): lax.all_to_all(jnp.broadcast_to(part[None], (PLANES, *part.shape)), 'z',...  7.26 us
    all_to_all x1, starting transfers between devices, on_device(): x = lax.all_to_all(packed, 'xy', 0, 0)  5.18 us
    ppermute x1, starting transfers between devices, on_device(): lax.ppermute(x[TILES - 1, V_ROW:], 'z', [(i, i + 1) for i in range(PLANES...  4.58 us
  transfers between devices with their start and end apart: 7, of which 3 were waited for; matrix products, arithmetic and copies ran while one was open for 2% of the time, Pallas kernels for 12%

profile of v1, /device:TPU:96, one launch (start us, length us, event | category | flops | bytes accessed | tf_op | source)
XLA Modules:
  0.0 109.1 jit_solution(7909599204018980210)
XLA Ops:
  0.0 1.9 %shard_map.46 = bf16[64,4,192]{2,1,0:T(4,128)(2,1)} custom-call(bf16[128,1536]{1,0:T(8,128)(2,1)} %bitcast.19), custom_call_target="tpu_custom_call" | custom-call | flops 300000000 | bytes 2000000 | tf_op jit(solution)/shard_map/pallas_call | solution.py:34
  1.9 11.8 %all-to-all-start = ((bf16[64,4,192]{2,1,0:T(4,128)(2,1)}), bf16[64,4,192]{2,1,0:T(4,128)(2,1)S(1)}, u32[]{:S(2)}, u32[]{:S(2)}) async-start(bf16[64,4,192]{2,1,0:T(4,128)(2,1)} %shard_map.46), calls=%async_computation | async-start | bytes 262144 | tf_op jit(solution)/shard_map/all_to_all | solution.py:191
  13.8 1.3 %collective-permute-start.1 = (bf16[32,1536]{1,0:T(8,128)(2,1)S(1)}, bf16[32,1536]{1,0:T(8,128)(2,1)S(1)}, u32[]{:S(2)}, u32[]{:S(2)}) collective-permute-start(bf16[32,1536]{1,0:T(8,128)(2,1)S(1)} %get-tuple-element.11), channel_id=1, source_target_pairs={{64,0},{128,64},{192,128},{65,1},{129,65},{193,129},{66,2},{130,66... | collective-permute-start | bytes 294920 | tf_op jit(solution)/shard_map/ppermute | solution.py:188
  15.1 3.0 %collective-permute-start = (bf16[32,1536]{1,0:T(8,128)(2,1)S(1)}, bf16[32,1536]{1,0:T(8,128)(2,1)S(1)}, u32[]{:S(2)}, u32[]{:S(2)}) collective-permute-start(bf16[32,1536]{1,0:T(8,128)(2,1)S(1)} %get-tuple-element.12), channel_id=1, source_target_pairs={{0,64},{64,128},{128,192},{1,65},{65,129},{129,193},{2,66},{66,130... | collective-permute-start | bytes 294920 | tf_op jit(solution)/shard_map/ppermute | solution.py:187
  18.2 0.9 collective-permute-done.before_ref
  19.7 2.9 %shard_map.47 = bf16[8,672,128]{2,1,0:T(8,128)(2,1)} custom-call(bf16[128,1536]{1,0:T(8,128)(2,1)} %bitcast.20, bf16[128,1536]{1,0:T(8,128)(2,1)} %bitcast.21, bf16[128,1536]{1,0:T(8,128)(2,1)} %bitcast.17, bf16[32,1536]{1,0:T(8,128)(2,1)} %copy-done.5, bf16[32,1536]{1,0:T(8,128)(2,1)} %copy-done.4), custom_call_target="tpu_custom_call" | custom-call | flops 900000000 | bytes 6000000 | tf_op jit(solution)/shard_map/pallas_call | solution.py:34
  22.6 5.2 %all-to-all-start.1 = ((bf16[8,672,128]{2,1,0:T(8,128)(2,1)}), bf16[8,672,128]{2,1,0:T(8,128)(2,1)S(1)}, u32[]{:S(2)}, u32[]{:S(2)}) async-start(bf16[8,672,128]{2,1,0:T(8,128)(2,1)} %shard_map.47), calls=%async_computation.1 | async-start | bytes 2752512 | tf_op jit(solution)/shard_map/all_to_all | solution.py:196
  27.8 0.7 reshape.22.a_ref
  28.6 18.6 %all-to-all-done.1.x_ref = bf16[8,672,128]{2,1,0:T(8,128)(2,1)S(1)} async-done(((bf16[8,672,128]{2,1,0:T(8,128)(2,1)}), bf16[8,672,128]{2,1,0:T(8,128)(2,1)S(1)}, u32[]{:S(2)}, u32[]{:S(2)}) %all-to-all-start.1) | async-done | bytes 1376288 | tf_op jit(solution)/shard_map/all_to_all | solution.py:196
  47.2 1.1 copy-done.1
  48.2 3.8 %shard_map.48 = bf16[208,256]{1,0:T(8,128)(2,1)} custom-call(bf16[256,192]{1,0:T(8,128)(2,1)} %reshape.22.a_ref, bf16[8,672,128]{2,1,0:T(8,128)(2,1)} %copy-done.1), custom_call_target="tpu_custom_call" | custom-call | flops 1200000000 | bytes 8000000 | tf_op jit(solution)/shard_map/pallas_call | solution.py:34
  52.1 1.9 %broadcast_in_dim.2 = bf16[8,208,256]{2,1,0:T(8,128)(2,1)} broadcast(bf16[208,256]{1,0:T(8,128)(2,1)} %shard_map.48), dimensions={1,2} | broadcast | bytes 958464 | tf_op jit(solution)/shard_map/broadcast_in_dim | solution.py:204
  54.0 7.3 %all-to-all-start.2 = ((bf16[8,208,256]{2,1,0:T(8,128)(2,1)}), bf16[8,208,256]{2,1,0:T(8,128)(2,1)S(1)}, u32[]{:S(2)}, u32[]{:S(2)}) async-start(bf16[8,208,256]{2,1,0:T(8,128)(2,1)} %broadcast_in_dim.2), calls=%async_computation.2 | async-start | bytes 1703936 | tf_op jit(solution)/shard_map/all_to_all | solution.py:204
  61.4 0.8 copy.9
  62.2 0.9 slice_bitcast_fusion.2
  63.1 2.5 %collective-permute-start.3 = (bf16[288,128]{1,0:T(8,128)(2,1)S(1)}, bf16[288,128]{1,0:T(8,128)(2,1)S(1)}, u32[]{:S(2)}, u32[]{:S(2)}) collective-permute-start(bf16[288,128]{1,0:T(8,128)(2,1)S(1)} %get-tuple-element.9), channel_id=1, source_target_pairs={{8,0},{16,8},{24,16},{32,24},{40,32},{48,40},{56,48},{9,1},{17,9},... | collective-permute-start | bytes 221192 | tf_op jit(solution)/shard_map/ppermute | solution.py:199
  65.6 4.6 %collective-permute-start.2 = (bf16[288,128]{1,0:T(8,128)(2,1)S(1)}, bf16[288,128]{1,0:T(8,128)(2,1)S(1)}, u32[]{:S(2)}, u32[]{:S(2)}) collective-permute-start(bf16[288,128]{1,0:T(8,128)(2,1)S(1)} %get-tuple-element.10), channel_id=1, source_target_pairs={{0,8},{8,16},{16,24},{24,32},{32,40},{40,48},{48,56},{1,9},{9,17},... | collective-permute-start | bytes 221192 | tf_op jit(solution)/shard_map/ppermute | solution.py:198
  70.2 3.7 %shard_map.49 = (bf16[3,256,1024]{2,1,0:T(8,128)(2,1)}, f32[8,1024]{1,0:T(8,128)}) custom-call(bf16[256,192]{1,0:T(8,128)(2,1)} %reshape.22.a_ref, bf16[8,672,128]{2,1,0:T(8,128)(2,1)} %copy-done.1), custom_call_target="tpu_custom_call" | custom-call | flops 1200000000 | bytes 8000000 | tf_op jit(solution)/shard_map/pallas_call | solution.py:34
  73.9 10.5 %collective-permute-done.3.below_ref = bf16[288,128]{1,0:T(8,128)(2,1)S(1)} collective-permute-done((bf16[288,128]{1,0:T(8,128)(2,1)S(1)}, bf16[288,128]{1,0:T(8,128)(2,1)S(1)}, u32[]{:S(2)}, u32[]{:S(2)}) %collective-permute-start.3) | collective-permute-done | bytes 73760 | tf_op jit(solution)/shard_map/ppermute | solution.py:199
  85.1 5.9 %shard_map.50.local_ref = f32[8,192,128]{2,1,0:T(8,128)} custom-call(bf16[8,672,128]{2,1,0:T(8,128)(2,1)} %copy-done.1, bf16[288,128]{1,0:T(8,128)(2,1)} %copy-done.7, bf16[288,128]{1,0:T(8,128)(2,1)} %copy-done.6, f32[192,27]{1,0:T(8,128)} %bitcast.18), custom_call_target="tpu_custom_call" | custom-call | flops 1800000000 | bytes 12000000 | tf_op jit(solution)/shard_map/pallas_call | solution.py:34
  91.1 0.9 copy-done
  92.0 3.1 %shard_map.51 = bf16[8,192,128]{2,1,0:T(8,128)(2,1)} custom-call(bf16[8,208,256]{2,1,0:T(8,128)(2,1)} %copy-done, bf16[3,256,1024]{2,1,0:T(8,128)(2,1)} %get-tuple-element.7.e_ref, f32[8,1024]{1,0:T(8,128)} %get-tuple-element.8.total_ref, f32[8,192,128]{2,1,0:T(8,128)} %shard_map.50.local_ref), custom_call_target="tpu_custom_call" | custom-call | flops 900000000 | bytes 6000000 | tf_op jit(solution)/shard_map/pallas_call | solution.py:34
  95.1 12.2 %all_to_all.20.x_ref = bf16[8,192,128]{2,1,0:T(8,128)(2,1)} all-to-all(bf16[8,192,128]{2,1,0:T(8,128)(2,1)} %shard_map.51), channel_id=1, replica_groups=mesh['tm'=4,'z'=8,'xy'=8] {'xy'}, dimensions={0} | all-to-all | bytes 786432 | tf_op jit(solution)/shard_map/all_to_all | solution.py:231
  107.2 1.9 %shard_map.52 = bf16[128,1536]{1,0:T(8,128)(2,1)} custom-call(bf16[8,192,128]{2,1,0:T(8,128)(2,1)} %all_to_all.20.x_ref), custom_call_target="tpu_custom_call" | custom-call | flops 300000000 | bytes 2000000 | tf_op jit(solution)/shard_map/pallas_call | solution.py:34
  (21 shorter events, 1.5 us)
Async XLA Ops:
  0.0 13.8 %copy-start.3 = (bf16[1,4,1,32,1536]{4,3,2,1,0:T(8,128)(2,1)S(1)}, bf16[1,4,1,32,1536]{4,3,2,1,0:T(8,128)(2,1)}, u32[]{:S(2)}) copy-start(bf16[1,4,1,32,1536]{4,3,2,1,0:T(8,128)(2,1)} %param.6) | copy-start | bytes 1179652
  1.9 20.7 %all-to-all-start = ((bf16[64,4,192]{2,1,0:T(4,128)(2,1)}), bf16[64,4,192]{2,1,0:T(4,128)(2,1)S(1)}, u32[]{:S(2)}, u32[]{:S(2)}) async-start(bf16[64,4,192]{2,1,0:T(4,128)(2,1)} %shard_map.46), calls=%async_computation | async-start | bytes 262144 | tf_op jit(solution)/shard_map/all_to_all | solution.py:191
  13.8 4.3 %collective-permute-start.1 = (bf16[32,1536]{1,0:T(8,128)(2,1)S(1)}, bf16[32,1536]{1,0:T(8,128)(2,1)S(1)}, u32[]{:S(2)}, u32[]{:S(2)}) collective-permute-start(bf16[32,1536]{1,0:T(8,128)(2,1)S(1)} %get-tuple-element.11), channel_id=1, source_target_pairs={{64,0},{128,64},{192,128},{65,1},{129,65},{193,129},{66,2},{130,66... | collective-permute-start | bytes 294920 | tf_op jit(solution)/shard_map/ppermute | solution.py:188
  15.1 4.0 %collective-permute-start = (bf16[32,1536]{1,0:T(8,128)(2,1)S(1)}, bf16[32,1536]{1,0:T(8,128)(2,1)S(1)}, u32[]{:S(2)}, u32[]{:S(2)}) collective-permute-start(bf16[32,1536]{1,0:T(8,128)(2,1)S(1)} %get-tuple-element.12), channel_id=1, source_target_pairs={{0,64},{64,128},{128,192},{1,65},{65,129},{129,193},{2,66},{66,130... | collective-permute-start | bytes 294920 | tf_op jit(solution)/shard_map/ppermute | solution.py:187
  18.2 0.9 copy-start.4
  19.1 0.6 copy-start.5
  22.6 24.5 %all-to-all-start.1 = ((bf16[8,672,128]{2,1,0:T(8,128)(2,1)}), bf16[8,672,128]{2,1,0:T(8,128)(2,1)S(1)}, u32[]{:S(2)}, u32[]{:S(2)}) async-start(bf16[8,672,128]{2,1,0:T(8,128)(2,1)} %shard_map.47), calls=%async_computation.1 | async-start | bytes 2752512 | tf_op jit(solution)/shard_map/all_to_all | solution.py:196
  47.2 1.1 copy-start.1
  52.1 9.2 %copy-start.2 = (f32[3,3,3,1536]{3,2,1,0:T(4,128)S(1)}, f32[3,3,3,1536]{3,2,1,0:T(4,128)}, u32[]{:S(2)}) copy-start(f32[3,3,3,1536]{3,2,1,0:T(4,128)} %param.7) | copy-start | bytes 497668
  54.0 37.1 %all-to-all-start.2 = ((bf16[8,208,256]{2,1,0:T(8,128)(2,1)}), bf16[8,208,256]{2,1,0:T(8,128)(2,1)S(1)}, u32[]{:S(2)}, u32[]{:S(2)}) async-start(bf16[8,208,256]{2,1,0:T(8,128)(2,1)} %broadcast_in_dim.2), calls=%async_computation.2 | async-start | bytes 1703936 | tf_op jit(solution)/shard_map/all_to_all | solution.py:204
  63.1 21.4 %collective-permute-start.3 = (bf16[288,128]{1,0:T(8,128)(2,1)S(1)}, bf16[288,128]{1,0:T(8,128)(2,1)S(1)}, u32[]{:S(2)}, u32[]{:S(2)}) collective-permute-start(bf16[288,128]{1,0:T(8,128)(2,1)S(1)} %get-tuple-element.9), channel_id=1, source_target_pairs={{8,0},{16,8},{24,16},{32,24},{40,32},{48,40},{56,48},{9,1},{17,9},... | collective-permute-start | bytes 221192 | tf_op jit(solution)/shard_map/ppermute | solution.py:199
  65.6 18.9 %collective-permute-start.2 = (bf16[288,128]{1,0:T(8,128)(2,1)S(1)}, bf16[288,128]{1,0:T(8,128)(2,1)S(1)}, u32[]{:S(2)}, u32[]{:S(2)}) collective-permute-start(bf16[288,128]{1,0:T(8,128)(2,1)S(1)} %get-tuple-element.10), channel_id=1, source_target_pairs={{0,8},{8,16},{16,24},{24,32},{32,40},{40,48},{48,56},{1,9},{9,17},... | collective-permute-start | bytes 221192 | tf_op jit(solution)/shard_map/ppermute | solution.py:198
  84.4 0.6 copy-start.6
  84.5 0.7 copy-start.7
  91.0 0.9 copy-start

commit v2 on v1

v2 whole, which is shorter than its diff:
```python
import jax
import jax.numpy as jnp
from jax import lax
from jax.experimental import pallas as pl
from jax.experimental.pallas import tpu as pltpu
from jax.sharding import Mesh
from jax.sharding import PartitionSpec as P


HEADS = 24
HEAD_DIM = 64
D = 1536
FRAMES = 4
COLUMNS = 32
TOKENS = FRAMES * COLUMNS
AGENT_DEV = 4
PLANES = 8
TILES = 8
AGENTS = 256
GROUP_HEADS = HEADS // TILES
GROUP = GROUP_HEADS * HEAD_DIM
K_ROW = GROUP
V_ROW = 2 * GROUP
SENT = 3 * GROUP
PLANE_AGENTS = TILES * AGENT_DEV
EDGE_ROWS = TILES + 2
EDGE = 3 * TOKENS
STATS = 16
GRANT = 6 * 1024 * 1024
INV_ROOT = HEAD_DIM ** (-0.5)
F32 = jnp.float32
BF16 = jnp.bfloat16


VMEM = pl.BlockSpec(memory_space=pltpu.VMEM)

SMEM = pl.BlockSpec(memory_space=pltpu.SMEM)


def call(kernel, out_shape, us, *args, scalars=(), scratch=()):
    cost = pl.CostEstimate(flops=int(us * 3.0e8), bytes_accessed=int(us * 2.0e6), transcendentals=0)
    many = isinstance(out_shape, tuple)
    return pl.pallas_call(
        kernel,
        out_shape=out_shape,
        in_specs=[SMEM] * len(scalars) + [VMEM] * len(args),
        out_specs=(VMEM,) * len(out_shape) if many else VMEM,
        scratch_shapes=list(scratch),
        cost_estimate=cost,
        compiler_params=pltpu.CompilerParams(vmem_limit_bytes=GRANT),
    )(*scalars, *args)


def exchange(x, axes):
    return lax.all_to_all(x, axes, 0, 0)


def shift(x, axis, step):
    count = lax.axis_size(axis)
    pairs = [(i, i + step) for i in range(count) if 0 <= i + step < count]
    return lax.ppermute(x, axis, pairs)


def pool_kernel(q_ref, out_ref):
    shape = (8, TOKENS)
    token = lax.broadcasted_iota(jnp.int32, shape, 1)
    agent = lax.broadcasted_iota(jnp.int32, shape, 0)
    width = COLUMNS // AGENT_DEV
    pick = ((token % COLUMNS) // width == agent).astype(F32).astype(BF16)
    sums = jnp.dot(pick, q_ref[...], preferred_element_type=F32)
    pooled = (sums[:AGENT_DEV] * (1.0 / (FRAMES * width))).astype(BF16)
    for tile in range(TILES):
        out_ref[tile] = pooled[:, tile * GROUP : (tile + 1) * GROUP]


def pack_kernel(q_ref, k_ref, v_ref, out_ref):
    for row, ref in ((0, q_ref), (K_ROW, k_ref), (V_ROW, v_ref)):
        flipped = ref[...].T
        for tile in range(TILES):
            out_ref[tile, row : row + GROUP, :] = flipped[tile * GROUP : (tile + 1) * GROUP]


def rows_of(x_ref, start, size):
    return jnp.concatenate([x_ref[s, start : start + size, :] for s in range(TILES)], axis=1)


def agent_kernel(z_ref, *refs):
    came, (x_ref, out_ref, a_ref) = refs[:PLANES], refs[PLANES:]
    for hop, ref in enumerate(came):
        z = lax.rem(z_ref[0] + PLANES - hop, PLANES)
        a_ref[pl.ds(pl.multiple_of(z * PLANE_AGENTS, PLANE_AGENTS), PLANE_AGENTS), :] = ref[...]
    columns = []
    lane = lax.broadcasted_iota(jnp.int32, (AGENTS, HEAD_DIM), 1)
    stats = jnp.zeros((AGENTS, HEAD_DIM), F32)
    for h in range(GROUP_HEADS):
        keys = rows_of(x_ref, K_ROW + h * HEAD_DIM, HEAD_DIM)
        values = rows_of(x_ref, V_ROW + h * HEAD_DIM, HEAD_DIM)
        agents = a_ref[:, h * HEAD_DIM : (h + 1) * HEAD_DIM]
        scores = jnp.dot(agents, keys, preferred_element_type=F32) * INV_ROOT
        peak = jnp.max(scores, axis=1, keepdims=True)
        weights = jnp.exp(scores - peak)
        total = jnp.sum(weights, axis=1, keepdims=True)
        acc = lax.dot_general(
            weights.astype(BF16), values, (((1,), (1,)), ((), ())), preferred_element_type=F32
        )
        columns.append(acc / total)
        left = peak + jnp.log(total)
        for piece in range(3):
            short = left.astype(BF16).astype(F32)
            left = left - short
            stats = jnp.where(lane == piece * GROUP_HEADS + h, short, stats)
    flipped = jnp.concatenate(columns + [stats], axis=1).T
    part = flipped[: GROUP + STATS].astype(BF16)
    for z in range(PLANES):
        out_ref[z] = part


def query_kernel(a_ref, x_ref, e_ref, total_ref):
    for h in range(GROUP_HEADS):
        queries = rows_of(x_ref, h * HEAD_DIM, HEAD_DIM)
        agents = a_ref[:, h * HEAD_DIM : (h + 1) * HEAD_DIM]
        scores = jnp.dot(agents, queries, preferred_element_type=F32) * INV_ROOT
        weights = jnp.exp(scores - jnp.max(scores, axis=0, keepdims=True))
        total_ref[h : h + 1, :] = jnp.sum(weights, axis=0, keepdims=True)
        e_ref[h] = weights.astype(BF16)


def edge_kernel(x_ref, above_ref, below_ref, last_ref, first_ref):
    spot = lax.broadcasted_iota(jnp.int32, (GROUP, TOKENS), 1) // COLUMNS
    for block in range(EDGE // TOKENS):
        last = first = jnp.zeros((GROUP, TOKENS), F32)
        for j in range(FRAMES):
            row = block * FRAMES + j
            if row >= EDGE_ROWS:
                break
            if row == 0:
                cells = above_ref[...]
            elif row == EDGE_ROWS - 1:
                cells = below_ref[...]
            else:
                cells = x_ref[row - 1, V_ROW:, :]
            cells = cells.astype(F32)
            late = cells if j == FRAMES - 1 else pltpu.roll(cells, (j + 1) * COLUMNS, 1)
            early = cells if j == 0 else pltpu.roll(cells, j * COLUMNS, 1)
            last = jnp.where(spot == j, late, last)
            first = jnp.where(spot == j, early, first)
        lanes = slice(block * TOKENS, (block + 1) * TOKENS)
        last_ref[:, lanes] = last.astype(BF16)
        first_ref[:, lanes] = first.astype(BF16)


def conv_kernel(x_ref, above_ref, below_ref, before_ref, after_ref, w_ref, out_ref):
    tall = 16
    lane = lax.broadcasted_iota(jnp.int32, (tall, TOKENS), 1)
    column = lane % COLUMNS
    head, tail = lane < COLUMNS, lane >= TOKENS - COLUMNS

    def turned(cells, by):
        by %= TOKENS
        return cells if by == 0 else pltpu.roll(cells, by, 1)

    def frames_of(r, at):
        if r < 0:
            cells = above_ref[pl.ds(at, tall), :]
        elif r == TILES:
            cells = below_ref[pl.ds(at, tall), :]
        else:
            cells = x_ref[r, pl.ds(V_ROW + at, tall), :]
        cells = cells.astype(F32)
        block, j = divmod(r + 1, FRAMES)
        lanes = slice(block * TOKENS, (block + 1) * TOKENS)
        before = turned(before_ref[pl.ds(at, tall), lanes].astype(F32), -j * COLUMNS)
        after = turned(after_ref[pl.ds(at, tall), lanes].astype(F32), (FRAMES - 1 - j) * COLUMNS)
        return (
            jnp.where(head, before, turned(cells, COLUMNS)),
            cells,
            jnp.where(tail, after, turned(cells, -COLUMNS)),
        )

    def step(i, carry):
        at = pl.multiple_of(i * tall, tall)
        w = w_ref[pl.ds(at, tall), :]
        taps = [jnp.broadcast_to(w[:, n : n + 1], (tall, TOKENS)) for n in range(27)]
        rows = {r: frames_of(r, at) for r in range(-1, 1)}
        for r in range(TILES):
            rows[r + 1] = frames_of(r + 1, at)
            sums = []
            for k in range(3):
                total = None
                for j in range(3):
                    for i3 in range(3):
                        term = rows[r + j - 1][i3] * taps[i3 * 9 + j * 3 + k]
                        total = term if total is None else total + term
                sums.append(total)
            left = jnp.where(column == 0, 0.0, pltpu.roll(sums[0], 1, 1))
            right = jnp.where(column == COLUMNS - 1, 0.0, pltpu.roll(sums[2], TOKENS - 1, 1))
            out_ref[r, pl.ds(at, tall), :] = left + sums[1] + right
        return carry

    lax.fori_loop(0, GROUP // tall, step, 0)


def mix_kernel(parts_ref, e_ref, total_ref, local_ref, out_ref):
    logs = []
    for z in range(PLANES):
        pieces = parts_ref[z, GROUP : GROUP + STATS, :].astype(F32)
        n = GROUP_HEADS
        logs.append(pieces[:n] + pieces[n : 2 * n] + pieces[2 * n : 3 * n])
    peak = logs[0]
    for log in logs[1:]:
        peak = jnp.maximum(peak, log)
    shares = [jnp.exp(log - peak) for log in logs]
    whole = sum(shares[1:], shares[0])
    shares = [share / whole for share in shares]
    for h in range(GROUP_HEADS):
        rows = slice(h * HEAD_DIM, (h + 1) * HEAD_DIM)
        values = None
        for z in range(PLANES):
            term = parts_ref[z, rows, :].astype(F32) * shares[z][h : h + 1]
            values = term if values is None else values + term
        mixed = jnp.dot(values.astype(BF16), e_ref[h], preferred_element_type=F32)
        mixed = mixed / total_ref[h : h + 1, :]
        for s in range(TILES):
            cells = mixed[:, s * TOKENS : (s + 1) * TOKENS]
            out_ref[s, rows, :] = (cells + local_ref[s, rows, :]).astype(BF16)


def unpack_kernel(x_ref, out_ref):
    out_ref[...] = x_ref[...].reshape(D, TOKENS).T


def turn(x, axis, step):
    count = lax.axis_size(axis)
    return lax.ppermute(x, axis, [(i, (i + step) % count) for i in range(count)])


def body(queries, key_states, value_states, conv_weight):
    q = queries.reshape(TOKENS, D)
    k = key_states.reshape(TOKENS, D)
    v = value_states.reshape(TOKENS, D)
    shape = jax.ShapeDtypeStruct
    pooled = call(pool_kernel, shape((TILES, AGENT_DEV, GROUP), BF16), 1.0, q)
    packed = call(pack_kernel, shape((TILES, SENT, TOKENS), BF16), 3.0, q, k, v)
    own = exchange(pooled, "xy").reshape(PLANE_AGENTS, GROUP)
    x = exchange(packed, "xy")
    came = [own] + [turn(own, "z", n) for n in range(1, PLANES)]

    above = shift(x[TILES - 1, V_ROW:], "z", 1)
    below = shift(x[0, V_ROW:], "z", -1)

    part, agents = call(
        agent_kernel,
        (shape((PLANES, GROUP + STATS, AGENTS), BF16), shape((AGENTS, GROUP), BF16)),
        4.0,
        *came,
        x,
        scalars=(lax.axis_index("z").astype(jnp.int32).reshape(1),),
    )
    parts = exchange(part, "z")

    rim = shape((GROUP, EDGE), BF16)
    last, first = call(edge_kernel, (rim, rim), 1.0, x, above, below)
    before = shift(last, "tm", 1)
    after = shift(first, "tm", -1)
    weights, totals = call(
        query_kernel,
        (
            shape((GROUP_HEADS, AGENTS, TILES * TOKENS), BF16),
            shape((8, TILES * TOKENS), F32),
        ),
        4.0,
        agents,
        x,
    )
    taps = lax.dynamic_index_in_dim(
        conv_weight.reshape(27, TILES, GROUP), lax.axis_index("xy"), 1, keepdims=False
    ).T
    local = call(
        conv_kernel, shape((TILES, GROUP, TOKENS), F32), 6.0, x, above, below, before, after, taps
    )
    mixed = call(
        mix_kernel, shape((TILES, GROUP, TOKENS), BF16), 3.0, parts, weights, totals, local
    )
    mine = exchange(mixed, "xy")
    out = call(unpack_kernel, shape((TOKENS, D), BF16), 1.0, mine)
    return out.reshape(value_states.shape)


def solution(mesh):
    devices = mesh.devices
    fine = Mesh(devices.reshape(devices.shape[0], PLANES, TILES), ("tm", "z", "xy"))
    spec = P("tm", None, ("z", "xy"), None, None)
    return jax.shard_map(
        body,
        mesh=fine,
        in_specs=(spec, spec, spec, P()),
        out_specs=spec,
        check_vma=False,
    )
```

time: 110 us -> 97.9 us (0.89)
  the two profiles are of different devices: /device:TPU:96 before, /device:TPU:1 now
where the time goes in v2:
time: 97.9 us; the launch traced here: 97.3 us
  starting transfers between devices  50.4 us (51%)
  waiting for transfers between devices  17.5 us (18%)
  Pallas kernels  12.4 us (13%)
  blocking collectives  10.1 us (10%)
  local copies, waits for them, and re-layouts  6.86 us (7%)
    ppermute x4, starting transfers between devices, shift(): return lax.ppermute(x, axis, pairs)  17.7 us
    all_to_all x3, starting transfers between devices, exchange(): return lax.all_to_all(x, axes, 0, 0)  17.3 us
    ppermute x7, starting transfers between devices, turn(): lax.ppermute(x, axis, [(i, (i + step) % count) for i in range(count)])  15.3 us
    ppermute x4, waiting for transfers between devices, shift(): return lax.ppermute(x, axis, pairs)  14.4 us
    pallas_call x8, Pallas kernels, call(): pl.pallas_call(kernel, out_shape=out_shape, in_specs=[SMEM] * len(scalars...  12.4 us
    all_to_all x1, blocking collectives, exchange(): return lax.all_to_all(x, axes, 0, 0)  10.1 us
    unnamed x15, local copies, waits for them, and re-layouts  6.67 us
    ppermute x7, waiting for transfers between devices, turn(): lax.ppermute(x, axis, [(i, (i + step) % count) for i in range(count)])  2.43 us
  transfers between devices with their start and end apart: 14, of which 5 were waited for; matrix products, arithmetic and copies ran while one was open for 0% of the time, Pallas kernels for 8%

profile of v2, /device:TPU:1, one launch (start us, length us, event | category | flops | bytes accessed | tf_op | source)
XLA Modules:
  0.0 97.3 jit_solution(8385228740651611254)
XLA Ops:
  0.0 1.0 %copy-done.2 = bf16[1,4,1,32,1536]{4,3,2,1,0:T(8,128)(2,1)S(1)} copy-done((bf16[1,4,1,32,1536]{4,3,2,1,0:T(8,128)(2,1)S(1)}, bf16[1,4,1,32,1536]{4,3,2,1,0:T(8,128)(2,1)}, u32[]{:S(2)}) %copy-start.2) | copy-done | bytes 393240
  1.8 5.9 %all-to-all-start = ((bf16[8,4,192]{2,1,0:T(4,128)(2,1)}), bf16[8,4,192]{2,1,0:T(4,128)(2,1)S(1)}, u32[]{:S(2)}, u32[]{:S(2)}) async-start(bf16[8,4,192]{2,1,0:T(4,128)(2,1)} %shard_map.46), calls=%async_computation | async-start | bytes 32768 | tf_op jit(solution)/shard_map/all_to_all | solution.py:55
  8.8 1.0 %copy-done.4 = bf16[1,4,1,32,1536]{4,3,2,1,0:T(8,128)(2,1)S(1)} copy-done((bf16[1,4,1,32,1536]{4,3,2,1,0:T(8,128)(2,1)S(1)}, bf16[1,4,1,32,1536]{4,3,2,1,0:T(8,128)(2,1)}, u32[]{:S(2)}) %copy-start.4) | copy-done | bytes 393240
  10.8 1.4 %shard_map.47 = bf16[8,576,128]{2,1,0:T(8,128)(2,1)} custom-call(bf16[128,1536]{1,0:T(8,128)(2,1)S(1)} %bitcast.16, bf16[128,1536]{1,0:T(8,128)(2,1)S(1)} %bitcast.17, bf16[128,1536]{1,0:T(8,128)(2,1)S(1)} %bitcast.18), custom_call_target="tpu_custom_call" | custom-call | flops 900000000 | bytes 6000000 | tf_op jit(solution)/shard_map/pallas_call | solution.py:43
  12.8 4.5 %all-to-all-start.1 = ((bf16[8,576,128]{2,1,0:T(8,128)(2,1)}), bf16[8,576,128]{2,1,0:T(8,128)(2,1)S(1)}, u32[]{:S(2)}, u32[]{:S(2)}) async-start(bf16[8,576,128]{2,1,0:T(8,128)(2,1)} %shard_map.47), calls=%async_computation.1 | async-start | bytes 2359296 | tf_op jit(solution)/shard_map/all_to_all | solution.py:55
  17.3 5.7 %collective-permute-start.6 = (bf16[32,192]{1,0:T(8,128)(2,1)S(1)}, bf16[32,192]{1,0:T(8,128)(2,1)S(1)}, u32[]{:S(2)}, u32[]{:S(2)}) collective-permute-start(bf16[32,192]{1,0:T(8,128)(2,1)S(1)} %reshape.23.refs_0_), channel_id=1, source_target_pairs={{0,56},{8,0},{16,8},{24,16},{32,24},{40,32},{48,40},{56,48},{1,57}... | collective-permute-start | bytes 36872 | tf_op jit(solution)/shard_map/ppermute | solution.py:234
  23.0 1.2 %collective-permute-start.5 = (bf16[32,192]{1,0:T(8,128)(2,1)S(1)}, bf16[32,192]{1,0:T(8,128)(2,1)S(1)}, u32[]{:S(2)}, u32[]{:S(2)}) collective-permute-start(bf16[32,192]{1,0:T(8,128)(2,1)S(1)} %reshape.23.refs_0_), channel_id=1, source_target_pairs={{0,48},{8,56},{16,0},{24,8},{32,16},{40,24},{48,32},{56,40},{1,49}... | collective-permute-start | bytes 36872 | tf_op jit(solution)/shard_map/ppermute | solution.py:234
  24.6 4.5 %collective-permute-start.3 = (bf16[32,192]{1,0:T(8,128)(2,1)S(1)}, bf16[32,192]{1,0:T(8,128)(2,1)S(1)}, u32[]{:S(2)}, u32[]{:S(2)}) collective-permute-start(bf16[32,192]{1,0:T(8,128)(2,1)S(1)} %reshape.23.refs_0_), channel_id=1, source_target_pairs={{0,32},{8,40},{16,48},{24,56},{32,0},{40,8},{48,16},{56,24},{1,33}... | collective-permute-start | bytes 36872 | tf_op jit(solution)/shard_map/ppermute | solution.py:234
  29.1 2.2 %collective-permute-start.1 = (bf16[32,192]{1,0:T(8,128)(2,1)S(1)}, bf16[32,192]{1,0:T(8,128)(2,1)S(1)}, u32[]{:S(2)}, u32[]{:S(2)}) collective-permute-start(bf16[32,192]{1,0:T(8,128)(2,1)S(1)} %reshape.23.refs_0_), channel_id=1, source_target_pairs={{0,16},{8,24},{16,32},{24,40},{32,48},{40,56},{48,0},{56,8},{1,17}... | collective-permute-start | bytes 36872 | tf_op jit(solution)/shard_map/ppermute | solution.py:234
  31.3 1.4 %collective-permute-start = (bf16[32,192]{1,0:T(8,128)(2,1)S(1)}, bf16[32,192]{1,0:T(8,128)(2,1)S(1)}, u32[]{:S(2)}, u32[]{:S(2)}) collective-permute-start(bf16[32,192]{1,0:T(8,128)(2,1)S(1)} %reshape.23.refs_0_), channel_id=1, source_target_pairs={{0,8},{8,16},{16,24},{24,32},{32,40},{40,48},{48,56},{56,0},{1,9},... | collective-permute-start | bytes 36872 | tf_op jit(solution)/shard_map/ppermute | solution.py:234
  32.7 2.1 %collective-permute-done.2.refs_3_ = bf16[32,192]{1,0:T(8,128)(2,1)S(1)} collective-permute-done((bf16[32,192]{1,0:T(8,128)(2,1)S(1)}, bf16[32,192]{1,0:T(8,128)(2,1)S(1)}, u32[]{:S(2)}, u32[]{:S(2)}) %collective-permute-start.2) | collective-permute-done | bytes 12320 | tf_op jit(solution)/shard_map/ppermute | solution.py:234
  35.1 2.7 %shard_map.48 = (bf16[8,208,256]{2,1,0:T(8,128)(2,1)}, bf16[256,192]{1,0:T(8,128)(2,1)S(1)}) custom-call(s32[1]{0:T(128)} %bitcast.z_ref, bf16[32,192]{1,0:T(8,128)(2,1)S(1)} %reshape.23.refs_0_, bf16[32,192]{1,0:T(8,128)(2,1)S(1)} %collective-permute-done.refs_1_, bf16[32,192]{1,0:T(8,128)(2,1)S(1)} %collective-permute-done.1.refs_2_, ...), custom_call_target="tpu_custom_call" | custom-call | flops 1200000000 | bytes 8000000 | tf_op jit(solution)/shard_map/pallas_call | solution.py:43
  37.8 6.9 %all-to-all-start.2 = ((bf16[8,208,256]{2,1,0:T(8,128)(2,1)}), bf16[8,208,256]{2,1,0:T(8,128)(2,1)S(1)}, u32[]{:S(2)}, u32[]{:S(2)}) async-start(bf16[8,208,256]{2,1,0:T(8,128)(2,1)} %get-tuple-element.11), calls=%async_computation.2 | async-start | bytes 1703936 | tf_op jit(solution)/shard_map/all_to_all | solution.py:55
  44.7 1.3 %collective-permute-start.8 = (bf16[192,128]{1,0:T(8,128)(2,1)S(1)}, bf16[192,128]{1,0:T(8,128)(2,1)S(1)}, u32[]{:S(2)}, u32[]{:S(2)}) collective-permute-start(bf16[192,128]{1,0:T(8,128)(2,1)S(1)} %get-tuple-element.17), channel_id=1, source_target_pairs={{8,0},{16,8},{24,16},{32,24},{40,32},{48,40},{56,48},{9,1},{17,9},... | collective-permute-start | bytes 147464 | tf_op jit(solution)/shard_map/ppermute | solution.py:61
  46.0 4.0 %collective-permute-start.7 = (bf16[192,128]{1,0:T(8,128)(2,1)S(1)}, bf16[192,128]{1,0:T(8,128)(2,1)S(1)}, u32[]{:S(2)}, u32[]{:S(2)}) collective-permute-start(bf16[192,128]{1,0:T(8,128)(2,1)S(1)} %get-tuple-element.18), channel_id=1, source_target_pairs={{0,8},{8,16},{16,24},{24,32},{32,40},{40,48},{48,56},{1,9},{9,17},... | collective-permute-start | bytes 147464 | tf_op jit(solution)/shard_map/ppermute | solution.py:61
  50.2 10.9 %collective-permute-done.8.below_ref = bf16[192,128]{1,0:T(8,128)(2,1)S(1)} collective-permute-done((bf16[192,128]{1,0:T(8,128)(2,1)S(1)}, bf16[192,128]{1,0:T(8,128)(2,1)S(1)}, u32[]{:S(2)}, u32[]{:S(2)}) %collective-permute-start.8) | collective-permute-done | bytes 49184 | tf_op jit(solution)/shard_map/ppermute | solution.py:61
  61.3 10.5 %collective-permute-start.9 = (bf16[192,384]{1,0:T(8,128)(2,1)S(1)}, bf16[192,384]{1,0:T(8,128)(2,1)S(1)}, u32[]{:S(2)}, u32[]{:S(2)}) collective-permute-start(bf16[192,384]{1,0:T(8,128)(2,1)S(1)} %get-tuple-element.15), channel_id=1, source_target_pairs={{0,64},{64,128},{128,192},{1,65},{65,129},{129,193},{2,66},{66,130... | collective-permute-start | bytes 442376 | tf_op jit(solution)/shard_map/ppermute | solution.py:61
  71.9 1.9 %collective-permute-start.10 = (bf16[192,384]{1,0:T(8,128)(2,1)S(1)}, bf16[192,384]{1,0:T(8,128)(2,1)S(1)}, u32[]{:S(2)}, u32[]{:S(2)}) collective-permute-start(bf16[192,384]{1,0:T(8,128)(2,1)S(1)} %get-tuple-element.16), channel_id=1, source_target_pairs={{64,0},{128,64},{192,128},{65,1},{129,65},{193,129},{66,2},{130,66... | collective-permute-start | bytes 442376 | tf_op jit(solution)/shard_map/ppermute | solution.py:61
  73.9 1.2 %shard_map.49 = (bf16[3,256,1024]{2,1,0:T(8,128)(2,1)S(1)}, f32[8,1024]{1,0:T(8,128)S(1)}) custom-call(bf16[256,192]{1,0:T(8,128)(2,1)S(1)} %get-tuple-element.12.a_ref, bf16[8,576,128]{2,1,0:T(8,128)(2,1)S(1)} %all-to-all-done.1.refs_8_.x_ref), custom_call_target="tpu_custom_call" | custom-call | flops 1200000000 | bytes 8000000 | tf_op jit(solution)/shard_map/pallas_call | solution.py:43
  75.1 1.2 %copy-done = bf16[3,256,1024]{2,1,0:T(8,128)(2,1)} copy-done((bf16[3,256,1024]{2,1,0:T(8,128)(2,1)}, bf16[3,256,1024]{2,1,0:T(8,128)(2,1)S(1)}, u32[]{:S(2)}) %copy-start) | copy-done | bytes 1572888
  76.3 3.5 %collective-permute-done.10.after_ref = bf16[192,384]{1,0:T(8,128)(2,1)S(1)} collective-permute-done((bf16[192,384]{1,0:T(8,128)(2,1)S(1)}, bf16[192,384]{1,0:T(8,128)(2,1)S(1)}, u32[]{:S(2)}, u32[]{:S(2)}) %collective-permute-start.10) | collective-permute-done | bytes 147488 | tf_op jit(solution)/shard_map/ppermute | solution.py:61
  79.8 4.6 %shard_map.51.local_ref = f32[8,192,128]{2,1,0:T(8,128)S(1)} custom-call(bf16[8,576,128]{2,1,0:T(8,128)(2,1)S(1)} %all-to-all-done.1.refs_8_.x_ref, bf16[192,128]{1,0:T(8,128)(2,1)S(1)} %collective-permute-done.7.above_ref, bf16[192,128]{1,0:T(8,128)(2,1)S(1)} %collective-permute-done.8.below_ref, bf16[192,384]{1,0:T(8,128)(2,1)S(1)} %collective-permute-done.9.before_ref, ...), custom_call_target="tpu_custom_call" | custom-call | flops 1800000000 | bytes 12000000 | tf_op jit(solution)/shard_map/pallas_call | solution.py:43
  84.4 1.4 %copy-done.1 = bf16[3,256,1024]{2,1,0:T(8,128)(2,1)S(1)} copy-done((bf16[3,256,1024]{2,1,0:T(8,128)(2,1)S(1)}, bf16[3,256,1024]{2,1,0:T(8,128)(2,1)}, u32[]{:S(2)}) %copy-start.1) | copy-done | bytes 1572888
  86.3 10.1 %all_to_all.20.x_ref = bf16[8,192,128]{2,1,0:T(8,128)(2,1)S(1)} all-to-all(bf16[8,192,128]{2,1,0:T(8,128)(2,1)S(1)} %shard_map.52), channel_id=1, replica_groups=mesh['tm'=4,'z'=8,'xy'=8] {'xy'}, dimensions={0} | all-to-all | bytes 786432 | tf_op jit(solution)/shard_map/all_to_all | solution.py:55
  (32 shorter events, 6.3 us)
Async XLA Ops:
  0.0 1.0 %copy-start.2 = (bf16[1,4,1,32,1536]{4,3,2,1,0:T(8,128)(2,1)S(1)}, bf16[1,4,1,32,1536]{4,3,2,1,0:T(8,128)(2,1)}, u32[]{:S(2)}) copy-start(bf16[1,4,1,32,1536]{4,3,2,1,0:T(8,128)(2,1)} %param.4) | copy-start | bytes 1179652
  1.8 11.0 %all-to-all-start = ((bf16[8,4,192]{2,1,0:T(4,128)(2,1)}), bf16[8,4,192]{2,1,0:T(4,128)(2,1)S(1)}, u32[]{:S(2)}, u32[]{:S(2)}) async-start(bf16[8,4,192]{2,1,0:T(4,128)(2,1)} %shard_map.46), calls=%async_computation | async-start | bytes 32768 | tf_op jit(solution)/shard_map/all_to_all | solution.py:55
  7.8 1.0 %copy-start.3 = (bf16[1,4,1,32,1536]{4,3,2,1,0:T(8,128)(2,1)S(1)}, bf16[1,4,1,32,1536]{4,3,2,1,0:T(8,128)(2,1)}, u32[]{:S(2)}) copy-start(bf16[1,4,1,32,1536]{4,3,2,1,0:T(8,128)(2,1)} %param.4) | copy-start | bytes 1179652
  8.8 1.0 %copy-start.4 = (bf16[1,4,1,32,1536]{4,3,2,1,0:T(8,128)(2,1)S(1)}, bf16[1,4,1,32,1536]{4,3,2,1,0:T(8,128)(2,1)}, u32[]{:S(2)}) copy-start(bf16[1,4,1,32,1536]{4,3,2,1,0:T(8,128)(2,1)} %param.5) | copy-start | bytes 1179652
  9.8 1.0 %copy-start.5 = (bf16[1,4,1,32,1536]{4,3,2,1,0:T(8,128)(2,1)S(1)}, bf16[1,4,1,32,1536]{4,3,2,1,0:T(8,128)(2,1)}, u32[]{:S(2)}) copy-start(bf16[1,4,1,32,1536]{4,3,2,1,0:T(8,128)(2,1)} %param.6) | copy-start | bytes 1179652
  12.8 22.2 %all-to-all-start.1 = ((bf16[8,576,128]{2,1,0:T(8,128)(2,1)}), bf16[8,576,128]{2,1,0:T(8,128)(2,1)S(1)}, u32[]{:S(2)}, u32[]{:S(2)}) async-start(bf16[8,576,128]{2,1,0:T(8,128)(2,1)} %shard_map.47), calls=%async_computation.1 | async-start | bytes 2359296 | tf_op jit(solution)/shard_map/all_to_all | solution.py:55
  17.3 11.8 %collective-permute-start.6 = (bf16[32,192]{1,0:T(8,128)(2,1)S(1)}, bf16[32,192]{1,0:T(8,128)(2,1)S(1)}, u32[]{:S(2)}, u32[]{:S(2)}) collective-permute-start(bf16[32,192]{1,0:T(8,128)(2,1)S(1)} %reshape.23.refs_0_), channel_id=1, source_target_pairs={{0,56},{8,0},{16,8},{24,16},{32,24},{40,32},{48,40},{56,48},{1,57}... | collective-permute-start | bytes 36872 | tf_op jit(solution)/shard_map/ppermute | solution.py:234
  23.0 8.3 %collective-permute-start.5 = (bf16[32,192]{1,0:T(8,128)(2,1)S(1)}, bf16[32,192]{1,0:T(8,128)(2,1)S(1)}, u32[]{:S(2)}, u32[]{:S(2)}) collective-permute-start(bf16[32,192]{1,0:T(8,128)(2,1)S(1)} %reshape.23.refs_0_), channel_id=1, source_target_pairs={{0,48},{8,56},{16,0},{24,8},{32,16},{40,24},{48,32},{56,40},{1,49}... | collective-permute-start | bytes 36872 | tf_op jit(solution)/shard_map/ppermute | solution.py:234
  24.2 8.5 %collective-permute-start.4 = (bf16[32,192]{1,0:T(8,128)(2,1)S(1)}, bf16[32,192]{1,0:T(8,128)(2,1)S(1)}, u32[]{:S(2)}, u32[]{:S(2)}) collective-permute-start(bf16[32,192]{1,0:T(8,128)(2,1)S(1)} %reshape.23.refs_0_), channel_id=1, source_target_pairs={{0,40},{8,48},{16,56},{24,0},{32,8},{40,16},{48,24},{56,32},{1,41}... | collective-permute-start | bytes 36872 | tf_op jit(solution)/shard_map/ppermute | solution.py:234
  24.6 8.0 %collective-permute-start.3 = (bf16[32,192]{1,0:T(8,128)(2,1)S(1)}, bf16[32,192]{1,0:T(8,128)(2,1)S(1)}, u32[]{:S(2)}, u32[]{:S(2)}) collective-permute-start(bf16[32,192]{1,0:T(8,128)(2,1)S(1)} %reshape.23.refs_0_), channel_id=1, source_target_pairs={{0,32},{8,40},{16,48},{24,56},{32,0},{40,8},{48,16},{56,24},{1,33}... | collective-permute-start | bytes 36872 | tf_op jit(solution)/shard_map/ppermute | solution.py:234
  29.1 5.6 %collective-permute-start.2 = (bf16[32,192]{1,0:T(8,128)(2,1)S(1)}, bf16[32,192]{1,0:T(8,128)(2,1)S(1)}, u32[]{:S(2)}, u32[]{:S(2)}) collective-permute-start(bf16[32,192]{1,0:T(8,128)(2,1)S(1)} %reshape.23.refs_0_), channel_id=1, source_target_pairs={{0,24},{8,32},{16,40},{24,48},{32,56},{40,0},{48,8},{56,16},{1,25}... | collective-permute-start | bytes 36872 | tf_op jit(solution)/shard_map/ppermute | solution.py:234
  29.1 5.6 %collective-permute-start.1 = (bf16[32,192]{1,0:T(8,128)(2,1)S(1)}, bf16[32,192]{1,0:T(8,128)(2,1)S(1)}, u32[]{:S(2)}, u32[]{:S(2)}) collective-permute-start(bf16[32,192]{1,0:T(8,128)(2,1)S(1)} %reshape.23.refs_0_), channel_id=1, source_target_pairs={{0,16},{8,24},{16,32},{24,40},{32,48},{40,56},{48,0},{56,8},{1,17}... | collective-permute-start | bytes 36872 | tf_op jit(solution)/shard_map/ppermute | solution.py:234
  31.3 3.8 %collective-permute-start = (bf16[32,192]{1,0:T(8,128)(2,1)S(1)}, bf16[32,192]{1,0:T(8,128)(2,1)S(1)}, u32[]{:S(2)}, u32[]{:S(2)}) collective-permute-start(bf16[32,192]{1,0:T(8,128)(2,1)S(1)} %reshape.23.refs_0_), channel_id=1, source_target_pairs={{0,8},{8,16},{16,24},{24,32},{32,40},{40,48},{48,56},{56,0},{1,9},... | collective-permute-start | bytes 36872 | tf_op jit(solution)/shard_map/ppermute | solution.py:234
  37.8 12.2 %copy-start.6 = (f32[3,3,3,1536]{3,2,1,0:T(4,128)S(1)}, f32[3,3,3,1536]{3,2,1,0:T(4,128)}, u32[]{:S(2)}) copy-start(f32[3,3,3,1536]{3,2,1,0:T(4,128)} %param.7) | copy-start | bytes 497668
  37.8 46.6 %all-to-all-start.2 = ((bf16[8,208,256]{2,1,0:T(8,128)(2,1)}), bf16[8,208,256]{2,1,0:T(8,128)(2,1)S(1)}, u32[]{:S(2)}, u32[]{:S(2)}) async-start(bf16[8,208,256]{2,1,0:T(8,128)(2,1)} %get-tuple-element.11), calls=%async_computation.2 | async-start | bytes 1703936 | tf_op jit(solution)/shard_map/all_to_all | solution.py:55
  44.7 16.3 %collective-permute-start.8 = (bf16[192,128]{1,0:T(8,128)(2,1)S(1)}, bf16[192,128]{1,0:T(8,128)(2,1)S(1)}, u32[]{:S(2)}, u32[]{:S(2)}) collective-permute-start(bf16[192,128]{1,0:T(8,128)(2,1)S(1)} %get-tuple-element.17), channel_id=1, source_target_pairs={{8,0},{16,8},{24,16},{32,24},{40,32},{48,40},{56,48},{9,1},{17,9},... | collective-permute-start | bytes 147464 | tf_op jit(solution)/shard_map/ppermute | solution.py:61
  46.0 15.0 %collective-permute-start.7 = (bf16[192,128]{1,0:T(8,128)(2,1)S(1)}, bf16[192,128]{1,0:T(8,128)(2,1)S(1)}, u32[]{:S(2)}, u32[]{:S(2)}) collective-permute-start(bf16[192,128]{1,0:T(8,128)(2,1)S(1)} %get-tuple-element.18), channel_id=1, source_target_pairs={{0,8},{8,16},{16,24},{24,32},{32,40},{40,48},{48,56},{1,9},{9,17},... | collective-permute-start | bytes 147464 | tf_op jit(solution)/shard_map/ppermute | solution.py:61
  61.3 15.0 %collective-permute-start.9 = (bf16[192,384]{1,0:T(8,128)(2,1)S(1)}, bf16[192,384]{1,0:T(8,128)(2,1)S(1)}, u32[]{:S(2)}, u32[]{:S(2)}) collective-permute-start(bf16[192,384]{1,0:T(8,128)(2,1)S(1)} %get-tuple-element.15), channel_id=1, source_target_pairs={{0,64},{64,128},{128,192},{1,65},{65,129},{129,193},{2,66},{66,130... | collective-permute-start | bytes 442376 | tf_op jit(solution)/shard_map/ppermute | solution.py:61
  71.9 8.0 %collective-permute-start.10 = (bf16[192,384]{1,0:T(8,128)(2,1)S(1)}, bf16[192,384]{1,0:T(8,128)(2,1)S(1)}, u32[]{:S(2)}, u32[]{:S(2)}) collective-permute-start(bf16[192,384]{1,0:T(8,128)(2,1)S(1)} %get-tuple-element.16), channel_id=1, source_target_pairs={{64,0},{128,64},{192,128},{65,1},{129,65},{193,129},{66,2},{130,66... | collective-permute-start | bytes 442376 | tf_op jit(solution)/shard_map/ppermute | solution.py:61
  75.1 1.2 %copy-start = (bf16[3,256,1024]{2,1,0:T(8,128)(2,1)}, bf16[3,256,1024]{2,1,0:T(8,128)(2,1)S(1)}, u32[]{:S(2)}) copy-start(bf16[3,256,1024]{2,1,0:T(8,128)(2,1)S(1)} %get-tuple-element.13.e_ref) | copy-start | bytes 4718596
  84.4 1.4 %copy-start.1 = (bf16[3,256,1024]{2,1,0:T(8,128)(2,1)S(1)}, bf16[3,256,1024]{2,1,0:T(8,128)(2,1)}, u32[]{:S(2)}) copy-start(bf16[3,256,1024]{2,1,0:T(8,128)(2,1)} %copy-done) | copy-start | bytes 4718596

commit v3 on v2

--- a/solution.py
+++ b/solution.py
@@ -27,6 +27,7 @@
 EDGE = 3 * TOKENS
 STATS = 16
 GRANT = 6 * 1024 * 1024
+ALL = 60 * 1024 * 1024
 INV_ROOT = HEAD_DIM ** (-0.5)
 F32 = jnp.float32
 BF16 = jnp.bfloat16
@@ -35,19 +36,20 @@
 VMEM = pl.BlockSpec(memory_space=pltpu.VMEM)
 
 SMEM = pl.BlockSpec(memory_space=pltpu.SMEM)
-
-
-def call(kernel, out_shape, us, *args, scalars=(), scratch=()):
+HBM = pl.BlockSpec(memory_space=pltpu.HBM)
+
+
+def call(kernel, out_shape, us, *args, scalars=(), scratch=(), far=False):
     cost = pl.CostEstimate(flops=int(us * 3.0e8), bytes_accessed=int(us * 2.0e6), transcendentals=0)
     many = isinstance(out_shape, tuple)
     return pl.pallas_call(
         kernel,
         out_shape=out_shape,
-        in_specs=[SMEM] * len(scalars) + [VMEM] * len(args),
-        out_specs=(VMEM,) * len(out_shape) if many else VMEM,
+        in_specs=[SMEM] * len(scalars) + [HBM if far else VMEM] * len(args),
+        out_specs=(VMEM,) * len(out_shape) if many else HBM if far else VMEM,
         scratch_shapes=list(scratch),
         cost_estimate=cost,
-        compiler_params=pltpu.CompilerParams(vmem_limit_bytes=GRANT),
+        compiler_params=pltpu.CompilerParams(vmem_limit_bytes=ALL if far else GRANT),
     )(*scalars, *args)
 
 
@@ -73,11 +75,23 @@
         out_ref[tile] = pooled[:, tile * GROUP : (tile + 1) * GROUP]
 
 
-def pack_kernel(q_ref, k_ref, v_ref, out_ref):
-    for row, ref in ((0, q_ref), (K_ROW, k_ref), (V_ROW, v_ref)):
-        flipped = ref[...].T
+def pack_kernel(q_ref, k_ref, v_ref, out_ref, came, turned, in_sems, out_sems):
+    refs = (q_ref, k_ref, v_ref)
+    loads = [pltpu.make_async_copy(ref, came.at[n], in_sems.at[n]) for n, ref in enumerate(refs)]
+    for load in loads:
+        load.start()
+    stores = []
+    for n, load in enumerate(loads):
+        load.wait()
+        flipped = came[n].T
         for tile in range(TILES):
-            out_ref[tile, row : row + GROUP, :] = flipped[tile * GROUP : (tile + 1) * GROUP]
+            turned[n, tile] = flipped[tile * GROUP : (tile + 1) * GROUP]
+        rows = pl.ds(n * GROUP, GROUP)
+        store = pltpu.make_async_copy(turned.at[n], out_ref.at[:, rows, :], out_sems.at[n])
+        store.start()
+        stores.append(store)
+    for store in stores:
+        store.wait()
 
 
 def rows_of(x_ref, start, size):
@@ -115,14 +129,15 @@
         out_ref[z] = part
 
 
-def query_kernel(a_ref, x_ref, e_ref, total_ref):
+def query_kernel(a_ref, x_ref, *refs):
+    e_refs, total_ref = refs[:GROUP_HEADS], refs[GROUP_HEADS]
     for h in range(GROUP_HEADS):
         queries = rows_of(x_ref, h * HEAD_DIM, HEAD_DIM)
         agents = a_ref[:, h * HEAD_DIM : (h + 1) * HEAD_DIM]
         scores = jnp.dot(agents, queries, preferred_element_type=F32) * INV_ROOT
         weights = jnp.exp(scores - jnp.max(scores, axis=0, keepdims=True))
         total_ref[h : h + 1, :] = jnp.sum(weights, axis=0, keepdims=True)
-        e_ref[h] = weights.astype(BF16)
+        e_refs[h][...] = weights.astype(BF16)
 
 
 def edge_kernel(x_ref, above_ref, below_ref, last_ref, first_ref):
@@ -200,7 +215,8 @@
     lax.fori_loop(0, GROUP // tall, step, 0)
 
 
-def mix_kernel(parts_ref, e_ref, total_ref, local_ref, out_ref):
+def mix_kernel(parts_ref, *refs):
+    e_refs, (total_ref, local_ref, out_ref) = refs[:GROUP_HEADS], refs[GROUP_HEADS:]
     logs = []
     for z in range(PLANES):
         pieces = parts_ref[z, GROUP : GROUP + STATS, :].astype(F32)
@@ -218,7 +234,7 @@
         for z in range(PLANES):
             term = parts_ref[z, rows, :].astype(F32) * shares[z][h : h + 1]
             values = term if values is None else values + term
-        mixed = jnp.dot(values.astype(BF16), e_ref[h], preferred_element_type=F32)
+        mixed = jnp.dot(values.astype(BF16), e_refs[h][...], preferred_element_type=F32)
         mixed = mixed / total_ref[h : h + 1, :]
         for s in range(TILES):
             cells = mixed[:, s * TOKENS : (s + 1) * TOKENS]
@@ -240,7 +256,21 @@
     v = value_states.reshape(TOKENS, D)
     shape = jax.ShapeDtypeStruct
     pooled = call(pool_kernel, shape((TILES, AGENT_DEV, GROUP), BF16), 1.0, q)
-    packed = call(pack_kernel, shape((TILES, SENT, TOKENS), BF16), 3.0, q, k, v)
+    packed = call(
+        pack_kernel,
+        shape((TILES, SENT, TOKENS), BF16),
+        3.0,
+        q,
+        k,
+        v,
+        scratch=(
+            pltpu.VMEM((3, TOKENS, D), BF16),
+            pltpu.VMEM((3, TILES, GROUP, TOKENS), BF16),
+            pltpu.SemaphoreType.DMA((3,)),
+            pltpu.SemaphoreType.DMA((3,)),
+        ),
+        far=True,
+    )
     own = exchange(pooled, "xy").reshape(PLANE_AGENTS, GROUP)
     x = exchange(packed, "xy")
     came = [own] + [turn(own, "z", n) for n in range(1, PLANES)]
@@ -262,10 +292,10 @@
     last, first = call(edge_kernel, (rim, rim), 1.0, x, above, below)
     before = shift(last, "tm", 1)
     after = shift(first, "tm", -1)
-    weights, totals = call(
+    *weights, totals = call(
         query_kernel,
         (
-            shape((GROUP_HEADS, AGENTS, TILES * TOKENS), BF16),
+            *(shape((AGENTS, TILES * TOKENS), BF16) for _ in range(GROUP_HEADS)),
             shape((8, TILES * TOKENS), F32),
         ),
         4.0,
@@ -279,7 +309,7 @@
         conv_kernel, shape((TILES, GROUP, TOKENS), F32), 6.0, x, above, below, before, after, taps
     )
     mixed = call(
-        mix_kernel, shape((TILES, GROUP, TOKENS), BF16), 3.0, parts, weights, totals, local
+        mix_kernel, shape((TILES, GROUP, TOKENS), BF16), 3.0, parts, *weights, totals, local
     )
     mine = exchange(mixed, "xy")
     out = call(unpack_kernel, shape((TOKENS, D), BF16), 1.0, mine)

time: 97.9 us -> 102 us (1.042)
  local copies, waits for them, and re-layouts: 6.86 us -> 9.51 us
  Pallas kernels: 12.4 us -> 14.8 us
  waiting for transfers between devices: 17.5 us -> 16.4 us
    ppermute x4, waiting for transfers between devices: 14.4 us -> 10.9 us  [shift(): return lax.ppermute(x, axis, pairs)]
    unnamed x15 -> x25, local copies, waits for them, and re-layouts: 6.67 us -> 9.31 us
    pallas_call x8, Pallas kernels: 12.4 us -> 14.8 us  [call(): pl.pallas_call(kernel, out_shape=out_shape, in_specs=[SMEM] * len(scalars...]
    all_to_all x3, waiting for transfers between devices: 0.68 us -> 2.79 us  [exchange(): return lax.all_to_all(x, axes, 0, 0)]
    all_to_all x3, starting transfers between devices: 17.3 us -> 15.5 us  [exchange(): return lax.all_to_all(x, axes, 0, 0)]
    ppermute x4, starting transfers between devices: 17.7 us -> 18.8 us  [shift(): return lax.ppermute(x, axis, pairs)]
  transfers between devices with their start and end apart: 14 -> 14, of which waited for: 5 -> 6; matrix products, arithmetic and copies ran while one was open for 0% -> 0% of each run, Pallas kernels for 8% -> 10%
where the time goes in v3:
time: 102 us; the launch traced here: 101 us
  starting transfers between devices  49.7 us (49%)
  waiting for transfers between devices  16.4 us (16%)
  Pallas kernels  14.8 us (15%)
  blocking collectives  10.5 us (10%)
  local copies, waits for them, and re-layouts  9.51 us (9%)
    ppermute x4, starting transfers between devices, shift(): return lax.ppermute(x, axis, pairs)  18.8 us
    all_to_all x3, starting transfers between devices, exchange(): return lax.all_to_all(x, axes, 0, 0)  15.5 us
    ppermute x7, starting transfers between devices, turn(): lax.ppermute(x, axis, [(i, (i + step) % count) for i in range(count)])  15.3 us
    pallas_call x8, Pallas kernels, call(): pl.pallas_call(kernel, out_shape=out_shape, in_specs=[SMEM] * len(scalars...  14.8 us
    ppermute x4, waiting for transfers between devices, shift(): return lax.ppermute(x, axis, pairs)  10.9 us
    all_to_all x1, blocking collectives, exchange(): return lax.all_to_all(x, axes, 0, 0)  10.5 us
    unnamed x25, local copies, waits for them, and re-layouts  9.31 us
    all_to_all x3, waiting for transfers between devices, exchange(): return lax.all_to_all(x, axes, 0, 0)  2.79 us
  transfers between devices with their start and end apart: 14, of which 6 were waited for; matrix products, arithmetic and copies ran while one was open for 0% of the time, Pallas kernels for 10%

profile of v3, /device:TPU:1, one launch (start us, length us, event | category | flops | bytes accessed | tf_op | source)
XLA Modules:
  0.0 101.0 jit_solution(9514531589430699245)
XLA Ops:
  0.0 1.0 copy-done.6
  1.8 5.9 %all-to-all-start = ((bf16[8,4,192]{2,1,0:T(4,128)(2,1)}), bf16[8,4,192]{2,1,0:T(4,128)(2,1)S(1)}, u32[]{:S(2)}, u32[]{:S(2)}) async-start(bf16[8,4,192]{2,1,0:T(4,128)(2,1)} %shard_map.46), calls=%async_computation | async-start | bytes 32768 | tf_op jit(solution)/shard_map/all_to_all | solution.py:57
  7.8 2.3 %shard_map.47 = bf16[8,576,128]{2,1,0:T(8,128)(2,1)} custom-call(bf16[128,1536]{1,0:T(8,128)(2,1)} %bitcast.15, bf16[128,1536]{1,0:T(8,128)(2,1)} %bitcast.17, bf16[128,1536]{1,0:T(8,128)(2,1)} %bitcast.18), custom_call_target="tpu_custom_call" | custom-call | flops 900000000 | bytes 6000000 | tf_op jit(solution)/shard_map/pallas_call | solution.py:45
  10.1 2.8 %all-to-all-done = bf16[8,4,192]{2,1,0:T(4,128)(2,1)S(1)} async-done(((bf16[8,4,192]{2,1,0:T(4,128)(2,1)}), bf16[8,4,192]{2,1,0:T(4,128)(2,1)S(1)}, u32[]{:S(2)}, u32[]{:S(2)}) %all-to-all-start) | async-done | bytes 12320 | tf_op jit(solution)/shard_map/all_to_all | solution.py:57
  12.8 3.6 %all-to-all-start.1 = ((bf16[8,576,128]{2,1,0:T(8,128)(2,1)}), bf16[8,576,128]{2,1,0:T(8,128)(2,1)S(1)}, u32[]{:S(2)}, u32[]{:S(2)}) async-start(bf16[8,576,128]{2,1,0:T(8,128)(2,1)} %shard_map.47), calls=%async_computation.1 | async-start | bytes 2359296 | tf_op jit(solution)/shard_map/all_to_all | solution.py:57
  16.4 5.7 %collective-permute-start.6 = (bf16[32,192]{1,0:T(8,128)(2,1)S(1)}, bf16[32,192]{1,0:T(8,128)(2,1)S(1)}, u32[]{:S(2)}, u32[]{:S(2)}) collective-permute-start(bf16[32,192]{1,0:T(8,128)(2,1)S(1)} %reshape.23.refs_0_), channel_id=1, source_target_pairs={{0,56},{8,0},{16,8},{24,16},{32,24},{40,32},{48,40},{56,48},{1,57}... | collective-permute-start | bytes 36872 | tf_op jit(solution)/shard_map/ppermute | solution.py:250
  22.1 1.2 %collective-permute-start.5 = (bf16[32,192]{1,0:T(8,128)(2,1)S(1)}, bf16[32,192]{1,0:T(8,128)(2,1)S(1)}, u32[]{:S(2)}, u32[]{:S(2)}) collective-permute-start(bf16[32,192]{1,0:T(8,128)(2,1)S(1)} %reshape.23.refs_0_), channel_id=1, source_target_pairs={{0,48},{8,56},{16,0},{24,8},{32,16},{40,24},{48,32},{56,40},{1,49}... | collective-permute-start | bytes 36872 | tf_op jit(solution)/shard_map/ppermute | solution.py:250
  23.7 4.5 %collective-permute-start.3 = (bf16[32,192]{1,0:T(8,128)(2,1)S(1)}, bf16[32,192]{1,0:T(8,128)(2,1)S(1)}, u32[]{:S(2)}, u32[]{:S(2)}) collective-permute-start(bf16[32,192]{1,0:T(8,128)(2,1)S(1)} %reshape.23.refs_0_), channel_id=1, source_target_pairs={{0,32},{8,40},{16,48},{24,56},{32,0},{40,8},{48,16},{56,24},{1,33}... | collective-permute-start | bytes 36872 | tf_op jit(solution)/shard_map/ppermute | solution.py:250
  28.2 2.2 %collective-permute-start.1 = (bf16[32,192]{1,0:T(8,128)(2,1)S(1)}, bf16[32,192]{1,0:T(8,128)(2,1)S(1)}, u32[]{:S(2)}, u32[]{:S(2)}) collective-permute-start(bf16[32,192]{1,0:T(8,128)(2,1)S(1)} %reshape.23.refs_0_), channel_id=1, source_target_pairs={{0,16},{8,24},{16,32},{24,40},{32,48},{40,56},{48,0},{56,8},{1,17}... | collective-permute-start | bytes 36872 | tf_op jit(solution)/shard_map/ppermute | solution.py:250
  30.4 1.4 %collective-permute-start = (bf16[32,192]{1,0:T(8,128)(2,1)S(1)}, bf16[32,192]{1,0:T(8,128)(2,1)S(1)}, u32[]{:S(2)}, u32[]{:S(2)}) collective-permute-start(bf16[32,192]{1,0:T(8,128)(2,1)S(1)} %reshape.23.refs_0_), channel_id=1, source_target_pairs={{0,8},{8,16},{16,24},{24,32},{32,40},{40,48},{48,56},{56,0},{1,9},... | collective-permute-start | bytes 36872 | tf_op jit(solution)/shard_map/ppermute | solution.py:250
  31.7 2.1 %collective-permute-done.2.refs_3_ = bf16[32,192]{1,0:T(8,128)(2,1)S(1)} collective-permute-done((bf16[32,192]{1,0:T(8,128)(2,1)S(1)}, bf16[32,192]{1,0:T(8,128)(2,1)S(1)}, u32[]{:S(2)}, u32[]{:S(2)}) %collective-permute-start.2) | collective-permute-done | bytes 12320 | tf_op jit(solution)/shard_map/ppermute | solution.py:250
  34.4 2.7 %shard_map.48 = (bf16[8,208,256]{2,1,0:T(8,128)(2,1)}, bf16[256,192]{1,0:T(8,128)(2,1)S(1)}) custom-call(s32[1]{0:T(128)} %bitcast.z_ref, bf16[32,192]{1,0:T(8,128)(2,1)S(1)} %reshape.23.refs_0_, bf16[32,192]{1,0:T(8,128)(2,1)S(1)} %collective-permute-done.refs_1_, bf16[32,192]{1,0:T(8,128)(2,1)S(1)} %collective-permute-done.1.refs_2_, ...), custom_call_target="tpu_custom_call" | custom-call | flops 1200000000 | bytes 8000000 | tf_op jit(solution)/shard_map/pallas_call | solution.py:45
  37.8 6.0 %all-to-all-start.2 = ((bf16[8,208,256]{2,1,0:T(8,128)(2,1)}), bf16[8,208,256]{2,1,0:T(8,128)(2,1)S(1)}, u32[]{:S(2)}, u32[]{:S(2)}) async-start(bf16[8,208,256]{2,1,0:T(8,128)(2,1)} %get-tuple-element.13), calls=%async_computation.2 | async-start | bytes 1703936 | tf_op jit(solution)/shard_map/all_to_all | solution.py:57
  43.8 1.3 %collective-permute-start.8 = (bf16[192,128]{1,0:T(8,128)(2,1)S(1)}, bf16[192,128]{1,0:T(8,128)(2,1)S(1)}, u32[]{:S(2)}, u32[]{:S(2)}) collective-permute-start(bf16[192,128]{1,0:T(8,128)(2,1)S(1)} %get-tuple-element.21), channel_id=1, source_target_pairs={{8,0},{16,8},{24,16},{32,24},{40,32},{48,40},{56,48},{9,1},{17,9},... | collective-permute-start | bytes 147464 | tf_op jit(solution)/shard_map/ppermute | solution.py:63
  45.1 4.0 %collective-permute-start.7 = (bf16[192,128]{1,0:T(8,128)(2,1)S(1)}, bf16[192,128]{1,0:T(8,128)(2,1)S(1)}, u32[]{:S(2)}, u32[]{:S(2)}) collective-permute-start(bf16[192,128]{1,0:T(8,128)(2,1)S(1)} %get-tuple-element.22), channel_id=1, source_target_pairs={{0,8},{8,16},{16,24},{24,32},{32,40},{40,48},{48,56},{1,9},{9,17},... | collective-permute-start | bytes 147464 | tf_op jit(solution)/shard_map/ppermute | solution.py:63
  49.3 9.8 %collective-permute-done.8.below_ref = bf16[192,128]{1,0:T(8,128)(2,1)S(1)} collective-permute-done((bf16[192,128]{1,0:T(8,128)(2,1)S(1)}, bf16[192,128]{1,0:T(8,128)(2,1)S(1)}, u32[]{:S(2)}, u32[]{:S(2)}) %collective-permute-start.8) | collective-permute-done | bytes 49184 | tf_op jit(solution)/shard_map/ppermute | solution.py:63
  60.0 11.6 %collective-permute-start.9 = (bf16[192,384]{1,0:T(8,128)(2,1)}, bf16[192,384]{1,0:T(8,128)(2,1)S(1)}, u32[]{:S(2)}, u32[]{:S(2)}) collective-permute-start(bf16[192,384]{1,0:T(8,128)(2,1)} %get-tuple-element.19), channel_id=1, source_target_pairs={{0,64},{64,128},{128,192},{1,65},{65,129},{129,193},{2,66},{66,130... | collective-permute-start | bytes 442376 | tf_op jit(solution)/shard_map/ppermute | solution.py:63
  71.6 1.9 %collective-permute-start.10 = (bf16[192,384]{1,0:T(8,128)(2,1)}, bf16[192,384]{1,0:T(8,128)(2,1)}, u32[]{:S(2)}, u32[]{:S(2)}) collective-permute-start(bf16[192,384]{1,0:T(8,128)(2,1)} %get-tuple-element.20), channel_id=1, source_target_pairs={{64,0},{128,64},{192,128},{65,1},{129,65},{193,129},{66,2},{130,66... | collective-permute-start | bytes 442376 | tf_op jit(solution)/shard_map/ppermute | solution.py:63
  74.6 1.2 %shard_map.49 = (bf16[256,1024]{1,0:T(8,128)(2,1)S(1)}, bf16[256,1024]{1,0:T(8,128)(2,1)S(1)}, bf16[256,1024]{1,0:T(8,128)(2,1)S(1)}, f32[8,1024]{1,0:T(8,128)S(1)}) custom-call(bf16[256,192]{1,0:T(8,128)(2,1)S(1)} %copy-done.10, bf16[8,576,128]{2,1,0:T(8,128)(2,1)S(1)} %all-to-all-done.1.refs_8_.x_ref), custom_call_target="tpu_custom_call" | custom-call | flops 1200000000 | bytes 8000000 | tf_op jit(solution)/shard_map/pallas_call | solution.py:45
  78.7 1.2 %collective-permute-done.10.after_ref = bf16[192,384]{1,0:T(8,128)(2,1)} collective-permute-done((bf16[192,384]{1,0:T(8,128)(2,1)}, bf16[192,384]{1,0:T(8,128)(2,1)}, u32[]{:S(2)}, u32[]{:S(2)}) %collective-permute-start.10) | collective-permute-done | bytes 147488 | tf_op jit(solution)/shard_map/ppermute | solution.py:63
  80.8 5.5 %shard_map.51.refs_4_ = f32[8,192,128]{2,1,0:T(8,128)S(1)} custom-call(bf16[8,576,128]{2,1,0:T(8,128)(2,1)S(1)} %all-to-all-done.1.refs_8_.x_ref, bf16[192,128]{1,0:T(8,128)(2,1)S(1)} %collective-permute-done.7.above_ref, bf16[192,128]{1,0:T(8,128)(2,1)S(1)} %collective-permute-done.8.below_ref, bf16[192,384]{1,0:T(8,128)(2,1)S(1)} %copy-done.8, ...), custom_call_target="tpu_custom_call" | custom-call | flops 1800000000 | bytes 12000000 | tf_op jit(solution)/shard_map/pallas_call | solution.py:45
  86.3 1.0 %copy-done.1 = bf16[256,1024]{1,0:T(8,128)(2,1)S(1)} copy-done((bf16[256,1024]{1,0:T(8,128)(2,1)S(1)}, bf16[256,1024]{1,0:T(8,128)(2,1)}, u32[]{:S(2)}) %copy-start.1) | copy-done | bytes 524312
  87.3 1.0 %copy-done.3 = bf16[256,1024]{1,0:T(8,128)(2,1)S(1)} copy-done((bf16[256,1024]{1,0:T(8,128)(2,1)S(1)}, bf16[256,1024]{1,0:T(8,128)(2,1)}, u32[]{:S(2)}) %copy-start.3) | copy-done | bytes 524312
  89.6 10.5 %all_to_all.20.x_ref = bf16[8,192,128]{2,1,0:T(8,128)(2,1)S(1)} all-to-all(bf16[8,192,128]{2,1,0:T(8,128)(2,1)S(1)} %shard_map.52), channel_id=1, replica_groups=mesh['tm'=4,'z'=8,'xy'=8] {'xy'}, dimensions={0} | all-to-all | bytes 786432 | tf_op jit(solution)/shard_map/all_to_all | solution.py:57
  (42 shorter events, 10.6 us)
Async XLA Ops:
  0.0 1.0 copy-start.6
  1.8 11.0 %all-to-all-start = ((bf16[8,4,192]{2,1,0:T(4,128)(2,1)}), bf16[8,4,192]{2,1,0:T(4,128)(2,1)S(1)}, u32[]{:S(2)}, u32[]{:S(2)}) async-start(bf16[8,4,192]{2,1,0:T(4,128)(2,1)} %shard_map.46), calls=%async_computation | async-start | bytes 32768 | tf_op jit(solution)/shard_map/all_to_all | solution.py:57
  12.8 21.6 %all-to-all-start.1 = ((bf16[8,576,128]{2,1,0:T(8,128)(2,1)}), bf16[8,576,128]{2,1,0:T(8,128)(2,1)S(1)}, u32[]{:S(2)}, u32[]{:S(2)}) async-start(bf16[8,576,128]{2,1,0:T(8,128)(2,1)} %shard_map.47), calls=%async_computation.1 | async-start | bytes 2359296 | tf_op jit(solution)/shard_map/all_to_all | solution.py:57
  16.4 11.8 %collective-permute-start.6 = (bf16[32,192]{1,0:T(8,128)(2,1)S(1)}, bf16[32,192]{1,0:T(8,128)(2,1)S(1)}, u32[]{:S(2)}, u32[]{:S(2)}) collective-permute-start(bf16[32,192]{1,0:T(8,128)(2,1)S(1)} %reshape.23.refs_0_), channel_id=1, source_target_pairs={{0,56},{8,0},{16,8},{24,16},{32,24},{40,32},{48,40},{56,48},{1,57}... | collective-permute-start | bytes 36872 | tf_op jit(solution)/shard_map/ppermute | solution.py:250
  22.1 8.3 %collective-permute-start.5 = (bf16[32,192]{1,0:T(8,128)(2,1)S(1)}, bf16[32,192]{1,0:T(8,128)(2,1)S(1)}, u32[]{:S(2)}, u32[]{:S(2)}) collective-permute-start(bf16[32,192]{1,0:T(8,128)(2,1)S(1)} %reshape.23.refs_0_), channel_id=1, source_target_pairs={{0,48},{8,56},{16,0},{24,8},{32,16},{40,24},{48,32},{56,40},{1,49}... | collective-permute-start | bytes 36872 | tf_op jit(solution)/shard_map/ppermute | solution.py:250
  23.3 8.5 %collective-permute-start.4 = (bf16[32,192]{1,0:T(8,128)(2,1)S(1)}, bf16[32,192]{1,0:T(8,128)(2,1)S(1)}, u32[]{:S(2)}, u32[]{:S(2)}) collective-permute-start(bf16[32,192]{1,0:T(8,128)(2,1)S(1)} %reshape.23.refs_0_), channel_id=1, source_target_pairs={{0,40},{8,48},{16,56},{24,0},{32,8},{40,16},{48,24},{56,32},{1,41}... | collective-permute-start | bytes 36872 | tf_op jit(solution)/shard_map/ppermute | solution.py:250
  23.7 8.0 %collective-permute-start.3 = (bf16[32,192]{1,0:T(8,128)(2,1)S(1)}, bf16[32,192]{1,0:T(8,128)(2,1)S(1)}, u32[]{:S(2)}, u32[]{:S(2)}) collective-permute-start(bf16[32,192]{1,0:T(8,128)(2,1)S(1)} %reshape.23.refs_0_), channel_id=1, source_target_pairs={{0,32},{8,40},{16,48},{24,56},{32,0},{40,8},{48,16},{56,24},{1,33}... | collective-permute-start | bytes 36872 | tf_op jit(solution)/shard_map/ppermute | solution.py:250
  28.2 5.7 %collective-permute-start.2 = (bf16[32,192]{1,0:T(8,128)(2,1)S(1)}, bf16[32,192]{1,0:T(8,128)(2,1)S(1)}, u32[]{:S(2)}, u32[]{:S(2)}) collective-permute-start(bf16[32,192]{1,0:T(8,128)(2,1)S(1)} %reshape.23.refs_0_), channel_id=1, source_target_pairs={{0,24},{8,32},{16,40},{24,48},{32,56},{40,0},{48,8},{56,16},{1,25}... | collective-permute-start | bytes 36872 | tf_op jit(solution)/shard_map/ppermute | solution.py:250
  28.2 5.9 %collective-permute-start.1 = (bf16[32,192]{1,0:T(8,128)(2,1)S(1)}, bf16[32,192]{1,0:T(8,128)(2,1)S(1)}, u32[]{:S(2)}, u32[]{:S(2)}) collective-permute-start(bf16[32,192]{1,0:T(8,128)(2,1)S(1)} %reshape.23.refs_0_), channel_id=1, source_target_pairs={{0,16},{8,24},{16,32},{24,40},{32,48},{40,56},{48,0},{56,8},{1,17}... | collective-permute-start | bytes 36872 | tf_op jit(solution)/shard_map/ppermute | solution.py:250
  30.4 4.0 %collective-permute-start = (bf16[32,192]{1,0:T(8,128)(2,1)S(1)}, bf16[32,192]{1,0:T(8,128)(2,1)S(1)}, u32[]{:S(2)}, u32[]{:S(2)}) collective-permute-start(bf16[32,192]{1,0:T(8,128)(2,1)S(1)} %reshape.23.refs_0_), channel_id=1, source_target_pairs={{0,8},{8,16},{16,24},{24,32},{32,40},{40,48},{48,56},{56,0},{1,9},... | collective-permute-start | bytes 36872 | tf_op jit(solution)/shard_map/ppermute | solution.py:250
  37.8 11.3 %copy-start.11 = (f32[3,3,3,1536]{3,2,1,0:T(4,128)S(1)}, f32[3,3,3,1536]{3,2,1,0:T(4,128)}, u32[]{:S(2)}) copy-start(f32[3,3,3,1536]{3,2,1,0:T(4,128)} %param.7) | copy-start | bytes 497668
  37.8 48.5 %all-to-all-start.2 = ((bf16[8,208,256]{2,1,0:T(8,128)(2,1)}), bf16[8,208,256]{2,1,0:T(8,128)(2,1)S(1)}, u32[]{:S(2)}, u32[]{:S(2)}) async-start(bf16[8,208,256]{2,1,0:T(8,128)(2,1)} %get-tuple-element.13), calls=%async_computation.2 | async-start | bytes 1703936 | tf_op jit(solution)/shard_map/all_to_all | solution.py:57
  43.8 15.2 %collective-permute-start.8 = (bf16[192,128]{1,0:T(8,128)(2,1)S(1)}, bf16[192,128]{1,0:T(8,128)(2,1)S(1)}, u32[]{:S(2)}, u32[]{:S(2)}) collective-permute-start(bf16[192,128]{1,0:T(8,128)(2,1)S(1)} %get-tuple-element.21), channel_id=1, source_target_pairs={{8,0},{16,8},{24,16},{32,24},{40,32},{48,40},{56,48},{9,1},{17,9},... | collective-permute-start | bytes 147464 | tf_op jit(solution)/shard_map/ppermute | solution.py:63
  45.1 13.9 %collective-permute-start.7 = (bf16[192,128]{1,0:T(8,128)(2,1)S(1)}, bf16[192,128]{1,0:T(8,128)(2,1)S(1)}, u32[]{:S(2)}, u32[]{:S(2)}) collective-permute-start(bf16[192,128]{1,0:T(8,128)(2,1)S(1)} %get-tuple-element.22), channel_id=1, source_target_pairs={{0,8},{8,16},{16,24},{24,32},{32,40},{40,48},{48,56},{1,9},{9,17},... | collective-permute-start | bytes 147464 | tf_op jit(solution)/shard_map/ppermute | solution.py:63
  60.0 18.1 %collective-permute-start.9 = (bf16[192,384]{1,0:T(8,128)(2,1)}, bf16[192,384]{1,0:T(8,128)(2,1)S(1)}, u32[]{:S(2)}, u32[]{:S(2)}) collective-permute-start(bf16[192,384]{1,0:T(8,128)(2,1)} %get-tuple-element.19), channel_id=1, source_target_pairs={{0,64},{64,128},{128,192},{1,65},{65,129},{129,193},{2,66},{66,130... | collective-permute-start | bytes 442376 | tf_op jit(solution)/shard_map/ppermute | solution.py:63
  71.6 8.3 %collective-permute-start.10 = (bf16[192,384]{1,0:T(8,128)(2,1)}, bf16[192,384]{1,0:T(8,128)(2,1)}, u32[]{:S(2)}, u32[]{:S(2)}) collective-permute-start(bf16[192,384]{1,0:T(8,128)(2,1)} %get-tuple-element.20), channel_id=1, source_target_pairs={{64,0},{128,64},{192,128},{65,1},{129,65},{193,129},{66,2},{130,66... | collective-permute-start | bytes 442376 | tf_op jit(solution)/shard_map/ppermute | solution.py:63
  73.7 0.9 copy-start.10
  75.8 0.8 copy-start
  76.6 0.8 copy-start.2
  78.0 0.7 copy-start.7
  79.9 0.9 copy-start.8
  86.3 1.0 %copy-start.1 = (bf16[256,1024]{1,0:T(8,128)(2,1)S(1)}, bf16[256,1024]{1,0:T(8,128)(2,1)}, u32[]{:S(2)}) copy-start(bf16[256,1024]{1,0:T(8,128)(2,1)} %copy-done) | copy-start | bytes 1572868
  87.3 1.0 %copy-start.3 = (bf16[256,1024]{1,0:T(8,128)(2,1)S(1)}, bf16[256,1024]{1,0:T(8,128)(2,1)}, u32[]{:S(2)}) copy-start(bf16[256,1024]{1,0:T(8,128)(2,1)} %copy-done.2) | copy-start | bytes 1572868
  88.4 0.8 copy-start.5
  (2 other events, 1.3 us)

commit v4 on v3

--- a/solution.py
+++ b/solution.py
@@ -23,8 +23,7 @@
 V_ROW = 2 * GROUP
 SENT = 3 * GROUP
 PLANE_AGENTS = TILES * AGENT_DEV
-EDGE_ROWS = TILES + 2
-EDGE = 3 * TOKENS
+EDGE = TILES * COLUMNS
 STATS = 16
 GRANT = 6 * 1024 * 1024
 ALL = 60 * 1024 * 1024
@@ -129,32 +128,25 @@
         out_ref[z] = part
 
 
-def query_kernel(a_ref, x_ref, *refs):
-    e_refs, total_ref = refs[:GROUP_HEADS], refs[GROUP_HEADS]
+def query_kernel(a_ref, x_ref, one_ref, rest_ref, total_ref):
     for h in range(GROUP_HEADS):
         queries = rows_of(x_ref, h * HEAD_DIM, HEAD_DIM)
         agents = a_ref[:, h * HEAD_DIM : (h + 1) * HEAD_DIM]
         scores = jnp.dot(agents, queries, preferred_element_type=F32) * INV_ROOT
         weights = jnp.exp(scores - jnp.max(scores, axis=0, keepdims=True))
         total_ref[h : h + 1, :] = jnp.sum(weights, axis=0, keepdims=True)
-        e_refs[h][...] = weights.astype(BF16)
-
-
-def edge_kernel(x_ref, above_ref, below_ref, last_ref, first_ref):
+        if h == 0:
+            one_ref[...] = weights.astype(BF16)
+        else:
+            rest_ref[h - 1] = weights.astype(BF16)
+
+
+def edge_kernel(x_ref, last_ref, first_ref):
     spot = lax.broadcasted_iota(jnp.int32, (GROUP, TOKENS), 1) // COLUMNS
     for block in range(EDGE // TOKENS):
         last = first = jnp.zeros((GROUP, TOKENS), F32)
         for j in range(FRAMES):
-            row = block * FRAMES + j
-            if row >= EDGE_ROWS:
-                break
-            if row == 0:
-                cells = above_ref[...]
-            elif row == EDGE_ROWS - 1:
-                cells = below_ref[...]
-            else:
-                cells = x_ref[row - 1, V_ROW:, :]
-            cells = cells.astype(F32)
+            cells = x_ref[block * FRAMES + j, V_ROW:, :].astype(F32)
             late = cells if j == FRAMES - 1 else pltpu.roll(cells, (j + 1) * COLUMNS, 1)
             early = cells if j == 0 else pltpu.roll(cells, j * COLUMNS, 1)
             last = jnp.where(spot == j, late, last)
@@ -164,59 +156,82 @@
         first_ref[:, lanes] = first.astype(BF16)
 
 
-def conv_kernel(x_ref, above_ref, below_ref, before_ref, after_ref, w_ref, out_ref):
-    tall = 16
-    lane = lax.broadcasted_iota(jnp.int32, (tall, TOKENS), 1)
-    column = lane % COLUMNS
-    head, tail = lane < COLUMNS, lane >= TOKENS - COLUMNS
-
-    def turned(cells, by):
-        by %= TOKENS
-        return cells if by == 0 else pltpu.roll(cells, by, 1)
-
-    def frames_of(r, at):
-        if r < 0:
-            cells = above_ref[pl.ds(at, tall), :]
-        elif r == TILES:
-            cells = below_ref[pl.ds(at, tall), :]
-        else:
-            cells = x_ref[r, pl.ds(V_ROW + at, tall), :]
-        cells = cells.astype(F32)
-        block, j = divmod(r + 1, FRAMES)
-        lanes = slice(block * TOKENS, (block + 1) * TOKENS)
-        before = turned(before_ref[pl.ds(at, tall), lanes].astype(F32), -j * COLUMNS)
-        after = turned(after_ref[pl.ds(at, tall), lanes].astype(F32), (FRAMES - 1 - j) * COLUMNS)
-        return (
-            jnp.where(head, before, turned(cells, COLUMNS)),
-            cells,
-            jnp.where(tail, after, turned(cells, -COLUMNS)),
-        )
-
-    def step(i, carry):
-        at = pl.multiple_of(i * tall, tall)
-        w = w_ref[pl.ds(at, tall), :]
-        taps = [jnp.broadcast_to(w[:, n : n + 1], (tall, TOKENS)) for n in range(27)]
-        rows = {r: frames_of(r, at) for r in range(-1, 1)}
+TALL = 16
+
+
+def turned(cells, by):
+    by %= TOKENS
+    return cells if by == 0 else pltpu.roll(cells, by, 1)
+
+
+def frames_of(r, at, x_ref, before_ref, after_ref):
+    lane = lax.broadcasted_iota(jnp.int32, (TALL, TOKENS), 1)
+    cells = x_ref[r, pl.ds(V_ROW + at, TALL), :].astype(F32)
+    block, j = divmod(r, FRAMES)
+    lanes = slice(block * TOKENS, (block + 1) * TOKENS)
+    before = turned(before_ref[pl.ds(at, TALL), lanes].astype(F32), -j * COLUMNS)
+    after = turned(after_ref[pl.ds(at, TALL), lanes].astype(F32), (FRAMES - 1 - j) * COLUMNS)
+    return (
+        jnp.where(lane < COLUMNS, before, turned(cells, COLUMNS)),
+        cells,
+        jnp.where(lane >= TOKENS - COLUMNS, after, turned(cells, -COLUMNS)),
+    )
+
+
+def taps_of(w_ref, at, rows=range(3)):
+    w = w_ref[pl.ds(at, TALL), :]
+    return {
+        (i, j, k): jnp.broadcast_to(w[:, n : n + 1], (TALL, TOKENS))
+        for i in range(3)
+        for j in rows
+        for k in range(3)
+        for n in (i * 9 + j * 3 + k,)
+    }
+
+
+def stencil(rows, taps):
+    column = lax.broadcasted_iota(jnp.int32, (TALL, TOKENS), 1) % COLUMNS
+    sums = []
+    for k in range(3):
+        total = None
+        for j, frames in rows.items():
+            for i in range(3):
+                term = frames[i] * taps[i, j, k]
+                total = term if total is None else total + term
+        sums.append(total)
+    left = jnp.where(column == 0, 0.0, pltpu.roll(sums[0], 1, 1))
+    right = jnp.where(column == COLUMNS - 1, 0.0, pltpu.roll(sums[2], TOKENS - 1, 1))
+    return left + sums[1] + right
+
+
+def rim_kernel(x_ref, before_ref, after_ref, w_ref, up_ref, down_ref):
+    def step(n, carry):
+        at = pl.multiple_of(n * TALL, TALL)
+        for r, j, ref in ((TILES - 1, 0, up_ref), (0, 2, down_ref)):
+            frames = frames_of(r, at, x_ref, before_ref, after_ref)
+            ref[pl.ds(at, TALL), :] = stencil({j: frames}, taps_of(w_ref, at, (j,))).astype(BF16)
+        return carry
+
+    lax.fori_loop(0, GROUP // TALL, step, 0)
+
+
+def conv_kernel(x_ref, before_ref, after_ref, w_ref, out_ref):
+    def step(n, carry):
+        at = pl.multiple_of(n * TALL, TALL)
+        taps = taps_of(w_ref, at)
+        rows = {0: frames_of(0, at, x_ref, before_ref, after_ref)}
         for r in range(TILES):
-            rows[r + 1] = frames_of(r + 1, at)
-            sums = []
-            for k in range(3):
-                total = None
-                for j in range(3):
-                    for i3 in range(3):
-                        term = rows[r + j - 1][i3] * taps[i3 * 9 + j * 3 + k]
-                        total = term if total is None else total + term
-                sums.append(total)
-            left = jnp.where(column == 0, 0.0, pltpu.roll(sums[0], 1, 1))
-            right = jnp.where(column == COLUMNS - 1, 0.0, pltpu.roll(sums[2], TOKENS - 1, 1))
-            out_ref[r, pl.ds(at, tall), :] = left + sums[1] + right
+            if r + 1 < TILES:
+                rows[r + 1] = frames_of(r + 1, at, x_ref, before_ref, after_ref)
+            near = {j: rows[r + j - 1] for j in range(3) if r + j - 1 in rows}
+            out_ref[r, pl.ds(at, TALL), :] = stencil(near, taps)
+            rows.pop(r - 1, None)
         return carry
 
-    lax.fori_loop(0, GROUP // tall, step, 0)
-
-
-def mix_kernel(parts_ref, *refs):
-    e_refs, (total_ref, local_ref, out_ref) = refs[:GROUP_HEADS], refs[GROUP_HEADS:]
+    lax.fori_loop(0, GROUP // TALL, step, 0)
+
+
+def mix_kernel(parts_ref, one_ref, rest_ref, total_ref, local_ref, up_ref, down_ref, out_ref):
     logs = []
     for z in range(PLANES):
         pieces = parts_ref[z, GROUP : GROUP + STATS, :].astype(F32)
@@ -234,11 +249,16 @@
         for z in range(PLANES):
             term = parts_ref[z, rows, :].astype(F32) * shares[z][h : h + 1]
             values = term if values is None else values + term
-        mixed = jnp.dot(values.astype(BF16), e_refs[h][...], preferred_element_type=F32)
+        weights = one_ref[...] if h == 0 else rest_ref[h - 1]
+        mixed = jnp.dot(values.astype(BF16), weights, preferred_element_type=F32)
         mixed = mixed / total_ref[h : h + 1, :]
         for s in range(TILES):
-            cells = mixed[:, s * TOKENS : (s + 1) * TOKENS]
-            out_ref[s, rows, :] = (cells + local_ref[s, rows, :]).astype(BF16)
+            cells = mixed[:, s * TOKENS : (s + 1) * TOKENS] + local_ref[s, rows, :]
+            if s == 0:
+                cells += up_ref[rows, :].astype(F32)
+            if s == TILES - 1:
+                cells += down_ref[rows, :].astype(F32)
+            out_ref[s, rows, :] = cells.astype(BF16)
 
 
 def unpack_kernel(x_ref, out_ref):
@@ -275,9 +295,6 @@
     x = exchange(packed, "xy")
     came = [own] + [turn(own, "z", n) for n in range(1, PLANES)]
 
-    above = shift(x[TILES - 1, V_ROW:], "z", 1)
-    below = shift(x[0, V_ROW:], "z", -1)
-
     part, agents = call(
         agent_kernel,
         (shape((PLANES, GROUP + STATS, AGENTS), BF16), shape((AGENTS, GROUP), BF16)),
@@ -288,28 +305,41 @@
     )
     parts = exchange(part, "z")
 
-    rim = shape((GROUP, EDGE), BF16)
-    last, first = call(edge_kernel, (rim, rim), 1.0, x, above, below)
+    edges = shape((GROUP, EDGE), BF16)
+    last, first = call(edge_kernel, (edges, edges), 1.0, x)
     before = shift(last, "tm", 1)
     after = shift(first, "tm", -1)
-    *weights, totals = call(
+    cells = TILES * TOKENS
+    one, rest, totals = call(
         query_kernel,
         (
-            *(shape((AGENTS, TILES * TOKENS), BF16) for _ in range(GROUP_HEADS)),
-            shape((8, TILES * TOKENS), F32),
+            shape((AGENTS, cells), BF16),
+            shape((GROUP_HEADS - 1, AGENTS, cells), BF16),
+            shape((8, cells), F32),
         ),
-        4.0,
+        2.0,
         agents,
         x,
     )
     taps = lax.dynamic_index_in_dim(
         conv_weight.reshape(27, TILES, GROUP), lax.axis_index("xy"), 1, keepdims=False
     ).T
-    local = call(
-        conv_kernel, shape((TILES, GROUP, TOKENS), F32), 6.0, x, above, below, before, after, taps
-    )
+    row = shape((GROUP, TOKENS), BF16)
+    to_next, to_last = call(rim_kernel, (row, row), 1.0, x, before, after, taps)
+    up = shift(to_next, "z", 1)
+    down = shift(to_last, "z", -1)
+    local = call(conv_kernel, shape((TILES, GROUP, TOKENS), F32), 5.0, x, before, after, taps)
     mixed = call(
-        mix_kernel, shape((TILES, GROUP, TOKENS), BF16), 3.0, parts, *weights, totals, local
+        mix_kernel,
+        shape((TILES, GROUP, TOKENS), BF16),
+        1.0,
+        parts,
+        one,
+        rest,
+        totals,
+        local,
+        up,
+        down,
     )
     mine = exchange(mixed, "xy")
     out = call(unpack_kernel, shape((TOKENS, D), BF16), 1.0, mine)

time: 102 us -> 88.3 us (0.87)
  waiting for transfers between devices: 16.4 us -> 8.99 us
  local copies, waits for them, and re-layouts: 9.51 us -> 5.95 us
  starting transfers between devices: 49.7 us -> 46.2 us
    ppermute x4, waiting for transfers between devices: 10.9 us -> 3.55 us  [shift(): return lax.ppermute(x, axis, pairs)]
    unnamed x25 -> x17, local copies, waits for them, and re-layouts: 9.31 us -> 5.76 us
    ppermute x4, starting transfers between devices: 18.8 us -> 15.4 us  [shift(): return lax.ppermute(x, axis, pairs)]
    pallas_call x8 -> x9, Pallas kernels: 14.8 us -> 15.1 us  [call(): pl.pallas_call(kernel, out_shape=out_shape, in_specs=[SMEM] * len(scalars...]
  transfers between devices with their start and end apart: 14 -> 14, of which waited for: 6 -> 5; matrix products, arithmetic and copies ran while one was open for 0% -> 0% of each run, Pallas kernels for 10% -> 12%
where the time goes in v4:
time: 88.3 us; the launch traced here: 87.8 us
  starting transfers between devices  46.2 us (52%)
  Pallas kernels  15.1 us (17%)
  blocking collectives  11.4 us (13%)
  waiting for transfers between devices  8.99 us (10%)
  local copies, waits for them, and re-layouts  5.95 us (7%)
    all_to_all x3, starting transfers between devices, exchange(): return lax.all_to_all(x, axes, 0, 0)  15.5 us
    ppermute x4, starting transfers between devices, shift(): return lax.ppermute(x, axis, pairs)  15.4 us
    ppermute x7, starting transfers between devices, turn(): lax.ppermute(x, axis, [(i, (i + step) % count) for i in range(count)])  15.3 us
    pallas_call x9, Pallas kernels, call(): pl.pallas_call(kernel, out_shape=out_shape, in_specs=[SMEM] * len(scalars...  15.1 us
    all_to_all x1, blocking collectives, exchange(): return lax.all_to_all(x, axes, 0, 0)  11.4 us
    unnamed x17, local copies, waits for them, and re-layouts  5.76 us
    ppermute x4, waiting for transfers between devices, shift(): return lax.ppermute(x, axis, pairs)  3.55 us
    all_to_all x3, waiting for transfers between devices, exchange(): return lax.all_to_all(x, axes, 0, 0)  2.78 us
  transfers between devices with their start and end apart: 14, of which 5 were waited for; matrix products, arithmetic and copies ran while one was open for 0% of the time, Pallas kernels for 12%

profile of v4, /device:TPU:1, one launch (start us, length us, event | category | flops | bytes accessed | tf_op | source)
XLA Modules:
  0.0 87.8 jit_solution(5413503685634241376)
XLA Ops:
  0.0 1.0 %copy-done.4 = bf16[1,4,1,32,1536]{4,3,2,1,0:T(8,128)(2,1)S(1)} copy-done((bf16[1,4,1,32,1536]{4,3,2,1,0:T(8,128)(2,1)S(1)}, bf16[1,4,1,32,1536]{4,3,2,1,0:T(8,128)(2,1)}, u32[]{:S(2)}) %copy-start.4) | copy-done | bytes 393240
  1.8 5.9 %all-to-all-start = ((bf16[8,4,192]{2,1,0:T(4,128)(2,1)}), bf16[8,4,192]{2,1,0:T(4,128)(2,1)S(1)}, u32[]{:S(2)}, u32[]{:S(2)}) async-start(bf16[8,4,192]{2,1,0:T(4,128)(2,1)} %shard_map.46), calls=%async_computation | async-start | bytes 32768 | tf_op jit(solution)/shard_map/all_to_all | solution.py:56
  7.8 2.3 %shard_map.47 = bf16[8,576,128]{2,1,0:T(8,128)(2,1)} custom-call(bf16[128,1536]{1,0:T(8,128)(2,1)} %bitcast.12, bf16[128,1536]{1,0:T(8,128)(2,1)} %bitcast.14, bf16[128,1536]{1,0:T(8,128)(2,1)} %bitcast.15), custom_call_target="tpu_custom_call" | custom-call | flops 900000000 | bytes 6000000 | tf_op jit(solution)/shard_map/pallas_call | solution.py:44
  10.1 2.8 %all-to-all-done = bf16[8,4,192]{2,1,0:T(4,128)(2,1)S(1)} async-done(((bf16[8,4,192]{2,1,0:T(4,128)(2,1)}), bf16[8,4,192]{2,1,0:T(4,128)(2,1)S(1)}, u32[]{:S(2)}, u32[]{:S(2)}) %all-to-all-start) | async-done | bytes 12320 | tf_op jit(solution)/shard_map/all_to_all | solution.py:56
  12.8 3.6 %all-to-all-start.1 = ((bf16[8,576,128]{2,1,0:T(8,128)(2,1)}), bf16[8,576,128]{2,1,0:T(8,128)(2,1)S(1)}, u32[]{:S(2)}, u32[]{:S(2)}) async-start(bf16[8,576,128]{2,1,0:T(8,128)(2,1)} %shard_map.47), calls=%async_computation.1 | async-start | bytes 2359296 | tf_op jit(solution)/shard_map/all_to_all | solution.py:56
  16.4 5.7 %collective-permute-start.6 = (bf16[32,192]{1,0:T(8,128)(2,1)S(1)}, bf16[32,192]{1,0:T(8,128)(2,1)S(1)}, u32[]{:S(2)}, u32[]{:S(2)}) collective-permute-start(bf16[32,192]{1,0:T(8,128)(2,1)S(1)} %reshape.23.refs_0_), channel_id=1, source_target_pairs={{0,56},{8,0},{16,8},{24,16},{32,24},{40,32},{48,40},{56,48},{1,57}... | collective-permute-start | bytes 36872 | tf_op jit(solution)/shard_map/ppermute | solution.py:270
  22.1 1.2 %collective-permute-start.5 = (bf16[32,192]{1,0:T(8,128)(2,1)S(1)}, bf16[32,192]{1,0:T(8,128)(2,1)S(1)}, u32[]{:S(2)}, u32[]{:S(2)}) collective-permute-start(bf16[32,192]{1,0:T(8,128)(2,1)S(1)} %reshape.23.refs_0_), channel_id=1, source_target_pairs={{0,48},{8,56},{16,0},{24,8},{32,16},{40,24},{48,32},{56,40},{1,49}... | collective-permute-start | bytes 36872 | tf_op jit(solution)/shard_map/ppermute | solution.py:270
  23.7 4.5 %collective-permute-start.3 = (bf16[32,192]{1,0:T(8,128)(2,1)S(1)}, bf16[32,192]{1,0:T(8,128)(2,1)S(1)}, u32[]{:S(2)}, u32[]{:S(2)}) collective-permute-start(bf16[32,192]{1,0:T(8,128)(2,1)S(1)} %reshape.23.refs_0_), channel_id=1, source_target_pairs={{0,32},{8,40},{16,48},{24,56},{32,0},{40,8},{48,16},{56,24},{1,33}... | collective-permute-start | bytes 36872 | tf_op jit(solution)/shard_map/ppermute | solution.py:270
  28.2 2.2 %collective-permute-start.1 = (bf16[32,192]{1,0:T(8,128)(2,1)S(1)}, bf16[32,192]{1,0:T(8,128)(2,1)S(1)}, u32[]{:S(2)}, u32[]{:S(2)}) collective-permute-start(bf16[32,192]{1,0:T(8,128)(2,1)S(1)} %reshape.23.refs_0_), channel_id=1, source_target_pairs={{0,16},{8,24},{16,32},{24,40},{32,48},{40,56},{48,0},{56,8},{1,17}... | collective-permute-start | bytes 36872 | tf_op jit(solution)/shard_map/ppermute | solution.py:270
  30.4 1.4 %collective-permute-start = (bf16[32,192]{1,0:T(8,128)(2,1)S(1)}, bf16[32,192]{1,0:T(8,128)(2,1)S(1)}, u32[]{:S(2)}, u32[]{:S(2)}) collective-permute-start(bf16[32,192]{1,0:T(8,128)(2,1)S(1)} %reshape.23.refs_0_), channel_id=1, source_target_pairs={{0,8},{8,16},{16,24},{24,32},{32,40},{40,48},{48,56},{56,0},{1,9},... | collective-permute-start | bytes 36872 | tf_op jit(solution)/shard_map/ppermute | solution.py:270
  31.7 2.1 %collective-permute-done.2.refs_3_ = bf16[32,192]{1,0:T(8,128)(2,1)S(1)} collective-permute-done((bf16[32,192]{1,0:T(8,128)(2,1)S(1)}, bf16[32,192]{1,0:T(8,128)(2,1)S(1)}, u32[]{:S(2)}, u32[]{:S(2)}) %collective-permute-start.2) | collective-permute-done | bytes 12320 | tf_op jit(solution)/shard_map/ppermute | solution.py:270
  34.4 2.7 %shard_map.48 = (bf16[8,208,256]{2,1,0:T(8,128)(2,1)}, bf16[256,192]{1,0:T(8,128)(2,1)S(1)}) custom-call(s32[1]{0:T(128)} %bitcast.z_ref, bf16[32,192]{1,0:T(8,128)(2,1)S(1)} %reshape.23.refs_0_, bf16[32,192]{1,0:T(8,128)(2,1)S(1)} %collective-permute-done.refs_1_, bf16[32,192]{1,0:T(8,128)(2,1)S(1)} %collective-permute-done.1.refs_2_, ...), custom_call_target="tpu_custom_call" | custom-call | flops 1200000000 | bytes 8000000 | tf_op jit(solution)/shard_map/pallas_call | solution.py:44
  37.8 6.0 %all-to-all-start.2 = ((bf16[8,208,256]{2,1,0:T(8,128)(2,1)}), bf16[8,208,256]{2,1,0:T(8,128)(2,1)S(1)}, u32[]{:S(2)}, u32[]{:S(2)}) async-start(bf16[8,208,256]{2,1,0:T(8,128)(2,1)} %get-tuple-element.14), calls=%async_computation.2 | async-start | bytes 1703936 | tf_op jit(solution)/shard_map/all_to_all | solution.py:56
  44.8 8.5 %collective-permute-start.7 = (bf16[192,256]{1,0:T(8,128)(2,1)}, bf16[192,256]{1,0:T(8,128)(2,1)S(1)}, u32[]{:S(2)}, u32[]{:S(2)}) collective-permute-start(bf16[192,256]{1,0:T(8,128)(2,1)} %get-tuple-element.19), channel_id=1, source_target_pairs={{0,64},{64,128},{128,192},{1,65},{65,129},{129,193},{2,66},{66,130... | collective-permute-start | bytes 294920 | tf_op jit(solution)/shard_map/ppermute | solution.py:62
  53.3 1.9 %collective-permute-start.8 = (bf16[192,256]{1,0:T(8,128)(2,1)S(1)}, bf16[192,256]{1,0:T(8,128)(2,1)S(1)}, u32[]{:S(2)}, u32[]{:S(2)}) collective-permute-start(bf16[192,256]{1,0:T(8,128)(2,1)S(1)} %get-tuple-element.20), channel_id=1, source_target_pairs={{64,0},{128,64},{192,128},{65,1},{129,65},{193,129},{66,2},{130,66... | collective-permute-start | bytes 294920 | tf_op jit(solution)/shard_map/ppermute | solution.py:62
  56.3 1.2 %shard_map.49 = (bf16[256,1024]{1,0:T(8,128)(2,1)S(1)}, bf16[2,256,1024]{2,1,0:T(8,128)(2,1)S(1)}, f32[8,1024]{1,0:T(8,128)S(1)}) custom-call(bf16[256,192]{1,0:T(8,128)(2,1)S(1)} %copy-done.6, bf16[8,576,128]{2,1,0:T(8,128)(2,1)S(1)} %all-to-all-done.1.refs_8_.x_ref), custom_call_target="tpu_custom_call" | custom-call | flops 600000000 | bytes 4000000 | tf_op jit(solution)/shard_map/pallas_call | solution.py:44
  57.5 3.5 %collective-permute-done.8.after_ref = bf16[192,256]{1,0:T(8,128)(2,1)S(1)} collective-permute-done((bf16[192,256]{1,0:T(8,128)(2,1)S(1)}, bf16[192,256]{1,0:T(8,128)(2,1)S(1)}, u32[]{:S(2)}, u32[]{:S(2)}) %collective-permute-start.8) | collective-permute-done | bytes 98336 | tf_op jit(solution)/shard_map/ppermute | solution.py:62
  61.1 2.3 %shard_map.52 = (bf16[192,128]{1,0:T(8,128)(2,1)S(1)}, bf16[192,128]{1,0:T(8,128)(2,1)S(1)}) custom-call(bf16[8,576,128]{2,1,0:T(8,128)(2,1)S(1)} %all-to-all-done.1.refs_8_.x_ref, bf16[192,256]{1,0:T(8,128)(2,1)S(1)} %collective-permute-done.7.before_ref, bf16[192,256]{1,0:T(8,128)(2,1)S(1)} %collective-permute-done.8.after_ref, f32[192,27]{1,0:T(8,128)S(1)} %bitcast.10), custom_call_target="tpu_custom_call" | custom-call | flops 300000000 | bytes 2000000 | tf_op jit(solution)/shard_map/pallas_call | solution.py:44
  63.3 3.6 %collective-permute-start.9 = (bf16[192,128]{1,0:T(8,128)(2,1)S(1)}, bf16[192,128]{1,0:T(8,128)(2,1)S(1)}, u32[]{:S(2)}, u32[]{:S(2)}) collective-permute-start(bf16[192,128]{1,0:T(8,128)(2,1)S(1)} %get-tuple-element.21), channel_id=1, source_target_pairs={{0,8},{8,16},{16,24},{24,32},{32,40},{40,48},{48,56},{1,9},{9,17},... | collective-permute-start | bytes 147464 | tf_op jit(solution)/shard_map/ppermute | solution.py:62
  67.0 1.3 %collective-permute-start.10 = (bf16[192,128]{1,0:T(8,128)(2,1)S(1)}, bf16[192,128]{1,0:T(8,128)(2,1)S(1)}, u32[]{:S(2)}, u32[]{:S(2)}) collective-permute-start(bf16[192,128]{1,0:T(8,128)(2,1)S(1)} %get-tuple-element.22), channel_id=1, source_target_pairs={{8,0},{16,8},{24,16},{32,24},{40,32},{48,40},{56,48},{9,1},{17,9},... | collective-permute-start | bytes 147464 | tf_op jit(solution)/shard_map/ppermute | solution.py:62
  68.3 3.6 %shard_map.51.local_ref = f32[8,192,128]{2,1,0:T(8,128)S(1)} custom-call(bf16[8,576,128]{2,1,0:T(8,128)(2,1)S(1)} %all-to-all-done.1.refs_8_.x_ref, bf16[192,256]{1,0:T(8,128)(2,1)S(1)} %collective-permute-done.7.before_ref, bf16[192,256]{1,0:T(8,128)(2,1)S(1)} %collective-permute-done.8.after_ref, f32[192,27]{1,0:T(8,128)S(1)} %bitcast.11), custom_call_target="tpu_custom_call" | custom-call | flops 1500000000 | bytes 10000000 | tf_op jit(solution)/shard_map/pallas_call | solution.py:44
  72.8 1.1 %copy-done.1 = f32[8,192,128]{2,1,0:T(8,128)S(1)} copy-done((f32[8,192,128]{2,1,0:T(8,128)S(1)}, f32[8,192,128]{2,1,0:T(8,128)}, u32[]{:S(2)}) %copy-start.1) | copy-done | bytes 786456
  74.0 1.0 %copy-done.3 = bf16[256,1024]{1,0:T(8,128)(2,1)S(1)} copy-done((bf16[256,1024]{1,0:T(8,128)(2,1)S(1)}, bf16[256,1024]{1,0:T(8,128)(2,1)}, u32[]{:S(2)}) %copy-start.3) | copy-done | bytes 524312
  75.5 11.4 %all_to_all.20.x_ref = bf16[8,192,128]{2,1,0:T(8,128)(2,1)S(1)} all-to-all(bf16[8,192,128]{2,1,0:T(8,128)(2,1)S(1)} %shard_map.53), channel_id=1, replica_groups=mesh['tm'=4,'z'=8,'xy'=8] {'xy'}, dimensions={0} | all-to-all | bytes 786432 | tf_op jit(solution)/shard_map/all_to_all | solution.py:56
  (34 shorter events, 6.9 us)
Async XLA Ops:
  0.0 1.0 %copy-start.4 = (bf16[1,4,1,32,1536]{4,3,2,1,0:T(8,128)(2,1)S(1)}, bf16[1,4,1,32,1536]{4,3,2,1,0:T(8,128)(2,1)}, u32[]{:S(2)}) copy-start(bf16[1,4,1,32,1536]{4,3,2,1,0:T(8,128)(2,1)} %param.4) | copy-start | bytes 1179652
  1.8 11.0 %all-to-all-start = ((bf16[8,4,192]{2,1,0:T(4,128)(2,1)}), bf16[8,4,192]{2,1,0:T(4,128)(2,1)S(1)}, u32[]{:S(2)}, u32[]{:S(2)}) async-start(bf16[8,4,192]{2,1,0:T(4,128)(2,1)} %shard_map.46), calls=%async_computation | async-start | bytes 32768 | tf_op jit(solution)/shard_map/all_to_all | solution.py:56
  12.8 21.6 %all-to-all-start.1 = ((bf16[8,576,128]{2,1,0:T(8,128)(2,1)}), bf16[8,576,128]{2,1,0:T(8,128)(2,1)S(1)}, u32[]{:S(2)}, u32[]{:S(2)}) async-start(bf16[8,576,128]{2,1,0:T(8,128)(2,1)} %shard_map.47), calls=%async_computation.1 | async-start | bytes 2359296 | tf_op jit(solution)/shard_map/all_to_all | solution.py:56
  16.4 11.8 %collective-permute-start.6 = (bf16[32,192]{1,0:T(8,128)(2,1)S(1)}, bf16[32,192]{1,0:T(8,128)(2,1)S(1)}, u32[]{:S(2)}, u32[]{:S(2)}) collective-permute-start(bf16[32,192]{1,0:T(8,128)(2,1)S(1)} %reshape.23.refs_0_), channel_id=1, source_target_pairs={{0,56},{8,0},{16,8},{24,16},{32,24},{40,32},{48,40},{56,48},{1,57}... | collective-permute-start | bytes 36872 | tf_op jit(solution)/shard_map/ppermute | solution.py:270
  22.1 8.3 %collective-permute-start.5 = (bf16[32,192]{1,0:T(8,128)(2,1)S(1)}, bf16[32,192]{1,0:T(8,128)(2,1)S(1)}, u32[]{:S(2)}, u32[]{:S(2)}) collective-permute-start(bf16[32,192]{1,0:T(8,128)(2,1)S(1)} %reshape.23.refs_0_), channel_id=1, source_target_pairs={{0,48},{8,56},{16,0},{24,8},{32,16},{40,24},{48,32},{56,40},{1,49}... | collective-permute-start | bytes 36872 | tf_op jit(solution)/shard_map/ppermute | solution.py:270
  23.3 8.5 %collective-permute-start.4 = (bf16[32,192]{1,0:T(8,128)(2,1)S(1)}, bf16[32,192]{1,0:T(8,128)(2,1)S(1)}, u32[]{:S(2)}, u32[]{:S(2)}) collective-permute-start(bf16[32,192]{1,0:T(8,128)(2,1)S(1)} %reshape.23.refs_0_), channel_id=1, source_target_pairs={{0,40},{8,48},{16,56},{24,0},{32,8},{40,16},{48,24},{56,32},{1,41}... | collective-permute-start | bytes 36872 | tf_op jit(solution)/shard_map/ppermute | solution.py:270
  23.7 8.0 %collective-permute-start.3 = (bf16[32,192]{1,0:T(8,128)(2,1)S(1)}, bf16[32,192]{1,0:T(8,128)(2,1)S(1)}, u32[]{:S(2)}, u32[]{:S(2)}) collective-permute-start(bf16[32,192]{1,0:T(8,128)(2,1)S(1)} %reshape.23.refs_0_), channel_id=1, source_target_pairs={{0,32},{8,40},{16,48},{24,56},{32,0},{40,8},{48,16},{56,24},{1,33}... | collective-permute-start | bytes 36872 | tf_op jit(solution)/shard_map/ppermute | solution.py:270
  28.2 5.7 %collective-permute-start.2 = (bf16[32,192]{1,0:T(8,128)(2,1)S(1)}, bf16[32,192]{1,0:T(8,128)(2,1)S(1)}, u32[]{:S(2)}, u32[]{:S(2)}) collective-permute-start(bf16[32,192]{1,0:T(8,128)(2,1)S(1)} %reshape.23.refs_0_), channel_id=1, source_target_pairs={{0,24},{8,32},{16,40},{24,48},{32,56},{40,0},{48,8},{56,16},{1,25}... | collective-permute-start | bytes 36872 | tf_op jit(solution)/shard_map/ppermute | solution.py:270
  28.2 5.9 %collective-permute-start.1 = (bf16[32,192]{1,0:T(8,128)(2,1)S(1)}, bf16[32,192]{1,0:T(8,128)(2,1)S(1)}, u32[]{:S(2)}, u32[]{:S(2)}) collective-permute-start(bf16[32,192]{1,0:T(8,128)(2,1)S(1)} %reshape.23.refs_0_), channel_id=1, source_target_pairs={{0,16},{8,24},{16,32},{24,40},{32,48},{40,56},{48,0},{56,8},{1,17}... | collective-permute-start | bytes 36872 | tf_op jit(solution)/shard_map/ppermute | solution.py:270
  30.4 4.0 %collective-permute-start = (bf16[32,192]{1,0:T(8,128)(2,1)S(1)}, bf16[32,192]{1,0:T(8,128)(2,1)S(1)}, u32[]{:S(2)}, u32[]{:S(2)}) collective-permute-start(bf16[32,192]{1,0:T(8,128)(2,1)S(1)} %reshape.23.refs_0_), channel_id=1, source_target_pairs={{0,8},{8,16},{16,24},{24,32},{32,40},{40,48},{48,56},{56,0},{1,9},... | collective-permute-start | bytes 36872 | tf_op jit(solution)/shard_map/ppermute | solution.py:270
  37.1 0.7 copy-start.5
  37.8 6.0 %copy-start.7 = (f32[3,3,3,1536]{3,2,1,0:T(4,128)S(1)}, f32[3,3,3,1536]{3,2,1,0:T(4,128)}, u32[]{:S(2)}) copy-start(f32[3,3,3,1536]{3,2,1,0:T(4,128)} %param.7) | copy-start | bytes 497668
  37.8 35.0 %all-to-all-start.2 = ((bf16[8,208,256]{2,1,0:T(8,128)(2,1)}), bf16[8,208,256]{2,1,0:T(8,128)(2,1)S(1)}, u32[]{:S(2)}, u32[]{:S(2)}) async-start(bf16[8,208,256]{2,1,0:T(8,128)(2,1)} %get-tuple-element.14), calls=%async_computation.2 | async-start | bytes 1703936 | tf_op jit(solution)/shard_map/all_to_all | solution.py:56
  44.8 12.7 %collective-permute-start.7 = (bf16[192,256]{1,0:T(8,128)(2,1)}, bf16[192,256]{1,0:T(8,128)(2,1)S(1)}, u32[]{:S(2)}, u32[]{:S(2)}) collective-permute-start(bf16[192,256]{1,0:T(8,128)(2,1)} %get-tuple-element.19), channel_id=1, source_target_pairs={{0,64},{64,128},{128,192},{1,65},{65,129},{129,193},{2,66},{66,130... | collective-permute-start | bytes 294920 | tf_op jit(solution)/shard_map/ppermute | solution.py:62
  53.3 7.7 %collective-permute-start.8 = (bf16[192,256]{1,0:T(8,128)(2,1)S(1)}, bf16[192,256]{1,0:T(8,128)(2,1)S(1)}, u32[]{:S(2)}, u32[]{:S(2)}) collective-permute-start(bf16[192,256]{1,0:T(8,128)(2,1)S(1)} %get-tuple-element.20), channel_id=1, source_target_pairs={{64,0},{128,64},{192,128},{65,1},{129,65},{193,129},{66,2},{130,66... | collective-permute-start | bytes 294920 | tf_op jit(solution)/shard_map/ppermute | solution.py:62
  55.4 0.9 %copy-start.6 = (bf16[256,192]{1,0:T(8,128)(2,1)S(1)}, bf16[256,192]{1,0:T(8,128)(2,1)}, u32[]{:S(2)}) copy-start(bf16[256,192]{1,0:T(8,128)(2,1)} %copy-done.5) | copy-start | bytes 294916
  57.5 9.5 %copy-start.2 = (bf16[256,1024]{1,0:T(8,128)(2,1)}, bf16[256,1024]{1,0:T(8,128)(2,1)S(1)}, u32[]{:S(2)}) copy-start(bf16[256,1024]{1,0:T(8,128)(2,1)S(1)} %get-tuple-element.16.one_ref) | copy-start | bytes 1572868
  63.3 9.5 %collective-permute-start.9 = (bf16[192,128]{1,0:T(8,128)(2,1)S(1)}, bf16[192,128]{1,0:T(8,128)(2,1)S(1)}, u32[]{:S(2)}, u32[]{:S(2)}) collective-permute-start(bf16[192,128]{1,0:T(8,128)(2,1)S(1)} %get-tuple-element.21), channel_id=1, source_target_pairs={{0,8},{8,16},{16,24},{24,32},{32,40},{40,48},{48,56},{1,9},{9,17},... | collective-permute-start | bytes 147464 | tf_op jit(solution)/shard_map/ppermute | solution.py:62
  67.0 5.8 %collective-permute-start.10 = (bf16[192,128]{1,0:T(8,128)(2,1)S(1)}, bf16[192,128]{1,0:T(8,128)(2,1)S(1)}, u32[]{:S(2)}, u32[]{:S(2)}) collective-permute-start(bf16[192,128]{1,0:T(8,128)(2,1)S(1)} %get-tuple-element.22), channel_id=1, source_target_pairs={{8,0},{16,8},{24,16},{32,24},{40,32},{48,40},{56,48},{9,1},{17,9},... | collective-permute-start | bytes 147464 | tf_op jit(solution)/shard_map/ppermute | solution.py:62
  71.9 0.9 %copy-start = (f32[8,192,128]{2,1,0:T(8,128)}, f32[8,192,128]{2,1,0:T(8,128)S(1)}, u32[]{:S(2)}) copy-start(f32[8,192,128]{2,1,0:T(8,128)S(1)} %shard_map.51.local_ref) | copy-start | bytes 2359300
  72.8 1.1 %copy-start.1 = (f32[8,192,128]{2,1,0:T(8,128)S(1)}, f32[8,192,128]{2,1,0:T(8,128)}, u32[]{:S(2)}) copy-start(f32[8,192,128]{2,1,0:T(8,128)} %copy-done) | copy-start | bytes 2359300
  74.0 1.0 %copy-start.3 = (bf16[256,1024]{1,0:T(8,128)(2,1)S(1)}, bf16[256,1024]{1,0:T(8,128)(2,1)}, u32[]{:S(2)}) copy-start(bf16[256,1024]{1,0:T(8,128)(2,1)} %copy-done.2) | copy-start | bytes 1572868

commit v5 on v4

--- a/solution.py
+++ b/solution.py
@@ -14,7 +14,8 @@
 COLUMNS = 32
 TOKENS = FRAMES * COLUMNS
 AGENT_DEV = 4
-PLANES = 8
+PAIRS = 4
+PLANES = 2 * PAIRS
 TILES = 8
 AGENTS = 256
 GROUP_HEADS = HEADS // TILES
@@ -22,7 +23,7 @@
 K_ROW = GROUP
 V_ROW = 2 * GROUP
 SENT = 3 * GROUP
-PLANE_AGENTS = TILES * AGENT_DEV
+PAIR_AGENTS = 2 * TILES * AGENT_DEV
 EDGE = TILES * COLUMNS
 STATS = 16
 GRANT = 6 * 1024 * 1024
@@ -57,7 +58,7 @@
 
 
 def shift(x, axis, step):
-    count = lax.axis_size(axis)
+    count = PLANES
     pairs = [(i, i + step) for i in range(count) if 0 <= i + step < count]
     return lax.ppermute(x, axis, pairs)
 
@@ -71,7 +72,9 @@
     sums = jnp.dot(pick, q_ref[...], preferred_element_type=F32)
     pooled = (sums[:AGENT_DEV] * (1.0 / (FRAMES * width))).astype(BF16)
     for tile in range(TILES):
-        out_ref[tile] = pooled[:, tile * GROUP : (tile + 1) * GROUP]
+        part = pooled[:, tile * GROUP : (tile + 1) * GROUP]
+        out_ref[tile] = part
+        out_ref[TILES + tile] = part
 
 
 def pack_kernel(q_ref, k_ref, v_ref, out_ref, came, turned, in_sems, out_sems):
@@ -98,10 +101,10 @@
 
 
 def agent_kernel(z_ref, *refs):
-    came, (x_ref, out_ref, a_ref) = refs[:PLANES], refs[PLANES:]
+    came, (x_ref, out_ref, a_ref) = refs[:PAIRS], refs[PAIRS:]
     for hop, ref in enumerate(came):
-        z = lax.rem(z_ref[0] + PLANES - hop, PLANES)
-        a_ref[pl.ds(pl.multiple_of(z * PLANE_AGENTS, PLANE_AGENTS), PLANE_AGENTS), :] = ref[...]
+        z = lax.rem(z_ref[0] + PAIRS - hop, PAIRS)
+        a_ref[pl.ds(pl.multiple_of(z * PAIR_AGENTS, PAIR_AGENTS), PAIR_AGENTS), :] = ref[...]
     columns = []
     lane = lax.broadcasted_iota(jnp.int32, (AGENTS, HEAD_DIM), 1)
     stats = jnp.zeros((AGENTS, HEAD_DIM), F32)
@@ -141,7 +144,18 @@
             rest_ref[h - 1] = weights.astype(BF16)
 
 
-def edge_kernel(x_ref, last_ref, first_ref):
+def taps_kernel(tile_ref, w_ref, out_ref):
+    for tile in range(TILES):
+
+        @pl.when(tile_ref[0] == tile)
+        def _(tile=tile):
+            lanes = slice(tile * GROUP, (tile + 1) * GROUP)
+            rows = [w_ref[i, j, :, lanes] for i in range(3) for j in range(3)]
+            rows.append(jnp.zeros((5, GROUP), F32))
+            out_ref[...] = jnp.concatenate(rows, axis=0).T
+
+
+def edge_kernel(even_ref, x_ref, near_ref, far_ref):
     spot = lax.broadcasted_iota(jnp.int32, (GROUP, TOKENS), 1) // COLUMNS
     for block in range(EDGE // TOKENS):
         last = first = jnp.zeros((GROUP, TOKENS), F32)
@@ -152,8 +166,17 @@
             last = jnp.where(spot == j, late, last)
             first = jnp.where(spot == j, early, first)
         lanes = slice(block * TOKENS, (block + 1) * TOKENS)
-        last_ref[:, lanes] = last.astype(BF16)
-        first_ref[:, lanes] = first.astype(BF16)
+        last, first = last.astype(BF16), first.astype(BF16)
+
+        @pl.when(even_ref[0] == 1)
+        def _(last=last, first=first, lanes=lanes):
+            near_ref[:, lanes] = last
+            far_ref[:, lanes] = first
+
+        @pl.when(even_ref[0] != 1)
+        def _(last=last, first=first, lanes=lanes):
+            near_ref[:, lanes] = first
+            far_ref[:, lanes] = last
 
 
 TALL = 16
@@ -164,13 +187,15 @@
     return cells if by == 0 else pltpu.roll(cells, by, 1)
 
 
-def frames_of(r, at, x_ref, before_ref, after_ref):
+def frames_of(r, at, even, x_ref, near_ref, far_ref):
     lane = lax.broadcasted_iota(jnp.int32, (TALL, TOKENS), 1)
     cells = x_ref[r, pl.ds(V_ROW + at, TALL), :].astype(F32)
     block, j = divmod(r, FRAMES)
     lanes = slice(block * TOKENS, (block + 1) * TOKENS)
-    before = turned(before_ref[pl.ds(at, TALL), lanes].astype(F32), -j * COLUMNS)
-    after = turned(after_ref[pl.ds(at, TALL), lanes].astype(F32), (FRAMES - 1 - j) * COLUMNS)
+    near = near_ref[pl.ds(at, TALL), lanes].astype(F32)
+    far = far_ref[pl.ds(at, TALL), lanes].astype(F32)
+    before = turned(jnp.where(even, far, near), -j * COLUMNS)
+    after = turned(jnp.where(even, near, far), (FRAMES - 1 - j) * COLUMNS)
     return (
         jnp.where(lane < COLUMNS, before, turned(cells, COLUMNS)),
         cells,
@@ -204,25 +229,24 @@
     return left + sums[1] + right
 
 
-def rim_kernel(x_ref, before_ref, after_ref, w_ref, up_ref, down_ref):
-    def step(n, carry):
-        at = pl.multiple_of(n * TALL, TALL)
+def rim_kernel(even_ref, x_ref, near_ref, far_ref, w_ref, up_ref, down_ref):
+    even = even_ref[0] == 1
+    for at in range(0, GROUP, TALL):
         for r, j, ref in ((TILES - 1, 0, up_ref), (0, 2, down_ref)):
-            frames = frames_of(r, at, x_ref, before_ref, after_ref)
+            frames = frames_of(r, at, even, x_ref, near_ref, far_ref)
             ref[pl.ds(at, TALL), :] = stencil({j: frames}, taps_of(w_ref, at, (j,))).astype(BF16)
-        return carry
-
-    lax.fori_loop(0, GROUP // TALL, step, 0)
-
-
-def conv_kernel(x_ref, before_ref, after_ref, w_ref, out_ref):
+
+
+def conv_kernel(even_ref, x_ref, near_ref, far_ref, w_ref, out_ref):
+    even = even_ref[0] == 1
+
     def step(n, carry):
         at = pl.multiple_of(n * TALL, TALL)
         taps = taps_of(w_ref, at)
-        rows = {0: frames_of(0, at, x_ref, before_ref, after_ref)}
+        rows = {0: frames_of(0, at, even, x_ref, near_ref, far_ref)}
         for r in range(TILES):
             if r + 1 < TILES:
-                rows[r + 1] = frames_of(r + 1, at, x_ref, before_ref, after_ref)
+                rows[r + 1] = frames_of(r + 1, at, even, x_ref, near_ref, far_ref)
             near = {j: rows[r + j - 1] for j in range(3) if r + j - 1 in rows}
             out_ref[r, pl.ds(at, TALL), :] = stencil(near, taps)
             rows.pop(r - 1, None)
@@ -265,9 +289,8 @@
     out_ref[...] = x_ref[...].reshape(D, TOKENS).T
 
 
-def turn(x, axis, step):
-    count = lax.axis_size(axis)
-    return lax.ppermute(x, axis, [(i, (i + step) % count) for i in range(count)])
+def scalar(x):
+    return x.astype(jnp.int32).reshape(1)
 
 
 def body(queries, key_states, value_states, conv_weight):
@@ -275,7 +298,7 @@
     k = key_states.reshape(TOKENS, D)
     v = value_states.reshape(TOKENS, D)
     shape = jax.ShapeDtypeStruct
-    pooled = call(pool_kernel, shape((TILES, AGENT_DEV, GROUP), BF16), 1.0, q)
+    pooled = call(pool_kernel, shape((2 * TILES, AGENT_DEV, GROUP), BF16), 1.0, q)
     packed = call(
         pack_kernel,
         shape((TILES, SENT, TOKENS), BF16),
@@ -291,9 +314,13 @@
         ),
         far=True,
     )
-    own = exchange(pooled, "xy").reshape(PLANE_AGENTS, GROUP)
+    own = exchange(pooled, ("zl", "xy")).reshape(PAIR_AGENTS, GROUP)
     x = exchange(packed, "xy")
-    came = [own] + [turn(own, "z", n) for n in range(1, PLANES)]
+    came = [own]
+    for n in range(1, PAIRS):
+        came.append(lax.ppermute(own, "zh", [(i, (i + n) % PAIRS) for i in range(PAIRS)]))
+    tile = scalar(lax.axis_index("xy"))
+    taps = call(taps_kernel, shape((GROUP, 32), F32), 1.0, conv_weight, scalars=(tile,))
 
     part, agents = call(
         agent_kernel,
@@ -301,14 +328,18 @@
         4.0,
         *came,
         x,
-        scalars=(lax.axis_index("z").astype(jnp.int32).reshape(1),),
-    )
-    parts = exchange(part, "z")
+        scalars=(scalar(lax.axis_index("zh")),),
+    )
+    parts = exchange(part, ("zh", "zl"))
 
     edges = shape((GROUP, EDGE), BF16)
-    last, first = call(edge_kernel, (edges, edges), 1.0, x)
-    before = shift(last, "tm", 1)
-    after = shift(first, "tm", -1)
+    even = scalar(1 - lax.axis_index("tm") % 2)
+    near, far = call(edge_kernel, (edges, edges), 1.0, x, scalars=(even,))
+    groups = lax.axis_size("tm")
+    pairs = [(i, i + 1) for i in range(0, groups - 1, 2)]
+    near = lax.ppermute(near, "tm", pairs + [(b, a) for a, b in pairs])
+    pairs = [(i, i + 1) for i in range(1, groups - 1, 2)]
+    far = lax.ppermute(far, "tm", pairs + [(b, a) for a, b in pairs])
     cells = TILES * TOKENS
     one, rest, totals = call(
         query_kernel,
@@ -321,14 +352,13 @@
         agents,
         x,
     )
-    taps = lax.dynamic_index_in_dim(
-        conv_weight.reshape(27, TILES, GROUP), lax.axis_index("xy"), 1, keepdims=False
-    ).T
     row = shape((GROUP, TOKENS), BF16)
-    to_next, to_last = call(rim_kernel, (row, row), 1.0, x, before, after, taps)
-    up = shift(to_next, "z", 1)
-    down = shift(to_last, "z", -1)
-    local = call(conv_kernel, shape((TILES, GROUP, TOKENS), F32), 5.0, x, before, after, taps)
+    to_next, to_last = call(rim_kernel, (row, row), 1.0, x, near, far, taps, scalars=(even,))
+    up = shift(to_next, ("zh", "zl"), 1)
+    down = shift(to_last, ("zh", "zl"), -1)
+    local = call(
+        conv_kernel, shape((TILES, GROUP, TOKENS), F32), 5.0, x, near, far, taps, scalars=(even,)
+    )
     mixed = call(
         mix_kernel,
         shape((TILES, GROUP, TOKENS), BF16),
@@ -348,8 +378,8 @@
 
 def solution(mesh):
     devices = mesh.devices
-    fine = Mesh(devices.reshape(devices.shape[0], PLANES, TILES), ("tm", "z", "xy"))
-    spec = P("tm", None, ("z", "xy"), None, None)
+    fine = Mesh(devices.reshape(devices.shape[0], PAIRS, 2, TILES), ("tm", "zh", "zl", "xy"))
+    spec = P("tm", None, ("zh", "zl", "xy"), None, None)
     return jax.shard_map(
         body,
         mesh=fine,

time: 88.3 us -> 86.3 us (0.977)
  the two profiles are of different devices: /device:TPU:1 before, /device:TPU:4 now
where the time goes in v5:
time: 86.3 us; the launch traced here: 85.7 us
  starting transfers between devices  35.2 us (41%)
  waiting for transfers between devices  16 us (19%)
  Pallas kernels  14.7 us (17%)
  blocking collectives  13.9 us (16%)
  local copies, waits for them, and re-layouts  5.67 us (7%)
    all_to_all x3, starting transfers between devices, exchange(): return lax.all_to_all(x, axes, 0, 0)  17.8 us
    pallas_call x10, Pallas kernels, call(): pl.pallas_call(kernel, out_shape=out_shape, in_specs=[SMEM] * len(scalars...  14.7 us
    all_to_all x1, blocking collectives, exchange(): return lax.all_to_all(x, axes, 0, 0)  13.9 us
    ppermute x3, starting transfers between devices, body(): lax.ppermute(own, 'zh', [(i, (i + n) % PAIRS) for i in range(PAIRS)])  9.29 us
    all_to_all x3, waiting for transfers between devices, exchange(): return lax.all_to_all(x, axes, 0, 0)  9.24 us
    unnamed x16, local copies, waits for them, and re-layouts  5.65 us
    ppermute x2, starting transfers between devices, shift(): return lax.ppermute(x, axis, pairs)  5.22 us
    ppermute x3, waiting for transfers between devices, body(): lax.ppermute(own, 'zh', [(i, (i + n) % PAIRS) for i in range(PAIRS)])  4.01 us
  transfers between devices with their start and end apart: 10, of which 6 were waited for; matrix products, arithmetic and copies ran while one was open for 0% of the time, Pallas kernels for 11%

profile of v5, /device:TPU:4, one launch (start us, length us, event | category | flops | bytes accessed | tf_op | source)
XLA Modules:
  0.0 85.7 jit_solution(13550767522576253550)
XLA Ops:
  0.0 1.0 %copy-done.4 = bf16[1,4,1,32,1536]{4,3,2,1,0:T(8,128)(2,1)S(1)} copy-done((bf16[1,4,1,32,1536]{4,3,2,1,0:T(8,128)(2,1)S(1)}, bf16[1,4,1,32,1536]{4,3,2,1,0:T(8,128)(2,1)}, u32[]{:S(2)}) %copy-start.4) | copy-done | bytes 393240
  1.9 6.6 %all-to-all-start = ((bf16[16,4,192]{2,1,0:T(4,128)(2,1)}), bf16[16,4,192]{2,1,0:T(4,128)(2,1)S(1)}, u32[]{:S(2)}, u32[]{:S(2)}) async-start(bf16[16,4,192]{2,1,0:T(4,128)(2,1)} %shard_map.46), calls=%async_computation | async-start | bytes 65536 | tf_op jit(solution)/shard_map/all_to_all | solution.py:57
  8.4 2.3 %shard_map.47 = bf16[8,576,128]{2,1,0:T(8,128)(2,1)} custom-call(bf16[128,1536]{1,0:T(8,128)(2,1)} %bitcast.9, bf16[128,1536]{1,0:T(8,128)(2,1)} %bitcast.11, bf16[128,1536]{1,0:T(8,128)(2,1)} %bitcast.12), custom_call_target="tpu_custom_call" | custom-call | flops 900000000 | bytes 6000000 | tf_op jit(solution)/shard_map/pallas_call | solution.py:45
  10.7 4.9 %all-to-all-done = bf16[16,4,192]{2,1,0:T(4,128)(2,1)S(1)} async-done(((bf16[16,4,192]{2,1,0:T(4,128)(2,1)}), bf16[16,4,192]{2,1,0:T(4,128)(2,1)S(1)}, u32[]{:S(2)}, u32[]{:S(2)}) %all-to-all-start) | async-done | bytes 24608 | tf_op jit(solution)/shard_map/all_to_all | solution.py:57
  15.6 3.6 %all-to-all-start.1 = ((bf16[8,576,128]{2,1,0:T(8,128)(2,1)}), bf16[8,576,128]{2,1,0:T(8,128)(2,1)S(1)}, u32[]{:S(2)}, u32[]{:S(2)}) async-start(bf16[8,576,128]{2,1,0:T(8,128)(2,1)} %shard_map.47), calls=%async_computation.1 | async-start | bytes 2359296 | tf_op jit(solution)/shard_map/all_to_all | solution.py:57
  19.2 5.5 %collective-permute-start.2 = (bf16[64,192]{1,0:T(8,128)(2,1)S(1)}, bf16[64,192]{1,0:T(8,128)(2,1)S(1)}, u32[]{:S(2)}, u32[]{:S(2)}) collective-permute-start(bf16[64,192]{1,0:T(8,128)(2,1)S(1)} %reshape.26.refs_0_), channel_id=1, source_target_pairs={{0,48},{16,0},{32,16},{48,32},{1,49},{17,1},{33,17},{49,33},{2,50}... | collective-permute-start | bytes 73736 | tf_op jit(solution)/shard_map/ppermute | solution.py:321
  24.7 1.4 %collective-permute-start.1 = (bf16[64,192]{1,0:T(8,128)(2,1)S(1)}, bf16[64,192]{1,0:T(8,128)(2,1)S(1)}, u32[]{:S(2)}, u32[]{:S(2)}) collective-permute-start(bf16[64,192]{1,0:T(8,128)(2,1)S(1)} %reshape.26.refs_0_), channel_id=1, source_target_pairs={{0,32},{16,48},{32,0},{48,16},{1,33},{17,49},{33,1},{49,17},{2,34}... | collective-permute-start | bytes 73736 | tf_op jit(solution)/shard_map/ppermute | solution.py:321
  26.1 2.4 %collective-permute-start = (bf16[64,192]{1,0:T(8,128)(2,1)S(1)}, bf16[64,192]{1,0:T(8,128)(2,1)S(1)}, u32[]{:S(2)}, u32[]{:S(2)}) collective-permute-start(bf16[64,192]{1,0:T(8,128)(2,1)S(1)} %reshape.26.refs_0_), channel_id=1, source_target_pairs={{0,16},{16,32},{32,48},{48,0},{1,17},{17,33},{33,49},{49,1},{2,18}... | collective-permute-start | bytes 73736 | tf_op jit(solution)/shard_map/ppermute | solution.py:321
  28.5 4.0 %collective-permute-done.1.refs_2_ = bf16[64,192]{1,0:T(8,128)(2,1)S(1)} collective-permute-done((bf16[64,192]{1,0:T(8,128)(2,1)S(1)}, bf16[64,192]{1,0:T(8,128)(2,1)S(1)}, u32[]{:S(2)}, u32[]{:S(2)}) %collective-permute-start.1) | collective-permute-done | bytes 24608 | tf_op jit(solution)/shard_map/ppermute | solution.py:321
  32.5 1.6 %all-to-all-done.1.refs_4_.x_ref = bf16[8,576,128]{2,1,0:T(8,128)(2,1)S(1)} async-done(((bf16[8,576,128]{2,1,0:T(8,128)(2,1)}), bf16[8,576,128]{2,1,0:T(8,128)(2,1)S(1)}, u32[]{:S(2)}, u32[]{:S(2)}) %all-to-all-start.1) | async-done | bytes 1179680 | tf_op jit(solution)/shard_map/all_to_all | solution.py:57
  34.1 2.7 %shard_map.48 = (bf16[8,208,256]{2,1,0:T(8,128)(2,1)}, bf16[256,192]{1,0:T(8,128)(2,1)S(1)}) custom-call(s32[1]{0:T(128)} %bitcast.z_ref, bf16[64,192]{1,0:T(8,128)(2,1)S(1)} %reshape.26.refs_0_, bf16[64,192]{1,0:T(8,128)(2,1)S(1)} %collective-permute-done.refs_1_, bf16[64,192]{1,0:T(8,128)(2,1)S(1)} %collective-permute-done.1.refs_2_, ...), custom_call_target="tpu_custom_call" | custom-call | flops 1200000000 | bytes 8000000 | tf_op jit(solution)/shard_map/pallas_call | solution.py:45
  37.5 7.7 %all-to-all-start.2 = ((bf16[8,208,256]{2,1,0:T(8,128)(2,1)}), bf16[8,208,256]{2,1,0:T(8,128)(2,1)S(1)}, u32[]{:S(2)}, u32[]{:S(2)}) async-start(bf16[8,208,256]{2,1,0:T(8,128)(2,1)} %get-tuple-element.14), calls=%async_computation.2 | async-start | bytes 1703936 | tf_op jit(solution)/shard_map/all_to_all | solution.py:57
  45.6 2.8 %collective-permute-start.4 = (bf16[192,256]{1,0:T(8,128)(2,1)S(1)}, bf16[192,256]{1,0:T(8,128)(2,1)S(1)}, u32[]{:S(2)}, u32[]{:S(2)}) collective-permute-start(bf16[192,256]{1,0:T(8,128)(2,1)S(1)} %get-tuple-element.20), channel_id=1, source_target_pairs={{64,128},{128,64},{65,129},{129,65},{66,130},{130,66},{67,131},{13... | collective-permute-start | bytes 294920 | tf_op jit(solution)/shard_map/ppermute | solution.py:342
  49.5 1.2 %shard_map.49 = (bf16[256,1024]{1,0:T(8,128)(2,1)S(1)}, bf16[2,256,1024]{2,1,0:T(8,128)(2,1)S(1)}, f32[8,1024]{1,0:T(8,128)S(1)}) custom-call(bf16[256,192]{1,0:T(8,128)(2,1)S(1)} %copy-done.7, bf16[8,576,128]{2,1,0:T(8,128)(2,1)S(1)} %all-to-all-done.1.refs_4_.x_ref), custom_call_target="tpu_custom_call" | custom-call | flops 600000000 | bytes 4000000 | tf_op jit(solution)/shard_map/pallas_call | solution.py:45
  50.7 2.3 %collective-permute-done.4.far_ref = bf16[192,256]{1,0:T(8,128)(2,1)S(1)} collective-permute-done((bf16[192,256]{1,0:T(8,128)(2,1)S(1)}, bf16[192,256]{1,0:T(8,128)(2,1)S(1)}, u32[]{:S(2)}, u32[]{:S(2)}) %collective-permute-start.4) | collective-permute-done | bytes 98336 | tf_op jit(solution)/shard_map/ppermute | solution.py:342
  53.0 2.3 %shard_map.53 = (bf16[192,128]{1,0:T(8,128)(2,1)S(1)}, bf16[192,128]{1,0:T(8,128)(2,1)S(1)}) custom-call(s32[1]{0:T(128)} %bitcast.4.even_ref, bf16[8,576,128]{2,1,0:T(8,128)(2,1)S(1)} %all-to-all-done.1.refs_4_.x_ref, bf16[192,256]{1,0:T(8,128)(2,1)S(1)} %collective-permute-done.3.near_ref, bf16[192,256]{1,0:T(8,128)(2,1)S(1)} %collective-permute-done.4.far_ref, ...), custom_call_target="tpu_custom_call" | custom-call | flops 300000000 | bytes 2000000 | tf_op jit(solution)/shard_map/pallas_call | solution.py:45
  55.4 3.9 %collective-permute-start.5 = (bf16[192,128]{1,0:T(8,128)(2,1)S(1)}, bf16[192,128]{1,0:T(8,128)(2,1)S(1)}, u32[]{:S(2)}, u32[]{:S(2)}) collective-permute-start(bf16[192,128]{1,0:T(8,128)(2,1)S(1)} %get-tuple-element.21), channel_id=1, source_target_pairs={{0,8},{8,16},{16,24},{24,32},{32,40},{40,48},{48,56},{1,9},{9,17},... | collective-permute-start | bytes 147464 | tf_op jit(solution)/shard_map/ppermute | solution.py:63
  59.3 1.3 %collective-permute-start.6 = (bf16[192,128]{1,0:T(8,128)(2,1)S(1)}, bf16[192,128]{1,0:T(8,128)(2,1)S(1)}, u32[]{:S(2)}, u32[]{:S(2)}) collective-permute-start(bf16[192,128]{1,0:T(8,128)(2,1)S(1)} %get-tuple-element.22), channel_id=1, source_target_pairs={{8,0},{16,8},{24,16},{32,24},{40,32},{48,40},{56,48},{9,1},{17,9},... | collective-permute-start | bytes 147464 | tf_op jit(solution)/shard_map/ppermute | solution.py:63
  60.6 3.5 %shard_map.52.local_ref = f32[8,192,128]{2,1,0:T(8,128)S(1)} custom-call(s32[1]{0:T(128)} %bitcast.4.even_ref, bf16[8,576,128]{2,1,0:T(8,128)(2,1)S(1)} %all-to-all-done.1.refs_4_.x_ref, bf16[192,256]{1,0:T(8,128)(2,1)S(1)} %collective-permute-done.3.near_ref, bf16[192,256]{1,0:T(8,128)(2,1)S(1)} %collective-permute-done.4.far_ref, ...), custom_call_target="tpu_custom_call" | custom-call | flops 1500000000 | bytes 10000000 | tf_op jit(solution)/shard_map/pallas_call | solution.py:45
  64.2 0.9 %copy-done = f32[8,192,128]{2,1,0:T(8,128)} copy-done((f32[8,192,128]{2,1,0:T(8,128)}, f32[8,192,128]{2,1,0:T(8,128)S(1)}, u32[]{:S(2)}) %copy-start) | copy-done | bytes 786456
  65.5 2.7 %all-to-all-done.2.parts_ref = bf16[8,208,256]{2,1,0:T(8,128)(2,1)S(1)} async-done(((bf16[8,208,256]{2,1,0:T(8,128)(2,1)}), bf16[8,208,256]{2,1,0:T(8,128)(2,1)S(1)}, u32[]{:S(2)}, u32[]{:S(2)}) %all-to-all-start.2) | async-done | bytes 852000 | tf_op jit(solution)/shard_map/all_to_all | solution.py:57
  68.2 1.1 %copy-done.1 = f32[8,192,128]{2,1,0:T(8,128)S(1)} copy-done((f32[8,192,128]{2,1,0:T(8,128)S(1)}, f32[8,192,128]{2,1,0:T(8,128)}, u32[]{:S(2)}) %copy-start.1) | copy-done | bytes 786456
  69.3 1.0 %copy-done.3 = bf16[256,1024]{1,0:T(8,128)(2,1)S(1)} copy-done((bf16[256,1024]{1,0:T(8,128)(2,1)S(1)}, bf16[256,1024]{1,0:T(8,128)(2,1)}, u32[]{:S(2)}) %copy-start.3) | copy-done | bytes 524312
  70.9 13.9 %all_to_all.20.x_ref = bf16[8,192,128]{2,1,0:T(8,128)(2,1)S(1)} all-to-all(bf16[8,192,128]{2,1,0:T(8,128)(2,1)S(1)} %shard_map.54), channel_id=1, replica_groups=mesh['tm'=4,'zh'=4,'zl'=2,'xy'=8] {'xy'}, dimensions={0} | all-to-all | bytes 786432 | tf_op jit(solution)/shard_map/all_to_all | solution.py:57
  (24 shorter events, 4.8 us)
Async XLA Ops:
  0.0 1.0 %copy-start.4 = (bf16[1,4,1,32,1536]{4,3,2,1,0:T(8,128)(2,1)S(1)}, bf16[1,4,1,32,1536]{4,3,2,1,0:T(8,128)(2,1)}, u32[]{:S(2)}) copy-start(bf16[1,4,1,32,1536]{4,3,2,1,0:T(8,128)(2,1)} %param.4) | copy-start | bytes 1179652
  1.9 13.7 %all-to-all-start = ((bf16[16,4,192]{2,1,0:T(4,128)(2,1)}), bf16[16,4,192]{2,1,0:T(4,128)(2,1)S(1)}, u32[]{:S(2)}, u32[]{:S(2)}) async-start(bf16[16,4,192]{2,1,0:T(4,128)(2,1)} %shard_map.46), calls=%async_computation | async-start | bytes 65536 | tf_op jit(solution)/shard_map/all_to_all | solution.py:57
  15.6 18.5 %all-to-all-start.1 = ((bf16[8,576,128]{2,1,0:T(8,128)(2,1)}), bf16[8,576,128]{2,1,0:T(8,128)(2,1)S(1)}, u32[]{:S(2)}, u32[]{:S(2)}) async-start(bf16[8,576,128]{2,1,0:T(8,128)(2,1)} %shard_map.47), calls=%async_computation.1 | async-start | bytes 2359296 | tf_op jit(solution)/shard_map/all_to_all | solution.py:57
  19.2 9.3 %collective-permute-start.2 = (bf16[64,192]{1,0:T(8,128)(2,1)S(1)}, bf16[64,192]{1,0:T(8,128)(2,1)S(1)}, u32[]{:S(2)}, u32[]{:S(2)}) collective-permute-start(bf16[64,192]{1,0:T(8,128)(2,1)S(1)} %reshape.26.refs_0_), channel_id=1, source_target_pairs={{0,48},{16,0},{32,16},{48,32},{1,49},{17,1},{33,17},{49,33},{2,50}... | collective-permute-start | bytes 73736 | tf_op jit(solution)/shard_map/ppermute | solution.py:321
  24.7 7.8 %collective-permute-start.1 = (bf16[64,192]{1,0:T(8,128)(2,1)S(1)}, bf16[64,192]{1,0:T(8,128)(2,1)S(1)}, u32[]{:S(2)}, u32[]{:S(2)}) collective-permute-start(bf16[64,192]{1,0:T(8,128)(2,1)S(1)} %reshape.26.refs_0_), channel_id=1, source_target_pairs={{0,32},{16,48},{32,0},{48,16},{1,33},{17,49},{33,1},{49,17},{2,34}... | collective-permute-start | bytes 73736 | tf_op jit(solution)/shard_map/ppermute | solution.py:321
  26.1 6.4 %collective-permute-start = (bf16[64,192]{1,0:T(8,128)(2,1)S(1)}, bf16[64,192]{1,0:T(8,128)(2,1)S(1)}, u32[]{:S(2)}, u32[]{:S(2)}) collective-permute-start(bf16[64,192]{1,0:T(8,128)(2,1)S(1)} %reshape.26.refs_0_), channel_id=1, source_target_pairs={{0,16},{16,32},{32,48},{48,0},{1,17},{17,33},{33,49},{49,1},{2,18}... | collective-permute-start | bytes 73736 | tf_op jit(solution)/shard_map/ppermute | solution.py:321
  36.8 0.7 copy-start.6
  37.5 11.0 %copy-start.5 = (f32[3,3,3,1536]{3,2,1,0:T(4,128)S(1)}, f32[3,3,3,1536]{3,2,1,0:T(4,128)}, u32[]{:S(2)}) copy-start(f32[3,3,3,1536]{3,2,1,0:T(4,128)} %w_ref.1) | copy-start | bytes 497668
  37.5 30.7 %all-to-all-start.2 = ((bf16[8,208,256]{2,1,0:T(8,128)(2,1)}), bf16[8,208,256]{2,1,0:T(8,128)(2,1)S(1)}, u32[]{:S(2)}, u32[]{:S(2)}) async-start(bf16[8,208,256]{2,1,0:T(8,128)(2,1)} %get-tuple-element.14), calls=%async_computation.2 | async-start | bytes 1703936 | tf_op jit(solution)/shard_map/all_to_all | solution.py:57
  45.5 5.2 %collective-permute-start.3 = (bf16[192,256]{1,0:T(8,128)(2,1)S(1)}, bf16[192,256]{1,0:T(8,128)(2,1)S(1)}, u32[]{:S(2)}, u32[]{:S(2)}) collective-permute-start(bf16[192,256]{1,0:T(8,128)(2,1)S(1)} %get-tuple-element.19), channel_id=1, source_target_pairs={{0,64},{128,192},{64,0},{192,128},{1,65},{129,193},{65,1},{193,129... | collective-permute-start | bytes 294920 | tf_op jit(solution)/shard_map/ppermute | solution.py:340
  45.6 7.4 %collective-permute-start.4 = (bf16[192,256]{1,0:T(8,128)(2,1)S(1)}, bf16[192,256]{1,0:T(8,128)(2,1)S(1)}, u32[]{:S(2)}, u32[]{:S(2)}) collective-permute-start(bf16[192,256]{1,0:T(8,128)(2,1)S(1)} %get-tuple-element.20), channel_id=1, source_target_pairs={{64,128},{128,64},{65,129},{129,65},{66,130},{130,66},{67,131},{13... | collective-permute-start | bytes 294920 | tf_op jit(solution)/shard_map/ppermute | solution.py:342
  48.6 0.9 %copy-start.7 = (bf16[256,192]{1,0:T(8,128)(2,1)S(1)}, bf16[256,192]{1,0:T(8,128)(2,1)}, u32[]{:S(2)}) copy-start(bf16[256,192]{1,0:T(8,128)(2,1)} %copy-done.6) | copy-start | bytes 294916
  50.7 8.6 %copy-start.2 = (bf16[256,1024]{1,0:T(8,128)(2,1)}, bf16[256,1024]{1,0:T(8,128)(2,1)S(1)}, u32[]{:S(2)}) copy-start(bf16[256,1024]{1,0:T(8,128)(2,1)S(1)} %get-tuple-element.16.one_ref) | copy-start | bytes 1572868
  55.4 9.7 %collective-permute-start.5 = (bf16[192,128]{1,0:T(8,128)(2,1)S(1)}, bf16[192,128]{1,0:T(8,128)(2,1)S(1)}, u32[]{:S(2)}, u32[]{:S(2)}) collective-permute-start(bf16[192,128]{1,0:T(8,128)(2,1)S(1)} %get-tuple-element.21), channel_id=1, source_target_pairs={{0,8},{8,16},{16,24},{24,32},{32,40},{40,48},{48,56},{1,9},{9,17},... | collective-permute-start | bytes 147464 | tf_op jit(solution)/shard_map/ppermute | solution.py:63
  59.3 6.2 %collective-permute-start.6 = (bf16[192,128]{1,0:T(8,128)(2,1)S(1)}, bf16[192,128]{1,0:T(8,128)(2,1)S(1)}, u32[]{:S(2)}, u32[]{:S(2)}) collective-permute-start(bf16[192,128]{1,0:T(8,128)(2,1)S(1)} %get-tuple-element.22), channel_id=1, source_target_pairs={{8,0},{16,8},{24,16},{32,24},{40,32},{48,40},{56,48},{9,1},{17,9},... | collective-permute-start | bytes 147464 | tf_op jit(solution)/shard_map/ppermute | solution.py:63
  64.1 0.9 %copy-start = (f32[8,192,128]{2,1,0:T(8,128)}, f32[8,192,128]{2,1,0:T(8,128)S(1)}, u32[]{:S(2)}) copy-start(f32[8,192,128]{2,1,0:T(8,128)S(1)} %shard_map.52.local_ref) | copy-start | bytes 2359300
  68.2 1.1 %copy-start.1 = (f32[8,192,128]{2,1,0:T(8,128)S(1)}, f32[8,192,128]{2,1,0:T(8,128)}, u32[]{:S(2)}) copy-start(f32[8,192,128]{2,1,0:T(8,128)} %copy-done) | copy-start | bytes 2359300
  69.3 1.0 %copy-start.3 = (bf16[256,1024]{1,0:T(8,128)(2,1)S(1)}, bf16[256,1024]{1,0:T(8,128)(2,1)}, u32[]{:S(2)}) copy-start(bf16[256,1024]{1,0:T(8,128)(2,1)} %copy-done.2) | copy-start | bytes 1572868

commit v6 on v5

v6 whole, which is shorter than its diff:
```python
import jax
import jax.numpy as jnp
from jax import lax
from jax.experimental import pallas as pl
from jax.experimental.pallas import tpu as pltpu
from jax.sharding import Mesh
from jax.sharding import PartitionSpec as P


HEADS = 24
HEAD_DIM = 64
D = 1536
FRAMES = 4
COLUMNS = 32
TOKENS = FRAMES * COLUMNS
AGENT_DEV = 4
PLANES = 8
TILES = 8
AGENTS = 256
OWNED = AGENTS // PLANES
SLOT = 8
GROUP_HEADS = HEADS // TILES
GROUP = GROUP_HEADS * HEAD_DIM
K_ROW = GROUP
V_ROW = 2 * GROUP
SENT = 3 * GROUP
EDGE_ROWS = TILES + 2
EDGE = 3 * TOKENS
PART = 256
GRANT = 6 * 1024 * 1024
ALL = 60 * 1024 * 1024
INV_ROOT = HEAD_DIM ** (-0.5)
F32 = jnp.float32
BF16 = jnp.bfloat16


VMEM = pl.BlockSpec(memory_space=pltpu.VMEM)

SMEM = pl.BlockSpec(memory_space=pltpu.SMEM)
HBM = pl.BlockSpec(memory_space=pltpu.HBM)


def call(kernel, out_shape, us, *args, scalars=(), scratch=(), far=None):
    cost = pl.CostEstimate(flops=int(us * 3.0e8), bytes_accessed=int(us * 2.0e6), transcendentals=0)
    outs = out_shape if isinstance(out_shape, tuple) else (out_shape,)
    out_specs = tuple(HBM if n == far else VMEM for n in range(len(outs)))
    return pl.pallas_call(
        kernel,
        out_shape=out_shape,
        in_specs=[SMEM] * len(scalars) + [VMEM if far is None else HBM] * len(args),
        out_specs=out_specs if isinstance(out_shape, tuple) else out_specs[0],
        scratch_shapes=list(scratch),
        cost_estimate=cost,
        compiler_params=pltpu.CompilerParams(vmem_limit_bytes=GRANT if far is None else ALL),
    )(*scalars, *args)


def exchange(x, axes):
    return lax.all_to_all(x, axes, 0, 0)


def shift(x, axis, step):
    count = PLANES
    pairs = [(i, i + step) for i in range(count) if 0 <= i + step < count]
    return lax.ppermute(x, axis, pairs)


def pack_kernel(q_ref, k_ref, v_ref, out_ref, pooled_ref, came, turned, in_sems, out_sems):
    refs = (q_ref, k_ref, v_ref)
    loads = [pltpu.make_async_copy(ref, came.at[n], in_sems.at[n]) for n, ref in enumerate(refs)]
    for load in loads:
        load.start()
    stores = []
    for n, load in enumerate(loads):
        load.wait()
        flipped = came[n].T
        for tile in range(TILES):
            turned[n, tile] = flipped[tile * GROUP : (tile + 1) * GROUP]
        rows = pl.ds(n * GROUP, GROUP)
        store = pltpu.make_async_copy(turned.at[n], out_ref.at[:, rows, :], out_sems.at[n])
        store.start()
        stores.append(store)
    shape = (SLOT, TOKENS)
    token = lax.broadcasted_iota(jnp.int32, shape, 1)
    agent = lax.broadcasted_iota(jnp.int32, shape, 0)
    width = COLUMNS // AGENT_DEV
    pick = ((token % COLUMNS) // width == agent).astype(F32).astype(BF16)
    sums = jnp.dot(pick, came[0], preferred_element_type=F32)
    pooled_ref[...] = (sums * (1.0 / (FRAMES * width))).astype(BF16)
    for store in stores:
        store.wait()


def route_kernel(z_ref, *refs):
    came, out_ref = refs[:PLANES], refs[PLANES]
    rows = jnp.concatenate([ref[...].astype(F32) for ref in came], axis=0).astype(BF16)
    shape = (OWNED, PLANES * SLOT)
    to = lax.broadcasted_iota(jnp.int32, shape, 0)
    at = lax.broadcasted_iota(jnp.int32, shape, 1)
    hop = (z_ref[0] + PLANES - to // AGENT_DEV) % PLANES
    pick = (at == hop * SLOT + to % AGENT_DEV).astype(F32).astype(BF16)
    agents = jnp.dot(pick, rows, preferred_element_type=F32).astype(BF16)
    for tile in range(TILES):
        out_ref[tile] = agents[:, tile * GROUP : (tile + 1) * GROUP]


def rows_of(x_ref, start, size):
    return jnp.concatenate([x_ref[s, start : start + size, :] for s in range(TILES)], axis=1)


def agent_kernel(a_ref, x_ref, out_ref):
    agents = a_ref[...].reshape(AGENTS, GROUP)
    columns = []
    lane = lax.broadcasted_iota(jnp.int32, (AGENTS, HEAD_DIM), 1)
    stats = jnp.zeros((AGENTS, HEAD_DIM), F32)
    for h in range(GROUP_HEADS):
        keys = rows_of(x_ref, K_ROW + h * HEAD_DIM, HEAD_DIM)
        values = rows_of(x_ref, V_ROW + h * HEAD_DIM, HEAD_DIM)
        head = agents[:, h * HEAD_DIM : (h + 1) * HEAD_DIM]
        scores = jnp.dot(head, keys, preferred_element_type=F32) * INV_ROOT
        peak = jnp.max(scores, axis=1, keepdims=True)
        weights = jnp.exp(scores - peak)
        total = jnp.sum(weights, axis=1, keepdims=True)
        acc = lax.dot_general(
            weights.astype(BF16), values, (((1,), (1,)), ((), ())), preferred_element_type=F32
        )
        columns.append(acc / total)
        left = peak + jnp.log(total)
        for piece in range(3):
            short = left.astype(BF16).astype(F32)
            left = left - short
            stats = jnp.where(lane == piece * GROUP_HEADS + h, short, stats)
    part = jnp.concatenate(columns + [stats], axis=1).astype(BF16)
    out_ref[...] = part.reshape(PLANES, OWNED, PART)


def comb_kernel(parts_ref, out_ref):
    logs = []
    for z in range(PLANES):
        pieces = parts_ref[z, :, PART - TOKENS :].astype(F32)
        n = GROUP_HEADS
        logs.append(pieces + turned(pieces, -n) + turned(pieces, -2 * n))
    peak = logs[0]
    for log in logs[1:]:
        peak = jnp.maximum(peak, log)
    shares = [jnp.exp(log - peak) for log in logs]
    whole = sum(shares[1:], shares[0])
    shares = [share / whole for share in shares]
    columns = []
    for h in range(GROUP_HEADS):
        lanes = slice(h * HEAD_DIM, (h + 1) * HEAD_DIM)
        at = GROUP + h - (PART - TOKENS)
        values = None
        for z in range(PLANES):
            term = parts_ref[z, :, lanes].astype(F32) * shares[z][:, at : at + 1]
            values = term if values is None else values + term
        columns.append(values)
    owned = jnp.concatenate(columns, axis=1).astype(BF16)
    for z in range(PLANES):
        out_ref[z] = owned


def taps_kernel(tile_ref, w_ref, out_ref):
    for tile in range(TILES):

        @pl.when(tile_ref[0] == tile)
        def _(tile=tile):
            lanes = slice(tile * GROUP, (tile + 1) * GROUP)
            rows = [w_ref[i, j, :, lanes] for i in range(3) for j in range(3)]
            rows.append(jnp.zeros((5, GROUP), F32))
            out_ref[...] = jnp.concatenate(rows, axis=0).T


def edge_kernel(even_ref, x_ref, above_ref, below_ref, near_ref, far_ref):
    even = even_ref[0] == 1
    spot = lax.broadcasted_iota(jnp.int32, (GROUP, TOKENS), 1) // COLUMNS
    for block in range(EDGE // TOKENS):
        last = first = jnp.zeros((GROUP, TOKENS), F32)
        for j in range(FRAMES):
            row = block * FRAMES + j
            if row >= EDGE_ROWS:
                break
            if row == 0:
                cells = above_ref[...]
            elif row == EDGE_ROWS - 1:
                cells = below_ref[...]
            else:
                cells = x_ref[row - 1, V_ROW:, :]
            cells = cells.astype(F32)
            last = jnp.where(spot == j, turned(cells, (j + 1) * COLUMNS), last)
            first = jnp.where(spot == j, turned(cells, j * COLUMNS), first)
        lanes = slice(block * TOKENS, (block + 1) * TOKENS)
        near_ref[:, lanes] = jnp.where(even, last, first).astype(BF16)
        far_ref[:, lanes] = jnp.where(even, first, last).astype(BF16)


TALL = 16


def turned(cells, by):
    by %= TOKENS
    return cells if by == 0 else pltpu.roll(cells, by, 1)


def frames_of(r, at, even, x_ref, above_ref, below_ref, near_ref, far_ref):
    lane = lax.broadcasted_iota(jnp.int32, (TALL, TOKENS), 1)
    if r < 0:
        cells = above_ref[pl.ds(at, TALL), :]
    elif r == TILES:
        cells = below_ref[pl.ds(at, TALL), :]
    else:
        cells = x_ref[r, pl.ds(V_ROW + at, TALL), :]
    cells = cells.astype(F32)
    block, j = divmod(r + 1, FRAMES)
    lanes = slice(block * TOKENS, (block + 1) * TOKENS)
    near = near_ref[pl.ds(at, TALL), lanes].astype(F32)
    far = far_ref[pl.ds(at, TALL), lanes].astype(F32)
    before = turned(jnp.where(even, far, near), -j * COLUMNS)
    after = turned(jnp.where(even, near, far), (FRAMES - 1 - j) * COLUMNS)
    return (
        jnp.where(lane < COLUMNS, before, turned(cells, COLUMNS)),
        cells,
        jnp.where(lane >= TOKENS - COLUMNS, after, turned(cells, -COLUMNS)),
    )


def taps_of(w_ref, at, rows=range(3)):
    w = w_ref[pl.ds(at, TALL), :]
    return {
        (i, j, k): jnp.broadcast_to(w[:, n : n + 1], (TALL, TOKENS))
        for i in range(3)
        for j in rows
        for k in range(3)
        for n in (i * 9 + j * 3 + k,)
    }


def stencil(rows, taps):
    column = lax.broadcasted_iota(jnp.int32, (TALL, TOKENS), 1) % COLUMNS
    sums = []
    for k in range(3):
        total = None
        for j, frames in rows.items():
            for i in range(3):
                term = frames[i] * taps[i, j, k]
                total = term if total is None else total + term
        sums.append(total)
    left = jnp.where(column == 0, 0.0, pltpu.roll(sums[0], 1, 1))
    right = jnp.where(column == COLUMNS - 1, 0.0, pltpu.roll(sums[2], TOKENS - 1, 1))
    return left + sums[1] + right


def conv_kernel(even_ref, x_ref, above_ref, below_ref, near_ref, far_ref, w_ref, out_ref):
    even = even_ref[0] == 1
    refs = (x_ref, above_ref, below_ref, near_ref, far_ref)

    def step(n, carry):
        at = pl.multiple_of(n * TALL, TALL)
        taps = taps_of(w_ref, at)
        rows = {r: frames_of(r, at, even, *refs) for r in range(-1, 1)}
        for r in range(TILES):
            rows[r + 1] = frames_of(r + 1, at, even, *refs)
            out_ref[r, pl.ds(at, TALL), :] = stencil({j: rows[r + j - 1] for j in range(3)}, taps)
            rows.pop(r - 1)
        return carry

    lax.fori_loop(0, GROUP // TALL, step, 0)


def mix_kernel(a_ref, values_ref, x_ref, local_ref, out_ref):
    agents = a_ref[...].reshape(AGENTS, GROUP)
    values = values_ref[...].reshape(AGENTS, GROUP).T
    for h in range(GROUP_HEADS):
        rows = slice(h * HEAD_DIM, (h + 1) * HEAD_DIM)
        queries = rows_of(x_ref, h * HEAD_DIM, HEAD_DIM)
        scores = jnp.dot(agents[:, rows], queries, preferred_element_type=F32) * INV_ROOT
        weights = jnp.exp(scores - jnp.max(scores, axis=0, keepdims=True))
        total = jnp.sum(weights, axis=0, keepdims=True)
        mixed = jnp.dot(values[rows], weights.astype(BF16), preferred_element_type=F32) / total
        for s in range(TILES):
            cells = mixed[:, s * TOKENS : (s + 1) * TOKENS] + local_ref[s, rows, :]
            out_ref[s, rows, :] = cells.astype(BF16)


def unpack_kernel(x_ref, out_ref):
    out_ref[...] = x_ref[...].reshape(D, TOKENS).T


def scalar(x):
    return x.astype(jnp.int32).reshape(1)


def body(queries, key_states, value_states, conv_weight):
    q = queries.reshape(TOKENS, D)
    k = key_states.reshape(TOKENS, D)
    v = value_states.reshape(TOKENS, D)
    shape = jax.ShapeDtypeStruct
    packed, pooled = call(
        pack_kernel,
        (shape((TILES, SENT, TOKENS), BF16), shape((SLOT, D), BF16)),
        3.0,
        q,
        k,
        v,
        scratch=(
            pltpu.VMEM((3, TOKENS, D), BF16),
            pltpu.VMEM((3, TILES, GROUP, TOKENS), BF16),
            pltpu.SemaphoreType.DMA((3,)),
            pltpu.SemaphoreType.DMA((3,)),
        ),
        far=0,
    )
    x = exchange(packed, "xy")
    came = [pooled]
    for n in range(1, PLANES):
        came.append(lax.ppermute(pooled, "z", [(i, (i + n) % PLANES) for i in range(PLANES)]))
    tile = scalar(lax.axis_index("xy"))
    taps = call(taps_kernel, shape((GROUP, 32), F32), 1.0, conv_weight, scalars=(tile,))
    z = scalar(lax.axis_index("z"))
    by_tile = shape((TILES, OWNED, GROUP), BF16)
    agents = exchange(call(route_kernel, by_tile, 1.0, *came, scalars=(z,)), "xy")
    above = shift(x[TILES - 1, V_ROW:], "z", 1)
    below = shift(x[0, V_ROW:], "z", -1)

    part = call(agent_kernel, shape((PLANES, OWNED, PART), BF16), 3.0, agents, x)
    parts = exchange(part, "z")
    edges = shape((GROUP, EDGE), BF16)
    even = scalar(1 - lax.axis_index("tm") % 2)
    near, far = call(edge_kernel, (edges, edges), 1.0, x, above, below, scalars=(even,))
    groups = lax.axis_size("tm")
    pairs = [(i, i + 1) for i in range(0, groups - 1, 2)]
    near = lax.ppermute(near, "tm", pairs + [(b, a) for a, b in pairs])
    pairs = [(i, i + 1) for i in range(1, groups - 1, 2)]
    far = lax.ppermute(far, "tm", pairs + [(b, a) for a, b in pairs])

    owned = call(comb_kernel, shape((PLANES, OWNED, GROUP), BF16), 1.0, parts)
    values = exchange(owned, "z")
    local = call(
        conv_kernel,
        shape((TILES, GROUP, TOKENS), F32),
        5.0,
        x,
        above,
        below,
        near,
        far,
        taps,
        scalars=(even,),
    )
    mixed = call(mix_kernel, shape((TILES, GROUP, TOKENS), BF16), 2.0, agents, values, x, local)
    mine = exchange(mixed, "xy")
    out = call(unpack_kernel, shape((TOKENS, D), BF16), 1.0, mine)
    return out.reshape(value_states.shape)


def solution(mesh):
    devices = mesh.devices
    fine = Mesh(devices.reshape(devices.shape[0], PLANES, TILES), ("tm", "z", "xy"))
    spec = P("tm", None, ("z", "xy"), None, None)
    return jax.shard_map(
        body,
        mesh=fine,
        in_specs=(spec, spec, spec, P()),
        out_specs=spec,
        check_vma=False,
    )
```

time: 86.3 us -> 105 us (1.22)
  the two profiles are of different devices: /device:TPU:4 before, /device:TPU:2 now
where the time goes in v6:
time: 105 us; the launch traced here: 104 us
  starting transfers between devices  39.3 us (37%)
  blocking collectives  37.6 us (36%)
  Pallas kernels  14 us (13%)
  waiting for transfers between devices  12.3 us (12%)
    all_to_all x3, blocking collectives, exchange(): return lax.all_to_all(x, axes, 0, 0)  37.6 us
    ppermute x7, starting transfers between devices, body(): lax.ppermute(pooled, 'z', [(i, (i + n) % PLANES) for i in range(PLANES)])  18.5 us
    pallas_call x9, Pallas kernels, call(): pl.pallas_call(kernel, out_shape=out_shape, in_specs=[SMEM] * len(scalars...  14 us
    all_to_all x2, starting transfers between devices, exchange(): return lax.all_to_all(x, axes, 0, 0)  11.4 us
    ppermute x2, starting transfers between devices, shift(): return lax.ppermute(x, axis, pairs)  5.22 us
    ppermute x2, waiting for transfers between devices, shift(): return lax.ppermute(x, axis, pairs)  4.67 us
    all_to_all x2, waiting for transfers between devices, exchange(): return lax.all_to_all(x, axes, 0, 0)  4.56 us
    ppermute x1, starting transfers between devices, body(): near = lax.ppermute(near, 'tm', pairs + [(b, a) for a, b in pairs])  3.56 us
  transfers between devices with their start and end apart: 13, of which 5 were waited for; matrix products, arithmetic and copies ran while one was open for 0% of the time, Pallas kernels for 6%

profile of v6, /device:TPU:2, one launch (start us, length us, event | category | flops | bytes accessed | tf_op | source)
XLA Modules:
  0.0 104.0 jit_solution(11997503431070286574)
XLA Ops:
  0.0 2.9 %shard_map.46 = (bf16[8,576,128]{2,1,0:T(8,128)(2,1)}, bf16[8,1536]{1,0:T(8,128)(2,1)}) custom-call(bf16[128,1536]{1,0:T(8,128)(2,1)} %bitcast.13, bf16[128,1536]{1,0:T(8,128)(2,1)} %bitcast.14, bf16[128,1536]{1,0:T(8,128)(2,1)} %bitcast.15), custom_call_target="tpu_custom_call" | custom-call | flops 900000000 | bytes 6000000 | tf_op jit(solution)/shard_map/pallas_call | solution.py:47
  2.9 2.0 %collective-permute-start = (bf16[8,1536]{1,0:T(8,128)(2,1)}, bf16[8,1536]{1,0:T(8,128)(2,1)S(1)}, u32[]{:S(2)}, u32[]{:S(2)}) collective-permute-start(bf16[8,1536]{1,0:T(8,128)(2,1)} %get-tuple-element.9.refs_0_), channel_id=1, source_target_pairs={{0,8},{8,16},{16,24},{24,32},{32,40},{40,48},{48,56},{56,0},{1,9},... | collective-permute-start | bytes 73736 | tf_op jit(solution)/shard_map/ppermute | solution.py:316
  4.9 3.3 %collective-permute-start.1 = (bf16[8,1536]{1,0:T(8,128)(2,1)}, bf16[8,1536]{1,0:T(8,128)(2,1)S(1)}, u32[]{:S(2)}, u32[]{:S(2)}) collective-permute-start(bf16[8,1536]{1,0:T(8,128)(2,1)} %get-tuple-element.9.refs_0_), channel_id=1, source_target_pairs={{0,16},{8,24},{16,32},{24,40},{32,48},{40,56},{48,0},{56,8},{1,17}... | collective-permute-start | bytes 73736 | tf_op jit(solution)/shard_map/ppermute | solution.py:316
  8.2 4.0 %collective-permute-start.2 = (bf16[8,1536]{1,0:T(8,128)(2,1)}, bf16[8,1536]{1,0:T(8,128)(2,1)S(1)}, u32[]{:S(2)}, u32[]{:S(2)}) collective-permute-start(bf16[8,1536]{1,0:T(8,128)(2,1)} %get-tuple-element.9.refs_0_), channel_id=1, source_target_pairs={{0,24},{8,32},{16,40},{24,48},{32,56},{40,0},{48,8},{56,16},{1,25}... | collective-permute-start | bytes 73736 | tf_op jit(solution)/shard_map/ppermute | solution.py:316
  12.8 4.9 %collective-permute-start.4 = (bf16[8,1536]{1,0:T(8,128)(2,1)}, bf16[8,1536]{1,0:T(8,128)(2,1)S(1)}, u32[]{:S(2)}, u32[]{:S(2)}) collective-permute-start(bf16[8,1536]{1,0:T(8,128)(2,1)} %get-tuple-element.9.refs_0_), channel_id=1, source_target_pairs={{0,40},{8,48},{16,56},{24,0},{32,8},{40,16},{48,24},{56,32},{1,41}... | collective-permute-start | bytes 73736 | tf_op jit(solution)/shard_map/ppermute | solution.py:316
  17.7 2.7 %collective-permute-start.5 = (bf16[8,1536]{1,0:T(8,128)(2,1)}, bf16[8,1536]{1,0:T(8,128)(2,1)S(1)}, u32[]{:S(2)}, u32[]{:S(2)}) collective-permute-start(bf16[8,1536]{1,0:T(8,128)(2,1)} %get-tuple-element.9.refs_0_), channel_id=1, source_target_pairs={{0,48},{8,56},{16,0},{24,8},{32,16},{40,24},{48,32},{56,40},{1,49}... | collective-permute-start | bytes 73736 | tf_op jit(solution)/shard_map/ppermute | solution.py:316
  20.4 1.0 collective-permute-start.6
  21.4 1.2 %collective-permute-done.5.refs_6_ = bf16[8,1536]{1,0:T(8,128)(2,1)S(1)} collective-permute-done((bf16[8,1536]{1,0:T(8,128)(2,1)}, bf16[8,1536]{1,0:T(8,128)(2,1)S(1)}, u32[]{:S(2)}, u32[]{:S(2)}) %collective-permute-start.5) | collective-permute-done | bytes 24608 | tf_op jit(solution)/shard_map/ppermute | solution.py:316
  22.7 1.8 %collective-permute-done.6.refs_7_ = bf16[8,1536]{1,0:T(8,128)(2,1)S(1)} collective-permute-done((bf16[8,1536]{1,0:T(8,128)(2,1)}, bf16[8,1536]{1,0:T(8,128)(2,1)S(1)}, u32[]{:S(2)}, u32[]{:S(2)}) %collective-permute-start.6) | collective-permute-done | bytes 24608 | tf_op jit(solution)/shard_map/ppermute | solution.py:316
  25.4 11.1 %all_to_all.25.a_ref = bf16[8,32,192]{2,1,0:T(8,128)(2,1)S(1)} all-to-all(bf16[8,32,192]{2,1,0:T(8,128)(2,1)S(1)} %shard_map.47), channel_id=1, replica_groups=mesh['tm'=4,'z'=8,'xy'=8] {'xy'}, dimensions={0} | all-to-all | bytes 196608 | tf_op jit(solution)/shard_map/all_to_all | solution.py:59
  36.5 15.5 %all_to_all.26.x_ref = bf16[8,576,128]{2,1,0:T(8,128)(2,1)S(1)} all-to-all(bf16[8,576,128]{2,1,0:T(8,128)(2,1)S(1)} %copy-done.2), channel_id=1, replica_groups=mesh['tm'=4,'z'=8,'xy'=8] {'xy'}, dimensions={0} | all-to-all | bytes 2359296 | tf_op jit(solution)/shard_map/all_to_all | solution.py:59
  52.0 2.4 %shard_map.48 = bf16[8,32,256]{2,1,0:T(8,128)(2,1)} custom-call(bf16[8,32,192]{2,1,0:T(8,128)(2,1)S(1)} %all_to_all.25.a_ref, bf16[8,576,128]{2,1,0:T(8,128)(2,1)S(1)} %all_to_all.26.x_ref), custom_call_target="tpu_custom_call" | custom-call | flops 900000000 | bytes 6000000 | tf_op jit(solution)/shard_map/pallas_call | solution.py:47
  54.5 4.4 %all-to-all-start.2 = ((bf16[8,32,256]{2,1,0:T(8,128)(2,1)}), bf16[8,32,256]{2,1,0:T(8,128)(2,1)S(1)}, u32[]{:S(2)}, u32[]{:S(2)}) async-start(bf16[8,32,256]{2,1,0:T(8,128)(2,1)} %shard_map.48), calls=%async_computation.2 | async-start | bytes 262144 | tf_op jit(solution)/shard_map/all_to_all | solution.py:59
  58.9 3.9 %collective-permute-start.7 = (bf16[192,128]{1,0:T(8,128)(2,1)S(1)}, bf16[192,128]{1,0:T(8,128)(2,1)S(1)}, u32[]{:S(2)}, u32[]{:S(2)}) collective-permute-start(bf16[192,128]{1,0:T(8,128)(2,1)S(1)} %get-tuple-element.14), channel_id=1, source_target_pairs={{0,8},{8,16},{16,24},{24,32},{32,40},{40,48},{48,56},{1,9},{9,17},... | collective-permute-start | bytes 147464 | tf_op jit(solution)/shard_map/ppermute | solution.py:65
  62.8 1.3 %collective-permute-start.8 = (bf16[192,128]{1,0:T(8,128)(2,1)S(1)}, bf16[192,128]{1,0:T(8,128)(2,1)S(1)}, u32[]{:S(2)}, u32[]{:S(2)}) collective-permute-start(bf16[192,128]{1,0:T(8,128)(2,1)S(1)} %get-tuple-element.13), channel_id=1, source_target_pairs={{8,0},{16,8},{24,16},{32,24},{40,32},{48,40},{56,48},{9,1},{17,9},... | collective-permute-start | bytes 147464 | tf_op jit(solution)/shard_map/ppermute | solution.py:65
  64.6 4.3 %collective-permute-done.8.below_ref = bf16[192,128]{1,0:T(8,128)(2,1)S(1)} collective-permute-done((bf16[192,128]{1,0:T(8,128)(2,1)S(1)}, bf16[192,128]{1,0:T(8,128)(2,1)S(1)}, u32[]{:S(2)}, u32[]{:S(2)}) %collective-permute-start.8) | collective-permute-done | bytes 49184 | tf_op jit(solution)/shard_map/ppermute | solution.py:65
  69.8 3.6 %collective-permute-start.9 = (bf16[192,384]{1,0:T(8,128)(2,1)S(1)}, bf16[192,384]{1,0:T(8,128)(2,1)S(1)}, u32[]{:S(2)}, u32[]{:S(2)}) collective-permute-start(bf16[192,384]{1,0:T(8,128)(2,1)S(1)} %get-tuple-element.11), channel_id=1, source_target_pairs={{0,64},{128,192},{64,0},{192,128},{1,65},{129,193},{65,1},{193,129... | collective-permute-start | bytes 442376 | tf_op jit(solution)/shard_map/ppermute | solution.py:332
  73.3 1.0 shard_map.49
  74.3 7.0 %all-to-all-start.3 = ((bf16[8,32,192]{2,1,0:T(8,128)(2,1)}), bf16[8,32,192]{2,1,0:T(8,128)(2,1)S(1)}, u32[]{:S(2)}, u32[]{:S(2)}) async-start(bf16[8,32,192]{2,1,0:T(8,128)(2,1)} %shard_map.49), calls=%async_computation.3 | async-start | bytes 262144 | tf_op jit(solution)/shard_map/all_to_all | solution.py:59
  81.5 4.5 %shard_map.52.local_ref = f32[8,192,128]{2,1,0:T(8,128)S(1)} custom-call(s32[1]{0:T(128)} %bitcast.4.even_ref, bf16[8,576,128]{2,1,0:T(8,128)(2,1)S(1)} %all_to_all.26.x_ref, bf16[192,128]{1,0:T(8,128)(2,1)S(1)} %collective-permute-done.7.above_ref, bf16[192,128]{1,0:T(8,128)(2,1)S(1)} %collective-permute-done.8.below_ref, ...), custom_call_target="tpu_custom_call" | custom-call | flops 1500000000 | bytes 10000000 | tf_op jit(solution)/shard_map/pallas_call | solution.py:47
  86.0 4.6 %all-to-all-done.3.values_ref = bf16[8,32,192]{2,1,0:T(8,128)(2,1)S(1)} async-done(((bf16[8,32,192]{2,1,0:T(8,128)(2,1)}), bf16[8,32,192]{2,1,0:T(8,128)(2,1)S(1)}, u32[]{:S(2)}, u32[]{:S(2)}) %all-to-all-start.3) | async-done | bytes 98336 | tf_op jit(solution)/shard_map/all_to_all | solution.py:59
  90.5 1.6 %shard_map.53 = bf16[8,192,128]{2,1,0:T(8,128)(2,1)S(1)} custom-call(bf16[8,32,192]{2,1,0:T(8,128)(2,1)S(1)} %all_to_all.25.a_ref, bf16[8,32,192]{2,1,0:T(8,128)(2,1)S(1)} %all-to-all-done.3.values_ref, bf16[8,576,128]{2,1,0:T(8,128)(2,1)S(1)} %all_to_all.26.x_ref, f32[8,192,128]{2,1,0:T(8,128)S(1)} %shard_map.52.local_ref), custom_call_target="tpu_custom_call" | custom-call | flops 600000000 | bytes 4000000 | tf_op jit(solution)/shard_map/pallas_call | solution.py:47
  92.1 11.0 %all_to_all.27.x_ref = bf16[8,192,128]{2,1,0:T(8,128)(2,1)S(1)} all-to-all(bf16[8,192,128]{2,1,0:T(8,128)(2,1)S(1)} %shard_map.53), channel_id=1, replica_groups=mesh['tm'=4,'z'=8,'xy'=8] {'xy'}, dimensions={0} | all-to-all | bytes 786432 | tf_op jit(solution)/shard_map/all_to_all | solution.py:59
  103.1 0.9 shard_map.54
  (21 shorter events, 3.1 us)
Async XLA Ops:
  2.9 14.8 %collective-permute-start = (bf16[8,1536]{1,0:T(8,128)(2,1)}, bf16[8,1536]{1,0:T(8,128)(2,1)S(1)}, u32[]{:S(2)}, u32[]{:S(2)}) collective-permute-start(bf16[8,1536]{1,0:T(8,128)(2,1)} %get-tuple-element.9.refs_0_), channel_id=1, source_target_pairs={{0,8},{8,16},{16,24},{24,32},{32,40},{40,48},{48,56},{56,0},{1,9},... | collective-permute-start | bytes 73736 | tf_op jit(solution)/shard_map/ppermute | solution.py:316
  4.9 15.5 %collective-permute-start.1 = (bf16[8,1536]{1,0:T(8,128)(2,1)}, bf16[8,1536]{1,0:T(8,128)(2,1)S(1)}, u32[]{:S(2)}, u32[]{:S(2)}) collective-permute-start(bf16[8,1536]{1,0:T(8,128)(2,1)} %get-tuple-element.9.refs_0_), channel_id=1, source_target_pairs={{0,16},{8,24},{16,32},{24,40},{32,48},{40,56},{48,0},{56,8},{1,17}... | collective-permute-start | bytes 73736 | tf_op jit(solution)/shard_map/ppermute | solution.py:316
  8.2 13.2 %collective-permute-start.2 = (bf16[8,1536]{1,0:T(8,128)(2,1)}, bf16[8,1536]{1,0:T(8,128)(2,1)S(1)}, u32[]{:S(2)}, u32[]{:S(2)}) collective-permute-start(bf16[8,1536]{1,0:T(8,128)(2,1)} %get-tuple-element.9.refs_0_), channel_id=1, source_target_pairs={{0,24},{8,32},{16,40},{24,48},{32,56},{40,0},{48,8},{56,16},{1,25}... | collective-permute-start | bytes 73736 | tf_op jit(solution)/shard_map/ppermute | solution.py:316
  12.2 9.2 %collective-permute-start.3 = (bf16[8,1536]{1,0:T(8,128)(2,1)}, bf16[8,1536]{1,0:T(8,128)(2,1)S(1)}, u32[]{:S(2)}, u32[]{:S(2)}) collective-permute-start(bf16[8,1536]{1,0:T(8,128)(2,1)} %get-tuple-element.9.refs_0_), channel_id=1, source_target_pairs={{0,32},{8,40},{16,48},{24,56},{32,0},{40,8},{48,16},{56,24},{1,33}... | collective-permute-start | bytes 73736 | tf_op jit(solution)/shard_map/ppermute | solution.py:316
  12.8 8.6 %collective-permute-start.4 = (bf16[8,1536]{1,0:T(8,128)(2,1)}, bf16[8,1536]{1,0:T(8,128)(2,1)S(1)}, u32[]{:S(2)}, u32[]{:S(2)}) collective-permute-start(bf16[8,1536]{1,0:T(8,128)(2,1)} %get-tuple-element.9.refs_0_), channel_id=1, source_target_pairs={{0,40},{8,48},{16,56},{24,0},{32,8},{40,16},{48,24},{56,32},{1,41}... | collective-permute-start | bytes 73736 | tf_op jit(solution)/shard_map/ppermute | solution.py:316
  17.7 4.9 %collective-permute-start.5 = (bf16[8,1536]{1,0:T(8,128)(2,1)}, bf16[8,1536]{1,0:T(8,128)(2,1)S(1)}, u32[]{:S(2)}, u32[]{:S(2)}) collective-permute-start(bf16[8,1536]{1,0:T(8,128)(2,1)} %get-tuple-element.9.refs_0_), channel_id=1, source_target_pairs={{0,48},{8,56},{16,0},{24,8},{32,16},{40,24},{48,32},{56,40},{1,49}... | collective-permute-start | bytes 73736 | tf_op jit(solution)/shard_map/ppermute | solution.py:316
  20.4 4.0 %collective-permute-start.6 = (bf16[8,1536]{1,0:T(8,128)(2,1)}, bf16[8,1536]{1,0:T(8,128)(2,1)S(1)}, u32[]{:S(2)}, u32[]{:S(2)}) collective-permute-start(bf16[8,1536]{1,0:T(8,128)(2,1)} %get-tuple-element.9.refs_0_), channel_id=1, source_target_pairs={{0,56},{8,0},{16,8},{24,16},{32,24},{40,32},{48,40},{56,48},{1,57}... | collective-permute-start | bytes 73736 | tf_op jit(solution)/shard_map/ppermute | solution.py:316
  24.4 0.7 copy-start.1
  25.2 11.3 %copy-start.2 = (bf16[8,576,128]{2,1,0:T(8,128)(2,1)S(1)}, bf16[8,576,128]{2,1,0:T(8,128)(2,1)}, u32[]{:S(2)}) copy-start(bf16[8,576,128]{2,1,0:T(8,128)(2,1)} %get-tuple-element.10) | copy-start | bytes 3538948
  54.5 18.9 %all-to-all-start.2 = ((bf16[8,32,256]{2,1,0:T(8,128)(2,1)}), bf16[8,32,256]{2,1,0:T(8,128)(2,1)S(1)}, u32[]{:S(2)}, u32[]{:S(2)}) async-start(bf16[8,32,256]{2,1,0:T(8,128)(2,1)} %shard_map.48), calls=%async_computation.2 | async-start | bytes 262144 | tf_op jit(solution)/shard_map/all_to_all | solution.py:59
  58.9 5.7 %collective-permute-start.7 = (bf16[192,128]{1,0:T(8,128)(2,1)S(1)}, bf16[192,128]{1,0:T(8,128)(2,1)S(1)}, u32[]{:S(2)}, u32[]{:S(2)}) collective-permute-start(bf16[192,128]{1,0:T(8,128)(2,1)S(1)} %get-tuple-element.14), channel_id=1, source_target_pairs={{0,8},{8,16},{16,24},{24,32},{32,40},{40,48},{48,56},{1,9},{9,17},... | collective-permute-start | bytes 147464 | tf_op jit(solution)/shard_map/ppermute | solution.py:65
  62.8 6.0 %collective-permute-start.8 = (bf16[192,128]{1,0:T(8,128)(2,1)S(1)}, bf16[192,128]{1,0:T(8,128)(2,1)S(1)}, u32[]{:S(2)}, u32[]{:S(2)}) collective-permute-start(bf16[192,128]{1,0:T(8,128)(2,1)S(1)} %get-tuple-element.13), channel_id=1, source_target_pairs={{8,0},{16,8},{24,16},{32,24},{40,32},{48,40},{56,48},{9,1},{17,9},... | collective-permute-start | bytes 147464 | tf_op jit(solution)/shard_map/ppermute | solution.py:65
  68.8 12.5 %copy-start = (f32[3,3,3,1536]{3,2,1,0:T(4,128)S(1)}, f32[3,3,3,1536]{3,2,1,0:T(4,128)}, u32[]{:S(2)}) copy-start(f32[3,3,3,1536]{3,2,1,0:T(4,128)} %w_ref.1) | copy-start | bytes 497668
  69.1 12.3 %collective-permute-start.10 = (bf16[192,384]{1,0:T(8,128)(2,1)S(1)}, bf16[192,384]{1,0:T(8,128)(2,1)S(1)}, u32[]{:S(2)}, u32[]{:S(2)}) collective-permute-start(bf16[192,384]{1,0:T(8,128)(2,1)S(1)} %get-tuple-element.12), channel_id=1, source_target_pairs={{64,128},{128,64},{65,129},{129,65},{66,130},{130,66},{67,131},{13... | collective-permute-start | bytes 442376 | tf_op jit(solution)/shard_map/ppermute | solution.py:334
  69.8 11.7 %collective-permute-start.9 = (bf16[192,384]{1,0:T(8,128)(2,1)S(1)}, bf16[192,384]{1,0:T(8,128)(2,1)S(1)}, u32[]{:S(2)}, u32[]{:S(2)}) collective-permute-start(bf16[192,384]{1,0:T(8,128)(2,1)S(1)} %get-tuple-element.11), channel_id=1, source_target_pairs={{0,64},{128,192},{64,0},{192,128},{1,65},{129,193},{65,1},{193,129... | collective-permute-start | bytes 442376 | tf_op jit(solution)/shard_map/ppermute | solution.py:332
  74.3 16.2 %all-to-all-start.3 = ((bf16[8,32,192]{2,1,0:T(8,128)(2,1)}), bf16[8,32,192]{2,1,0:T(8,128)(2,1)S(1)}, u32[]{:S(2)}, u32[]{:S(2)}) async-start(bf16[8,32,192]{2,1,0:T(8,128)(2,1)} %shard_map.49), calls=%async_computation.3 | async-start | bytes 262144 | tf_op jit(solution)/shard_map/all_to_all | solution.py:59

commit v7 on v5

--- a/solution.py
+++ b/solution.py
@@ -39,14 +39,14 @@
 HBM = pl.BlockSpec(memory_space=pltpu.HBM)
 
 
-def call(kernel, out_shape, us, *args, scalars=(), scratch=(), far=False):
+def call(kernel, out_shape, us, *args, scalars=(), scratch=(), far=False, far_out=False):
     cost = pl.CostEstimate(flops=int(us * 3.0e8), bytes_accessed=int(us * 2.0e6), transcendentals=0)
-    many = isinstance(out_shape, tuple)
+    out = HBM if far_out else VMEM
     return pl.pallas_call(
         kernel,
         out_shape=out_shape,
         in_specs=[SMEM] * len(scalars) + [HBM if far else VMEM] * len(args),
-        out_specs=(VMEM,) * len(out_shape) if many else HBM if far else VMEM,
+        out_specs=(out,) * len(out_shape) if isinstance(out_shape, tuple) else out,
         scratch_shapes=list(scratch),
         cost_estimate=cost,
         compiler_params=pltpu.CompilerParams(vmem_limit_bytes=ALL if far else GRANT),
@@ -63,18 +63,30 @@
     return lax.ppermute(x, axis, pairs)
 
 
-def pool_kernel(q_ref, out_ref):
+def pool_kernel(q_ref, out_ref, came, sems):
+    half = D // 2
+    loads = [
+        pltpu.make_async_copy(
+            q_ref.at[:, pl.ds(n * half, half)], came.at[:, pl.ds(n * half, half)], sems.at[n]
+        )
+        for n in range(2)
+    ]
+    for load in loads:
+        load.start()
     shape = (8, TOKENS)
     token = lax.broadcasted_iota(jnp.int32, shape, 1)
     agent = lax.broadcasted_iota(jnp.int32, shape, 0)
     width = COLUMNS // AGENT_DEV
     pick = ((token % COLUMNS) // width == agent).astype(F32).astype(BF16)
-    sums = jnp.dot(pick, q_ref[...], preferred_element_type=F32)
-    pooled = (sums[:AGENT_DEV] * (1.0 / (FRAMES * width))).astype(BF16)
-    for tile in range(TILES):
-        part = pooled[:, tile * GROUP : (tile + 1) * GROUP]
-        out_ref[tile] = part
-        out_ref[TILES + tile] = part
+    for n, load in enumerate(loads):
+        load.wait()
+        sums = jnp.dot(pick, came[:, n * half : (n + 1) * half], preferred_element_type=F32)
+        pooled = (sums[:AGENT_DEV] * (1.0 / (FRAMES * width))).astype(BF16)
+        for k in range(TILES // 2):
+            tile = n * (TILES // 2) + k
+            part = pooled[:, k * GROUP : (k + 1) * GROUP]
+            out_ref[tile] = part
+            out_ref[TILES + tile] = part
 
 
 def pack_kernel(q_ref, k_ref, v_ref, out_ref, came, turned, in_sems, out_sems):
@@ -101,7 +113,7 @@
 
 
 def agent_kernel(z_ref, *refs):
-    came, (x_ref, out_ref, a_ref) = refs[:PAIRS], refs[PAIRS:]
+    came, (x_ref, out_ref, a_ref, q_ref) = refs[:PAIRS], refs[PAIRS:]
     for hop, ref in enumerate(came):
         z = lax.rem(z_ref[0] + PAIRS - hop, PAIRS)
         a_ref[pl.ds(pl.multiple_of(z * PAIR_AGENTS, PAIR_AGENTS), PAIR_AGENTS), :] = ref[...]
@@ -129,19 +141,7 @@
     part = flipped[: GROUP + STATS].astype(BF16)
     for z in range(PLANES):
         out_ref[z] = part
-
-
-def query_kernel(a_ref, x_ref, one_ref, rest_ref, total_ref):
-    for h in range(GROUP_HEADS):
-        queries = rows_of(x_ref, h * HEAD_DIM, HEAD_DIM)
-        agents = a_ref[:, h * HEAD_DIM : (h + 1) * HEAD_DIM]
-        scores = jnp.dot(agents, queries, preferred_element_type=F32) * INV_ROOT
-        weights = jnp.exp(scores - jnp.max(scores, axis=0, keepdims=True))
-        total_ref[h : h + 1, :] = jnp.sum(weights, axis=0, keepdims=True)
-        if h == 0:
-            one_ref[...] = weights.astype(BF16)
-        else:
-            rest_ref[h - 1] = weights.astype(BF16)
+    q_ref[...] = rows_of(x_ref, 0, GROUP)
 
 
 def taps_kernel(tile_ref, w_ref, out_ref):
@@ -187,13 +187,13 @@
     return cells if by == 0 else pltpu.roll(cells, by, 1)
 
 
-def frames_of(r, at, even, x_ref, near_ref, far_ref):
-    lane = lax.broadcasted_iota(jnp.int32, (TALL, TOKENS), 1)
-    cells = x_ref[r, pl.ds(V_ROW + at, TALL), :].astype(F32)
+def frames_of(r, at, even, x_ref, near_ref, far_ref, tall=TALL):
+    lane = lax.broadcasted_iota(jnp.int32, (tall, TOKENS), 1)
+    cells = x_ref[r, pl.ds(V_ROW + at, tall), :].astype(F32)
     block, j = divmod(r, FRAMES)
     lanes = slice(block * TOKENS, (block + 1) * TOKENS)
-    near = near_ref[pl.ds(at, TALL), lanes].astype(F32)
-    far = far_ref[pl.ds(at, TALL), lanes].astype(F32)
+    near = near_ref[pl.ds(at, tall), lanes].astype(F32)
+    far = far_ref[pl.ds(at, tall), lanes].astype(F32)
     before = turned(jnp.where(even, far, near), -j * COLUMNS)
     after = turned(jnp.where(even, near, far), (FRAMES - 1 - j) * COLUMNS)
     return (
@@ -203,10 +203,10 @@
     )
 
 
-def taps_of(w_ref, at, rows=range(3)):
-    w = w_ref[pl.ds(at, TALL), :]
+def taps_of(w_ref, at, rows=range(3), tall=TALL):
+    w = w_ref[pl.ds(at, tall), :]
     return {
-        (i, j, k): jnp.broadcast_to(w[:, n : n + 1], (TALL, TOKENS))
+        (i, j, k): jnp.broadcast_to(w[:, n : n + 1], (tall, TOKENS))
         for i in range(3)
         for j in rows
         for k in range(3)
@@ -215,7 +215,8 @@
 
 
 def stencil(rows, taps):
-    column = lax.broadcasted_iota(jnp.int32, (TALL, TOKENS), 1) % COLUMNS
+    shape = next(iter(rows.values()))[1].shape
+    column = lax.broadcasted_iota(jnp.int32, shape, 1) % COLUMNS
     sums = []
     for k in range(3):
         total = None
@@ -231,10 +232,12 @@
 
 def rim_kernel(even_ref, x_ref, near_ref, far_ref, w_ref, up_ref, down_ref):
     even = even_ref[0] == 1
-    for at in range(0, GROUP, TALL):
+    tall = GROUP // 2
+    for at in range(0, GROUP, tall):
         for r, j, ref in ((TILES - 1, 0, up_ref), (0, 2, down_ref)):
-            frames = frames_of(r, at, even, x_ref, near_ref, far_ref)
-            ref[pl.ds(at, TALL), :] = stencil({j: frames}, taps_of(w_ref, at, (j,))).astype(BF16)
+            frames = frames_of(r, at, even, x_ref, near_ref, far_ref, tall)
+            taps = taps_of(w_ref, at, (j,), tall)
+            ref[pl.ds(at, tall), :] = stencil({j: frames}, taps).astype(BF16)
 
 
 def conv_kernel(even_ref, x_ref, near_ref, far_ref, w_ref, out_ref):
@@ -255,7 +258,7 @@
     lax.fori_loop(0, GROUP // TALL, step, 0)
 
 
-def mix_kernel(parts_ref, one_ref, rest_ref, total_ref, local_ref, up_ref, down_ref, out_ref):
+def mix_kernel(parts_ref, a_ref, q_ref, local_ref, up_ref, down_ref, out_ref):
     logs = []
     for z in range(PLANES):
         pieces = parts_ref[z, GROUP : GROUP + STATS, :].astype(F32)
@@ -273,9 +276,10 @@
         for z in range(PLANES):
             term = parts_ref[z, rows, :].astype(F32) * shares[z][h : h + 1]
             values = term if values is None else values + term
-        weights = one_ref[...] if h == 0 else rest_ref[h - 1]
-        mixed = jnp.dot(values.astype(BF16), weights, preferred_element_type=F32)
-        mixed = mixed / total_ref[h : h + 1, :]
+        scores = jnp.dot(a_ref[:, rows], q_ref[rows, :], preferred_element_type=F32) * INV_ROOT
+        weights = jnp.exp(scores - jnp.max(scores, axis=0, keepdims=True))
+        total = jnp.sum(weights, axis=0, keepdims=True)
+        mixed = jnp.dot(values.astype(BF16), weights.astype(BF16), preferred_element_type=F32) / total
         for s in range(TILES):
             cells = mixed[:, s * TOKENS : (s + 1) * TOKENS] + local_ref[s, rows, :]
             if s == 0:
@@ -285,8 +289,16 @@
             out_ref[s, rows, :] = cells.astype(BF16)
 
 
-def unpack_kernel(x_ref, out_ref):
-    out_ref[...] = x_ref[...].reshape(D, TOKENS).T
+def unpack_kernel(x_ref, out_ref, back, sems):
+    pieces, stores = TILES // 2, []
+    wide = D // pieces
+    for n in range(pieces):
+        back[n] = x_ref[2 * n : 2 * n + 2].reshape(wide, TOKENS).T
+        store = pltpu.make_async_copy(back.at[n], out_ref.at[:, pl.ds(n * wide, wide)], sems.at[n])
+        store.start()
+        stores.append(store)
+    for store in stores:
+        store.wait()
 
 
 def scalar(x):
@@ -298,7 +310,14 @@
     k = key_states.reshape(TOKENS, D)
     v = value_states.reshape(TOKENS, D)
     shape = jax.ShapeDtypeStruct
-    pooled = call(pool_kernel, shape((2 * TILES, AGENT_DEV, GROUP), BF16), 1.0, q)
+    pooled = call(
+        pool_kernel,
+        shape((2 * TILES, AGENT_DEV, GROUP), BF16),
+        1.0,
+        q,
+        scratch=(pltpu.VMEM((TOKENS, D), BF16), pltpu.SemaphoreType.DMA((2,))),
+        far=True,
+    )
     packed = call(
         pack_kernel,
         shape((TILES, SENT, TOKENS), BF16),
@@ -313,6 +332,7 @@
             pltpu.SemaphoreType.DMA((3,)),
         ),
         far=True,
+        far_out=True,
     )
     own = exchange(pooled, ("zl", "xy")).reshape(PAIR_AGENTS, GROUP)
     x = exchange(packed, "xy")
@@ -322,9 +342,13 @@
     tile = scalar(lax.axis_index("xy"))
     taps = call(taps_kernel, shape((GROUP, 32), F32), 1.0, conv_weight, scalars=(tile,))
 
-    part, agents = call(
+    part, agents, turned_q = call(
         agent_kernel,
-        (shape((PLANES, GROUP + STATS, AGENTS), BF16), shape((AGENTS, GROUP), BF16)),
+        (
+            shape((PLANES, GROUP + STATS, AGENTS), BF16),
+            shape((AGENTS, GROUP), BF16),
+            shape((GROUP, TILES * TOKENS), BF16),
+        ),
         4.0,
         *came,
         x,
@@ -340,18 +364,6 @@
     near = lax.ppermute(near, "tm", pairs + [(b, a) for a, b in pairs])
     pairs = [(i, i + 1) for i in range(1, groups - 1, 2)]
     far = lax.ppermute(far, "tm", pairs + [(b, a) for a, b in pairs])
-    cells = TILES * TOKENS
-    one, rest, totals = call(
-        query_kernel,
-        (
-            shape((AGENTS, cells), BF16),
-            shape((GROUP_HEADS - 1, AGENTS, cells), BF16),
-            shape((8, cells), F32),
-        ),
-        2.0,
-        agents,
-        x,
-    )
     row = shape((GROUP, TOKENS), BF16)
     to_next, to_last = call(rim_kernel, (row, row), 1.0, x, near, far, taps, scalars=(even,))
     up = shift(to_next, ("zh", "zl"), 1)
@@ -364,15 +376,25 @@
         shape((TILES, GROUP, TOKENS), BF16),
         1.0,
         parts,
-        one,
-        rest,
-        totals,
+        agents,
+        turned_q,
         local,
         up,
         down,
     )
     mine = exchange(mixed, "xy")
-    out = call(unpack_kernel, shape((TOKENS, D), BF16), 1.0, mine)
+    pieces = TILES // 2
+    out = call(
+        unpack_kernel,
+        shape((TOKENS, D), BF16),
+        1.0,
+        mine,
+        scratch=(
+            pltpu.VMEM((pieces, TOKENS, D // pieces), BF16),
+            pltpu.SemaphoreType.DMA((pieces,)),
+        ),
+        far_out=True,
+    )
     return out.reshape(value_states.shape)
 
 

time: 86.3 us -> 86.4 us (level)
  waiting for transfers between devices: 16 us -> 19.1 us
  local copies, waits for them, and re-layouts: 5.67 us -> 2.86 us
    unnamed x16 -> x10, local copies, waits for them, and re-layouts: 5.65 us -> 2.83 us
    ppermute x1, waiting for transfers between devices: 2.34 us -> 4.45 us  [body(): far = lax.ppermute(far, 'tm', pairs + [(b, a) for a, b in pairs])]
    ppermute x2, waiting for transfers between devices: 0.41 us -> 1.37 us  [shift(): return lax.ppermute(x, axis, pairs)]
    pallas_call x10 -> x9, Pallas kernels: 14.7 us -> 14.6 us  [call(): pl.pallas_call(kernel, out_shape=out_shape, in_specs=[SMEM] * len(scalars...]
  transfers between devices with their start and end apart: 10 -> 10, of which waited for: 6 -> 6; matrix products, arithmetic and copies ran while one was open for 0% -> 0% of each run, Pallas kernels for 11% -> 8%
where the time goes in v7:
time: 86.4 us; the launch traced here: 85.9 us
  starting transfers between devices  35.2 us (41%)
  waiting for transfers between devices  19.1 us (22%)
  Pallas kernels  14.6 us (17%)
  blocking collectives  13.9 us (16%)
  local copies, waits for them, and re-layouts  2.86 us (3%)
    all_to_all x3, starting transfers between devices, exchange(): return lax.all_to_all(x, axes, 0, 0)  17.8 us
    pallas_call x9, Pallas kernels, call(): pl.pallas_call(kernel, out_shape=out_shape, in_specs=[SMEM] * len(scalars...  14.6 us
    all_to_all x1, blocking collectives, exchange(): return lax.all_to_all(x, axes, 0, 0)  13.9 us
    ppermute x3, starting transfers between devices, body(): lax.ppermute(own, 'zh', [(i, (i + n) % PAIRS) for i in range(PAIRS)])  9.29 us
    all_to_all x3, waiting for transfers between devices, exchange(): return lax.all_to_all(x, axes, 0, 0)  9.29 us
    ppermute x2, starting transfers between devices, shift(): return lax.ppermute(x, axis, pairs)  5.22 us
    ppermute x1, waiting for transfers between devices, body(): far = lax.ppermute(far, 'tm', pairs + [(b, a) for a, b in pairs])  4.45 us
    ppermute x3, waiting for transfers between devices, body(): lax.ppermute(own, 'zh', [(i, (i + n) % PAIRS) for i in range(PAIRS)])  4.01 us
  transfers between devices with their start and end apart: 10, of which 6 were waited for; matrix products, arithmetic and copies ran while one was open for 0% of the time, Pallas kernels for 8%

profile of v7, /device:TPU:4, one launch (start us, length us, event | category | flops | bytes accessed | tf_op | source)
XLA Modules:
  0.0 85.9 jit_solution(17164302066807714272)
XLA Ops:
  0.0 2.0 %shard_map.46 = bf16[16,4,192]{2,1,0:T(4,128)(2,1)} custom-call(bf16[128,1536]{1,0:T(8,128)(2,1)} %bitcast.9), custom_call_target="tpu_custom_call" | custom-call | flops 300000000 | bytes 2000000 | tf_op jit(solution)/shard_map/pallas_call | solution.py:45
  2.0 6.6 %all-to-all-start = ((bf16[16,4,192]{2,1,0:T(4,128)(2,1)}), bf16[16,4,192]{2,1,0:T(4,128)(2,1)S(1)}, u32[]{:S(2)}, u32[]{:S(2)}) async-start(bf16[16,4,192]{2,1,0:T(4,128)(2,1)} %shard_map.46), calls=%async_computation | async-start | bytes 65536 | tf_op jit(solution)/shard_map/all_to_all | solution.py:57
  8.6 2.3 %shard_map.47 = bf16[8,576,128]{2,1,0:T(8,128)(2,1)} custom-call(bf16[128,1536]{1,0:T(8,128)(2,1)} %bitcast.10, bf16[128,1536]{1,0:T(8,128)(2,1)} %bitcast.11, bf16[128,1536]{1,0:T(8,128)(2,1)} %bitcast.12), custom_call_target="tpu_custom_call" | custom-call | flops 900000000 | bytes 6000000 | tf_op jit(solution)/shard_map/pallas_call | solution.py:45
  10.9 4.8 %all-to-all-done = bf16[16,4,192]{2,1,0:T(4,128)(2,1)S(1)} async-done(((bf16[16,4,192]{2,1,0:T(4,128)(2,1)}), bf16[16,4,192]{2,1,0:T(4,128)(2,1)S(1)}, u32[]{:S(2)}, u32[]{:S(2)}) %all-to-all-start) | async-done | bytes 24608 | tf_op jit(solution)/shard_map/all_to_all | solution.py:57
  15.7 3.6 %all-to-all-start.1 = ((bf16[8,576,128]{2,1,0:T(8,128)(2,1)}), bf16[8,576,128]{2,1,0:T(8,128)(2,1)S(1)}, u32[]{:S(2)}, u32[]{:S(2)}) async-start(bf16[8,576,128]{2,1,0:T(8,128)(2,1)} %shard_map.47), calls=%async_computation.1 | async-start | bytes 2359296 | tf_op jit(solution)/shard_map/all_to_all | solution.py:57
  19.3 5.5 %collective-permute-start.2 = (bf16[64,192]{1,0:T(8,128)(2,1)S(1)}, bf16[64,192]{1,0:T(8,128)(2,1)S(1)}, u32[]{:S(2)}, u32[]{:S(2)}) collective-permute-start(bf16[64,192]{1,0:T(8,128)(2,1)S(1)} %reshape.26.refs_0_), channel_id=1, source_target_pairs={{0,48},{16,0},{32,16},{48,32},{1,49},{17,1},{33,17},{49,33},{2,50}... | collective-permute-start | bytes 73736 | tf_op jit(solution)/shard_map/ppermute | solution.py:341
  24.8 1.4 %collective-permute-start.1 = (bf16[64,192]{1,0:T(8,128)(2,1)S(1)}, bf16[64,192]{1,0:T(8,128)(2,1)S(1)}, u32[]{:S(2)}, u32[]{:S(2)}) collective-permute-start(bf16[64,192]{1,0:T(8,128)(2,1)S(1)} %reshape.26.refs_0_), channel_id=1, source_target_pairs={{0,32},{16,48},{32,0},{48,16},{1,33},{17,49},{33,1},{49,17},{2,34}... | collective-permute-start | bytes 73736 | tf_op jit(solution)/shard_map/ppermute | solution.py:341
  26.3 2.4 %collective-permute-start = (bf16[64,192]{1,0:T(8,128)(2,1)S(1)}, bf16[64,192]{1,0:T(8,128)(2,1)S(1)}, u32[]{:S(2)}, u32[]{:S(2)}) collective-permute-start(bf16[64,192]{1,0:T(8,128)(2,1)S(1)} %reshape.26.refs_0_), channel_id=1, source_target_pairs={{0,16},{16,32},{32,48},{48,0},{1,17},{17,33},{33,49},{49,1},{2,18}... | collective-permute-start | bytes 73736 | tf_op jit(solution)/shard_map/ppermute | solution.py:341
  28.6 4.0 %collective-permute-done.1.refs_2_ = bf16[64,192]{1,0:T(8,128)(2,1)S(1)} collective-permute-done((bf16[64,192]{1,0:T(8,128)(2,1)S(1)}, bf16[64,192]{1,0:T(8,128)(2,1)S(1)}, u32[]{:S(2)}, u32[]{:S(2)}) %collective-permute-start.1) | collective-permute-done | bytes 24608 | tf_op jit(solution)/shard_map/ppermute | solution.py:341
  32.6 1.6 %all-to-all-done.1.refs_4_.x_ref = bf16[8,576,128]{2,1,0:T(8,128)(2,1)S(1)} async-done(((bf16[8,576,128]{2,1,0:T(8,128)(2,1)}), bf16[8,576,128]{2,1,0:T(8,128)(2,1)S(1)}, u32[]{:S(2)}, u32[]{:S(2)}) %all-to-all-start.1) | async-done | bytes 1179680 | tf_op jit(solution)/shard_map/all_to_all | solution.py:57
  34.3 2.7 %shard_map.48 = (bf16[8,208,256]{2,1,0:T(8,128)(2,1)}, bf16[256,192]{1,0:T(8,128)(2,1)S(1)}, bf16[192,1024]{1,0:T(8,128)(2,1)S(1)}) custom-call(s32[1]{0:T(128)} %bitcast.z_ref, bf16[64,192]{1,0:T(8,128)(2,1)S(1)} %reshape.26.refs_0_, bf16[64,192]{1,0:T(8,128)(2,1)S(1)} %collective-permute-done.refs_1_, bf16[64,192]{1,0:T(8,128)(2,1)S(1)} %collective-permute-done.1.refs_2_, ...), custom_call_target="tpu_custom_call" | custom-call | flops 1200000000 | bytes 8000000 | tf_op jit(solution)/shard_map/pallas_call | solution.py:45
  37.0 7.7 %all-to-all-start.2 = ((bf16[8,208,256]{2,1,0:T(8,128)(2,1)}), bf16[8,208,256]{2,1,0:T(8,128)(2,1)S(1)}, u32[]{:S(2)}, u32[]{:S(2)}) async-start(bf16[8,208,256]{2,1,0:T(8,128)(2,1)} %get-tuple-element.12), calls=%async_computation.2 | async-start | bytes 1703936 | tf_op jit(solution)/shard_map/all_to_all | solution.py:57
  45.1 2.8 %collective-permute-start.4 = (bf16[192,256]{1,0:T(8,128)(2,1)S(1)}, bf16[192,256]{1,0:T(8,128)(2,1)S(1)}, u32[]{:S(2)}, u32[]{:S(2)}) collective-permute-start(bf16[192,256]{1,0:T(8,128)(2,1)S(1)} %get-tuple-element.16), channel_id=1, source_target_pairs={{64,128},{128,64},{65,129},{129,65},{66,130},{130,66},{67,131},{13... | collective-permute-start | bytes 294920 | tf_op jit(solution)/shard_map/ppermute | solution.py:366
  48.1 4.4 %collective-permute-done.4.far_ref = bf16[192,256]{1,0:T(8,128)(2,1)S(1)} collective-permute-done((bf16[192,256]{1,0:T(8,128)(2,1)S(1)}, bf16[192,256]{1,0:T(8,128)(2,1)S(1)}, u32[]{:S(2)}, u32[]{:S(2)}) %collective-permute-start.4) | collective-permute-done | bytes 98336 | tf_op jit(solution)/shard_map/ppermute | solution.py:366
  52.6 0.9 %shard_map.52 = (bf16[192,128]{1,0:T(8,128)(2,1)S(1)}, bf16[192,128]{1,0:T(8,128)(2,1)S(1)}) custom-call(s32[1]{0:T(128)} %bitcast.4.even_ref, bf16[8,576,128]{2,1,0:T(8,128)(2,1)S(1)} %all-to-all-done.1.refs_4_.x_ref, bf16[192,256]{1,0:T(8,128)(2,1)S(1)} %collective-permute-done.3.near_ref, bf16[192,256]{1,0:T(8,128)(2,1)S(1)} %collective-permute-done.4.far_ref, ...), custom_call_target="tpu_custom_call" | custom-call | flops 300000000 | bytes 2000000 | tf_op jit(solution)/shard_map/pallas_call | solution.py:45
  53.5 3.9 %collective-permute-start.5 = (bf16[192,128]{1,0:T(8,128)(2,1)S(1)}, bf16[192,128]{1,0:T(8,128)(2,1)S(1)}, u32[]{:S(2)}, u32[]{:S(2)}) collective-permute-start(bf16[192,128]{1,0:T(8,128)(2,1)S(1)} %get-tuple-element.17), channel_id=1, source_target_pairs={{0,8},{8,16},{16,24},{24,32},{32,40},{40,48},{48,56},{1,9},{9,17},... | collective-permute-start | bytes 147464 | tf_op jit(solution)/shard_map/ppermute | solution.py:63
  57.4 1.3 %collective-permute-start.6 = (bf16[192,128]{1,0:T(8,128)(2,1)S(1)}, bf16[192,128]{1,0:T(8,128)(2,1)S(1)}, u32[]{:S(2)}, u32[]{:S(2)}) collective-permute-start(bf16[192,128]{1,0:T(8,128)(2,1)S(1)} %get-tuple-element.18), channel_id=1, source_target_pairs={{8,0},{16,8},{24,16},{32,24},{40,32},{48,40},{56,48},{9,1},{17,9},... | collective-permute-start | bytes 147464 | tf_op jit(solution)/shard_map/ppermute | solution.py:63
  58.7 3.5 %shard_map.51.local_ref = f32[8,192,128]{2,1,0:T(8,128)S(1)} custom-call(s32[1]{0:T(128)} %bitcast.4.even_ref, bf16[8,576,128]{2,1,0:T(8,128)(2,1)S(1)} %all-to-all-done.1.refs_4_.x_ref, bf16[192,256]{1,0:T(8,128)(2,1)S(1)} %collective-permute-done.3.near_ref, bf16[192,256]{1,0:T(8,128)(2,1)S(1)} %collective-permute-done.4.far_ref, ...), custom_call_target="tpu_custom_call" | custom-call | flops 1500000000 | bytes 10000000 | tf_op jit(solution)/shard_map/pallas_call | solution.py:45
  62.9 1.4 %collective-permute-done.6.down_ref = bf16[192,128]{1,0:T(8,128)(2,1)S(1)} collective-permute-done((bf16[192,128]{1,0:T(8,128)(2,1)S(1)}, bf16[192,128]{1,0:T(8,128)(2,1)S(1)}, u32[]{:S(2)}, u32[]{:S(2)}) %collective-permute-start.6) | collective-permute-done | bytes 49184 | tf_op jit(solution)/shard_map/ppermute | solution.py:63
  64.9 2.8 %all-to-all-done.2.parts_ref = bf16[8,208,256]{2,1,0:T(8,128)(2,1)S(1)} async-done(((bf16[8,208,256]{2,1,0:T(8,128)(2,1)}), bf16[8,208,256]{2,1,0:T(8,128)(2,1)S(1)}, u32[]{:S(2)}, u32[]{:S(2)}) %all-to-all-start.2) | async-done | bytes 852000 | tf_op jit(solution)/shard_map/all_to_all | solution.py:57
  67.7 0.8 copy-done.1
  69.3 1.8 %shard_map.53 = bf16[8,192,128]{2,1,0:T(8,128)(2,1)S(1)} custom-call(bf16[8,208,256]{2,1,0:T(8,128)(2,1)S(1)} %all-to-all-done.2.parts_ref, bf16[256,192]{1,0:T(8,128)(2,1)S(1)} %get-tuple-element.13.a_ref, bf16[192,1024]{1,0:T(8,128)(2,1)S(1)} %get-tuple-element.14.q_ref, f32[8,192,128]{2,1,0:T(8,128)S(1)} %shard_map.51.local_ref, ...), custom_call_target="tpu_custom_call" | custom-call | flops 300000000 | bytes 2000000 | tf_op jit(solution)/shard_map/pallas_call | solution.py:45
  71.1 13.9 %all_to_all.20.x_ref = bf16[8,192,128]{2,1,0:T(8,128)(2,1)S(1)} all-to-all(bf16[8,192,128]{2,1,0:T(8,128)(2,1)S(1)} %shard_map.53), channel_id=1, replica_groups=mesh['tm'=4,'zh'=4,'zl'=2,'xy'=8] {'xy'}, dimensions={0} | all-to-all | bytes 786432 | tf_op jit(solution)/shard_map/all_to_all | solution.py:57
  85.0 0.9 %shard_map.54 = bf16[128,1536]{1,0:T(8,128)(2,1)} custom-call(bf16[8,192,128]{2,1,0:T(8,128)(2,1)S(1)} %all_to_all.20.x_ref), custom_call_target="tpu_custom_call" | custom-call | flops 300000000 | bytes 2000000 | tf_op jit(solution)/shard_map/pallas_call | solution.py:45
  (17 shorter events, 2.6 us)
Async XLA Ops:
  2.0 13.7 %all-to-all-start = ((bf16[16,4,192]{2,1,0:T(4,128)(2,1)}), bf16[16,4,192]{2,1,0:T(4,128)(2,1)S(1)}, u32[]{:S(2)}, u32[]{:S(2)}) async-start(bf16[16,4,192]{2,1,0:T(4,128)(2,1)} %shard_map.46), calls=%async_computation | async-start | bytes 65536 | tf_op jit(solution)/shard_map/all_to_all | solution.py:57
  15.7 18.5 %all-to-all-start.1 = ((bf16[8,576,128]{2,1,0:T(8,128)(2,1)}), bf16[8,576,128]{2,1,0:T(8,128)(2,1)S(1)}, u32[]{:S(2)}, u32[]{:S(2)}) async-start(bf16[8,576,128]{2,1,0:T(8,128)(2,1)} %shard_map.47), calls=%async_computation.1 | async-start | bytes 2359296 | tf_op jit(solution)/shard_map/all_to_all | solution.py:57
  19.3 9.3 %collective-permute-start.2 = (bf16[64,192]{1,0:T(8,128)(2,1)S(1)}, bf16[64,192]{1,0:T(8,128)(2,1)S(1)}, u32[]{:S(2)}, u32[]{:S(2)}) collective-permute-start(bf16[64,192]{1,0:T(8,128)(2,1)S(1)} %reshape.26.refs_0_), channel_id=1, source_target_pairs={{0,48},{16,0},{32,16},{48,32},{1,49},{17,1},{33,17},{49,33},{2,50}... | collective-permute-start | bytes 73736 | tf_op jit(solution)/shard_map/ppermute | solution.py:341
  24.8 7.8 %collective-permute-start.1 = (bf16[64,192]{1,0:T(8,128)(2,1)S(1)}, bf16[64,192]{1,0:T(8,128)(2,1)S(1)}, u32[]{:S(2)}, u32[]{:S(2)}) collective-permute-start(bf16[64,192]{1,0:T(8,128)(2,1)S(1)} %reshape.26.refs_0_), channel_id=1, source_target_pairs={{0,32},{16,48},{32,0},{48,16},{1,33},{17,49},{33,1},{49,17},{2,34}... | collective-permute-start | bytes 73736 | tf_op jit(solution)/shard_map/ppermute | solution.py:341
  26.3 6.4 %collective-permute-start = (bf16[64,192]{1,0:T(8,128)(2,1)S(1)}, bf16[64,192]{1,0:T(8,128)(2,1)S(1)}, u32[]{:S(2)}, u32[]{:S(2)}) collective-permute-start(bf16[64,192]{1,0:T(8,128)(2,1)S(1)} %reshape.26.refs_0_), channel_id=1, source_target_pairs={{0,16},{16,32},{32,48},{48,0},{1,17},{17,33},{33,49},{49,1},{2,18}... | collective-permute-start | bytes 73736 | tf_op jit(solution)/shard_map/ppermute | solution.py:341
  37.0 11.0 %copy-start.4 = (f32[3,3,3,1536]{3,2,1,0:T(4,128)S(1)}, f32[3,3,3,1536]{3,2,1,0:T(4,128)}, u32[]{:S(2)}) copy-start(f32[3,3,3,1536]{3,2,1,0:T(4,128)} %w_ref.1) | copy-start | bytes 497668
  37.0 30.7 %all-to-all-start.2 = ((bf16[8,208,256]{2,1,0:T(8,128)(2,1)}), bf16[8,208,256]{2,1,0:T(8,128)(2,1)S(1)}, u32[]{:S(2)}, u32[]{:S(2)}) async-start(bf16[8,208,256]{2,1,0:T(8,128)(2,1)} %get-tuple-element.12), calls=%async_computation.2 | async-start | bytes 1703936 | tf_op jit(solution)/shard_map/all_to_all | solution.py:57
  45.0 3.1 %collective-permute-start.3 = (bf16[192,256]{1,0:T(8,128)(2,1)S(1)}, bf16[192,256]{1,0:T(8,128)(2,1)S(1)}, u32[]{:S(2)}, u32[]{:S(2)}) collective-permute-start(bf16[192,256]{1,0:T(8,128)(2,1)S(1)} %get-tuple-element.15), channel_id=1, source_target_pairs={{0,64},{128,192},{64,0},{192,128},{1,65},{129,193},{65,1},{193,129... | collective-permute-start | bytes 294920 | tf_op jit(solution)/shard_map/ppermute | solution.py:364
  45.1 7.4 %collective-permute-start.4 = (bf16[192,256]{1,0:T(8,128)(2,1)S(1)}, bf16[192,256]{1,0:T(8,128)(2,1)S(1)}, u32[]{:S(2)}, u32[]{:S(2)}) collective-permute-start(bf16[192,256]{1,0:T(8,128)(2,1)S(1)} %get-tuple-element.16), channel_id=1, source_target_pairs={{64,128},{128,64},{65,129},{129,65},{66,130},{130,66},{67,131},{13... | collective-permute-start | bytes 294920 | tf_op jit(solution)/shard_map/ppermute | solution.py:366
  53.5 8.8 %collective-permute-start.5 = (bf16[192,128]{1,0:T(8,128)(2,1)S(1)}, bf16[192,128]{1,0:T(8,128)(2,1)S(1)}, u32[]{:S(2)}, u32[]{:S(2)}) collective-permute-start(bf16[192,128]{1,0:T(8,128)(2,1)S(1)} %get-tuple-element.17), channel_id=1, source_target_pairs={{0,8},{8,16},{16,24},{24,32},{32,40},{40,48},{48,56},{1,9},{9,17},... | collective-permute-start | bytes 147464 | tf_op jit(solution)/shard_map/ppermute | solution.py:63
  57.4 6.9 %collective-permute-start.6 = (bf16[192,128]{1,0:T(8,128)(2,1)S(1)}, bf16[192,128]{1,0:T(8,128)(2,1)S(1)}, u32[]{:S(2)}, u32[]{:S(2)}) collective-permute-start(bf16[192,128]{1,0:T(8,128)(2,1)S(1)} %get-tuple-element.18), channel_id=1, source_target_pairs={{8,0},{16,8},{24,16},{32,24},{40,32},{48,40},{56,48},{9,1},{17,9},... | collective-permute-start | bytes 147464 | tf_op jit(solution)/shard_map/ppermute | solution.py:63
  62.3 0.6 copy-start
  64.3 0.6 copy-start.2
  67.7 0.8 copy-start.1
  68.5 0.8 copy-start.3

commit v8 on v7

--- a/solution.py
+++ b/solution.py
@@ -18,6 +18,7 @@
 PLANES = 2 * PAIRS
 TILES = 8
 AGENTS = 256
+HALF = AGENTS // 2
 GROUP_HEADS = HEADS // TILES
 GROUP = GROUP_HEADS * HEAD_DIM
 K_ROW = GROUP
@@ -113,13 +114,13 @@
 
 
 def agent_kernel(z_ref, *refs):
-    came, (x_ref, out_ref, a_ref, q_ref) = refs[:PAIRS], refs[PAIRS:]
+    came, (x_ref, keep_ref, send_ref, a_ref, q_ref) = refs[:PAIRS], refs[PAIRS:]
+    low = z_ref[1] == 0
     for hop, ref in enumerate(came):
         z = lax.rem(z_ref[0] + PAIRS - hop, PAIRS)
         a_ref[pl.ds(pl.multiple_of(z * PAIR_AGENTS, PAIR_AGENTS), PAIR_AGENTS), :] = ref[...]
     columns = []
-    lane = lax.broadcasted_iota(jnp.int32, (AGENTS, HEAD_DIM), 1)
-    stats = jnp.zeros((AGENTS, HEAD_DIM), F32)
+    logs = []
     for h in range(GROUP_HEADS):
         keys = rows_of(x_ref, K_ROW + h * HEAD_DIM, HEAD_DIM)
         values = rows_of(x_ref, V_ROW + h * HEAD_DIM, HEAD_DIM)
@@ -132,16 +133,51 @@
             weights.astype(BF16), values, (((1,), (1,)), ((), ())), preferred_element_type=F32
         )
         columns.append(acc / total)
-        left = peak + jnp.log(total)
-        for piece in range(3):
-            short = left.astype(BF16).astype(F32)
-            left = left - short
-            stats = jnp.where(lane == piece * GROUP_HEADS + h, short, stats)
-    flipped = jnp.concatenate(columns + [stats], axis=1).T
-    part = flipped[: GROUP + STATS].astype(BF16)
+        logs.append(peak + jnp.log(total))
+    lane = lax.broadcasted_iota(jnp.int32, (AGENTS, HEAD_DIM), 1)
+    stats = jnp.zeros((AGENTS, HEAD_DIM), F32)
+    for h, log in enumerate(logs):
+        stats = jnp.where(lane == h, log, stats)
+    part = jnp.concatenate(columns + [stats], axis=1).T
+    near, far = part[:, :HALF], part[:, HALF:]
+    keep_ref[...] = jnp.where(low, near, far)[: GROUP + 8]
+    away = jnp.where(low, far, near)
+    send_ref[:GROUP] = away[:GROUP].astype(BF16)
+    send_ref[GROUP:] = pieces_of(away[GROUP : GROUP + GROUP_HEADS])
+    q_ref[...] = rows_of(x_ref, 0, GROUP)
+
+
+def pieces_of(logs):
+    pieces = []
+    for _ in range(3):
+        short = logs.astype(BF16).astype(F32)
+        logs = logs - short
+        pieces.append(short)
+    pieces.append(jnp.zeros((STATS - 3 * GROUP_HEADS, HALF), F32))
+    return jnp.concatenate(pieces, axis=0).astype(BF16)
+
+
+def logs_of(pieces):
+    n = GROUP_HEADS
+    pieces = pieces.astype(F32)
+    return pieces[:n] + pieces[n : 2 * n] + pieces[2 * n : 3 * n]
+
+
+def blend_kernel(keep_ref, came_ref, out_ref):
+    ours, theirs = keep_ref[GROUP : GROUP + GROUP_HEADS, :], logs_of(came_ref[GROUP:, :])
+    peak = jnp.maximum(ours, theirs)
+    left, right = jnp.exp(ours - peak), jnp.exp(theirs - peak)
+    whole = left + right
+    left, right = left / whole, right / whole
+    stats = pieces_of(peak + jnp.log(whole))
+    for h in range(GROUP_HEADS):
+        rows = slice(h * HEAD_DIM, (h + 1) * HEAD_DIM)
+        part = keep_ref[rows, :] * left[h : h + 1] + came_ref[rows, :].astype(F32) * right[h : h + 1]
+        part = part.astype(BF16)
+        for z in range(PLANES):
+            out_ref[z, rows, :] = part
     for z in range(PLANES):
-        out_ref[z] = part
-    q_ref[...] = rows_of(x_ref, 0, GROUP)
+        out_ref[z, GROUP:, :] = stats
 
 
 def taps_kernel(tile_ref, w_ref, out_ref):
@@ -259,23 +295,25 @@
 
 
 def mix_kernel(parts_ref, a_ref, q_ref, local_ref, up_ref, down_ref, out_ref):
-    logs = []
-    for z in range(PLANES):
-        pieces = parts_ref[z, GROUP : GROUP + STATS, :].astype(F32)
-        n = GROUP_HEADS
-        logs.append(pieces[:n] + pieces[n : 2 * n] + pieces[2 * n : 3 * n])
-    peak = logs[0]
-    for log in logs[1:]:
-        peak = jnp.maximum(peak, log)
-    shares = [jnp.exp(log - peak) for log in logs]
-    whole = sum(shares[1:], shares[0])
-    shares = [share / whole for share in shares]
+    shares = []
+    for half in range(2):
+        logs = [logs_of(parts_ref[z, GROUP:, :]) for z in range(half, PLANES, 2)]
+        peak = logs[0]
+        for log in logs[1:]:
+            peak = jnp.maximum(peak, log)
+        some = [jnp.exp(log - peak) for log in logs]
+        whole = sum(some[1:], some[0])
+        shares.append([share / whole for share in some])
     for h in range(GROUP_HEADS):
         rows = slice(h * HEAD_DIM, (h + 1) * HEAD_DIM)
-        values = None
-        for z in range(PLANES):
-            term = parts_ref[z, rows, :].astype(F32) * shares[z][h : h + 1]
-            values = term if values is None else values + term
+        halves = []
+        for half in range(2):
+            terms = [
+                parts_ref[z, rows, :].astype(F32) * shares[half][z // 2][h : h + 1]
+                for z in range(half, PLANES, 2)
+            ]
+            halves.append(sum(terms[1:], terms[0]))
+        values = jnp.concatenate(halves, axis=1)
         scores = jnp.dot(a_ref[:, rows], q_ref[rows, :], preferred_element_type=F32) * INV_ROOT
         weights = jnp.exp(scores - jnp.max(scores, axis=0, keepdims=True))
         total = jnp.sum(weights, axis=0, keepdims=True)
@@ -342,19 +380,22 @@
     tile = scalar(lax.axis_index("xy"))
     taps = call(taps_kernel, shape((GROUP, 32), F32), 1.0, conv_weight, scalars=(tile,))
 
-    part, agents, turned_q = call(
+    keep, send, agents, turned_q = call(
         agent_kernel,
         (
-            shape((PLANES, GROUP + STATS, AGENTS), BF16),
+            shape((GROUP + 8, HALF), F32),
+            shape((GROUP + STATS, HALF), BF16),
             shape((AGENTS, GROUP), BF16),
             shape((GROUP, TILES * TOKENS), BF16),
         ),
-        4.0,
+        3.0,
         *came,
         x,
-        scalars=(scalar(lax.axis_index("zh")),),
-    )
-    parts = exchange(part, ("zh", "zl"))
+        scalars=(jnp.stack([lax.axis_index("zh"), lax.axis_index("zl")]).astype(jnp.int32),),
+    )
+    theirs = lax.ppermute(send, "zl", [(0, 1), (1, 0)])
+    blended = call(blend_kernel, shape((PLANES, GROUP + STATS, HALF), BF16), 1.0, keep, theirs)
+    parts = exchange(blended, ("zh", "zl"))
 
     edges = shape((GROUP, EDGE), BF16)
     even = scalar(1 - lax.axis_index("tm") % 2)

time: 86.4 us -> 83.5 us (0.966)
  the two profiles are of different devices: /device:TPU:4 before, /device:TPU:100 now
where the time goes in v8:
time: 83.5 us; the launch traced here: 83.1 us
  starting transfers between devices  38.1 us (46%)
  waiting for transfers between devices  18.4 us (22%)
  Pallas kernels  14.9 us (18%)
  blocking collectives  11.4 us (14%)
    all_to_all x3, starting transfers between devices, exchange(): return lax.all_to_all(x, axes, 0, 0)  18.4 us
    pallas_call x10, Pallas kernels, call(): pl.pallas_call(kernel, out_shape=out_shape, in_specs=[SMEM] * len(scalars...  14.9 us
    all_to_all x1, blocking collectives, exchange(): return lax.all_to_all(x, axes, 0, 0)  11.4 us
    ppermute x3, starting transfers between devices, body(): lax.ppermute(own, 'zh', [(i, (i + n) % PAIRS) for i in range(PAIRS)])  8.7 us
    all_to_all x3, waiting for transfers between devices, exchange(): return lax.all_to_all(x, axes, 0, 0)  7.57 us
    ppermute x2, starting transfers between devices, shift(): return lax.ppermute(x, axis, pairs)  6.5 us
    ppermute x1, waiting for transfers between devices, body(): far = lax.ppermute(far, 'tm', pairs + [(b, a) for a, b in pairs])  4.45 us
    ppermute x1, starting transfers between devices, body(): far = lax.ppermute(far, 'tm', pairs + [(b, a) for a, b in pairs])  2.8 us
  transfers between devices with their start and end apart: 11, of which 7 were waited for; matrix products, arithmetic and copies ran while one was open for 0% of the time, Pallas kernels for 9%

profile of v8, /device:TPU:100, one launch (start us, length us, event | category | flops | bytes accessed | tf_op | source)
XLA Modules:
  0.0 83.1 jit_solution(6688625296287580817)
XLA Ops:
  0.0 2.0 %shard_map.46 = bf16[16,4,192]{2,1,0:T(4,128)(2,1)} custom-call(bf16[128,1536]{1,0:T(8,128)(2,1)} %bitcast.10), custom_call_target="tpu_custom_call" | custom-call | flops 300000000 | bytes 2000000 | tf_op jit(solution)/shard_map/pallas_call | solution.py:46
  2.0 6.6 %all-to-all-start = ((bf16[16,4,192]{2,1,0:T(4,128)(2,1)}), bf16[16,4,192]{2,1,0:T(4,128)(2,1)S(1)}, u32[]{:S(2)}, u32[]{:S(2)}) async-start(bf16[16,4,192]{2,1,0:T(4,128)(2,1)} %shard_map.46), calls=%async_computation | async-start | bytes 65536 | tf_op jit(solution)/shard_map/all_to_all | solution.py:58
  8.6 2.3 %shard_map.47 = bf16[8,576,128]{2,1,0:T(8,128)(2,1)} custom-call(bf16[128,1536]{1,0:T(8,128)(2,1)} %bitcast.11, bf16[128,1536]{1,0:T(8,128)(2,1)} %bitcast.12, bf16[128,1536]{1,0:T(8,128)(2,1)} %bitcast.13), custom_call_target="tpu_custom_call" | custom-call | flops 900000000 | bytes 6000000 | tf_op jit(solution)/shard_map/pallas_call | solution.py:46
  10.9 3.5 %all-to-all-done = bf16[16,4,192]{2,1,0:T(4,128)(2,1)S(1)} async-done(((bf16[16,4,192]{2,1,0:T(4,128)(2,1)}), bf16[16,4,192]{2,1,0:T(4,128)(2,1)S(1)}, u32[]{:S(2)}, u32[]{:S(2)}) %all-to-all-start) | async-done | bytes 24608 | tf_op jit(solution)/shard_map/all_to_all | solution.py:58
  14.4 3.6 %all-to-all-start.1 = ((bf16[8,576,128]{2,1,0:T(8,128)(2,1)}), bf16[8,576,128]{2,1,0:T(8,128)(2,1)S(1)}, u32[]{:S(2)}, u32[]{:S(2)}) async-start(bf16[8,576,128]{2,1,0:T(8,128)(2,1)} %shard_map.47), calls=%async_computation.1 | async-start | bytes 2359296 | tf_op jit(solution)/shard_map/all_to_all | solution.py:58
  18.1 5.9 %collective-permute-start.1 = (bf16[64,192]{1,0:T(8,128)(2,1)S(1)}, bf16[64,192]{1,0:T(8,128)(2,1)S(1)}, u32[]{:S(2)}, u32[]{:S(2)}) collective-permute-start(bf16[64,192]{1,0:T(8,128)(2,1)S(1)} %reshape.22.refs_0_), channel_id=1, source_target_pairs={{0,32},{16,48},{32,0},{48,16},{1,33},{17,49},{33,1},{49,17},{2,34}... | collective-permute-start | bytes 73736 | tf_op jit(solution)/shard_map/ppermute | solution.py:379
  24.0 2.7 %collective-permute-start = (bf16[64,192]{1,0:T(8,128)(2,1)S(1)}, bf16[64,192]{1,0:T(8,128)(2,1)S(1)}, u32[]{:S(2)}, u32[]{:S(2)}) collective-permute-start(bf16[64,192]{1,0:T(8,128)(2,1)S(1)} %reshape.22.refs_0_), channel_id=1, source_target_pairs={{0,16},{16,32},{32,48},{48,0},{1,17},{17,33},{33,49},{49,1},{2,18}... | collective-permute-start | bytes 73736 | tf_op jit(solution)/shard_map/ppermute | solution.py:379
  27.0 1.9 %collective-permute-done.refs_1_ = bf16[64,192]{1,0:T(8,128)(2,1)S(1)} collective-permute-done((bf16[64,192]{1,0:T(8,128)(2,1)S(1)}, bf16[64,192]{1,0:T(8,128)(2,1)S(1)}, u32[]{:S(2)}, u32[]{:S(2)}) %collective-permute-start) | collective-permute-done | bytes 24608 | tf_op jit(solution)/shard_map/ppermute | solution.py:379
  28.8 4.1 %all-to-all-done.1.refs_4_.x_ref = bf16[8,576,128]{2,1,0:T(8,128)(2,1)S(1)} async-done(((bf16[8,576,128]{2,1,0:T(8,128)(2,1)}), bf16[8,576,128]{2,1,0:T(8,128)(2,1)S(1)}, u32[]{:S(2)}, u32[]{:S(2)}) %all-to-all-start.1) | async-done | bytes 1179680 | tf_op jit(solution)/shard_map/all_to_all | solution.py:58
  32.9 2.3 %shard_map.48 = (f32[200,128]{1,0:T(8,128)S(1)}, bf16[208,128]{1,0:T(8,128)(2,1)S(1)}, bf16[256,192]{1,0:T(8,128)(2,1)S(1)}, bf16[192,1024]{1,0:T(8,128)(2,1)S(1)}) custom-call(s32[2]{0:T(128)S(1)} %pad_add_fusion.z_ref, bf16[64,192]{1,0:T(8,128)(2,1)S(1)} %reshape.22.refs_0_, bf16[64,192]{1,0:T(8,128)(2,1)S(1)} %collective-permute-done.refs_1_, ...), custom_call_target="tpu_custom_call" | custom-call | flops 900000000 | bytes 6000000 | tf_op jit(solution)/shard_map/pallas_call | solution.py:46
  35.2 1.6 %collective-permute-start.3 = (bf16[208,128]{1,0:T(8,128)(2,1)S(1)}, bf16[208,128]{1,0:T(8,128)(2,1)S(1)}, u32[]{:S(2)}, u32[]{:S(2)}) collective-permute-start(bf16[208,128]{1,0:T(8,128)(2,1)S(1)} %get-tuple-element.14), channel_id=1, source_target_pairs={{0,8},{8,0},{1,9},{9,1},{2,10},{10,2},{3,11},{11,3},{4,12},{12,4},... | collective-permute-start | bytes 159752 | tf_op jit(solution)/shard_map/ppermute | solution.py:396
  36.8 2.7 %collective-permute-done.3.came_ref = bf16[208,128]{1,0:T(8,128)(2,1)S(1)} collective-permute-done((bf16[208,128]{1,0:T(8,128)(2,1)S(1)}, bf16[208,128]{1,0:T(8,128)(2,1)S(1)}, u32[]{:S(2)}, u32[]{:S(2)}) %collective-permute-start.3) | collective-permute-done | bytes 53280 | tf_op jit(solution)/shard_map/ppermute | solution.py:396
  39.5 0.8 shard_map.49
  40.3 8.3 %all-to-all-start.2 = ((bf16[8,208,128]{2,1,0:T(8,128)(2,1)}), bf16[8,208,128]{2,1,0:T(8,128)(2,1)S(1)}, u32[]{:S(2)}, u32[]{:S(2)}) async-start(bf16[8,208,128]{2,1,0:T(8,128)(2,1)} %shard_map.49), calls=%async_computation.2 | async-start | bytes 851968 | tf_op jit(solution)/shard_map/all_to_all | solution.py:58
  49.0 2.8 %collective-permute-start.5 = (bf16[192,256]{1,0:T(8,128)(2,1)S(1)}, bf16[192,256]{1,0:T(8,128)(2,1)S(1)}, u32[]{:S(2)}, u32[]{:S(2)}) collective-permute-start(bf16[192,256]{1,0:T(8,128)(2,1)S(1)} %get-tuple-element.18), channel_id=1, source_target_pairs={{64,128},{128,64},{65,129},{129,65},{66,130},{130,66},{67,131},{13... | collective-permute-start | bytes 294920 | tf_op jit(solution)/shard_map/ppermute | solution.py:407
  52.0 4.4 %collective-permute-done.5.far_ref = bf16[192,256]{1,0:T(8,128)(2,1)S(1)} collective-permute-done((bf16[192,256]{1,0:T(8,128)(2,1)S(1)}, bf16[192,256]{1,0:T(8,128)(2,1)S(1)}, u32[]{:S(2)}, u32[]{:S(2)}) %collective-permute-start.5) | collective-permute-done | bytes 98336 | tf_op jit(solution)/shard_map/ppermute | solution.py:407
  56.4 0.9 %shard_map.53 = (bf16[192,128]{1,0:T(8,128)(2,1)S(1)}, bf16[192,128]{1,0:T(8,128)(2,1)S(1)}) custom-call(s32[1]{0:T(128)} %bitcast.5.even_ref, bf16[8,576,128]{2,1,0:T(8,128)(2,1)S(1)} %all-to-all-done.1.refs_4_.x_ref, bf16[192,256]{1,0:T(8,128)(2,1)S(1)} %collective-permute-done.4.near_ref, bf16[192,256]{1,0:T(8,128)(2,1)S(1)} %collective-permute-done.5.far_ref, ...), custom_call_target="tpu_custom_call" | custom-call | flops 300000000 | bytes 2000000 | tf_op jit(solution)/shard_map/pallas_call | solution.py:46
  57.4 4.6 %collective-permute-start.6 = (bf16[192,128]{1,0:T(8,128)(2,1)S(1)}, bf16[192,128]{1,0:T(8,128)(2,1)S(1)}, u32[]{:S(2)}, u32[]{:S(2)}) collective-permute-start(bf16[192,128]{1,0:T(8,128)(2,1)S(1)} %get-tuple-element.19), channel_id=1, source_target_pairs={{0,8},{8,16},{16,24},{24,32},{32,40},{40,48},{48,56},{1,9},{9,17},... | collective-permute-start | bytes 147464 | tf_op jit(solution)/shard_map/ppermute | solution.py:64
  61.9 1.9 %collective-permute-start.7 = (bf16[192,128]{1,0:T(8,128)(2,1)S(1)}, bf16[192,128]{1,0:T(8,128)(2,1)S(1)}, u32[]{:S(2)}, u32[]{:S(2)}) collective-permute-start(bf16[192,128]{1,0:T(8,128)(2,1)S(1)} %get-tuple-element.20), channel_id=1, source_target_pairs={{8,0},{16,8},{24,16},{32,24},{40,32},{48,40},{56,48},{9,1},{17,9},... | collective-permute-start | bytes 147464 | tf_op jit(solution)/shard_map/ppermute | solution.py:64
  63.9 3.5 %shard_map.52.local_ref = f32[8,192,128]{2,1,0:T(8,128)S(1)} custom-call(s32[1]{0:T(128)} %bitcast.5.even_ref, bf16[8,576,128]{2,1,0:T(8,128)(2,1)S(1)} %all-to-all-done.1.refs_4_.x_ref, bf16[192,256]{1,0:T(8,128)(2,1)S(1)} %collective-permute-done.4.near_ref, bf16[192,256]{1,0:T(8,128)(2,1)S(1)} %collective-permute-done.5.far_ref, ...), custom_call_target="tpu_custom_call" | custom-call | flops 1500000000 | bytes 10000000 | tf_op jit(solution)/shard_map/pallas_call | solution.py:46
  67.4 1.7 %collective-permute-done.7.down_ref = bf16[192,128]{1,0:T(8,128)(2,1)S(1)} collective-permute-done((bf16[192,128]{1,0:T(8,128)(2,1)S(1)}, bf16[192,128]{1,0:T(8,128)(2,1)S(1)}, u32[]{:S(2)}, u32[]{:S(2)}) %collective-permute-start.7) | collective-permute-done | bytes 49184 | tf_op jit(solution)/shard_map/ppermute | solution.py:64
  69.1 1.7 %shard_map.54 = bf16[8,192,128]{2,1,0:T(8,128)(2,1)S(1)} custom-call(bf16[8,208,128]{2,1,0:T(8,128)(2,1)S(1)} %all-to-all-done.2.parts_ref, bf16[256,192]{1,0:T(8,128)(2,1)S(1)} %get-tuple-element.15.a_ref, bf16[192,1024]{1,0:T(8,128)(2,1)S(1)} %get-tuple-element.16.q_ref, f32[8,192,128]{2,1,0:T(8,128)S(1)} %shard_map.52.local_ref, ...), custom_call_target="tpu_custom_call" | custom-call | flops 300000000 | bytes 2000000 | tf_op jit(solution)/shard_map/pallas_call | solution.py:46
  70.8 11.4 %all_to_all.20.x_ref = bf16[8,192,128]{2,1,0:T(8,128)(2,1)S(1)} all-to-all(bf16[8,192,128]{2,1,0:T(8,128)(2,1)S(1)} %shard_map.54), channel_id=1, replica_groups=mesh['tm'=4,'zh'=4,'zl'=2,'xy'=8] {'xy'}, dimensions={0} | all-to-all | bytes 786432 | tf_op jit(solution)/shard_map/all_to_all | solution.py:58
  82.2 0.9 %shard_map.55 = bf16[128,1536]{1,0:T(8,128)(2,1)} custom-call(bf16[8,192,128]{2,1,0:T(8,128)(2,1)S(1)} %all_to_all.20.x_ref), custom_call_target="tpu_custom_call" | custom-call | flops 300000000 | bytes 2000000 | tf_op jit(solution)/shard_map/pallas_call | solution.py:46
  (13 shorter events, 0.9 us)
Async XLA Ops:
  2.0 12.4 %all-to-all-start = ((bf16[16,4,192]{2,1,0:T(4,128)(2,1)}), bf16[16,4,192]{2,1,0:T(4,128)(2,1)S(1)}, u32[]{:S(2)}, u32[]{:S(2)}) async-start(bf16[16,4,192]{2,1,0:T(4,128)(2,1)} %shard_map.46), calls=%async_computation | async-start | bytes 65536 | tf_op jit(solution)/shard_map/all_to_all | solution.py:58
  14.4 18.5 %all-to-all-start.1 = ((bf16[8,576,128]{2,1,0:T(8,128)(2,1)}), bf16[8,576,128]{2,1,0:T(8,128)(2,1)S(1)}, u32[]{:S(2)}, u32[]{:S(2)}) async-start(bf16[8,576,128]{2,1,0:T(8,128)(2,1)} %shard_map.47), calls=%async_computation.1 | async-start | bytes 2359296 | tf_op jit(solution)/shard_map/all_to_all | solution.py:58
  18.0 8.8 %collective-permute-start.2 = (bf16[64,192]{1,0:T(8,128)(2,1)S(1)}, bf16[64,192]{1,0:T(8,128)(2,1)S(1)}, u32[]{:S(2)}, u32[]{:S(2)}) collective-permute-start(bf16[64,192]{1,0:T(8,128)(2,1)S(1)} %reshape.22.refs_0_), channel_id=1, source_target_pairs={{0,48},{16,0},{32,16},{48,32},{1,49},{17,1},{33,17},{49,33},{2,50}... | collective-permute-start | bytes 73736 | tf_op jit(solution)/shard_map/ppermute | solution.py:379
  18.1 8.9 %collective-permute-start.1 = (bf16[64,192]{1,0:T(8,128)(2,1)S(1)}, bf16[64,192]{1,0:T(8,128)(2,1)S(1)}, u32[]{:S(2)}, u32[]{:S(2)}) collective-permute-start(bf16[64,192]{1,0:T(8,128)(2,1)S(1)} %reshape.22.refs_0_), channel_id=1, source_target_pairs={{0,32},{16,48},{32,0},{48,16},{1,33},{17,49},{33,1},{49,17},{2,34}... | collective-permute-start | bytes 73736 | tf_op jit(solution)/shard_map/ppermute | solution.py:379
  24.0 4.8 %collective-permute-start = (bf16[64,192]{1,0:T(8,128)(2,1)S(1)}, bf16[64,192]{1,0:T(8,128)(2,1)S(1)}, u32[]{:S(2)}, u32[]{:S(2)}) collective-permute-start(bf16[64,192]{1,0:T(8,128)(2,1)S(1)} %reshape.22.refs_0_), channel_id=1, source_target_pairs={{0,16},{16,32},{32,48},{48,0},{1,17},{17,33},{33,49},{49,1},{2,18}... | collective-permute-start | bytes 73736 | tf_op jit(solution)/shard_map/ppermute | solution.py:379
  35.2 4.2 %collective-permute-start.3 = (bf16[208,128]{1,0:T(8,128)(2,1)S(1)}, bf16[208,128]{1,0:T(8,128)(2,1)S(1)}, u32[]{:S(2)}, u32[]{:S(2)}) collective-permute-start(bf16[208,128]{1,0:T(8,128)(2,1)S(1)} %get-tuple-element.14), channel_id=1, source_target_pairs={{0,8},{8,0},{1,9},{9,1},{2,10},{10,2},{3,11},{11,3},{4,12},{12,4},... | collective-permute-start | bytes 159752 | tf_op jit(solution)/shard_map/ppermute | solution.py:396
  40.3 11.5 %copy-start = (f32[3,3,3,1536]{3,2,1,0:T(4,128)S(1)}, f32[3,3,3,1536]{3,2,1,0:T(4,128)}, u32[]{:S(2)}) copy-start(f32[3,3,3,1536]{3,2,1,0:T(4,128)} %w_ref.1) | copy-start | bytes 497668
  40.3 28.9 %all-to-all-start.2 = ((bf16[8,208,128]{2,1,0:T(8,128)(2,1)}), bf16[8,208,128]{2,1,0:T(8,128)(2,1)S(1)}, u32[]{:S(2)}, u32[]{:S(2)}) async-start(bf16[8,208,128]{2,1,0:T(8,128)(2,1)} %shard_map.49), calls=%async_computation.2 | async-start | bytes 851968 | tf_op jit(solution)/shard_map/all_to_all | solution.py:58
  48.9 3.1 %collective-permute-start.4 = (bf16[192,256]{1,0:T(8,128)(2,1)S(1)}, bf16[192,256]{1,0:T(8,128)(2,1)S(1)}, u32[]{:S(2)}, u32[]{:S(2)}) collective-permute-start(bf16[192,256]{1,0:T(8,128)(2,1)S(1)} %get-tuple-element.17), channel_id=1, source_target_pairs={{0,64},{128,192},{64,0},{192,128},{1,65},{129,193},{65,1},{193,129... | collective-permute-start | bytes 294920 | tf_op jit(solution)/shard_map/ppermute | solution.py:405
  49.0 7.4 %collective-permute-start.5 = (bf16[192,256]{1,0:T(8,128)(2,1)S(1)}, bf16[192,256]{1,0:T(8,128)(2,1)S(1)}, u32[]{:S(2)}, u32[]{:S(2)}) collective-permute-start(bf16[192,256]{1,0:T(8,128)(2,1)S(1)} %get-tuple-element.18), channel_id=1, source_target_pairs={{64,128},{128,64},{65,129},{129,65},{66,130},{130,66},{67,131},{13... | collective-permute-start | bytes 294920 | tf_op jit(solution)/shard_map/ppermute | solution.py:407
  57.4 10.1 %collective-permute-start.6 = (bf16[192,128]{1,0:T(8,128)(2,1)S(1)}, bf16[192,128]{1,0:T(8,128)(2,1)S(1)}, u32[]{:S(2)}, u32[]{:S(2)}) collective-permute-start(bf16[192,128]{1,0:T(8,128)(2,1)S(1)} %get-tuple-element.19), channel_id=1, source_target_pairs={{0,8},{8,16},{16,24},{24,32},{32,40},{40,48},{48,56},{1,9},{9,17},... | collective-permute-start | bytes 147464 | tf_op jit(solution)/shard_map/ppermute | solution.py:64
  61.9 7.2 %collective-permute-start.7 = (bf16[192,128]{1,0:T(8,128)(2,1)S(1)}, bf16[192,128]{1,0:T(8,128)(2,1)S(1)}, u32[]{:S(2)}, u32[]{:S(2)}) collective-permute-start(bf16[192,128]{1,0:T(8,128)(2,1)S(1)} %get-tuple-element.20), channel_id=1, source_target_pairs={{8,0},{16,8},{24,16},{32,24},{40,32},{48,40},{56,48},{9,1},{17,9},... | collective-permute-start | bytes 147464 | tf_op jit(solution)/shard_map/ppermute | solution.py:64

commit v9 on v8

--- a/solution.py
+++ b/solution.py
@@ -24,7 +24,7 @@
 K_ROW = GROUP
 V_ROW = 2 * GROUP
 SENT = 3 * GROUP
-PAIR_AGENTS = 2 * TILES * AGENT_DEV
+PLANE_AGENTS = TILES * AGENT_DEV
 EDGE = TILES * COLUMNS
 STATS = 16
 GRANT = 6 * 1024 * 1024
@@ -62,32 +62,6 @@
     count = PLANES
     pairs = [(i, i + step) for i in range(count) if 0 <= i + step < count]
     return lax.ppermute(x, axis, pairs)
-
-
-def pool_kernel(q_ref, out_ref, came, sems):
-    half = D // 2
-    loads = [
-        pltpu.make_async_copy(
-            q_ref.at[:, pl.ds(n * half, half)], came.at[:, pl.ds(n * half, half)], sems.at[n]
-        )
-        for n in range(2)
-    ]
-    for load in loads:
-        load.start()
-    shape = (8, TOKENS)
-    token = lax.broadcasted_iota(jnp.int32, shape, 1)
-    agent = lax.broadcasted_iota(jnp.int32, shape, 0)
-    width = COLUMNS // AGENT_DEV
-    pick = ((token % COLUMNS) // width == agent).astype(F32).astype(BF16)
-    for n, load in enumerate(loads):
-        load.wait()
-        sums = jnp.dot(pick, came[:, n * half : (n + 1) * half], preferred_element_type=F32)
-        pooled = (sums[:AGENT_DEV] * (1.0 / (FRAMES * width))).astype(BF16)
-        for k in range(TILES // 2):
-            tile = n * (TILES // 2) + k
-            part = pooled[:, k * GROUP : (k + 1) * GROUP]
-            out_ref[tile] = part
-            out_ref[TILES + tile] = part
 
 
 def pack_kernel(q_ref, k_ref, v_ref, out_ref, came, turned, in_sems, out_sems):
@@ -113,18 +87,30 @@
     return jnp.concatenate([x_ref[s, start : start + size, :] for s in range(TILES)], axis=1)
 
 
-def agent_kernel(z_ref, *refs):
-    came, (x_ref, keep_ref, send_ref, a_ref, q_ref) = refs[:PAIRS], refs[PAIRS:]
-    low = z_ref[1] == 0
-    for hop, ref in enumerate(came):
-        z = lax.rem(z_ref[0] + PAIRS - hop, PAIRS)
-        a_ref[pl.ds(pl.multiple_of(z * PAIR_AGENTS, PAIR_AGENTS), PAIR_AGENTS), :] = ref[...]
+def pool_kernel(x_ref, out_ref):
+    shape = (PLANE_AGENTS, TILES * TOKENS)
+    cell = lax.broadcasted_iota(jnp.int32, shape, 1)
+    agent = lax.broadcasted_iota(jnp.int32, shape, 0)
+    width = COLUMNS // AGENT_DEV
+    owner = cell // TOKENS * AGENT_DEV + cell % COLUMNS // width
+    pick = (owner == agent).astype(F32).astype(BF16)
+    sums = lax.dot_general(
+        pick, rows_of(x_ref, 0, GROUP), (((1,), (1,)), ((), ())), preferred_element_type=F32
+    )
+    pooled = (sums * (1.0 / (FRAMES * width))).astype(BF16)
+    for z in range(PLANES):
+        out_ref[z] = pooled
+
+
+def agent_kernel(low_ref, a_ref, x_ref, keep_ref, send_ref):
+    low = low_ref[0] == 1
+    everyone = a_ref[...].reshape(AGENTS, GROUP)
     columns = []
     logs = []
     for h in range(GROUP_HEADS):
         keys = rows_of(x_ref, K_ROW + h * HEAD_DIM, HEAD_DIM)
         values = rows_of(x_ref, V_ROW + h * HEAD_DIM, HEAD_DIM)
-        agents = a_ref[:, h * HEAD_DIM : (h + 1) * HEAD_DIM]
+        agents = everyone[:, h * HEAD_DIM : (h + 1) * HEAD_DIM]
         scores = jnp.dot(agents, keys, preferred_element_type=F32) * INV_ROOT
         peak = jnp.max(scores, axis=1, keepdims=True)
         weights = jnp.exp(scores - peak)
@@ -144,7 +130,6 @@
     away = jnp.where(low, far, near)
     send_ref[:GROUP] = away[:GROUP].astype(BF16)
     send_ref[GROUP:] = pieces_of(away[GROUP : GROUP + GROUP_HEADS])
-    q_ref[...] = rows_of(x_ref, 0, GROUP)
 
 
 def pieces_of(logs):
@@ -173,11 +158,26 @@
     for h in range(GROUP_HEADS):
         rows = slice(h * HEAD_DIM, (h + 1) * HEAD_DIM)
         part = keep_ref[rows, :] * left[h : h + 1] + came_ref[rows, :].astype(F32) * right[h : h + 1]
-        part = part.astype(BF16)
-        for z in range(PLANES):
-            out_ref[z, rows, :] = part
-    for z in range(PLANES):
-        out_ref[z, GROUP:, :] = stats
+        out_ref[rows, :] = part.astype(BF16)
+    out_ref[GROUP:, :] = stats
+
+
+def comb_kernel(*refs):
+    parts, out_ref = refs[:-1], refs[-1]
+    logs = [logs_of(part[GROUP:, :]) for part in parts]
+    peak = logs[0]
+    for log in logs[1:]:
+        peak = jnp.maximum(peak, log)
+    shares = [jnp.exp(log - peak) for log in logs]
+    whole = sum(shares[1:], shares[0])
+    shares = [share / whole for share in shares]
+    for h in range(GROUP_HEADS):
+        rows = slice(h * HEAD_DIM, (h + 1) * HEAD_DIM)
+        terms = [
+            part[rows, :].astype(F32) * share[h : h + 1]
+            for part, share in zip(parts, shares, strict=True)
+        ]
+        out_ref[rows, :] = sum(terms[1:], terms[0]).astype(BF16)
 
 
 def taps_kernel(tile_ref, w_ref, out_ref):
@@ -191,7 +191,8 @@
             out_ref[...] = jnp.concatenate(rows, axis=0).T
 
 
-def edge_kernel(even_ref, x_ref, near_ref, far_ref):
+def edge_kernel(even_ref, x_ref, near_ref, far_ref, q_ref):
+    q_ref[...] = rows_of(x_ref, 0, GROUP)
     spot = lax.broadcasted_iota(jnp.int32, (GROUP, TOKENS), 1) // COLUMNS
     for block in range(EDGE // TOKENS):
         last = first = jnp.zeros((GROUP, TOKENS), F32)
@@ -294,30 +295,19 @@
     lax.fori_loop(0, GROUP // TALL, step, 0)
 
 
-def mix_kernel(parts_ref, a_ref, q_ref, local_ref, up_ref, down_ref, out_ref):
-    shares = []
-    for half in range(2):
-        logs = [logs_of(parts_ref[z, GROUP:, :]) for z in range(half, PLANES, 2)]
-        peak = logs[0]
-        for log in logs[1:]:
-            peak = jnp.maximum(peak, log)
-        some = [jnp.exp(log - peak) for log in logs]
-        whole = sum(some[1:], some[0])
-        shares.append([share / whole for share in some])
+def mix_kernel(low_ref, a_ref, q_ref, ours_ref, theirs_ref, local_ref, up_ref, down_ref, out_ref):
+    low = low_ref[0] == 1
+    agents = a_ref[...].reshape(AGENTS, GROUP)
+    ours, theirs = ours_ref[...], theirs_ref[...]
+    values = jnp.concatenate(
+        [jnp.where(low, ours, theirs), jnp.where(low, theirs, ours)], axis=1
+    )
     for h in range(GROUP_HEADS):
         rows = slice(h * HEAD_DIM, (h + 1) * HEAD_DIM)
-        halves = []
-        for half in range(2):
-            terms = [
-                parts_ref[z, rows, :].astype(F32) * shares[half][z // 2][h : h + 1]
-                for z in range(half, PLANES, 2)
-            ]
-            halves.append(sum(terms[1:], terms[0]))
-        values = jnp.concatenate(halves, axis=1)
-        scores = jnp.dot(a_ref[:, rows], q_ref[rows, :], preferred_element_type=F32) * INV_ROOT
+        scores = jnp.dot(agents[:, rows], q_ref[rows, :], preferred_element_type=F32) * INV_ROOT
         weights = jnp.exp(scores - jnp.max(scores, axis=0, keepdims=True))
         total = jnp.sum(weights, axis=0, keepdims=True)
-        mixed = jnp.dot(values.astype(BF16), weights.astype(BF16), preferred_element_type=F32) / total
+        mixed = jnp.dot(values[rows], weights.astype(BF16), preferred_element_type=F32) / total
         for s in range(TILES):
             cells = mixed[:, s * TOKENS : (s + 1) * TOKENS] + local_ref[s, rows, :]
             if s == 0:
@@ -348,14 +338,6 @@
     k = key_states.reshape(TOKENS, D)
     v = value_states.reshape(TOKENS, D)
     shape = jax.ShapeDtypeStruct
-    pooled = call(
-        pool_kernel,
-        shape((2 * TILES, AGENT_DEV, GROUP), BF16),
-        1.0,
-        q,
-        scratch=(pltpu.VMEM((TOKENS, D), BF16), pltpu.SemaphoreType.DMA((2,))),
-        far=True,
-    )
     packed = call(
         pack_kernel,
         shape((TILES, SENT, TOKENS), BF16),
@@ -372,56 +354,58 @@
         far=True,
         far_out=True,
     )
-    own = exchange(pooled, ("zl", "xy")).reshape(PAIR_AGENTS, GROUP)
     x = exchange(packed, "xy")
-    came = [own]
-    for n in range(1, PAIRS):
-        came.append(lax.ppermute(own, "zh", [(i, (i + n) % PAIRS) for i in range(PAIRS)]))
     tile = scalar(lax.axis_index("xy"))
     taps = call(taps_kernel, shape((GROUP, 32), F32), 1.0, conv_weight, scalars=(tile,))
 
-    keep, send, agents, turned_q = call(
-        agent_kernel,
-        (
-            shape((GROUP + 8, HALF), F32),
-            shape((GROUP + STATS, HALF), BF16),
-            shape((AGENTS, GROUP), BF16),
-            shape((GROUP, TILES * TOKENS), BF16),
-        ),
-        3.0,
-        *came,
-        x,
-        scalars=(jnp.stack([lax.axis_index("zh"), lax.axis_index("zl")]).astype(jnp.int32),),
-    )
-    theirs = lax.ppermute(send, "zl", [(0, 1), (1, 0)])
-    blended = call(blend_kernel, shape((PLANES, GROUP + STATS, HALF), BF16), 1.0, keep, theirs)
-    parts = exchange(blended, ("zh", "zl"))
-
+    low = scalar(1 - lax.axis_index("zl"))
+    even = scalar(1 - lax.axis_index("tm") % 2)
+    pooled = call(pool_kernel, shape((PLANES, PLANE_AGENTS, GROUP), BF16), 1.0, x)
+    agents = exchange(pooled, ("zh", "zl"))
     edges = shape((GROUP, EDGE), BF16)
-    even = scalar(1 - lax.axis_index("tm") % 2)
-    near, far = call(edge_kernel, (edges, edges), 1.0, x, scalars=(even,))
+    near, far, turned_q = call(
+        edge_kernel, (edges, edges, shape((GROUP, TILES * TOKENS), BF16)), 1.0, x, scalars=(even,)
+    )
     groups = lax.axis_size("tm")
     pairs = [(i, i + 1) for i in range(0, groups - 1, 2)]
     near = lax.ppermute(near, "tm", pairs + [(b, a) for a, b in pairs])
     pairs = [(i, i + 1) for i in range(1, groups - 1, 2)]
     far = lax.ppermute(far, "tm", pairs + [(b, a) for a, b in pairs])
+    keep, send = call(
+        agent_kernel,
+        (shape((GROUP + 8, HALF), F32), shape((GROUP + STATS, HALF), BF16)),
+        3.0,
+        agents,
+        x,
+        scalars=(low,),
+    )
+    swap = [(0, 1), (1, 0)]
+    theirs = lax.ppermute(send, "zl", swap)
     row = shape((GROUP, TOKENS), BF16)
     to_next, to_last = call(rim_kernel, (row, row), 1.0, x, near, far, taps, scalars=(even,))
     up = shift(to_next, ("zh", "zl"), 1)
     down = shift(to_last, ("zh", "zl"), -1)
+    blended = call(blend_kernel, shape((GROUP + STATS, HALF), BF16), 1.0, keep, theirs)
+    parts = [blended]
+    for n in range(1, PAIRS):
+        parts.append(lax.ppermute(blended, "zh", [(i, (i + n) % PAIRS) for i in range(PAIRS)]))
     local = call(
         conv_kernel, shape((TILES, GROUP, TOKENS), F32), 5.0, x, near, far, taps, scalars=(even,)
     )
+    ours = call(comb_kernel, shape((GROUP, HALF), BF16), 1.0, *parts)
+    theirs = lax.ppermute(ours, "zl", swap)
     mixed = call(
         mix_kernel,
         shape((TILES, GROUP, TOKENS), BF16),
         1.0,
-        parts,
         agents,
         turned_q,
+        ours,
+        theirs,
         local,
         up,
         down,
+        scalars=(low,),
     )
     mine = exchange(mixed, "xy")
     pieces = TILES // 2

time: 83.5 us -> 80.8 us (0.968)
  the two profiles are of different devices: /device:TPU:100 before, /device:TPU:96 now
where the time goes in v9:
time: 80.8 us; the launch traced here: 79.5 us
  blocking collectives  33.8 us (42%)
  starting transfers between devices  24.5 us (30%)
  Pallas kernels  12.5 us (15%)
  waiting for transfers between devices  8.46 us (10%)
    all_to_all x2, blocking collectives, exchange(): return lax.all_to_all(x, axes, 0, 0)  33.8 us
    pallas_call x11, Pallas kernels, call(): pl.pallas_call(kernel, out_shape=out_shape, in_specs=[SMEM] * len(scalars...  12.5 us
    ppermute x2, starting transfers between devices, shift(): return lax.ppermute(x, axis, pairs)  7.96 us
    all_to_all x1, starting transfers between devices, exchange(): return lax.all_to_all(x, axes, 0, 0)  7.66 us
    ppermute x3, starting transfers between devices, body(): lax.ppermute(blended, 'zh', [(i, (i + n) % PAIRS) for i in range(PAIRS)])  6.36 us
    all_to_all x1, waiting for transfers between devices, exchange(): return lax.all_to_all(x, axes, 0, 0)  5.48 us
    ppermute x1, starting transfers between devices, body(): theirs = lax.ppermute(send, 'zl', swap)  1.72 us
  transfers between devices with their start and end apart: 10, of which 3 were waited for; matrix products, arithmetic and copies ran while one was open for 0% of the time, Pallas kernels for 6%

profile of v9, /device:TPU:96, one launch (start us, length us, event | category | flops | bytes accessed | tf_op | source)
XLA Modules:
  0.0 79.5 jit_solution(2327998019482689240)
XLA Ops:
  0.0 2.3 %shard_map.46 = bf16[8,576,128]{2,1,0:T(8,128)(2,1)} custom-call(bf16[128,1536]{1,0:T(8,128)(2,1)} %bitcast.9, bf16[128,1536]{1,0:T(8,128)(2,1)} %bitcast.10, bf16[128,1536]{1,0:T(8,128)(2,1)} %bitcast.11), custom_call_target="tpu_custom_call" | custom-call | flops 900000000 | bytes 6000000 | tf_op jit(solution)/shard_map/pallas_call | solution.py:46
  2.3 22.6 %all_to_all.15.x_ref = bf16[8,576,128]{2,1,0:T(8,128)(2,1)S(1)} all-to-all(bf16[8,576,128]{2,1,0:T(8,128)(2,1)} %shard_map.46), channel_id=1, replica_groups=mesh['tm'=4,'zh'=4,'zl'=2,'xy'=8] {'xy'}, dimensions={0} | all-to-all | bytes 2359296 | tf_op jit(solution)/shard_map/all_to_all | solution.py:58
  24.9 0.9 %shard_map.47 = bf16[8,32,192]{2,1,0:T(8,128)(2,1)} custom-call(bf16[8,576,128]{2,1,0:T(8,128)(2,1)S(1)} %all_to_all.15.x_ref), custom_call_target="tpu_custom_call" | custom-call | flops 300000000 | bytes 2000000 | tf_op jit(solution)/shard_map/pallas_call | solution.py:46
  25.8 7.7 %all-to-all-start.1 = ((bf16[8,32,192]{2,1,0:T(8,128)(2,1)}), bf16[8,32,192]{2,1,0:T(8,128)(2,1)S(1)}, u32[]{:S(2)}, u32[]{:S(2)}) async-start(bf16[8,32,192]{2,1,0:T(8,128)(2,1)} %shard_map.47), calls=%async_computation.1 | async-start | bytes 262144 | tf_op jit(solution)/shard_map/all_to_all | solution.py:58
  33.5 5.5 %all-to-all-done.1.a_ref = bf16[8,32,192]{2,1,0:T(8,128)(2,1)S(1)} async-done(((bf16[8,32,192]{2,1,0:T(8,128)(2,1)}), bf16[8,32,192]{2,1,0:T(8,128)(2,1)S(1)}, u32[]{:S(2)}, u32[]{:S(2)}) %all-to-all-start.1) | async-done | bytes 98336 | tf_op jit(solution)/shard_map/all_to_all | solution.py:58
  39.0 1.8 %shard_map.49 = (f32[200,128]{1,0:T(8,128)S(1)}, bf16[208,128]{1,0:T(8,128)(2,1)S(1)}) custom-call(s32[1]{0:T(128)} %bitcast.low_ref, bf16[8,32,192]{2,1,0:T(8,128)(2,1)S(1)} %all-to-all-done.1.a_ref, bf16[8,576,128]{2,1,0:T(8,128)(2,1)S(1)} %all_to_all.15.x_ref), custom_call_target="tpu_custom_call" | custom-call | flops 900000000 | bytes 6000000 | tf_op jit(solution)/shard_map/pallas_call | solution.py:46
  40.7 1.7 %collective-permute-start = (bf16[208,128]{1,0:T(8,128)(2,1)S(1)}, bf16[208,128]{1,0:T(8,128)(2,1)S(1)}, u32[]{:S(2)}, u32[]{:S(2)}) collective-permute-start(bf16[208,128]{1,0:T(8,128)(2,1)S(1)} %get-tuple-element.14), channel_id=1, source_target_pairs={{0,8},{8,0},{1,9},{9,1},{2,10},{10,2},{3,11},{11,3},{4,12},{12,4},... | collective-permute-start | bytes 159752 | tf_op jit(solution)/shard_map/ppermute | solution.py:383
  42.5 0.3 shard_map.48
  42.8 0.1 collective-permute-start.5
  42.9 0.7 collective-permute-start.6
  43.6 1.4 %collective-permute-done.came_ref = bf16[208,128]{1,0:T(8,128)(2,1)S(1)} collective-permute-done((bf16[208,128]{1,0:T(8,128)(2,1)S(1)}, bf16[208,128]{1,0:T(8,128)(2,1)S(1)}, u32[]{:S(2)}, u32[]{:S(2)}) %collective-permute-start) | collective-permute-done | bytes 53280 | tf_op jit(solution)/shard_map/ppermute | solution.py:383
  45.0 1.5 %collective-permute-start.1 = (bf16[208,128]{1,0:T(8,128)(2,1)S(1)}, bf16[208,128]{1,0:T(8,128)(2,1)S(1)}, u32[]{:S(2)}, u32[]{:S(2)}) collective-permute-start(bf16[208,128]{1,0:T(8,128)(2,1)S(1)} %shard_map.50.refs_0_), channel_id=1, source_target_pairs={{0,16},{16,32},{32,48},{48,0},{1,17},{17,33},{33,49},{49,1},{2,18}... | collective-permute-start | bytes 159752 | tf_op jit(solution)/shard_map/ppermute | solution.py:391
  46.5 4.8 %collective-permute-start.2 = (bf16[208,128]{1,0:T(8,128)(2,1)S(1)}, bf16[208,128]{1,0:T(8,128)(2,1)S(1)}, u32[]{:S(2)}, u32[]{:S(2)}) collective-permute-start(bf16[208,128]{1,0:T(8,128)(2,1)S(1)} %shard_map.50.refs_0_), channel_id=1, source_target_pairs={{0,32},{16,48},{32,0},{48,16},{1,33},{17,49},{33,1},{49,17},{2,34}... | collective-permute-start | bytes 159752 | tf_op jit(solution)/shard_map/ppermute | solution.py:391
  51.4 0.1 shard_map.52.w_ref
  51.5 0.9 %shard_map.54 = (bf16[192,128]{1,0:T(8,128)(2,1)S(1)}, bf16[192,128]{1,0:T(8,128)(2,1)S(1)}) custom-call(s32[1]{0:T(128)} %bitcast.4.even_ref, bf16[8,576,128]{2,1,0:T(8,128)(2,1)S(1)} %all_to_all.15.x_ref, bf16[192,256]{1,0:T(8,128)(2,1)S(1)} %collective-permute-done.5.near_ref, bf16[192,256]{1,0:T(8,128)(2,1)S(1)} %collective-permute-done.6.far_ref, ...), custom_call_target="tpu_custom_call" | custom-call | flops 300000000 | bytes 2000000 | tf_op jit(solution)/shard_map/pallas_call | solution.py:46
  52.5 6.0 %collective-permute-start.7 = (bf16[192,128]{1,0:T(8,128)(2,1)S(1)}, bf16[192,128]{1,0:T(8,128)(2,1)S(1)}, u32[]{:S(2)}, u32[]{:S(2)}) collective-permute-start(bf16[192,128]{1,0:T(8,128)(2,1)S(1)} %get-tuple-element.17), channel_id=1, source_target_pairs={{0,8},{8,16},{16,24},{24,32},{32,40},{40,48},{48,56},{1,9},{9,17},... | collective-permute-start | bytes 147464 | tf_op jit(solution)/shard_map/ppermute | solution.py:64
  58.5 1.9 %collective-permute-start.8 = (bf16[192,128]{1,0:T(8,128)(2,1)S(1)}, bf16[192,128]{1,0:T(8,128)(2,1)S(1)}, u32[]{:S(2)}, u32[]{:S(2)}) collective-permute-start(bf16[192,128]{1,0:T(8,128)(2,1)S(1)} %get-tuple-element.18), channel_id=1, source_target_pairs={{8,0},{16,8},{24,16},{32,24},{40,32},{48,40},{56,48},{9,1},{17,9},... | collective-permute-start | bytes 147464 | tf_op jit(solution)/shard_map/ppermute | solution.py:64
  60.5 0.1 shard_map.51.ours_ref
  60.6 0.1 collective-permute-start.4
  60.7 3.5 %shard_map.53.local_ref = f32[8,192,128]{2,1,0:T(8,128)S(1)} custom-call(s32[1]{0:T(128)} %bitcast.4.even_ref, bf16[8,576,128]{2,1,0:T(8,128)(2,1)S(1)} %all_to_all.15.x_ref, bf16[192,256]{1,0:T(8,128)(2,1)S(1)} %collective-permute-done.5.near_ref, bf16[192,256]{1,0:T(8,128)(2,1)S(1)} %collective-permute-done.6.far_ref, f32[192,32]{1,0:T(8,128)S(1)} %shard_map.52.w_ref), custom_call_target="tpu_custom_call" | custom-call | flops 1500000000 | bytes 10000000 | tf_op jit(solution)/shard_map/pallas_call | solution.py:46
  64.2 1.6 %collective-permute-done.8.down_ref = bf16[192,128]{1,0:T(8,128)(2,1)S(1)} collective-permute-done((bf16[192,128]{1,0:T(8,128)(2,1)S(1)}, bf16[192,128]{1,0:T(8,128)(2,1)S(1)}, u32[]{:S(2)}, u32[]{:S(2)}) %collective-permute-start.8) | collective-permute-done | bytes 49184 | tf_op jit(solution)/shard_map/ppermute | solution.py:64
  65.8 1.6 %shard_map.55 = bf16[8,192,128]{2,1,0:T(8,128)(2,1)S(1)} custom-call(s32[1]{0:T(128)} %bitcast.low_ref, bf16[8,32,192]{2,1,0:T(8,128)(2,1)S(1)} %all-to-all-done.1.a_ref, bf16[192,1024]{1,0:T(8,128)(2,1)S(1)} %get-tuple-element.12.q_ref, bf16[192,128]{1,0:T(8,128)(2,1)S(1)} %shard_map.51.ours_ref, bf16[192,128]{1,0:T(8,128)(2,1)S(1)} %collective-permute-done.4.theirs_ref, ...), custom_call_target="tpu_custom_call" | custom-call | flops 300000000 | bytes 2000000 | tf_op jit(solution)/shard_map/pallas_call | solution.py:46
  67.4 11.2 %all_to_all.16.x_ref = bf16[8,192,128]{2,1,0:T(8,128)(2,1)S(1)} all-to-all(bf16[8,192,128]{2,1,0:T(8,128)(2,1)S(1)} %shard_map.55), channel_id=1, replica_groups=mesh['tm'=4,'zh'=4,'zl'=2,'xy'=8] {'xy'}, dimensions={0} | all-to-all | bytes 786432 | tf_op jit(solution)/shard_map/all_to_all | solution.py:58
  78.6 0.9 %shard_map.56 = bf16[128,1536]{1,0:T(8,128)(2,1)} custom-call(bf16[8,192,128]{2,1,0:T(8,128)(2,1)S(1)} %all_to_all.16.x_ref), custom_call_target="tpu_custom_call" | custom-call | flops 300000000 | bytes 2000000 | tf_op jit(solution)/shard_map/pallas_call | solution.py:46
  (11 shorter events, 0.1 us)
Async XLA Ops:
  25.8 13.1 %all-to-all-start.1 = ((bf16[8,32,192]{2,1,0:T(8,128)(2,1)}), bf16[8,32,192]{2,1,0:T(8,128)(2,1)S(1)}, u32[]{:S(2)}, u32[]{:S(2)}) async-start(bf16[8,32,192]{2,1,0:T(8,128)(2,1)} %shard_map.47), calls=%async_computation.1 | async-start | bytes 262144 | tf_op jit(solution)/shard_map/all_to_all | solution.py:58
  40.7 10.6 %copy-start = (f32[3,3,3,1536]{3,2,1,0:T(4,128)S(1)}, f32[3,3,3,1536]{3,2,1,0:T(4,128)}, u32[]{:S(2)}) copy-start(f32[3,3,3,1536]{3,2,1,0:T(4,128)} %w_ref.1) | copy-start | bytes 497668
  40.7 4.2 %collective-permute-start = (bf16[208,128]{1,0:T(8,128)(2,1)S(1)}, bf16[208,128]{1,0:T(8,128)(2,1)S(1)}, u32[]{:S(2)}, u32[]{:S(2)}) collective-permute-start(bf16[208,128]{1,0:T(8,128)(2,1)S(1)} %get-tuple-element.14), channel_id=1, source_target_pairs={{0,8},{8,0},{1,9},{9,1},{2,10},{10,2},{3,11},{11,3},{4,12},{12,4},... | collective-permute-start | bytes 159752 | tf_op jit(solution)/shard_map/ppermute | solution.py:383
  42.8 8.7 %collective-permute-start.5 = (bf16[192,256]{1,0:T(8,128)(2,1)S(1)}, bf16[192,256]{1,0:T(8,128)(2,1)S(1)}, u32[]{:S(2)}, u32[]{:S(2)}) collective-permute-start(bf16[192,256]{1,0:T(8,128)(2,1)S(1)} %get-tuple-element.15), channel_id=1, source_target_pairs={{0,64},{128,192},{64,0},{192,128},{1,65},{129,193},{65,1},{193,129... | collective-permute-start | bytes 294920 | tf_op jit(solution)/shard_map/ppermute | solution.py:371
  42.9 8.6 %collective-permute-start.6 = (bf16[192,256]{1,0:T(8,128)(2,1)S(1)}, bf16[192,256]{1,0:T(8,128)(2,1)S(1)}, u32[]{:S(2)}, u32[]{:S(2)}) collective-permute-start(bf16[192,256]{1,0:T(8,128)(2,1)S(1)} %get-tuple-element.16), channel_id=1, source_target_pairs={{64,128},{128,64},{65,129},{129,65},{66,130},{130,66},{67,131},{13... | collective-permute-start | bytes 294920 | tf_op jit(solution)/shard_map/ppermute | solution.py:373
  45.0 15.5 %collective-permute-start.1 = (bf16[208,128]{1,0:T(8,128)(2,1)S(1)}, bf16[208,128]{1,0:T(8,128)(2,1)S(1)}, u32[]{:S(2)}, u32[]{:S(2)}) collective-permute-start(bf16[208,128]{1,0:T(8,128)(2,1)S(1)} %shard_map.50.refs_0_), channel_id=1, source_target_pairs={{0,16},{16,32},{32,48},{48,0},{1,17},{17,33},{33,49},{49,1},{2,18}... | collective-permute-start | bytes 159752 | tf_op jit(solution)/shard_map/ppermute | solution.py:391
  46.5 14.0 %collective-permute-start.2 = (bf16[208,128]{1,0:T(8,128)(2,1)S(1)}, bf16[208,128]{1,0:T(8,128)(2,1)S(1)}, u32[]{:S(2)}, u32[]{:S(2)}) collective-permute-start(bf16[208,128]{1,0:T(8,128)(2,1)S(1)} %shard_map.50.refs_0_), channel_id=1, source_target_pairs={{0,32},{16,48},{32,0},{48,16},{1,33},{17,49},{33,1},{49,17},{2,34}... | collective-permute-start | bytes 159752 | tf_op jit(solution)/shard_map/ppermute | solution.py:391
  51.4 9.1 %collective-permute-start.3 = (bf16[208,128]{1,0:T(8,128)(2,1)S(1)}, bf16[208,128]{1,0:T(8,128)(2,1)S(1)}, u32[]{:S(2)}, u32[]{:S(2)}) collective-permute-start(bf16[208,128]{1,0:T(8,128)(2,1)S(1)} %shard_map.50.refs_0_), channel_id=1, source_target_pairs={{0,48},{16,0},{32,16},{48,32},{1,49},{17,1},{33,17},{49,33},{2,50}... | collective-permute-start | bytes 159752 | tf_op jit(solution)/shard_map/ppermute | solution.py:391
  52.5 11.7 %collective-permute-start.7 = (bf16[192,128]{1,0:T(8,128)(2,1)S(1)}, bf16[192,128]{1,0:T(8,128)(2,1)S(1)}, u32[]{:S(2)}, u32[]{:S(2)}) collective-permute-start(bf16[192,128]{1,0:T(8,128)(2,1)S(1)} %get-tuple-element.17), channel_id=1, source_target_pairs={{0,8},{8,16},{16,24},{24,32},{32,40},{40,48},{48,56},{1,9},{9,17},... | collective-permute-start | bytes 147464 | tf_op jit(solution)/shard_map/ppermute | solution.py:64
  58.5 7.3 %collective-permute-start.8 = (bf16[192,128]{1,0:T(8,128)(2,1)S(1)}, bf16[192,128]{1,0:T(8,128)(2,1)S(1)}, u32[]{:S(2)}, u32[]{:S(2)}) collective-permute-start(bf16[192,128]{1,0:T(8,128)(2,1)S(1)} %get-tuple-element.18), channel_id=1, source_target_pairs={{8,0},{16,8},{24,16},{32,24},{40,32},{48,40},{56,48},{9,1},{17,9},... | collective-permute-start | bytes 147464 | tf_op jit(solution)/shard_map/ppermute | solution.py:64
  60.6 5.3 %collective-permute-start.4 = (bf16[192,128]{1,0:T(8,128)(2,1)S(1)}, bf16[192,128]{1,0:T(8,128)(2,1)S(1)}, u32[]{:S(2)}, u32[]{:S(2)}) collective-permute-start(bf16[192,128]{1,0:T(8,128)(2,1)S(1)} %shard_map.51.ours_ref), channel_id=1, source_target_pairs={{0,8},{8,0},{1,9},{9,1},{2,10},{10,2},{3,11},{11,3},{4,12},{12,4},... | collective-permute-start | bytes 147464 | tf_op jit(solution)/shard_map/ppermute | solution.py:396

commit v10 on v9

--- a/solution.py
+++ b/solution.py
@@ -58,12 +58,6 @@
     return lax.all_to_all(x, axes, 0, 0)
 
 
-def shift(x, axis, step):
-    count = PLANES
-    pairs = [(i, i + step) for i in range(count) if 0 <= i + step < count]
-    return lax.ppermute(x, axis, pairs)
-
-
 def pack_kernel(q_ref, k_ref, v_ref, out_ref, came, turned, in_sems, out_sems):
     refs = (q_ref, k_ref, v_ref)
     loads = [pltpu.make_async_copy(ref, came.at[n], in_sems.at[n]) for n, ref in enumerate(refs)]
@@ -102,8 +96,8 @@
         out_ref[z] = pooled
 
 
-def agent_kernel(low_ref, a_ref, x_ref, keep_ref, send_ref):
-    low = low_ref[0] == 1
+def agent_kernel(flags_ref, a_ref, x_ref, keep_ref, send_ref):
+    low = flags_ref[1] == 1
     everyone = a_ref[...].reshape(AGENTS, GROUP)
     columns = []
     logs = []
@@ -148,7 +142,7 @@
     return pieces[:n] + pieces[n : 2 * n] + pieces[2 * n : 3 * n]
 
 
-def blend_kernel(keep_ref, came_ref, out_ref):
+def blend_kernel(keep_ref, came_ref, cross_ref, out_ref, long_ref):
     ours, theirs = keep_ref[GROUP : GROUP + GROUP_HEADS, :], logs_of(came_ref[GROUP:, :])
     peak = jnp.maximum(ours, theirs)
     left, right = jnp.exp(ours - peak), jnp.exp(theirs - peak)
@@ -158,13 +152,18 @@
     for h in range(GROUP_HEADS):
         rows = slice(h * HEAD_DIM, (h + 1) * HEAD_DIM)
         part = keep_ref[rows, :] * left[h : h + 1] + came_ref[rows, :].astype(F32) * right[h : h + 1]
-        out_ref[rows, :] = part.astype(BF16)
+        part = part.astype(BF16)
+        out_ref[rows, :] = part
+        long_ref[rows, :] = part
     out_ref[GROUP:, :] = stats
+    long_ref[GROUP : GROUP + STATS, :] = stats
+    long_ref[GROUP + STATS :, :] = cross_ref[...]
 
 
 def comb_kernel(*refs):
-    parts, out_ref = refs[:-1], refs[-1]
-    logs = [logs_of(part[GROUP:, :]) for part in parts]
+    parts, (kin_ref, out_ref) = refs[:PAIRS], refs[PAIRS:]
+    out_ref[GROUP:, :] = kin_ref[...]
+    logs = [logs_of(part[GROUP : GROUP + STATS, :]) for part in parts]
     peak = logs[0]
     for log in logs[1:]:
         peak = jnp.maximum(peak, log)
@@ -191,7 +190,7 @@
             out_ref[...] = jnp.concatenate(rows, axis=0).T
 
 
-def edge_kernel(even_ref, x_ref, near_ref, far_ref, q_ref):
+def edge_kernel(flags_ref, x_ref, near_ref, far_ref, q_ref):
     q_ref[...] = rows_of(x_ref, 0, GROUP)
     spot = lax.broadcasted_iota(jnp.int32, (GROUP, TOKENS), 1) // COLUMNS
     for block in range(EDGE // TOKENS):
@@ -205,12 +204,12 @@
         lanes = slice(block * TOKENS, (block + 1) * TOKENS)
         last, first = last.astype(BF16), first.astype(BF16)
 
-        @pl.when(even_ref[0] == 1)
+        @pl.when(flags_ref[0] == 1)
         def _(last=last, first=first, lanes=lanes):
             near_ref[:, lanes] = last
             far_ref[:, lanes] = first
 
-        @pl.when(even_ref[0] != 1)
+        @pl.when(flags_ref[0] != 1)
         def _(last=last, first=first, lanes=lanes):
             near_ref[:, lanes] = first
             far_ref[:, lanes] = last
@@ -267,18 +266,20 @@
     return left + sums[1] + right
 
 
-def rim_kernel(even_ref, x_ref, near_ref, far_ref, w_ref, up_ref, down_ref):
-    even = even_ref[0] == 1
+def rim_kernel(flags_ref, x_ref, near_ref, far_ref, w_ref, cross_ref, kin_ref):
+    even, second = flags_ref[0] == 1, flags_ref[2] == 1
     tall = GROUP // 2
     for at in range(0, GROUP, tall):
-        for r, j, ref in ((TILES - 1, 0, up_ref), (0, 2, down_ref)):
+        sums = []
+        for r, j in ((TILES - 1, 0), (0, 2)):
             frames = frames_of(r, at, even, x_ref, near_ref, far_ref, tall)
-            taps = taps_of(w_ref, at, (j,), tall)
-            ref[pl.ds(at, tall), :] = stencil({j: frames}, taps).astype(BF16)
-
-
-def conv_kernel(even_ref, x_ref, near_ref, far_ref, w_ref, out_ref):
-    even = even_ref[0] == 1
+            sums.append(stencil({j: frames}, taps_of(w_ref, at, (j,), tall)).astype(BF16))
+        cross_ref[pl.ds(at, tall), :] = jnp.where(second, sums[0], sums[1])
+        kin_ref[pl.ds(at, tall), :] = jnp.where(second, sums[1], sums[0])
+
+
+def conv_kernel(flags_ref, x_ref, near_ref, far_ref, w_ref, out_ref):
+    even = flags_ref[0] == 1
 
     def step(n, carry):
         at = pl.multiple_of(n * TALL, TALL)
@@ -295,25 +296,38 @@
     lax.fori_loop(0, GROUP // TALL, step, 0)
 
 
-def mix_kernel(low_ref, a_ref, q_ref, ours_ref, theirs_ref, local_ref, up_ref, down_ref, out_ref):
-    low = low_ref[0] == 1
+def query_kernel(a_ref, q_ref, e_ref, total_ref):
     agents = a_ref[...].reshape(AGENTS, GROUP)
-    ours, theirs = ours_ref[...], theirs_ref[...]
-    values = jnp.concatenate(
-        [jnp.where(low, ours, theirs), jnp.where(low, theirs, ours)], axis=1
-    )
     for h in range(GROUP_HEADS):
         rows = slice(h * HEAD_DIM, (h + 1) * HEAD_DIM)
         scores = jnp.dot(agents[:, rows], q_ref[rows, :], preferred_element_type=F32) * INV_ROOT
         weights = jnp.exp(scores - jnp.max(scores, axis=0, keepdims=True))
-        total = jnp.sum(weights, axis=0, keepdims=True)
-        mixed = jnp.dot(values[rows], weights.astype(BF16), preferred_element_type=F32) / total
+        total_ref[h : h + 1, :] = jnp.sum(weights, axis=0, keepdims=True)
+        e_ref[h] = weights.astype(BF16)
+
+
+def mix_kernel(flags_ref, e_ref, total_ref, ours_ref, theirs_ref, one_ref, three_ref, local_ref, out_ref):
+    low, second = flags_ref[1] == 1, flags_ref[2] == 1
+    first, last = flags_ref[3] == 1, flags_ref[4] == 1
+    ours, theirs = ours_ref[:GROUP], theirs_ref[:GROUP]
+    values = jnp.concatenate(
+        [jnp.where(low, ours, theirs), jnp.where(low, theirs, ours)], axis=1
+    )
+    kin = theirs_ref[GROUP:].astype(F32)
+    below = three_ref[GROUP + STATS :].astype(F32)
+    above = one_ref[GROUP + STATS :].astype(F32)
+    above = jnp.where(first, 0.0, jnp.where(second, kin, above))
+    below = jnp.where(last, 0.0, jnp.where(second, below, kin))
+    for h in range(GROUP_HEADS):
+        rows = slice(h * HEAD_DIM, (h + 1) * HEAD_DIM)
+        mixed = jnp.dot(values[rows], e_ref[h], preferred_element_type=F32)
+        mixed = mixed / total_ref[h : h + 1, :]
         for s in range(TILES):
             cells = mixed[:, s * TOKENS : (s + 1) * TOKENS] + local_ref[s, rows, :]
             if s == 0:
-                cells += up_ref[rows, :].astype(F32)
+                cells += above[rows]
             if s == TILES - 1:
-                cells += down_ref[rows, :].astype(F32)
+                cells += below[rows]
             out_ref[s, rows, :] = cells.astype(BF16)
 
 
@@ -358,13 +372,22 @@
     tile = scalar(lax.axis_index("xy"))
     taps = call(taps_kernel, shape((GROUP, 32), F32), 1.0, conv_weight, scalars=(tile,))
 
-    low = scalar(1 - lax.axis_index("zl"))
-    even = scalar(1 - lax.axis_index("tm") % 2)
+    high, second = lax.axis_index("zh"), lax.axis_index("zl")
+    plane = 2 * high + second
+    flags = jnp.stack(
+        [
+            1 - lax.axis_index("tm") % 2,
+            1 - (high + second) % 2,
+            second,
+            plane == 0,
+            plane == PLANES - 1,
+        ]
+    ).astype(jnp.int32)
     pooled = call(pool_kernel, shape((PLANES, PLANE_AGENTS, GROUP), BF16), 1.0, x)
     agents = exchange(pooled, ("zh", "zl"))
     edges = shape((GROUP, EDGE), BF16)
     near, far, turned_q = call(
-        edge_kernel, (edges, edges, shape((GROUP, TILES * TOKENS), BF16)), 1.0, x, scalars=(even,)
+        edge_kernel, (edges, edges, shape((GROUP, TILES * TOKENS), BF16)), 1.0, x, scalars=(flags,)
     )
     groups = lax.axis_size("tm")
     pairs = [(i, i + 1) for i in range(0, groups - 1, 2)]
@@ -377,35 +400,49 @@
         3.0,
         agents,
         x,
-        scalars=(low,),
+        scalars=(flags,),
     )
     swap = [(0, 1), (1, 0)]
     theirs = lax.ppermute(send, "zl", swap)
     row = shape((GROUP, TOKENS), BF16)
-    to_next, to_last = call(rim_kernel, (row, row), 1.0, x, near, far, taps, scalars=(even,))
-    up = shift(to_next, ("zh", "zl"), 1)
-    down = shift(to_last, ("zh", "zl"), -1)
-    blended = call(blend_kernel, shape((GROUP + STATS, HALF), BF16), 1.0, keep, theirs)
+    cross, kin = call(rim_kernel, (row, row), 1.0, x, near, far, taps, scalars=(flags,))
+    blended, longer = call(
+        blend_kernel,
+        (shape((GROUP + STATS, HALF), BF16), shape((2 * GROUP + STATS, HALF), BF16)),
+        1.0,
+        keep,
+        theirs,
+        cross,
+    )
     parts = [blended]
     for n in range(1, PAIRS):
-        parts.append(lax.ppermute(blended, "zh", [(i, (i + n) % PAIRS) for i in range(PAIRS)]))
+        to = [2 * ((i // 2 + n) % PAIRS) + (i + n) % 2 for i in range(PLANES)]
+        moved = longer if n % 2 else blended
+        parts.append(lax.ppermute(moved, ("zh", "zl"), list(enumerate(to))))
     local = call(
-        conv_kernel, shape((TILES, GROUP, TOKENS), F32), 5.0, x, near, far, taps, scalars=(even,)
-    )
-    ours = call(comb_kernel, shape((GROUP, HALF), BF16), 1.0, *parts)
+        conv_kernel, shape((TILES, GROUP, TOKENS), F32), 5.0, x, near, far, taps, scalars=(flags,)
+    )
+    ours = call(comb_kernel, shape((2 * GROUP, HALF), BF16), 1.0, *parts, kin)
     theirs = lax.ppermute(ours, "zl", swap)
+    weights, totals = call(
+        query_kernel,
+        (shape((GROUP_HEADS, AGENTS, TILES * TOKENS), BF16), shape((8, TILES * TOKENS), F32)),
+        2.0,
+        agents,
+        turned_q,
+    )
     mixed = call(
         mix_kernel,
         shape((TILES, GROUP, TOKENS), BF16),
         1.0,
-        agents,
-        turned_q,
+        weights,
+        totals,
         ours,
         theirs,
+        parts[1],
+        parts[3],
         local,
-        up,
-        down,
-        scalars=(low,),
+        scalars=(flags,),
     )
     mine = exchange(mixed, "xy")
     pieces = TILES // 2

time: 80.8 us -> 81.1 us (level)
  starting transfers between devices: 24.5 us -> 20.8 us
  Pallas kernels: 12.5 us -> 15.2 us
  waiting for transfers between devices: 8.46 us -> 10.1 us
    ppermute x5 -> x3, starting transfers between devices: 14.3 us -> 6.37 us  [body(): parts.append(lax.ppermute(moved, ('zh', 'zl'), list(enumerate(to))))]
    ppermute x1, starting transfers between devices: 0.09 us -> 4.18 us  [body(): theirs = lax.ppermute(ours, 'zl', swap)]
    ppermute x5 -> x3, waiting for transfers between devices: 1.6 us -> 5.56 us  [body(): parts.append(lax.ppermute(moved, ('zh', 'zl'), list(enumerate(to))))]
    pallas_call x11 -> x12, Pallas kernels: 12.5 us -> 15.2 us  [call(): pl.pallas_call(kernel, out_shape=out_shape, in_specs=[SMEM] * len(scalars...]
    all_to_all x1, waiting for transfers between devices: 5.48 us -> 3.58 us  [exchange(): return lax.all_to_all(x, axes, 0, 0)]
  transfers between devices with their start and end apart: 10 -> 8, of which waited for: 3 -> 4; matrix products, arithmetic and copies ran while one was open for 0% -> 0% of each run, Pallas kernels for 6% -> 13%
where the time goes in v10:
time: 81.1 us; the launch traced here: 80.2 us
  blocking collectives  33.9 us (42%)
  starting transfers between devices  20.8 us (26%)
  Pallas kernels  15.2 us (19%)
  waiting for transfers between devices  10.1 us (12%)
    all_to_all x2, blocking collectives, exchange(): return lax.all_to_all(x, axes, 0, 0)  33.9 us
    pallas_call x12, Pallas kernels, call(): pl.pallas_call(kernel, out_shape=out_shape, in_specs=[SMEM] * len(scalars...  15.2 us
    all_to_all x1, starting transfers between devices, exchange(): return lax.all_to_all(x, axes, 0, 0)  7.66 us
    ppermute x3, starting transfers between devices, body(): parts.append(lax.ppermute(moved, ('zh', 'zl'), list(enumerate(to))))  6.37 us
    ppermute x3, waiting for transfers between devices, body(): parts.append(lax.ppermute(moved, ('zh', 'zl'), list(enumerate(to))))  5.56 us
    ppermute x1, starting transfers between devices, body(): theirs = lax.ppermute(ours, 'zl', swap)  4.18 us
    all_to_all x1, waiting for transfers between devices, exchange(): return lax.all_to_all(x, axes, 0, 0)  3.58 us
    ppermute x1, starting transfers between devices, body(): theirs = lax.ppermute(send, 'zl', swap)  1.72 us
  transfers between devices with their start and end apart: 8, of which 4 were waited for; matrix products, arithmetic and copies ran while one was open for 0% of the time, Pallas kernels for 13%

profile of v10, /device:TPU:96, one launch (start us, length us, event | category | flops | bytes accessed | tf_op | source)
XLA Modules:
  0.0 80.2 jit_solution(5248313204140403987)
XLA Ops:
  0.0 2.3 %shard_map.46 = bf16[8,576,128]{2,1,0:T(8,128)(2,1)} custom-call(bf16[128,1536]{1,0:T(8,128)(2,1)} %bitcast.12, bf16[128,1536]{1,0:T(8,128)(2,1)} %bitcast.13, bf16[128,1536]{1,0:T(8,128)(2,1)} %bitcast.14), custom_call_target="tpu_custom_call" | custom-call | flops 900000000 | bytes 6000000 | tf_op jit(solution)/shard_map/pallas_call | solution.py:46
  2.3 22.6 %all_to_all.15.x_ref = bf16[8,576,128]{2,1,0:T(8,128)(2,1)S(1)} all-to-all(bf16[8,576,128]{2,1,0:T(8,128)(2,1)} %shard_map.46), channel_id=1, replica_groups=mesh['tm'=4,'zh'=4,'zl'=2,'xy'=8] {'xy'}, dimensions={0} | all-to-all | bytes 2359296 | tf_op jit(solution)/shard_map/all_to_all | solution.py:58
  24.9 0.9 %shard_map.47 = bf16[8,32,192]{2,1,0:T(8,128)(2,1)} custom-call(bf16[8,576,128]{2,1,0:T(8,128)(2,1)S(1)} %all_to_all.15.x_ref), custom_call_target="tpu_custom_call" | custom-call | flops 300000000 | bytes 2000000 | tf_op jit(solution)/shard_map/pallas_call | solution.py:46
  25.8 7.7 %all-to-all-start.1 = ((bf16[8,32,192]{2,1,0:T(8,128)(2,1)}), bf16[8,32,192]{2,1,0:T(8,128)(2,1)S(1)}, u32[]{:S(2)}, u32[]{:S(2)}) async-start(bf16[8,32,192]{2,1,0:T(8,128)(2,1)} %shard_map.47), calls=%async_computation.1 | async-start | bytes 262144 | tf_op jit(solution)/shard_map/all_to_all | solution.py:58
  33.5 0.1 stack.31.flags_ref
  33.6 0.9 %shard_map.48 = (bf16[192,256]{1,0:T(8,128)(2,1)S(1)}, bf16[192,256]{1,0:T(8,128)(2,1)S(1)}, bf16[192,1024]{1,0:T(8,128)(2,1)S(1)}) custom-call(s32[5]{0:T(128)S(1)} %stack.31.flags_ref, bf16[8,576,128]{2,1,0:T(8,128)(2,1)S(1)} %all_to_all.15.x_ref), custom_call_target="tpu_custom_call" | custom-call | flops 300000000 | bytes 2000000 | tf_op jit(solution)/shard_map/pallas_call | solution.py:46
  34.5 0.1 collective-permute-start.1
  34.6 0.8 collective-permute-start.2
  35.4 3.6 %all-to-all-done.1.a_ref = bf16[8,32,192]{2,1,0:T(8,128)(2,1)S(1)} async-done(((bf16[8,32,192]{2,1,0:T(8,128)(2,1)}), bf16[8,32,192]{2,1,0:T(8,128)(2,1)S(1)}, u32[]{:S(2)}, u32[]{:S(2)}) %all-to-all-start.1) | async-done | bytes 98336 | tf_op jit(solution)/shard_map/all_to_all | solution.py:58
  39.0 2.3 %shard_map.50 = (f32[200,128]{1,0:T(8,128)S(1)}, bf16[208,128]{1,0:T(8,128)(2,1)S(1)}) custom-call(s32[5]{0:T(128)S(1)} %stack.31.flags_ref, bf16[8,32,192]{2,1,0:T(8,128)(2,1)S(1)} %all-to-all-done.1.a_ref, bf16[8,576,128]{2,1,0:T(8,128)(2,1)S(1)} %all_to_all.15.x_ref), custom_call_target="tpu_custom_call" | custom-call | flops 900000000 | bytes 6000000 | tf_op jit(solution)/shard_map/pallas_call | solution.py:46
  41.3 1.7 %collective-permute-start = (bf16[208,128]{1,0:T(8,128)(2,1)S(1)}, bf16[208,128]{1,0:T(8,128)(2,1)S(1)}, u32[]{:S(2)}, u32[]{:S(2)}) collective-permute-start(bf16[208,128]{1,0:T(8,128)(2,1)S(1)} %get-tuple-element.20), channel_id=1, source_target_pairs={{0,8},{8,0},{1,9},{9,1},{2,10},{10,2},{3,11},{11,3},{4,12},{12,4},... | collective-permute-start | bytes 159752 | tf_op jit(solution)/shard_map/ppermute | solution.py:406
  43.0 0.1 shard_map.51.w_ref
  43.2 1.5 %shard_map.52 = (bf16[192,128]{1,0:T(8,128)(2,1)S(1)}, bf16[192,128]{1,0:T(8,128)(2,1)S(1)}) custom-call(s32[5]{0:T(128)S(1)} %stack.31.flags_ref, bf16[8,576,128]{2,1,0:T(8,128)(2,1)S(1)} %all_to_all.15.x_ref, bf16[192,256]{1,0:T(8,128)(2,1)S(1)} %collective-permute-done.1.near_ref, bf16[192,256]{1,0:T(8,128)(2,1)S(1)} %collective-permute-done.2.far_ref, ...), custom_call_target="tpu_custom_call" | custom-call | flops 300000000 | bytes 2000000 | tf_op jit(solution)/shard_map/pallas_call | solution.py:46
  44.7 0.9 %collective-permute-done.came_ref = bf16[208,128]{1,0:T(8,128)(2,1)S(1)} collective-permute-done((bf16[208,128]{1,0:T(8,128)(2,1)S(1)}, bf16[208,128]{1,0:T(8,128)(2,1)S(1)}, u32[]{:S(2)}, u32[]{:S(2)}) %collective-permute-start) | collective-permute-done | bytes 53280 | tf_op jit(solution)/shard_map/ppermute | solution.py:406
  45.6 3.6 %collective-permute-start.5 = (bf16[400,128]{1,0:T(8,128)(2,1)S(1)}, bf16[400,128]{1,0:T(8,128)(2,1)S(1)}, u32[]{:S(2)}, u32[]{:S(2)}) collective-permute-start(bf16[400,128]{1,0:T(8,128)(2,1)S(1)} %get-tuple-element.25), channel_id=1, source_target_pairs={{0,56},{8,48},{16,8},{24,0},{32,24},{40,16},{48,40},{56,32},{1,57}... | collective-permute-start | bytes 307208 | tf_op jit(solution)/shard_map/ppermute | solution.py:421
  49.2 2.8 %collective-permute-start.4 = (bf16[208,128]{1,0:T(8,128)(2,1)S(1)}, bf16[208,128]{1,0:T(8,128)(2,1)S(1)}, u32[]{:S(2)}, u32[]{:S(2)}) collective-permute-start(bf16[208,128]{1,0:T(8,128)(2,1)S(1)} %get-tuple-element.24.refs_0_), channel_id=1, source_target_pairs={{0,32},{8,40},{16,48},{24,56},{32,0},{40,8},{48,16},{56,24},{1,33}... | collective-permute-start | bytes 159752 | tf_op jit(solution)/shard_map/ppermute | solution.py:421
  52.0 5.4 %collective-permute-done.4.refs_2_ = bf16[208,128]{1,0:T(8,128)(2,1)S(1)} collective-permute-done((bf16[208,128]{1,0:T(8,128)(2,1)S(1)}, bf16[208,128]{1,0:T(8,128)(2,1)S(1)}, u32[]{:S(2)}, u32[]{:S(2)}) %collective-permute-start.4) | collective-permute-done | bytes 53280 | tf_op jit(solution)/shard_map/ppermute | solution.py:421
  57.5 0.1 collective-permute-done.3.refs_1_.one_ref
  57.6 4.2 %collective-permute-start.6 = (bf16[384,128]{1,0:T(8,128)(2,1)S(1)}, bf16[384,128]{1,0:T(8,128)(2,1)S(1)}, u32[]{:S(2)}, u32[]{:S(2)}) collective-permute-start(bf16[384,128]{1,0:T(8,128)(2,1)S(1)} %shard_map.54.ours_ref), channel_id=1, source_target_pairs={{0,8},{8,0},{1,9},{9,1},{2,10},{10,2},{3,11},{11,3},{4,12},{12,4},... | collective-permute-start | bytes 294920 | tf_op jit(solution)/shard_map/ppermute | solution.py:426
  61.8 4.1 %shard_map.55.local_ref = f32[8,192,128]{2,1,0:T(8,128)S(1)} custom-call(s32[5]{0:T(128)S(1)} %stack.31.flags_ref, bf16[8,576,128]{2,1,0:T(8,128)(2,1)S(1)} %all_to_all.15.x_ref, bf16[192,256]{1,0:T(8,128)(2,1)S(1)} %collective-permute-done.1.near_ref, bf16[192,256]{1,0:T(8,128)(2,1)S(1)} %collective-permute-done.2.far_ref, f32[192,32]{1,0:T(8,128)S(1)} %shard_map.51.w_ref), custom_call_target="tpu_custom_call" | custom-call | flops 1500000000 | bytes 10000000 | tf_op jit(solution)/shard_map/pallas_call | solution.py:46
  65.9 1.2 %shard_map.49 = (bf16[3,256,1024]{2,1,0:T(8,128)(2,1)S(1)}, f32[8,1024]{1,0:T(8,128)S(1)}) custom-call(bf16[8,32,192]{2,1,0:T(8,128)(2,1)S(1)} %all-to-all-done.1.a_ref, bf16[192,1024]{1,0:T(8,128)(2,1)S(1)} %get-tuple-element.16.q_ref), custom_call_target="tpu_custom_call" | custom-call | flops 600000000 | bytes 4000000 | tf_op jit(solution)/shard_map/pallas_call | solution.py:46
  67.1 0.9 %shard_map.56 = bf16[8,192,128]{2,1,0:T(8,128)(2,1)S(1)} custom-call(s32[5]{0:T(128)S(1)} %stack.31.flags_ref, bf16[3,256,1024]{2,1,0:T(8,128)(2,1)S(1)} %get-tuple-element.17.e_ref, f32[8,1024]{1,0:T(8,128)S(1)} %get-tuple-element.18.total_ref, bf16[384,128]{1,0:T(8,128)(2,1)S(1)} %shard_map.54.ours_ref, ...), custom_call_target="tpu_custom_call" | custom-call | flops 300000000 | bytes 2000000 | tf_op jit(solution)/shard_map/pallas_call | solution.py:46
  68.1 11.2 %all_to_all.16.x_ref = bf16[8,192,128]{2,1,0:T(8,128)(2,1)S(1)} all-to-all(bf16[8,192,128]{2,1,0:T(8,128)(2,1)S(1)} %shard_map.56), channel_id=1, replica_groups=mesh['tm'=4,'zh'=4,'zl'=2,'xy'=8] {'xy'}, dimensions={0} | all-to-all | bytes 786432 | tf_op jit(solution)/shard_map/all_to_all | solution.py:58
  79.3 0.9 %shard_map.57 = bf16[128,1536]{1,0:T(8,128)(2,1)} custom-call(bf16[8,192,128]{2,1,0:T(8,128)(2,1)S(1)} %all_to_all.16.x_ref), custom_call_target="tpu_custom_call" | custom-call | flops 300000000 | bytes 2000000 | tf_op jit(solution)/shard_map/pallas_call | solution.py:46
  (9 shorter events, 0.1 us)
Async XLA Ops:
  25.8 13.1 %all-to-all-start.1 = ((bf16[8,32,192]{2,1,0:T(8,128)(2,1)}), bf16[8,32,192]{2,1,0:T(8,128)(2,1)S(1)}, u32[]{:S(2)}, u32[]{:S(2)}) async-start(bf16[8,32,192]{2,1,0:T(8,128)(2,1)} %shard_map.47), calls=%async_computation.1 | async-start | bytes 262144 | tf_op jit(solution)/shard_map/all_to_all | solution.py:58
  34.5 8.7 %collective-permute-start.1 = (bf16[192,256]{1,0:T(8,128)(2,1)S(1)}, bf16[192,256]{1,0:T(8,128)(2,1)S(1)}, u32[]{:S(2)}, u32[]{:S(2)}) collective-permute-start(bf16[192,256]{1,0:T(8,128)(2,1)S(1)} %get-tuple-element.21), channel_id=1, source_target_pairs={{0,64},{128,192},{64,0},{192,128},{1,65},{129,193},{65,1},{193,129... | collective-permute-start | bytes 294920 | tf_op jit(solution)/shard_map/ppermute | solution.py:394
  34.6 8.4 %copy-start = (f32[3,3,3,1536]{3,2,1,0:T(4,128)S(1)}, f32[3,3,3,1536]{3,2,1,0:T(4,128)}, u32[]{:S(2)}) copy-start(f32[3,3,3,1536]{3,2,1,0:T(4,128)} %w_ref.1) | copy-start | bytes 497668
  34.6 8.6 %collective-permute-start.2 = (bf16[192,256]{1,0:T(8,128)(2,1)S(1)}, bf16[192,256]{1,0:T(8,128)(2,1)S(1)}, u32[]{:S(2)}, u32[]{:S(2)}) collective-permute-start(bf16[192,256]{1,0:T(8,128)(2,1)S(1)} %get-tuple-element.22), channel_id=1, source_target_pairs={{64,128},{128,64},{65,129},{129,65},{66,130},{130,66},{67,131},{13... | collective-permute-start | bytes 294920 | tf_op jit(solution)/shard_map/ppermute | solution.py:396
  41.3 4.3 %collective-permute-start = (bf16[208,128]{1,0:T(8,128)(2,1)S(1)}, bf16[208,128]{1,0:T(8,128)(2,1)S(1)}, u32[]{:S(2)}, u32[]{:S(2)}) collective-permute-start(bf16[208,128]{1,0:T(8,128)(2,1)S(1)} %get-tuple-element.20), channel_id=1, source_target_pairs={{0,8},{8,0},{1,9},{9,1},{2,10},{10,2},{3,11},{11,3},{4,12},{12,4},... | collective-permute-start | bytes 159752 | tf_op jit(solution)/shard_map/ppermute | solution.py:406
  45.6 11.8 %collective-permute-start.5 = (bf16[400,128]{1,0:T(8,128)(2,1)S(1)}, bf16[400,128]{1,0:T(8,128)(2,1)S(1)}, u32[]{:S(2)}, u32[]{:S(2)}) collective-permute-start(bf16[400,128]{1,0:T(8,128)(2,1)S(1)} %get-tuple-element.25), channel_id=1, source_target_pairs={{0,56},{8,48},{16,8},{24,0},{32,24},{40,16},{48,40},{56,32},{1,57}... | collective-permute-start | bytes 307208 | tf_op jit(solution)/shard_map/ppermute | solution.py:421
  49.2 8.4 %collective-permute-start.3 = (bf16[400,128]{1,0:T(8,128)(2,1)S(1)}, bf16[400,128]{1,0:T(8,128)(2,1)S(1)}, u32[]{:S(2)}, u32[]{:S(2)}) collective-permute-start(bf16[400,128]{1,0:T(8,128)(2,1)S(1)} %get-tuple-element.25), channel_id=1, source_target_pairs={{0,24},{8,16},{16,40},{24,32},{32,56},{40,48},{48,8},{56,0},{1,25}... | collective-permute-start | bytes 307208 | tf_op jit(solution)/shard_map/ppermute | solution.py:421
  49.2 8.2 %collective-permute-start.4 = (bf16[208,128]{1,0:T(8,128)(2,1)S(1)}, bf16[208,128]{1,0:T(8,128)(2,1)S(1)}, u32[]{:S(2)}, u32[]{:S(2)}) collective-permute-start(bf16[208,128]{1,0:T(8,128)(2,1)S(1)} %get-tuple-element.24.refs_0_), channel_id=1, source_target_pairs={{0,32},{8,40},{16,48},{24,56},{32,0},{40,8},{48,16},{56,24},{1,33}... | collective-permute-start | bytes 159752 | tf_op jit(solution)/shard_map/ppermute | solution.py:421
  57.6 9.5 %collective-permute-start.6 = (bf16[384,128]{1,0:T(8,128)(2,1)S(1)}, bf16[384,128]{1,0:T(8,128)(2,1)S(1)}, u32[]{:S(2)}, u32[]{:S(2)}) collective-permute-start(bf16[384,128]{1,0:T(8,128)(2,1)S(1)} %shard_map.54.ours_ref), channel_id=1, source_target_pairs={{0,8},{8,0},{1,9},{9,1},{2,10},{10,2},{3,11},{11,3},{4,12},{12,4},... | collective-permute-start | bytes 294920 | tf_op jit(solution)/shard_map/ppermute | solution.py:426

commit v11 on v10

--- a/solution.py
+++ b/solution.py
@@ -18,13 +18,13 @@
 PLANES = 2 * PAIRS
 TILES = 8
 AGENTS = 256
+SLOT = 8
 HALF = AGENTS // 2
 GROUP_HEADS = HEADS // TILES
 GROUP = GROUP_HEADS * HEAD_DIM
 K_ROW = GROUP
 V_ROW = 2 * GROUP
 SENT = 3 * GROUP
-PLANE_AGENTS = TILES * AGENT_DEV
 EDGE = TILES * COLUMNS
 STATS = 16
 GRANT = 6 * 1024 * 1024
@@ -42,12 +42,13 @@
 
 def call(kernel, out_shape, us, *args, scalars=(), scratch=(), far=False, far_out=False):
     cost = pl.CostEstimate(flops=int(us * 3.0e8), bytes_accessed=int(us * 2.0e6), transcendentals=0)
-    out = HBM if far_out else VMEM
+    first = HBM if far_out else VMEM
+    several = isinstance(out_shape, tuple)
     return pl.pallas_call(
         kernel,
         out_shape=out_shape,
         in_specs=[SMEM] * len(scalars) + [HBM if far else VMEM] * len(args),
-        out_specs=(out,) * len(out_shape) if isinstance(out_shape, tuple) else out,
+        out_specs=(first,) + (VMEM,) * (len(out_shape) - 1) if several else first,
         scratch_shapes=list(scratch),
         cost_estimate=cost,
         compiler_params=pltpu.CompilerParams(vmem_limit_bytes=ALL if far else GRANT),
@@ -58,7 +59,7 @@
     return lax.all_to_all(x, axes, 0, 0)
 
 
-def pack_kernel(q_ref, k_ref, v_ref, out_ref, came, turned, in_sems, out_sems):
+def pack_kernel(q_ref, k_ref, v_ref, out_ref, pooled_ref, came, turned, in_sems, out_sems):
     refs = (q_ref, k_ref, v_ref)
     loads = [pltpu.make_async_copy(ref, came.at[n], in_sems.at[n]) for n, ref in enumerate(refs)]
     for load in loads:
@@ -73,6 +74,13 @@
         store = pltpu.make_async_copy(turned.at[n], out_ref.at[:, rows, :], out_sems.at[n])
         store.start()
         stores.append(store)
+    shape = (SLOT, TOKENS)
+    token = lax.broadcasted_iota(jnp.int32, shape, 1)
+    agent = lax.broadcasted_iota(jnp.int32, shape, 0)
+    width = COLUMNS // AGENT_DEV
+    pick = ((token % COLUMNS) // width == agent).astype(F32).astype(BF16)
+    sums = jnp.dot(pick, came[0], preferred_element_type=F32)
+    pooled_ref[...] = (sums * (1.0 / (FRAMES * width))).astype(BF16)
     for store in stores:
         store.wait()
 
@@ -81,23 +89,28 @@
     return jnp.concatenate([x_ref[s, start : start + size, :] for s in range(TILES)], axis=1)
 
 
-def pool_kernel(x_ref, out_ref):
-    shape = (PLANE_AGENTS, TILES * TOKENS)
-    cell = lax.broadcasted_iota(jnp.int32, shape, 1)
-    agent = lax.broadcasted_iota(jnp.int32, shape, 0)
-    width = COLUMNS // AGENT_DEV
-    owner = cell // TOKENS * AGENT_DEV + cell % COLUMNS // width
-    pick = (owner == agent).astype(F32).astype(BF16)
-    sums = lax.dot_general(
-        pick, rows_of(x_ref, 0, GROUP), (((1,), (1,)), ((), ())), preferred_element_type=F32
-    )
-    pooled = (sums * (1.0 / (FRAMES * width))).astype(BF16)
-    for z in range(PLANES):
-        out_ref[z] = pooled
-
-
-def agent_kernel(flags_ref, a_ref, x_ref, keep_ref, send_ref):
-    low = flags_ref[1] == 1
+def couple_kernel(z_ref, ours_ref, theirs_ref, out_ref):
+    ours, theirs = ours_ref[...].astype(F32), theirs_ref[...].astype(F32)
+    second = lax.rem(z_ref[0], 2) == 1
+    low, high = jnp.where(second, theirs, ours), jnp.where(second, ours, theirs)
+    out_ref[...] = (low + pltpu.roll(high, AGENT_DEV, 0)).astype(BF16)
+
+
+def route_kernel(z_ref, *refs):
+    came, out_ref = refs[:PAIRS], refs[PAIRS]
+    rows = jnp.concatenate([ref[...].astype(F32) for ref in came], axis=0).astype(BF16)
+    shape = (PAIRS * SLOT, PAIRS * SLOT)
+    to = lax.broadcasted_iota(jnp.int32, shape, 0)
+    at = lax.broadcasted_iota(jnp.int32, shape, 1)
+    hop = (z_ref[0] // 2 + PAIRS - to // SLOT) % PAIRS
+    pick = (at == hop * SLOT + to % SLOT).astype(F32).astype(BF16)
+    agents = jnp.dot(pick, rows, preferred_element_type=F32).astype(BF16)
+    for tile in range(TILES):
+        out_ref[tile] = agents[:, tile * GROUP : (tile + 1) * GROUP]
+
+
+def agent_kernel(tm_ref, z_ref, a_ref, x_ref, keep_ref, send_ref):
+    low = lax.rem(z_ref[0] // 2 + z_ref[0], 2) == 0
     everyone = a_ref[...].reshape(AGENTS, GROUP)
     columns = []
     logs = []
@@ -190,7 +203,7 @@
             out_ref[...] = jnp.concatenate(rows, axis=0).T
 
 
-def edge_kernel(flags_ref, x_ref, near_ref, far_ref, q_ref):
+def edge_kernel(tm_ref, z_ref, x_ref, near_ref, far_ref, q_ref):
     q_ref[...] = rows_of(x_ref, 0, GROUP)
     spot = lax.broadcasted_iota(jnp.int32, (GROUP, TOKENS), 1) // COLUMNS
     for block in range(EDGE // TOKENS):
@@ -204,12 +217,12 @@
         lanes = slice(block * TOKENS, (block + 1) * TOKENS)
         last, first = last.astype(BF16), first.astype(BF16)
 
-        @pl.when(flags_ref[0] == 1)
+        @pl.when(lax.rem(tm_ref[0], 2) == 0)
         def _(last=last, first=first, lanes=lanes):
             near_ref[:, lanes] = last
             far_ref[:, lanes] = first
 
-        @pl.when(flags_ref[0] != 1)
+        @pl.when(lax.rem(tm_ref[0], 2) != 0)
         def _(last=last, first=first, lanes=lanes):
             near_ref[:, lanes] = first
             far_ref[:, lanes] = last
@@ -266,8 +279,8 @@
     return left + sums[1] + right
 
 
-def rim_kernel(flags_ref, x_ref, near_ref, far_ref, w_ref, cross_ref, kin_ref):
-    even, second = flags_ref[0] == 1, flags_ref[2] == 1
+def rim_kernel(tm_ref, z_ref, x_ref, near_ref, far_ref, w_ref, cross_ref, kin_ref):
+    even, second = lax.rem(tm_ref[0], 2) == 0, lax.rem(z_ref[0], 2) == 1
     tall = GROUP // 2
     for at in range(0, GROUP, tall):
         sums = []
@@ -278,8 +291,8 @@
         kin_ref[pl.ds(at, tall), :] = jnp.where(second, sums[1], sums[0])
 
 
-def conv_kernel(flags_ref, x_ref, near_ref, far_ref, w_ref, out_ref):
-    even = flags_ref[0] == 1
+def conv_kernel(tm_ref, z_ref, x_ref, near_ref, far_ref, w_ref, out_ref):
+    even = lax.rem(tm_ref[0], 2) == 0
 
     def step(n, carry):
         at = pl.multiple_of(n * TALL, TALL)
@@ -306,9 +319,9 @@
         e_ref[h] = weights.astype(BF16)
 
 
-def mix_kernel(flags_ref, e_ref, total_ref, ours_ref, theirs_ref, one_ref, three_ref, local_ref, out_ref):
-    low, second = flags_ref[1] == 1, flags_ref[2] == 1
-    first, last = flags_ref[3] == 1, flags_ref[4] == 1
+def mix_kernel(tm_ref, z_ref, e_ref, total_ref, ours_ref, theirs_ref, one_ref, three_ref, local_ref, out_ref):
+    low, second = lax.rem(z_ref[0] // 2 + z_ref[0], 2) == 0, lax.rem(z_ref[0], 2) == 1
+    first, last = z_ref[0] == 0, z_ref[0] == PLANES - 1
     ours, theirs = ours_ref[:GROUP], theirs_ref[:GROUP]
     values = jnp.concatenate(
         [jnp.where(low, ours, theirs), jnp.where(low, theirs, ours)], axis=1
@@ -352,9 +365,9 @@
     k = key_states.reshape(TOKENS, D)
     v = value_states.reshape(TOKENS, D)
     shape = jax.ShapeDtypeStruct
-    packed = call(
+    packed, pooled = call(
         pack_kernel,
-        shape((TILES, SENT, TOKENS), BF16),
+        (shape((TILES, SENT, TOKENS), BF16), shape((SLOT, D), BF16)),
         3.0,
         q,
         k,
@@ -372,40 +385,32 @@
     tile = scalar(lax.axis_index("xy"))
     taps = call(taps_kernel, shape((GROUP, 32), F32), 1.0, conv_weight, scalars=(tile,))
 
-    high, second = lax.axis_index("zh"), lax.axis_index("zl")
-    plane = 2 * high + second
-    flags = jnp.stack(
-        [
-            1 - lax.axis_index("tm") % 2,
-            1 - (high + second) % 2,
-            second,
-            plane == 0,
-            plane == PLANES - 1,
-        ]
-    ).astype(jnp.int32)
-    pooled = call(pool_kernel, shape((PLANES, PLANE_AGENTS, GROUP), BF16), 1.0, x)
-    agents = exchange(pooled, ("zh", "zl"))
+    where = (
+        scalar(lax.axis_index("tm")),
+        scalar(2 * lax.axis_index("zh") + lax.axis_index("zl")),
+    )
+    swap = [(0, 1), (1, 0)]
+    met = lax.ppermute(pooled, "zl", swap)
+    couple = call(couple_kernel, shape((SLOT, D), BF16), 1.0, pooled, met, scalars=where[1:])
+    came = [couple]
+    for n in range(1, PAIRS):
+        came.append(lax.ppermute(couple, "zh", [(i, (i + n) % PAIRS) for i in range(PAIRS)]))
+    by_tile = shape((TILES, PAIRS * SLOT, GROUP), BF16)
+    routed = call(route_kernel, by_tile, 1.0, *came, scalars=where[1:])
+    agents = exchange(routed, "xy")
     edges = shape((GROUP, EDGE), BF16)
-    near, far, turned_q = call(
-        edge_kernel, (edges, edges, shape((GROUP, TILES * TOKENS), BF16)), 1.0, x, scalars=(flags,)
-    )
+    near, far, turned_q = call(edge_kernel, (edges, edges, shape((GROUP, TILES * TOKENS), BF16)), 1.0, x, scalars=where)
     groups = lax.axis_size("tm")
     pairs = [(i, i + 1) for i in range(0, groups - 1, 2)]
     near = lax.ppermute(near, "tm", pairs + [(b, a) for a, b in pairs])
     pairs = [(i, i + 1) for i in range(1, groups - 1, 2)]
     far = lax.ppermute(far, "tm", pairs + [(b, a) for a, b in pairs])
     keep, send = call(
-        agent_kernel,
-        (shape((GROUP + 8, HALF), F32), shape((GROUP + STATS, HALF), BF16)),
-        3.0,
-        agents,
-        x,
-        scalars=(flags,),
-    )
-    swap = [(0, 1), (1, 0)]
+        agent_kernel, (shape((GROUP + 8, HALF), F32), shape((GROUP + STATS, HALF), BF16)), 3.0, agents, x, scalars=where
+    )
     theirs = lax.ppermute(send, "zl", swap)
     row = shape((GROUP, TOKENS), BF16)
-    cross, kin = call(rim_kernel, (row, row), 1.0, x, near, far, taps, scalars=(flags,))
+    cross, kin = call(rim_kernel, (row, row), 1.0, x, near, far, taps, scalars=where)
     blended, longer = call(
         blend_kernel,
         (shape((GROUP + STATS, HALF), BF16), shape((2 * GROUP + STATS, HALF), BF16)),
@@ -419,9 +424,7 @@
         to = [2 * ((i // 2 + n) % PAIRS) + (i + n) % 2 for i in range(PLANES)]
         moved = longer if n % 2 else blended
         parts.append(lax.ppermute(moved, ("zh", "zl"), list(enumerate(to))))
-    local = call(
-        conv_kernel, shape((TILES, GROUP, TOKENS), F32), 5.0, x, near, far, taps, scalars=(flags,)
-    )
+    local = call(conv_kernel, shape((TILES, GROUP, TOKENS), F32), 5.0, x, near, far, taps, scalars=where)
     ours = call(comb_kernel, shape((2 * GROUP, HALF), BF16), 1.0, *parts, kin)
     theirs = lax.ppermute(ours, "zl", swap)
     weights, totals = call(
@@ -442,7 +445,7 @@
         parts[1],
         parts[3],
         local,
-        scalars=(flags,),
+        scalars=where,
     )
     mine = exchange(mixed, "xy")
     pieces = TILES // 2

time: 81.1 us -> 76.3 us (0.941)
  the two profiles are of different devices: /device:TPU:96 before, /device:TPU:4 now
where the time goes in v11:
time: 76.3 us; the launch traced here: 75.9 us
  starting transfers between devices  34.5 us (45%)
  waiting for transfers between devices  17.8 us (23%)
  Pallas kernels  13.1 us (17%)
  blocking collectives  10.4 us (14%)
    pallas_call x13, Pallas kernels, call(): pl.pallas_call(kernel, out_shape=out_shape, in_specs=[SMEM] * len(scalars...  13.1 us
    all_to_all x2, starting transfers between devices, exchange(): return lax.all_to_all(x, axes, 0, 0)  10.5 us
    all_to_all x1, blocking collectives, exchange(): return lax.all_to_all(x, axes, 0, 0)  10.4 us
    ppermute x3, starting transfers between devices, body(): lax.ppermute(couple, 'zh', [(i, (i + n) % PAIRS) for i in range(PAIRS)])  10.2 us
    ppermute x3, starting transfers between devices, body(): parts.append(lax.ppermute(moved, ('zh', 'zl'), list(enumerate(to))))  7.62 us
    ppermute x3, waiting for transfers between devices, body(): parts.append(lax.ppermute(moved, ('zh', 'zl'), list(enumerate(to))))  5.05 us
    ppermute x3, waiting for transfers between devices, body(): lax.ppermute(couple, 'zh', [(i, (i + n) % PAIRS) for i in range(PAIRS)])  4.18 us
    all_to_all x2, waiting for transfers between devices, exchange(): return lax.all_to_all(x, axes, 0, 0)  3.19 us
  transfers between devices with their start and end apart: 13, of which 6 were waited for; matrix products, arithmetic and copies ran while one was open for 0% of the time, Pallas kernels for 12%

profile of v11, /device:TPU:4, one launch (start us, length us, event | category | flops | bytes accessed | tf_op | source)
XLA Modules:
  0.0 75.9 jit_solution(760345564681401265)
XLA Ops:
  0.0 2.9 %shard_map.46 = (bf16[8,576,128]{2,1,0:T(8,128)(2,1)}, bf16[8,1536]{1,0:T(8,128)(2,1)}) custom-call(bf16[128,1536]{1,0:T(8,128)(2,1)} %bitcast.9, bf16[128,1536]{1,0:T(8,128)(2,1)} %bitcast.10, bf16[128,1536]{1,0:T(8,128)(2,1)} %bitcast.11), custom_call_target="tpu_custom_call" | custom-call | flops 900000000 | bytes 6000000 | tf_op jit(solution)/shard_map/pallas_call | solution.py:47
  2.9 5.1 %all-to-all-start.1 = ((bf16[8,576,128]{2,1,0:T(8,128)(2,1)}), bf16[8,576,128]{2,1,0:T(8,128)(2,1)S(1)}, u32[]{:S(2)}, u32[]{:S(2)}) async-start(bf16[8,576,128]{2,1,0:T(8,128)(2,1)} %get-tuple-element.19), calls=%async_computation.1 | async-start | bytes 2359296 | tf_op jit(solution)/shard_map/all_to_all | solution.py:59
  8.0 2.0 %collective-permute-start = (bf16[8,1536]{1,0:T(8,128)(2,1)S(1)}, bf16[8,1536]{1,0:T(8,128)(2,1)S(1)}, u32[]{:S(2)}, u32[]{:S(2)}) collective-permute-start(bf16[8,1536]{1,0:T(8,128)(2,1)S(1)} %copy-done.1), channel_id=1, source_target_pairs={{0,8},{8,0},{1,9},{9,1},{2,10},{10,2},{3,11},{11,3},{4,12},{12,4},... | collective-permute-start | bytes 73736 | tf_op jit(solution)/shard_map/ppermute | solution.py:393
  10.0 1.9 %collective-permute-done.theirs_ref = bf16[8,1536]{1,0:T(8,128)(2,1)S(1)} collective-permute-done((bf16[8,1536]{1,0:T(8,128)(2,1)S(1)}, bf16[8,1536]{1,0:T(8,128)(2,1)S(1)}, u32[]{:S(2)}, u32[]{:S(2)}) %collective-permute-start) | collective-permute-done | bytes 24608 | tf_op jit(solution)/shard_map/ppermute | solution.py:393
  12.0 6.4 %collective-permute-start.3 = (bf16[8,1536]{1,0:T(8,128)(2,1)S(1)}, bf16[8,1536]{1,0:T(8,128)(2,1)S(1)}, u32[]{:S(2)}, u32[]{:S(2)}) collective-permute-start(bf16[8,1536]{1,0:T(8,128)(2,1)S(1)} %shard_map.47.refs_0_), channel_id=1, source_target_pairs={{0,48},{16,0},{32,16},{48,32},{1,49},{17,1},{33,17},{49,33},{2,50}... | collective-permute-start | bytes 73736 | tf_op jit(solution)/shard_map/ppermute | solution.py:397
  18.3 1.0 %collective-permute-start.2 = (bf16[8,1536]{1,0:T(8,128)(2,1)S(1)}, bf16[8,1536]{1,0:T(8,128)(2,1)S(1)}, u32[]{:S(2)}, u32[]{:S(2)}) collective-permute-start(bf16[8,1536]{1,0:T(8,128)(2,1)S(1)} %shard_map.47.refs_0_), channel_id=1, source_target_pairs={{0,32},{16,48},{32,0},{48,16},{1,33},{17,49},{33,1},{49,17},{2,34}... | collective-permute-start | bytes 73736 | tf_op jit(solution)/shard_map/ppermute | solution.py:397
  19.3 2.8 %collective-permute-start.1 = (bf16[8,1536]{1,0:T(8,128)(2,1)S(1)}, bf16[8,1536]{1,0:T(8,128)(2,1)S(1)}, u32[]{:S(2)}, u32[]{:S(2)}) collective-permute-start(bf16[8,1536]{1,0:T(8,128)(2,1)S(1)} %shard_map.47.refs_0_), channel_id=1, source_target_pairs={{0,16},{16,32},{32,48},{48,0},{1,17},{17,33},{33,49},{49,1},{2,18}... | collective-permute-start | bytes 73736 | tf_op jit(solution)/shard_map/ppermute | solution.py:397
  22.2 4.2 %collective-permute-done.2.refs_2_ = bf16[8,1536]{1,0:T(8,128)(2,1)S(1)} collective-permute-done((bf16[8,1536]{1,0:T(8,128)(2,1)S(1)}, bf16[8,1536]{1,0:T(8,128)(2,1)S(1)}, u32[]{:S(2)}, u32[]{:S(2)}) %collective-permute-start.2) | collective-permute-done | bytes 24608 | tf_op jit(solution)/shard_map/ppermute | solution.py:397
  26.4 0.9 %shard_map.48 = bf16[8,32,192]{2,1,0:T(8,128)(2,1)} custom-call(s32[1]{0:T(128)} %bitcast.1.z_ref, bf16[8,1536]{1,0:T(8,128)(2,1)S(1)} %shard_map.47.refs_0_, bf16[8,1536]{1,0:T(8,128)(2,1)S(1)} %collective-permute-done.1.refs_1_, bf16[8,1536]{1,0:T(8,128)(2,1)S(1)} %collective-permute-done.2.refs_2_, bf16[8,1536]{1,0:T(8,128)(2,1)S(1)} %collective-permute-done.3.refs_3_), custom_call_target="tpu_custom_call" | custom-call | flops 300000000 | bytes 2000000 | tf_op jit(solution)/shard_map/pallas_call | solution.py:47
  27.2 5.4 %all-to-all-start = ((bf16[8,32,192]{2,1,0:T(8,128)(2,1)}), bf16[8,32,192]{2,1,0:T(8,128)(2,1)S(1)}, u32[]{:S(2)}, u32[]{:S(2)}) async-start(bf16[8,32,192]{2,1,0:T(8,128)(2,1)} %shard_map.48), calls=%async_computation | async-start | bytes 262144 | tf_op jit(solution)/shard_map/all_to_all | solution.py:59
  33.1 2.9 %collective-permute-start.6 = (bf16[192,256]{1,0:T(8,128)(2,1)S(1)}, bf16[192,256]{1,0:T(8,128)(2,1)S(1)}, u32[]{:S(2)}, u32[]{:S(2)}) collective-permute-start(bf16[192,256]{1,0:T(8,128)(2,1)S(1)} %get-tuple-element.26), channel_id=1, source_target_pairs={{64,128},{128,64},{65,129},{129,65},{66,130},{130,66},{67,131},{13... | collective-permute-start | bytes 294920 | tf_op jit(solution)/shard_map/ppermute | solution.py:407
  36.0 3.2 %all-to-all-done.a_ref = bf16[8,32,192]{2,1,0:T(8,128)(2,1)S(1)} async-done(((bf16[8,32,192]{2,1,0:T(8,128)(2,1)}), bf16[8,32,192]{2,1,0:T(8,128)(2,1)S(1)}, u32[]{:S(2)}, u32[]{:S(2)}) %all-to-all-start) | async-done | bytes 98336 | tf_op jit(solution)/shard_map/all_to_all | solution.py:59
  39.2 1.8 %shard_map.51 = (f32[200,128]{1,0:T(8,128)S(1)}, bf16[208,128]{1,0:T(8,128)(2,1)S(1)}) custom-call(s32[1]{0:T(128)} %bitcast.tm_ref, s32[1]{0:T(128)} %bitcast.1.z_ref, bf16[8,32,192]{2,1,0:T(8,128)(2,1)S(1)} %all-to-all-done.a_ref, bf16[8,576,128]{2,1,0:T(8,128)(2,1)S(1)} %all-to-all-done.1.x_ref), custom_call_target="tpu_custom_call" | custom-call | flops 900000000 | bytes 6000000 | tf_op jit(solution)/shard_map/pallas_call | solution.py:47
  40.9 1.1 %collective-permute-start.4 = (bf16[208,128]{1,0:T(8,128)(2,1)S(1)}, bf16[208,128]{1,0:T(8,128)(2,1)S(1)}, u32[]{:S(2)}, u32[]{:S(2)}) collective-permute-start(bf16[208,128]{1,0:T(8,128)(2,1)S(1)} %get-tuple-element.24), channel_id=1, source_target_pairs={{0,8},{8,0},{1,9},{9,1},{2,10},{10,2},{3,11},{11,3},{4,12},{12,4},... | collective-permute-start | bytes 159752 | tf_op jit(solution)/shard_map/ppermute | solution.py:411
  42.2 1.0 %shard_map.53 = (bf16[192,128]{1,0:T(8,128)(2,1)S(1)}, bf16[192,128]{1,0:T(8,128)(2,1)S(1)}) custom-call(s32[1]{0:T(128)} %bitcast.tm_ref, s32[1]{0:T(128)} %bitcast.1.z_ref, bf16[8,576,128]{2,1,0:T(8,128)(2,1)S(1)} %all-to-all-done.1.x_ref, bf16[192,256]{1,0:T(8,128)(2,1)S(1)} %collective-permute-done.5.near_ref, ...), custom_call_target="tpu_custom_call" | custom-call | flops 300000000 | bytes 2000000 | tf_op jit(solution)/shard_map/pallas_call | solution.py:47
  43.2 2.4 %collective-permute-done.4.came_ref = bf16[208,128]{1,0:T(8,128)(2,1)S(1)} collective-permute-done((bf16[208,128]{1,0:T(8,128)(2,1)S(1)}, bf16[208,128]{1,0:T(8,128)(2,1)S(1)}, u32[]{:S(2)}, u32[]{:S(2)}) %collective-permute-start.4) | collective-permute-done | bytes 53280 | tf_op jit(solution)/shard_map/ppermute | solution.py:411
  46.4 3.1 %collective-permute-start.7 = (bf16[400,128]{1,0:T(8,128)(2,1)S(1)}, bf16[400,128]{1,0:T(8,128)(2,1)S(1)}, u32[]{:S(2)}, u32[]{:S(2)}) collective-permute-start(bf16[400,128]{1,0:T(8,128)(2,1)S(1)} %get-tuple-element.29), channel_id=1, source_target_pairs={{0,24},{8,16},{16,40},{24,32},{32,56},{40,48},{48,8},{56,0},{1,25}... | collective-permute-start | bytes 307208 | tf_op jit(solution)/shard_map/ppermute | solution.py:426
  49.5 3.7 %collective-permute-start.8 = (bf16[208,128]{1,0:T(8,128)(2,1)S(1)}, bf16[208,128]{1,0:T(8,128)(2,1)S(1)}, u32[]{:S(2)}, u32[]{:S(2)}) collective-permute-start(bf16[208,128]{1,0:T(8,128)(2,1)S(1)} %get-tuple-element.28.refs_0_), channel_id=1, source_target_pairs={{0,32},{8,40},{16,48},{24,56},{32,0},{40,8},{48,16},{56,24},{1,33}... | collective-permute-start | bytes 159752 | tf_op jit(solution)/shard_map/ppermute | solution.py:426
  53.3 1.2 %shard_map.50 = (bf16[3,256,1024]{2,1,0:T(8,128)(2,1)S(1)}, f32[8,1024]{1,0:T(8,128)S(1)}) custom-call(bf16[8,32,192]{2,1,0:T(8,128)(2,1)S(1)} %all-to-all-done.a_ref, bf16[192,1024]{1,0:T(8,128)(2,1)S(1)} %get-tuple-element.20.q_ref), custom_call_target="tpu_custom_call" | custom-call | flops 600000000 | bytes 4000000 | tf_op jit(solution)/shard_map/pallas_call | solution.py:47
  54.5 5.0 %collective-permute-done.8.refs_2_ = bf16[208,128]{1,0:T(8,128)(2,1)S(1)} collective-permute-done((bf16[208,128]{1,0:T(8,128)(2,1)S(1)}, bf16[208,128]{1,0:T(8,128)(2,1)S(1)}, u32[]{:S(2)}, u32[]{:S(2)}) %collective-permute-start.8) | collective-permute-done | bytes 53280 | tf_op jit(solution)/shard_map/ppermute | solution.py:426
  59.7 3.5 %shard_map.56.local_ref = f32[8,192,128]{2,1,0:T(8,128)S(1)} custom-call(s32[1]{0:T(128)} %bitcast.tm_ref, s32[1]{0:T(128)} %bitcast.1.z_ref, bf16[8,576,128]{2,1,0:T(8,128)(2,1)S(1)} %all-to-all-done.1.x_ref, bf16[192,256]{1,0:T(8,128)(2,1)S(1)} %collective-permute-done.5.near_ref, bf16[192,256]{1,0:T(8,128)(2,1)S(1)} %collective-permute-done.6.far_ref, ...), custom_call_target="tpu_custom_call" | custom-call | flops 1500000000 | bytes 10000000 | tf_op jit(solution)/shard_map/pallas_call | solution.py:47
  63.2 1.0 %collective-permute-done.10.theirs_ref = bf16[384,128]{1,0:T(8,128)(2,1)S(1)} collective-permute-done((bf16[384,128]{1,0:T(8,128)(2,1)S(1)}, bf16[384,128]{1,0:T(8,128)(2,1)S(1)}, u32[]{:S(2)}, u32[]{:S(2)}) %collective-permute-start.10) | collective-permute-done | bytes 98336 | tf_op jit(solution)/shard_map/ppermute | solution.py:429
  64.7 10.4 %all_to_all.15.x_ref = bf16[8,192,128]{2,1,0:T(8,128)(2,1)S(1)} all-to-all(bf16[8,192,128]{2,1,0:T(8,128)(2,1)S(1)} %shard_map.57), channel_id=1, replica_groups=mesh['tm'=4,'zh'=4,'zl'=2,'xy'=8] {'xy'}, dimensions={0} | all-to-all | bytes 786432 | tf_op jit(solution)/shard_map/all_to_all | solution.py:59
  75.1 0.9 %shard_map.58 = bf16[128,1536]{1,0:T(8,128)(2,1)} custom-call(bf16[8,192,128]{2,1,0:T(8,128)(2,1)S(1)} %all_to_all.15.x_ref), custom_call_target="tpu_custom_call" | custom-call | flops 300000000 | bytes 2000000 | tf_op jit(solution)/shard_map/pallas_call | solution.py:47
  (20 shorter events, 2.0 us)
Async XLA Ops:
  2.9 5.1 %copy-start.1 = (bf16[8,1536]{1,0:T(8,128)(2,1)S(1)}, bf16[8,1536]{1,0:T(8,128)(2,1)}, u32[]{:S(2)}) copy-start(bf16[8,1536]{1,0:T(8,128)(2,1)} %get-tuple-element.18.ours_ref) | copy-start | bytes 73732
  2.9 24.3 %all-to-all-start.1 = ((bf16[8,576,128]{2,1,0:T(8,128)(2,1)}), bf16[8,576,128]{2,1,0:T(8,128)(2,1)S(1)}, u32[]{:S(2)}, u32[]{:S(2)}) async-start(bf16[8,576,128]{2,1,0:T(8,128)(2,1)} %get-tuple-element.19), calls=%async_computation.1 | async-start | bytes 2359296 | tf_op jit(solution)/shard_map/all_to_all | solution.py:59
  8.0 3.9 %collective-permute-start = (bf16[8,1536]{1,0:T(8,128)(2,1)S(1)}, bf16[8,1536]{1,0:T(8,128)(2,1)S(1)}, u32[]{:S(2)}, u32[]{:S(2)}) collective-permute-start(bf16[8,1536]{1,0:T(8,128)(2,1)S(1)} %copy-done.1), channel_id=1, source_target_pairs={{0,8},{8,0},{1,9},{9,1},{2,10},{10,2},{3,11},{11,3},{4,12},{12,4},... | collective-permute-start | bytes 73736 | tf_op jit(solution)/shard_map/ppermute | solution.py:393
  12.0 10.2 %collective-permute-start.3 = (bf16[8,1536]{1,0:T(8,128)(2,1)S(1)}, bf16[8,1536]{1,0:T(8,128)(2,1)S(1)}, u32[]{:S(2)}, u32[]{:S(2)}) collective-permute-start(bf16[8,1536]{1,0:T(8,128)(2,1)S(1)} %shard_map.47.refs_0_), channel_id=1, source_target_pairs={{0,48},{16,0},{32,16},{48,32},{1,49},{17,1},{33,17},{49,33},{2,50}... | collective-permute-start | bytes 73736 | tf_op jit(solution)/shard_map/ppermute | solution.py:397
  18.3 8.0 %collective-permute-start.2 = (bf16[8,1536]{1,0:T(8,128)(2,1)S(1)}, bf16[8,1536]{1,0:T(8,128)(2,1)S(1)}, u32[]{:S(2)}, u32[]{:S(2)}) collective-permute-start(bf16[8,1536]{1,0:T(8,128)(2,1)S(1)} %shard_map.47.refs_0_), channel_id=1, source_target_pairs={{0,32},{16,48},{32,0},{48,16},{1,33},{17,49},{33,1},{49,17},{2,34}... | collective-permute-start | bytes 73736 | tf_op jit(solution)/shard_map/ppermute | solution.py:397
  19.3 7.0 %collective-permute-start.1 = (bf16[8,1536]{1,0:T(8,128)(2,1)S(1)}, bf16[8,1536]{1,0:T(8,128)(2,1)S(1)}, u32[]{:S(2)}, u32[]{:S(2)}) collective-permute-start(bf16[8,1536]{1,0:T(8,128)(2,1)S(1)} %shard_map.47.refs_0_), channel_id=1, source_target_pairs={{0,16},{16,32},{32,48},{48,0},{1,17},{17,33},{33,49},{49,1},{2,18}... | collective-permute-start | bytes 73736 | tf_op jit(solution)/shard_map/ppermute | solution.py:397
  27.2 11.9 %all-to-all-start = ((bf16[8,32,192]{2,1,0:T(8,128)(2,1)}), bf16[8,32,192]{2,1,0:T(8,128)(2,1)S(1)}, u32[]{:S(2)}, u32[]{:S(2)}) async-start(bf16[8,32,192]{2,1,0:T(8,128)(2,1)} %shard_map.48), calls=%async_computation | async-start | bytes 262144 | tf_op jit(solution)/shard_map/all_to_all | solution.py:59
  33.0 9.3 %collective-permute-start.5 = (bf16[192,256]{1,0:T(8,128)(2,1)S(1)}, bf16[192,256]{1,0:T(8,128)(2,1)S(1)}, u32[]{:S(2)}, u32[]{:S(2)}) collective-permute-start(bf16[192,256]{1,0:T(8,128)(2,1)S(1)} %get-tuple-element.25), channel_id=1, source_target_pairs={{0,64},{128,192},{64,0},{192,128},{1,65},{129,193},{65,1},{193,129... | collective-permute-start | bytes 294920 | tf_op jit(solution)/shard_map/ppermute | solution.py:405
  33.1 9.0 %copy-start = (f32[3,3,3,1536]{3,2,1,0:T(4,128)S(1)}, f32[3,3,3,1536]{3,2,1,0:T(4,128)}, u32[]{:S(2)}) copy-start(f32[3,3,3,1536]{3,2,1,0:T(4,128)} %w_ref.1) | copy-start | bytes 497668
  33.1 9.2 %collective-permute-start.6 = (bf16[192,256]{1,0:T(8,128)(2,1)S(1)}, bf16[192,256]{1,0:T(8,128)(2,1)S(1)}, u32[]{:S(2)}, u32[]{:S(2)}) collective-permute-start(bf16[192,256]{1,0:T(8,128)(2,1)S(1)} %get-tuple-element.26), channel_id=1, source_target_pairs={{64,128},{128,64},{65,129},{129,65},{66,130},{130,66},{67,131},{13... | collective-permute-start | bytes 294920 | tf_op jit(solution)/shard_map/ppermute | solution.py:407
  40.9 4.6 %collective-permute-start.4 = (bf16[208,128]{1,0:T(8,128)(2,1)S(1)}, bf16[208,128]{1,0:T(8,128)(2,1)S(1)}, u32[]{:S(2)}, u32[]{:S(2)}) collective-permute-start(bf16[208,128]{1,0:T(8,128)(2,1)S(1)} %get-tuple-element.24), channel_id=1, source_target_pairs={{0,8},{8,0},{1,9},{9,1},{2,10},{10,2},{3,11},{11,3},{4,12},{12,4},... | collective-permute-start | bytes 159752 | tf_op jit(solution)/shard_map/ppermute | solution.py:411
  45.6 13.9 %collective-permute-start.9 = (bf16[400,128]{1,0:T(8,128)(2,1)S(1)}, bf16[400,128]{1,0:T(8,128)(2,1)S(1)}, u32[]{:S(2)}, u32[]{:S(2)}) collective-permute-start(bf16[400,128]{1,0:T(8,128)(2,1)S(1)} %get-tuple-element.29), channel_id=1, source_target_pairs={{0,56},{8,48},{16,8},{24,0},{32,24},{40,16},{48,40},{56,32},{1,57}... | collective-permute-start | bytes 307208 | tf_op jit(solution)/shard_map/ppermute | solution.py:426
  46.4 13.1 %collective-permute-start.7 = (bf16[400,128]{1,0:T(8,128)(2,1)S(1)}, bf16[400,128]{1,0:T(8,128)(2,1)S(1)}, u32[]{:S(2)}, u32[]{:S(2)}) collective-permute-start(bf16[400,128]{1,0:T(8,128)(2,1)S(1)} %get-tuple-element.29), channel_id=1, source_target_pairs={{0,24},{8,16},{16,40},{24,32},{32,56},{40,48},{48,8},{56,0},{1,25}... | collective-permute-start | bytes 307208 | tf_op jit(solution)/shard_map/ppermute | solution.py:426
  49.5 10.0 %collective-permute-start.8 = (bf16[208,128]{1,0:T(8,128)(2,1)S(1)}, bf16[208,128]{1,0:T(8,128)(2,1)S(1)}, u32[]{:S(2)}, u32[]{:S(2)}) collective-permute-start(bf16[208,128]{1,0:T(8,128)(2,1)S(1)} %get-tuple-element.28.refs_0_), channel_id=1, source_target_pairs={{0,32},{8,40},{16,48},{24,56},{32,0},{40,8},{48,16},{56,24},{1,33}... | collective-permute-start | bytes 159752 | tf_op jit(solution)/shard_map/ppermute | solution.py:426
  59.6 4.7 %collective-permute-start.10 = (bf16[384,128]{1,0:T(8,128)(2,1)S(1)}, bf16[384,128]{1,0:T(8,128)(2,1)S(1)}, u32[]{:S(2)}, u32[]{:S(2)}) collective-permute-start(bf16[384,128]{1,0:T(8,128)(2,1)S(1)} %shard_map.55.ours_ref), channel_id=1, source_target_pairs={{0,8},{8,0},{1,9},{9,1},{2,10},{10,2},{3,11},{11,3},{4,12},{12,4},... | collective-permute-start | bytes 294920 | tf_op jit(solution)/shard_map/ppermute | solution.py:429

commit v12 on v11

--- a/solution.py
+++ b/solution.py
@@ -321,14 +321,15 @@
 
 def mix_kernel(tm_ref, z_ref, e_ref, total_ref, ours_ref, theirs_ref, one_ref, three_ref, local_ref, out_ref):
     low, second = lax.rem(z_ref[0] // 2 + z_ref[0], 2) == 0, lax.rem(z_ref[0], 2) == 1
-    first, last = z_ref[0] == 0, z_ref[0] == PLANES - 1
+    odd = lax.rem(tm_ref[0], 2)
+    first, last = z_ref[0] == (PLANES - 1) * odd, z_ref[0] == PLANES - 1 - odd
     ours, theirs = ours_ref[:GROUP], theirs_ref[:GROUP]
     values = jnp.concatenate(
         [jnp.where(low, ours, theirs), jnp.where(low, theirs, ours)], axis=1
     )
     kin = theirs_ref[GROUP:].astype(F32)
-    below = three_ref[GROUP + STATS :].astype(F32)
-    above = one_ref[GROUP + STATS :].astype(F32)
+    one, three = one_ref[GROUP + STATS :].astype(F32), three_ref[GROUP + STATS :].astype(F32)
+    above, below = jnp.where(odd == 1, three, one), jnp.where(odd == 1, one, three)
     above = jnp.where(first, 0.0, jnp.where(second, kin, above))
     below = jnp.where(last, 0.0, jnp.where(second, below, kin))
     for h in range(GROUP_HEADS):
@@ -354,6 +355,31 @@
         stores.append(store)
     for store in stores:
         store.wait()
+
+
+LINE = ("tm", "zh", "zl")
+
+
+def along(step):
+    pairs = []
+    for group in range(lax.axis_size("tm")):
+        odd = group % 2
+        for z in range(PLANES):
+            to = (step((z - odd) % PLANES, odd) + odd) % PLANES
+            pairs.append((group * PLANES + z, group * PLANES + to))
+    return pairs
+
+
+def pair_plane(at, odd):
+    return at ^ 1
+
+
+def same_side(at, n):
+    return 2 * ((at // 2 + n) % PAIRS) + at % 2
+
+
+def other_side(at, n):
+    return 2 * ((at // 2 + n) % PAIRS) + (at + n) % 2
 
 
 def scalar(x):
@@ -385,30 +411,37 @@
     tile = scalar(lax.axis_index("xy"))
     taps = call(taps_kernel, shape((GROUP, 32), F32), 1.0, conv_weight, scalars=(tile,))
 
+    tm = lax.axis_index("tm")
     where = (
-        scalar(lax.axis_index("tm")),
-        scalar(2 * lax.axis_index("zh") + lax.axis_index("zl")),
-    )
-    swap = [(0, 1), (1, 0)]
-    met = lax.ppermute(pooled, "zl", swap)
+        scalar(tm),
+        scalar((2 * lax.axis_index("zh") + lax.axis_index("zl") + 7 * (tm & 1)) & 7),
+    )
+    met = lax.ppermute(pooled, LINE, along(pair_plane))
     couple = call(couple_kernel, shape((SLOT, D), BF16), 1.0, pooled, met, scalars=where[1:])
     came = [couple]
     for n in range(1, PAIRS):
-        came.append(lax.ppermute(couple, "zh", [(i, (i + n) % PAIRS) for i in range(PAIRS)]))
+        came.append(lax.ppermute(couple, LINE, along(lambda at, odd: same_side(at, n))))
     by_tile = shape((TILES, PAIRS * SLOT, GROUP), BF16)
     routed = call(route_kernel, by_tile, 1.0, *came, scalars=where[1:])
     agents = exchange(routed, "xy")
     edges = shape((GROUP, EDGE), BF16)
-    near, far, turned_q = call(edge_kernel, (edges, edges, shape((GROUP, TILES * TOKENS), BF16)), 1.0, x, scalars=where)
+    near, far, turned_q = call(
+        edge_kernel, (edges, edges, shape((GROUP, TILES * TOKENS), BF16)), 1.0, x, scalars=where
+    )
     groups = lax.axis_size("tm")
     pairs = [(i, i + 1) for i in range(0, groups - 1, 2)]
     near = lax.ppermute(near, "tm", pairs + [(b, a) for a, b in pairs])
     pairs = [(i, i + 1) for i in range(1, groups - 1, 2)]
     far = lax.ppermute(far, "tm", pairs + [(b, a) for a, b in pairs])
     keep, send = call(
-        agent_kernel, (shape((GROUP + 8, HALF), F32), shape((GROUP + STATS, HALF), BF16)), 3.0, agents, x, scalars=where
-    )
-    theirs = lax.ppermute(send, "zl", swap)
+        agent_kernel,
+        (shape((GROUP + 8, HALF), F32), shape((GROUP + STATS, HALF), BF16)),
+        3.0,
+        agents,
+        x,
+        scalars=where,
+    )
+    theirs = lax.ppermute(send, LINE, along(pair_plane))
     row = shape((GROUP, TOKENS), BF16)
     cross, kin = call(rim_kernel, (row, row), 1.0, x, near, far, taps, scalars=where)
     blended, longer = call(
@@ -421,12 +454,15 @@
     )
     parts = [blended]
     for n in range(1, PAIRS):
-        to = [2 * ((i // 2 + n) % PAIRS) + (i + n) % 2 for i in range(PLANES)]
         moved = longer if n % 2 else blended
-        parts.append(lax.ppermute(moved, ("zh", "zl"), list(enumerate(to))))
-    local = call(conv_kernel, shape((TILES, GROUP, TOKENS), F32), 5.0, x, near, far, taps, scalars=where)
+        parts.append(
+            lax.ppermute(moved, LINE, along(lambda at, odd: other_side(at, -n if odd else n)))
+        )
+    local = call(
+        conv_kernel, shape((TILES, GROUP, TOKENS), F32), 5.0, x, near, far, taps, scalars=where
+    )
     ours = call(comb_kernel, shape((2 * GROUP, HALF), BF16), 1.0, *parts, kin)
-    theirs = lax.ppermute(ours, "zl", swap)
+    theirs = lax.ppermute(ours, LINE, along(pair_plane))
     weights, totals = call(
         query_kernel,
         (shape((GROUP_HEADS, AGENTS, TILES * TOKENS), BF16), shape((8, TILES * TOKENS), F32)),

time: 76.3 us -> 76.2 us (level)
  the two profiles are of different devices: /device:TPU:4 before, /device:TPU:96 now
where the time goes in v12:
time: 76.2 us; the launch traced here: 74.7 us
  starting transfers between devices  31.1 us (41%)
  waiting for transfers between devices  18 us (24%)
  Pallas kernels  13.1 us (17%)
  blocking collectives  12.3 us (16%)
    pallas_call x13, Pallas kernels, call(): pl.pallas_call(kernel, out_shape=out_shape, in_specs=[SMEM] * len(scalars...  13.1 us
    all_to_all x1, blocking collectives, exchange(): return lax.all_to_all(x, axes, 0, 0)  12.3 us
    all_to_all x2, starting transfers between devices, exchange(): return lax.all_to_all(x, axes, 0, 0)  10.4 us
    ppermute x3, starting transfers between devices, body(): lax.ppermute(couple, LINE, along(lambda at, odd: same_side(at, n)))  8.7 us
    ppermute x3, starting transfers between devices, body(): lax.ppermute(moved, LINE, along(lambda at, odd: other_side(at, -n if odd...  6.79 us
    all_to_all x2, waiting for transfers between devices, exchange(): return lax.all_to_all(x, axes, 0, 0)  5.93 us
    ppermute x3, waiting for transfers between devices, body(): lax.ppermute(moved, LINE, along(lambda at, odd: other_side(at, -n if odd...  4.3 us
    ppermute x1, waiting for transfers between devices, body(): met = lax.ppermute(pooled, LINE, along(pair_plane))  3.72 us
  transfers between devices with their start and end apart: 13, of which 6 were waited for; matrix products, arithmetic and copies ran while one was open for 0% of the time, Pallas kernels for 12%

profile of v12, /device:TPU:96, one launch (start us, length us, event | category | flops | bytes accessed | tf_op | source)
XLA Modules:
  0.0 74.7 jit_solution(14713609191850744132)
XLA Ops:
  0.0 2.9 %shard_map.46 = (bf16[8,576,128]{2,1,0:T(8,128)(2,1)}, bf16[8,1536]{1,0:T(8,128)(2,1)}) custom-call(bf16[128,1536]{1,0:T(8,128)(2,1)} %bitcast.9, bf16[128,1536]{1,0:T(8,128)(2,1)} %bitcast.10, bf16[128,1536]{1,0:T(8,128)(2,1)} %bitcast.11), custom_call_target="tpu_custom_call" | custom-call | flops 900000000 | bytes 6000000 | tf_op jit(solution)/shard_map/pallas_call | solution.py:47
  2.9 5.4 %all-to-all-start.1 = ((bf16[8,576,128]{2,1,0:T(8,128)(2,1)}), bf16[8,576,128]{2,1,0:T(8,128)(2,1)S(1)}, u32[]{:S(2)}, u32[]{:S(2)}) async-start(bf16[8,576,128]{2,1,0:T(8,128)(2,1)} %get-tuple-element.19), calls=%async_computation.1 | async-start | bytes 2359296 | tf_op jit(solution)/shard_map/all_to_all | solution.py:59
  8.5 3.7 %collective-permute-done.theirs_ref = bf16[8,1536]{1,0:T(8,128)(2,1)S(1)} collective-permute-done((bf16[8,1536]{1,0:T(8,128)(2,1)S(1)}, bf16[8,1536]{1,0:T(8,128)(2,1)S(1)}, u32[]{:S(2)}, u32[]{:S(2)}) %collective-permute-start) | collective-permute-done | bytes 24608 | tf_op jit(solution)/shard_map/ppermute | solution.py:419
  12.4 5.9 %collective-permute-start.2 = (bf16[8,1536]{1,0:T(8,128)(2,1)S(1)}, bf16[8,1536]{1,0:T(8,128)(2,1)S(1)}, u32[]{:S(2)}, u32[]{:S(2)}) collective-permute-start(bf16[8,1536]{1,0:T(8,128)(2,1)S(1)} %shard_map.47.refs_0_), channel_id=1, source_target_pairs={{0,32},{8,40},{16,48},{24,56},{32,0},{40,8},{48,16},{56,24},{64,96... | collective-permute-start | bytes 73736 | tf_op jit(solution)/shard_map/ppermute | solution.py:423
  18.3 2.7 %collective-permute-start.1 = (bf16[8,1536]{1,0:T(8,128)(2,1)S(1)}, bf16[8,1536]{1,0:T(8,128)(2,1)S(1)}, u32[]{:S(2)}, u32[]{:S(2)}) collective-permute-start(bf16[8,1536]{1,0:T(8,128)(2,1)S(1)} %shard_map.47.refs_0_), channel_id=1, source_target_pairs={{0,16},{8,24},{16,32},{24,40},{32,48},{40,56},{48,0},{56,8},{64,80... | collective-permute-start | bytes 73736 | tf_op jit(solution)/shard_map/ppermute | solution.py:423
  21.0 2.0 %collective-permute-done.1.refs_1_ = bf16[8,1536]{1,0:T(8,128)(2,1)S(1)} collective-permute-done((bf16[8,1536]{1,0:T(8,128)(2,1)S(1)}, bf16[8,1536]{1,0:T(8,128)(2,1)S(1)}, u32[]{:S(2)}, u32[]{:S(2)}) %collective-permute-start.1) | collective-permute-done | bytes 24608 | tf_op jit(solution)/shard_map/ppermute | solution.py:423
  23.0 0.9 %shard_map.48 = bf16[8,32,192]{2,1,0:T(8,128)(2,1)} custom-call(s32[1]{0:T(128)} %bitcast.1.z_ref, bf16[8,1536]{1,0:T(8,128)(2,1)S(1)} %shard_map.47.refs_0_, bf16[8,1536]{1,0:T(8,128)(2,1)S(1)} %collective-permute-done.1.refs_1_, bf16[8,1536]{1,0:T(8,128)(2,1)S(1)} %collective-permute-done.2.refs_2_, bf16[8,1536]{1,0:T(8,128)(2,1)S(1)} %collective-permute-done.3.refs_3_), custom_call_target="tpu_custom_call" | custom-call | flops 300000000 | bytes 2000000 | tf_op jit(solution)/shard_map/pallas_call | solution.py:47
  23.9 0.6 all-to-all-done.1.x_ref
  24.5 5.0 %all-to-all-start = ((bf16[8,32,192]{2,1,0:T(8,128)(2,1)}), bf16[8,32,192]{2,1,0:T(8,128)(2,1)S(1)}, u32[]{:S(2)}, u32[]{:S(2)}) async-start(bf16[8,32,192]{2,1,0:T(8,128)(2,1)} %shard_map.48), calls=%async_computation | async-start | bytes 262144 | tf_op jit(solution)/shard_map/all_to_all | solution.py:59
  30.0 0.8 %collective-permute-start.6 = (bf16[192,256]{1,0:T(8,128)(2,1)S(1)}, bf16[192,256]{1,0:T(8,128)(2,1)S(1)}, u32[]{:S(2)}, u32[]{:S(2)}) collective-permute-start(bf16[192,256]{1,0:T(8,128)(2,1)S(1)} %get-tuple-element.26), channel_id=1, source_target_pairs={{64,128},{128,64},{65,129},{129,65},{66,130},{130,66},{67,131},{13... | collective-permute-start | bytes 294920 | tf_op jit(solution)/shard_map/ppermute | solution.py:435
  30.8 5.3 %all-to-all-done.a_ref = bf16[8,32,192]{2,1,0:T(8,128)(2,1)S(1)} async-done(((bf16[8,32,192]{2,1,0:T(8,128)(2,1)}), bf16[8,32,192]{2,1,0:T(8,128)(2,1)S(1)}, u32[]{:S(2)}, u32[]{:S(2)}) %all-to-all-start) | async-done | bytes 98336 | tf_op jit(solution)/shard_map/all_to_all | solution.py:59
  36.1 1.8 %shard_map.51 = (f32[200,128]{1,0:T(8,128)S(1)}, bf16[208,128]{1,0:T(8,128)(2,1)S(1)}) custom-call(s32[1]{0:T(128)} %bitcast.tm_ref, s32[1]{0:T(128)} %bitcast.1.z_ref, bf16[8,32,192]{2,1,0:T(8,128)(2,1)S(1)} %all-to-all-done.a_ref, bf16[8,576,128]{2,1,0:T(8,128)(2,1)S(1)} %all-to-all-done.1.x_ref), custom_call_target="tpu_custom_call" | custom-call | flops 900000000 | bytes 6000000 | tf_op jit(solution)/shard_map/pallas_call | solution.py:47
  37.9 1.1 %collective-permute-start.4 = (bf16[208,128]{1,0:T(8,128)(2,1)S(1)}, bf16[208,128]{1,0:T(8,128)(2,1)S(1)}, u32[]{:S(2)}, u32[]{:S(2)}) collective-permute-start(bf16[208,128]{1,0:T(8,128)(2,1)S(1)} %get-tuple-element.24), channel_id=1, source_target_pairs={{0,8},{8,0},{16,24},{24,16},{32,40},{40,32},{48,56},{56,48},{64,12... | collective-permute-start | bytes 159752 | tf_op jit(solution)/shard_map/ppermute | solution.py:444
  39.1 1.0 %shard_map.53 = (bf16[192,128]{1,0:T(8,128)(2,1)S(1)}, bf16[192,128]{1,0:T(8,128)(2,1)S(1)}) custom-call(s32[1]{0:T(128)} %bitcast.tm_ref, s32[1]{0:T(128)} %bitcast.1.z_ref, bf16[8,576,128]{2,1,0:T(8,128)(2,1)S(1)} %all-to-all-done.1.x_ref, bf16[192,256]{1,0:T(8,128)(2,1)S(1)} %collective-permute-done.5.near_ref, ...), custom_call_target="tpu_custom_call" | custom-call | flops 300000000 | bytes 2000000 | tf_op jit(solution)/shard_map/pallas_call | solution.py:47
  40.1 2.0 %collective-permute-done.4.came_ref = bf16[208,128]{1,0:T(8,128)(2,1)S(1)} collective-permute-done((bf16[208,128]{1,0:T(8,128)(2,1)S(1)}, bf16[208,128]{1,0:T(8,128)(2,1)S(1)}, u32[]{:S(2)}, u32[]{:S(2)}) %collective-permute-start.4) | collective-permute-done | bytes 53280 | tf_op jit(solution)/shard_map/ppermute | solution.py:444
  42.1 2.7 %collective-permute-start.9 = (bf16[400,128]{1,0:T(8,128)(2,1)S(1)}, bf16[400,128]{1,0:T(8,128)(2,1)S(1)}, u32[]{:S(2)}, u32[]{:S(2)}) collective-permute-start(bf16[400,128]{1,0:T(8,128)(2,1)S(1)} %get-tuple-element.29), channel_id=1, source_target_pairs={{0,56},{8,48},{16,8},{24,0},{32,24},{40,16},{48,40},{56,32},{64,72... | collective-permute-start | bytes 307208 | tf_op jit(solution)/shard_map/ppermute | solution.py:459
  44.8 1.0 %collective-permute-start.7 = (bf16[400,128]{1,0:T(8,128)(2,1)S(1)}, bf16[400,128]{1,0:T(8,128)(2,1)S(1)}, u32[]{:S(2)}, u32[]{:S(2)}) collective-permute-start(bf16[400,128]{1,0:T(8,128)(2,1)S(1)} %get-tuple-element.29), channel_id=1, source_target_pairs={{0,24},{8,16},{16,40},{24,32},{32,56},{40,48},{48,8},{56,0},{64,10... | collective-permute-start | bytes 307208 | tf_op jit(solution)/shard_map/ppermute | solution.py:459
  45.8 3.2 %collective-permute-start.8 = (bf16[208,128]{1,0:T(8,128)(2,1)S(1)}, bf16[208,128]{1,0:T(8,128)(2,1)S(1)}, u32[]{:S(2)}, u32[]{:S(2)}) collective-permute-start(bf16[208,128]{1,0:T(8,128)(2,1)S(1)} %get-tuple-element.28.refs_0_), channel_id=1, source_target_pairs={{0,32},{8,40},{16,48},{24,56},{32,0},{40,8},{48,16},{56,24},{64,96... | collective-permute-start | bytes 159752 | tf_op jit(solution)/shard_map/ppermute | solution.py:459
  48.9 1.2 %shard_map.50 = (bf16[3,256,1024]{2,1,0:T(8,128)(2,1)S(1)}, f32[8,1024]{1,0:T(8,128)S(1)}) custom-call(bf16[8,32,192]{2,1,0:T(8,128)(2,1)S(1)} %all-to-all-done.a_ref, bf16[192,1024]{1,0:T(8,128)(2,1)S(1)} %get-tuple-element.20.q_ref), custom_call_target="tpu_custom_call" | custom-call | flops 600000000 | bytes 4000000 | tf_op jit(solution)/shard_map/pallas_call | solution.py:47
  50.1 4.3 %collective-permute-done.8.refs_2_ = bf16[208,128]{1,0:T(8,128)(2,1)S(1)} collective-permute-done((bf16[208,128]{1,0:T(8,128)(2,1)S(1)}, bf16[208,128]{1,0:T(8,128)(2,1)S(1)}, u32[]{:S(2)}, u32[]{:S(2)}) %collective-permute-start.8) | collective-permute-done | bytes 53280 | tf_op jit(solution)/shard_map/ppermute | solution.py:459
  54.5 3.1 %collective-permute-start.10 = (bf16[384,128]{1,0:T(8,128)(2,1)S(1)}, bf16[384,128]{1,0:T(8,128)(2,1)S(1)}, u32[]{:S(2)}, u32[]{:S(2)}) collective-permute-start(bf16[384,128]{1,0:T(8,128)(2,1)S(1)} %shard_map.55.ours_ref), channel_id=1, source_target_pairs={{0,8},{8,0},{16,24},{24,16},{32,40},{40,32},{48,56},{56,48},{64,12... | collective-permute-start | bytes 294920 | tf_op jit(solution)/shard_map/ppermute | solution.py:465
  57.6 3.5 %shard_map.56.local_ref = f32[8,192,128]{2,1,0:T(8,128)S(1)} custom-call(s32[1]{0:T(128)} %bitcast.tm_ref, s32[1]{0:T(128)} %bitcast.1.z_ref, bf16[8,576,128]{2,1,0:T(8,128)(2,1)S(1)} %all-to-all-done.1.x_ref, bf16[192,256]{1,0:T(8,128)(2,1)S(1)} %collective-permute-done.5.near_ref, bf16[192,256]{1,0:T(8,128)(2,1)S(1)} %collective-permute-done.6.far_ref, ...), custom_call_target="tpu_custom_call" | custom-call | flops 1500000000 | bytes 10000000 | tf_op jit(solution)/shard_map/pallas_call | solution.py:47
  61.6 12.3 %all_to_all.15.x_ref = bf16[8,192,128]{2,1,0:T(8,128)(2,1)S(1)} all-to-all(bf16[8,192,128]{2,1,0:T(8,128)(2,1)S(1)} %shard_map.57), channel_id=1, replica_groups=mesh['tm'=4,'zh'=4,'zl'=2,'xy'=8] {'xy'}, dimensions={0} | all-to-all | bytes 786432 | tf_op jit(solution)/shard_map/all_to_all | solution.py:59
  73.9 0.9 %shard_map.58 = bf16[128,1536]{1,0:T(8,128)(2,1)} custom-call(bf16[8,192,128]{2,1,0:T(8,128)(2,1)S(1)} %all_to_all.15.x_ref), custom_call_target="tpu_custom_call" | custom-call | flops 300000000 | bytes 2000000 | tf_op jit(solution)/shard_map/pallas_call | solution.py:47
  (20 shorter events, 1.4 us)
Async XLA Ops:
  2.9 5.4 %copy-start.1 = (bf16[8,1536]{1,0:T(8,128)(2,1)S(1)}, bf16[8,1536]{1,0:T(8,128)(2,1)}, u32[]{:S(2)}) copy-start(bf16[8,1536]{1,0:T(8,128)(2,1)} %get-tuple-element.18.ours_ref) | copy-start | bytes 73732
  2.9 21.6 %all-to-all-start.1 = ((bf16[8,576,128]{2,1,0:T(8,128)(2,1)}), bf16[8,576,128]{2,1,0:T(8,128)(2,1)S(1)}, u32[]{:S(2)}, u32[]{:S(2)}) async-start(bf16[8,576,128]{2,1,0:T(8,128)(2,1)} %get-tuple-element.19), calls=%async_computation.1 | async-start | bytes 2359296 | tf_op jit(solution)/shard_map/all_to_all | solution.py:59
  8.3 3.9 %collective-permute-start = (bf16[8,1536]{1,0:T(8,128)(2,1)S(1)}, bf16[8,1536]{1,0:T(8,128)(2,1)S(1)}, u32[]{:S(2)}, u32[]{:S(2)}) collective-permute-start(bf16[8,1536]{1,0:T(8,128)(2,1)S(1)} %copy-done.1), channel_id=1, source_target_pairs={{0,8},{8,0},{16,24},{24,16},{32,40},{40,32},{48,56},{56,48},{64,12... | collective-permute-start | bytes 73736 | tf_op jit(solution)/shard_map/ppermute | solution.py:419
  12.3 8.7 %collective-permute-start.3 = (bf16[8,1536]{1,0:T(8,128)(2,1)S(1)}, bf16[8,1536]{1,0:T(8,128)(2,1)S(1)}, u32[]{:S(2)}, u32[]{:S(2)}) collective-permute-start(bf16[8,1536]{1,0:T(8,128)(2,1)S(1)} %shard_map.47.refs_0_), channel_id=1, source_target_pairs={{0,48},{8,56},{16,0},{24,8},{32,16},{40,24},{48,32},{56,40},{64,11... | collective-permute-start | bytes 73736 | tf_op jit(solution)/shard_map/ppermute | solution.py:423
  12.4 8.6 %collective-permute-start.2 = (bf16[8,1536]{1,0:T(8,128)(2,1)S(1)}, bf16[8,1536]{1,0:T(8,128)(2,1)S(1)}, u32[]{:S(2)}, u32[]{:S(2)}) collective-permute-start(bf16[8,1536]{1,0:T(8,128)(2,1)S(1)} %shard_map.47.refs_0_), channel_id=1, source_target_pairs={{0,32},{8,40},{16,48},{24,56},{32,0},{40,8},{48,16},{56,24},{64,96... | collective-permute-start | bytes 73736 | tf_op jit(solution)/shard_map/ppermute | solution.py:423
  18.3 4.7 %collective-permute-start.1 = (bf16[8,1536]{1,0:T(8,128)(2,1)S(1)}, bf16[8,1536]{1,0:T(8,128)(2,1)S(1)}, u32[]{:S(2)}, u32[]{:S(2)}) collective-permute-start(bf16[8,1536]{1,0:T(8,128)(2,1)S(1)} %shard_map.47.refs_0_), channel_id=1, source_target_pairs={{0,16},{8,24},{16,32},{24,40},{32,48},{40,56},{48,0},{56,8},{64,80... | collective-permute-start | bytes 73736 | tf_op jit(solution)/shard_map/ppermute | solution.py:423
  24.5 11.6 %all-to-all-start = ((bf16[8,32,192]{2,1,0:T(8,128)(2,1)}), bf16[8,32,192]{2,1,0:T(8,128)(2,1)S(1)}, u32[]{:S(2)}, u32[]{:S(2)}) async-start(bf16[8,32,192]{2,1,0:T(8,128)(2,1)} %shard_map.48), calls=%async_computation | async-start | bytes 262144 | tf_op jit(solution)/shard_map/all_to_all | solution.py:59
  29.9 9.2 %collective-permute-start.5 = (bf16[192,256]{1,0:T(8,128)(2,1)S(1)}, bf16[192,256]{1,0:T(8,128)(2,1)S(1)}, u32[]{:S(2)}, u32[]{:S(2)}) collective-permute-start(bf16[192,256]{1,0:T(8,128)(2,1)S(1)} %get-tuple-element.25), channel_id=1, source_target_pairs={{0,64},{128,192},{64,0},{192,128},{1,65},{129,193},{65,1},{193,129... | collective-permute-start | bytes 294920 | tf_op jit(solution)/shard_map/ppermute | solution.py:433
  30.0 9.0 %copy-start = (f32[3,3,3,1536]{3,2,1,0:T(4,128)S(1)}, f32[3,3,3,1536]{3,2,1,0:T(4,128)}, u32[]{:S(2)}) copy-start(f32[3,3,3,1536]{3,2,1,0:T(4,128)} %w_ref.1) | copy-start | bytes 497668
  30.0 9.1 %collective-permute-start.6 = (bf16[192,256]{1,0:T(8,128)(2,1)S(1)}, bf16[192,256]{1,0:T(8,128)(2,1)S(1)}, u32[]{:S(2)}, u32[]{:S(2)}) collective-permute-start(bf16[192,256]{1,0:T(8,128)(2,1)S(1)} %get-tuple-element.26), channel_id=1, source_target_pairs={{64,128},{128,64},{65,129},{129,65},{66,130},{130,66},{67,131},{13... | collective-permute-start | bytes 294920 | tf_op jit(solution)/shard_map/ppermute | solution.py:435
  37.9 4.2 %collective-permute-start.4 = (bf16[208,128]{1,0:T(8,128)(2,1)S(1)}, bf16[208,128]{1,0:T(8,128)(2,1)S(1)}, u32[]{:S(2)}, u32[]{:S(2)}) collective-permute-start(bf16[208,128]{1,0:T(8,128)(2,1)S(1)} %get-tuple-element.24), channel_id=1, source_target_pairs={{0,8},{8,0},{16,24},{24,16},{32,40},{40,32},{48,56},{56,48},{64,12... | collective-permute-start | bytes 159752 | tf_op jit(solution)/shard_map/ppermute | solution.py:444
  42.1 12.3 %collective-permute-start.9 = (bf16[400,128]{1,0:T(8,128)(2,1)S(1)}, bf16[400,128]{1,0:T(8,128)(2,1)S(1)}, u32[]{:S(2)}, u32[]{:S(2)}) collective-permute-start(bf16[400,128]{1,0:T(8,128)(2,1)S(1)} %get-tuple-element.29), channel_id=1, source_target_pairs={{0,56},{8,48},{16,8},{24,0},{32,24},{40,16},{48,40},{56,32},{64,72... | collective-permute-start | bytes 307208 | tf_op jit(solution)/shard_map/ppermute | solution.py:459
  44.8 9.6 %collective-permute-start.7 = (bf16[400,128]{1,0:T(8,128)(2,1)S(1)}, bf16[400,128]{1,0:T(8,128)(2,1)S(1)}, u32[]{:S(2)}, u32[]{:S(2)}) collective-permute-start(bf16[400,128]{1,0:T(8,128)(2,1)S(1)} %get-tuple-element.29), channel_id=1, source_target_pairs={{0,24},{8,16},{16,40},{24,32},{32,56},{40,48},{48,8},{56,0},{64,10... | collective-permute-start | bytes 307208 | tf_op jit(solution)/shard_map/ppermute | solution.py:459
  45.8 8.7 %collective-permute-start.8 = (bf16[208,128]{1,0:T(8,128)(2,1)S(1)}, bf16[208,128]{1,0:T(8,128)(2,1)S(1)}, u32[]{:S(2)}, u32[]{:S(2)}) collective-permute-start(bf16[208,128]{1,0:T(8,128)(2,1)S(1)} %get-tuple-element.28.refs_0_), channel_id=1, source_target_pairs={{0,32},{8,40},{16,48},{24,56},{32,0},{40,8},{48,16},{56,24},{64,96... | collective-permute-start | bytes 159752 | tf_op jit(solution)/shard_map/ppermute | solution.py:459
  54.5 6.6 %collective-permute-start.10 = (bf16[384,128]{1,0:T(8,128)(2,1)S(1)}, bf16[384,128]{1,0:T(8,128)(2,1)S(1)}, u32[]{:S(2)}, u32[]{:S(2)}) collective-permute-start(bf16[384,128]{1,0:T(8,128)(2,1)S(1)} %shard_map.55.ours_ref), channel_id=1, source_target_pairs={{0,8},{8,0},{16,24},{24,16},{32,40},{40,32},{48,56},{56,48},{64,12... | collective-permute-start | bytes 294920 | tf_op jit(solution)/shard_map/ppermute | solution.py:465

commit v13 on v12

--- a/solution.py
+++ b/solution.py
@@ -74,13 +74,10 @@
         store = pltpu.make_async_copy(turned.at[n], out_ref.at[:, rows, :], out_sems.at[n])
         store.start()
         stores.append(store)
-    shape = (SLOT, TOKENS)
-    token = lax.broadcasted_iota(jnp.int32, shape, 1)
-    agent = lax.broadcasted_iota(jnp.int32, shape, 0)
     width = COLUMNS // AGENT_DEV
-    pick = ((token % COLUMNS) // width == agent).astype(F32).astype(BF16)
-    sums = jnp.dot(pick, came[0], preferred_element_type=F32)
-    pooled_ref[...] = (sums * (1.0 / (FRAMES * width))).astype(BF16)
+    cells = came[0].astype(F32).reshape(FRAMES, AGENT_DEV, width, D)
+    means = jnp.sum(jnp.sum(cells, axis=0), axis=1) * (1.0 / (FRAMES * width))
+    pooled_ref[...] = jnp.concatenate([means, jnp.zeros_like(means)], axis=0).astype(BF16)
     for store in stores:
         store.wait()
 
@@ -98,13 +95,15 @@
 
 def route_kernel(z_ref, *refs):
     came, out_ref = refs[:PAIRS], refs[PAIRS]
-    rows = jnp.concatenate([ref[...].astype(F32) for ref in came], axis=0).astype(BF16)
-    shape = (PAIRS * SLOT, PAIRS * SLOT)
-    to = lax.broadcasted_iota(jnp.int32, shape, 0)
-    at = lax.broadcasted_iota(jnp.int32, shape, 1)
-    hop = (z_ref[0] // 2 + PAIRS - to // SLOT) % PAIRS
-    pick = (at == hop * SLOT + to % SLOT).astype(F32).astype(BF16)
-    agents = jnp.dot(pick, rows, preferred_element_type=F32).astype(BF16)
+    slots = [ref[...].astype(F32) for ref in came]
+    rows = []
+    for pair in range(PAIRS):
+        hop = (z_ref[0] // 2 + PAIRS - pair) % PAIRS
+        row = slots[0]
+        for n in range(1, PAIRS):
+            row = jnp.where(hop == n, slots[n], row)
+        rows.append(row)
+    agents = jnp.concatenate(rows, axis=0).astype(BF16)
     for tile in range(TILES):
         out_ref[tile] = agents[:, tile * GROUP : (tile + 1) * GROUP]
 

time: 76.2 us -> 76.1 us (level)
  no operation moved by 1% of the time
where the time goes in v13:
time: 76.1 us; the launch traced here: 74.6 us
  starting transfers between devices  30.7 us (40%)
  waiting for transfers between devices  18.5 us (24%)
  Pallas kernels  13.1 us (17%)
  blocking collectives  12.3 us (16%)
    pallas_call x13, Pallas kernels, call(): pl.pallas_call(kernel, out_shape=out_shape, in_specs=[SMEM] * len(scalars...  13.1 us
    all_to_all x1, blocking collectives, exchange(): return lax.all_to_all(x, axes, 0, 0)  12.3 us
    all_to_all x2, starting transfers between devices, exchange(): return lax.all_to_all(x, axes, 0, 0)  10.3 us
    ppermute x3, starting transfers between devices, body(): lax.ppermute(couple, LINE, along(lambda at, odd: same_side(at, n)))  8.7 us
    ppermute x3, starting transfers between devices, body(): lax.ppermute(moved, LINE, along(lambda at, odd: other_side(at, -n if odd...  6.78 us
    all_to_all x2, waiting for transfers between devices, exchange(): return lax.all_to_all(x, axes, 0, 0)  6.05 us
    ppermute x3, waiting for transfers between devices, body(): lax.ppermute(moved, LINE, along(lambda at, odd: other_side(at, -n if odd...  4.65 us
    ppermute x1, waiting for transfers between devices, body(): met = lax.ppermute(pooled, LINE, along(pair_plane))  3.72 us
  transfers between devices with their start and end apart: 13, of which 6 were waited for; matrix products, arithmetic and copies ran while one was open for 0% of the time, Pallas kernels for 12%

profile of v13, /device:TPU:96, one launch (start us, length us, event | category | flops | bytes accessed | tf_op | source)
XLA Modules:
  0.0 74.6 jit_solution(3670237659659453956)
XLA Ops:
  0.0 2.9 %shard_map.46 = (bf16[8,576,128]{2,1,0:T(8,128)(2,1)}, bf16[8,1536]{1,0:T(8,128)(2,1)}) custom-call(bf16[128,1536]{1,0:T(8,128)(2,1)} %bitcast.9, bf16[128,1536]{1,0:T(8,128)(2,1)} %bitcast.10, bf16[128,1536]{1,0:T(8,128)(2,1)} %bitcast.11), custom_call_target="tpu_custom_call" | custom-call | flops 900000000 | bytes 6000000 | tf_op jit(solution)/shard_map/pallas_call | solution.py:47
  2.9 5.4 %all-to-all-start.1 = ((bf16[8,576,128]{2,1,0:T(8,128)(2,1)}), bf16[8,576,128]{2,1,0:T(8,128)(2,1)S(1)}, u32[]{:S(2)}, u32[]{:S(2)}) async-start(bf16[8,576,128]{2,1,0:T(8,128)(2,1)} %get-tuple-element.19), calls=%async_computation.1 | async-start | bytes 2359296 | tf_op jit(solution)/shard_map/all_to_all | solution.py:59
  8.6 3.7 %collective-permute-done.theirs_ref = bf16[8,1536]{1,0:T(8,128)(2,1)S(1)} collective-permute-done((bf16[8,1536]{1,0:T(8,128)(2,1)S(1)}, bf16[8,1536]{1,0:T(8,128)(2,1)S(1)}, u32[]{:S(2)}, u32[]{:S(2)}) %collective-permute-start) | collective-permute-done | bytes 24608 | tf_op jit(solution)/shard_map/ppermute | solution.py:418
  12.4 5.9 %collective-permute-start.2 = (bf16[8,1536]{1,0:T(8,128)(2,1)S(1)}, bf16[8,1536]{1,0:T(8,128)(2,1)S(1)}, u32[]{:S(2)}, u32[]{:S(2)}) collective-permute-start(bf16[8,1536]{1,0:T(8,128)(2,1)S(1)} %shard_map.47.refs_0_), channel_id=1, source_target_pairs={{0,32},{8,40},{16,48},{24,56},{32,0},{40,8},{48,16},{56,24},{64,96... | collective-permute-start | bytes 73736 | tf_op jit(solution)/shard_map/ppermute | solution.py:422
  18.3 2.7 %collective-permute-start.1 = (bf16[8,1536]{1,0:T(8,128)(2,1)S(1)}, bf16[8,1536]{1,0:T(8,128)(2,1)S(1)}, u32[]{:S(2)}, u32[]{:S(2)}) collective-permute-start(bf16[8,1536]{1,0:T(8,128)(2,1)S(1)} %shard_map.47.refs_0_), channel_id=1, source_target_pairs={{0,16},{8,24},{16,32},{24,40},{32,48},{40,56},{48,0},{56,8},{64,80... | collective-permute-start | bytes 73736 | tf_op jit(solution)/shard_map/ppermute | solution.py:422
  21.0 2.0 %collective-permute-done.1.refs_1_ = bf16[8,1536]{1,0:T(8,128)(2,1)S(1)} collective-permute-done((bf16[8,1536]{1,0:T(8,128)(2,1)S(1)}, bf16[8,1536]{1,0:T(8,128)(2,1)S(1)}, u32[]{:S(2)}, u32[]{:S(2)}) %collective-permute-start.1) | collective-permute-done | bytes 24608 | tf_op jit(solution)/shard_map/ppermute | solution.py:422
  23.0 0.8 %shard_map.48 = bf16[8,32,192]{2,1,0:T(8,128)(2,1)} custom-call(s32[1]{0:T(128)} %bitcast.1.z_ref, bf16[8,1536]{1,0:T(8,128)(2,1)S(1)} %shard_map.47.refs_0_, bf16[8,1536]{1,0:T(8,128)(2,1)S(1)} %collective-permute-done.1.refs_1_, bf16[8,1536]{1,0:T(8,128)(2,1)S(1)} %collective-permute-done.2.refs_2_, bf16[8,1536]{1,0:T(8,128)(2,1)S(1)} %collective-permute-done.3.refs_3_), custom_call_target="tpu_custom_call" | custom-call | flops 300000000 | bytes 2000000 | tf_op jit(solution)/shard_map/pallas_call | solution.py:47
  23.8 0.7 %all-to-all-done.1.x_ref = bf16[8,576,128]{2,1,0:T(8,128)(2,1)S(1)} async-done(((bf16[8,576,128]{2,1,0:T(8,128)(2,1)}), bf16[8,576,128]{2,1,0:T(8,128)(2,1)S(1)}, u32[]{:S(2)}, u32[]{:S(2)}) %all-to-all-start.1) | async-done | bytes 1179680 | tf_op jit(solution)/shard_map/all_to_all | solution.py:59
  24.6 4.9 %all-to-all-start = ((bf16[8,32,192]{2,1,0:T(8,128)(2,1)}), bf16[8,32,192]{2,1,0:T(8,128)(2,1)S(1)}, u32[]{:S(2)}, u32[]{:S(2)}) async-start(bf16[8,32,192]{2,1,0:T(8,128)(2,1)} %shard_map.48), calls=%async_computation | async-start | bytes 262144 | tf_op jit(solution)/shard_map/all_to_all | solution.py:59
  29.9 0.8 %collective-permute-start.6 = (bf16[192,256]{1,0:T(8,128)(2,1)S(1)}, bf16[192,256]{1,0:T(8,128)(2,1)S(1)}, u32[]{:S(2)}, u32[]{:S(2)}) collective-permute-start(bf16[192,256]{1,0:T(8,128)(2,1)S(1)} %get-tuple-element.26), channel_id=1, source_target_pairs={{64,128},{128,64},{65,129},{129,65},{66,130},{130,66},{67,131},{13... | collective-permute-start | bytes 294920 | tf_op jit(solution)/shard_map/ppermute | solution.py:434
  30.7 5.3 %all-to-all-done.a_ref = bf16[8,32,192]{2,1,0:T(8,128)(2,1)S(1)} async-done(((bf16[8,32,192]{2,1,0:T(8,128)(2,1)}), bf16[8,32,192]{2,1,0:T(8,128)(2,1)S(1)}, u32[]{:S(2)}, u32[]{:S(2)}) %all-to-all-start) | async-done | bytes 98336 | tf_op jit(solution)/shard_map/all_to_all | solution.py:59
  36.0 1.8 %shard_map.51 = (f32[200,128]{1,0:T(8,128)S(1)}, bf16[208,128]{1,0:T(8,128)(2,1)S(1)}) custom-call(s32[1]{0:T(128)} %bitcast.tm_ref, s32[1]{0:T(128)} %bitcast.1.z_ref, bf16[8,32,192]{2,1,0:T(8,128)(2,1)S(1)} %all-to-all-done.a_ref, bf16[8,576,128]{2,1,0:T(8,128)(2,1)S(1)} %all-to-all-done.1.x_ref), custom_call_target="tpu_custom_call" | custom-call | flops 900000000 | bytes 6000000 | tf_op jit(solution)/shard_map/pallas_call | solution.py:47
  37.8 1.1 %collective-permute-start.4 = (bf16[208,128]{1,0:T(8,128)(2,1)S(1)}, bf16[208,128]{1,0:T(8,128)(2,1)S(1)}, u32[]{:S(2)}, u32[]{:S(2)}) collective-permute-start(bf16[208,128]{1,0:T(8,128)(2,1)S(1)} %get-tuple-element.24), channel_id=1, source_target_pairs={{0,8},{8,0},{16,24},{24,16},{32,40},{40,32},{48,56},{56,48},{64,12... | collective-permute-start | bytes 159752 | tf_op jit(solution)/shard_map/ppermute | solution.py:443
  39.1 1.0 %shard_map.53 = (bf16[192,128]{1,0:T(8,128)(2,1)S(1)}, bf16[192,128]{1,0:T(8,128)(2,1)S(1)}) custom-call(s32[1]{0:T(128)} %bitcast.tm_ref, s32[1]{0:T(128)} %bitcast.1.z_ref, bf16[8,576,128]{2,1,0:T(8,128)(2,1)S(1)} %all-to-all-done.1.x_ref, bf16[192,256]{1,0:T(8,128)(2,1)S(1)} %collective-permute-done.5.near_ref, ...), custom_call_target="tpu_custom_call" | custom-call | flops 300000000 | bytes 2000000 | tf_op jit(solution)/shard_map/pallas_call | solution.py:47
  40.0 2.0 %collective-permute-done.4.came_ref = bf16[208,128]{1,0:T(8,128)(2,1)S(1)} collective-permute-done((bf16[208,128]{1,0:T(8,128)(2,1)S(1)}, bf16[208,128]{1,0:T(8,128)(2,1)S(1)}, u32[]{:S(2)}, u32[]{:S(2)}) %collective-permute-start.4) | collective-permute-done | bytes 53280 | tf_op jit(solution)/shard_map/ppermute | solution.py:443
  42.0 2.6 %collective-permute-start.9 = (bf16[400,128]{1,0:T(8,128)(2,1)S(1)}, bf16[400,128]{1,0:T(8,128)(2,1)S(1)}, u32[]{:S(2)}, u32[]{:S(2)}) collective-permute-start(bf16[400,128]{1,0:T(8,128)(2,1)S(1)} %get-tuple-element.29), channel_id=1, source_target_pairs={{0,56},{8,48},{16,8},{24,0},{32,24},{40,16},{48,40},{56,32},{64,72... | collective-permute-start | bytes 307208 | tf_op jit(solution)/shard_map/ppermute | solution.py:458
  44.7 1.0 %collective-permute-start.7 = (bf16[400,128]{1,0:T(8,128)(2,1)S(1)}, bf16[400,128]{1,0:T(8,128)(2,1)S(1)}, u32[]{:S(2)}, u32[]{:S(2)}) collective-permute-start(bf16[400,128]{1,0:T(8,128)(2,1)S(1)} %get-tuple-element.29), channel_id=1, source_target_pairs={{0,24},{8,16},{16,40},{24,32},{32,56},{40,48},{48,8},{56,0},{64,10... | collective-permute-start | bytes 307208 | tf_op jit(solution)/shard_map/ppermute | solution.py:458
  45.7 3.2 %collective-permute-start.8 = (bf16[208,128]{1,0:T(8,128)(2,1)S(1)}, bf16[208,128]{1,0:T(8,128)(2,1)S(1)}, u32[]{:S(2)}, u32[]{:S(2)}) collective-permute-start(bf16[208,128]{1,0:T(8,128)(2,1)S(1)} %get-tuple-element.28.refs_0_), channel_id=1, source_target_pairs={{0,32},{8,40},{16,48},{24,56},{32,0},{40,8},{48,16},{56,24},{64,96... | collective-permute-start | bytes 159752 | tf_op jit(solution)/shard_map/ppermute | solution.py:458
  48.8 1.2 %shard_map.50 = (bf16[3,256,1024]{2,1,0:T(8,128)(2,1)S(1)}, f32[8,1024]{1,0:T(8,128)S(1)}) custom-call(bf16[8,32,192]{2,1,0:T(8,128)(2,1)S(1)} %all-to-all-done.a_ref, bf16[192,1024]{1,0:T(8,128)(2,1)S(1)} %get-tuple-element.20.q_ref), custom_call_target="tpu_custom_call" | custom-call | flops 600000000 | bytes 4000000 | tf_op jit(solution)/shard_map/pallas_call | solution.py:47
  50.0 4.6 %collective-permute-done.8.refs_2_ = bf16[208,128]{1,0:T(8,128)(2,1)S(1)} collective-permute-done((bf16[208,128]{1,0:T(8,128)(2,1)S(1)}, bf16[208,128]{1,0:T(8,128)(2,1)S(1)}, u32[]{:S(2)}, u32[]{:S(2)}) %collective-permute-start.8) | collective-permute-done | bytes 53280 | tf_op jit(solution)/shard_map/ppermute | solution.py:458
  54.8 2.7 %collective-permute-start.10 = (bf16[384,128]{1,0:T(8,128)(2,1)S(1)}, bf16[384,128]{1,0:T(8,128)(2,1)S(1)}, u32[]{:S(2)}, u32[]{:S(2)}) collective-permute-start(bf16[384,128]{1,0:T(8,128)(2,1)S(1)} %shard_map.55.ours_ref), channel_id=1, source_target_pairs={{0,8},{8,0},{16,24},{24,16},{32,40},{40,32},{48,56},{56,48},{64,12... | collective-permute-start | bytes 294920 | tf_op jit(solution)/shard_map/ppermute | solution.py:464
  57.5 3.5 %shard_map.56.local_ref = f32[8,192,128]{2,1,0:T(8,128)S(1)} custom-call(s32[1]{0:T(128)} %bitcast.tm_ref, s32[1]{0:T(128)} %bitcast.1.z_ref, bf16[8,576,128]{2,1,0:T(8,128)(2,1)S(1)} %all-to-all-done.1.x_ref, bf16[192,256]{1,0:T(8,128)(2,1)S(1)} %collective-permute-done.5.near_ref, bf16[192,256]{1,0:T(8,128)(2,1)S(1)} %collective-permute-done.6.far_ref, ...), custom_call_target="tpu_custom_call" | custom-call | flops 1500000000 | bytes 10000000 | tf_op jit(solution)/shard_map/pallas_call | solution.py:47
  61.5 12.3 %all_to_all.15.x_ref = bf16[8,192,128]{2,1,0:T(8,128)(2,1)S(1)} all-to-all(bf16[8,192,128]{2,1,0:T(8,128)(2,1)S(1)} %shard_map.57), channel_id=1, replica_groups=mesh['tm'=4,'zh'=4,'zl'=2,'xy'=8] {'xy'}, dimensions={0} | all-to-all | bytes 786432 | tf_op jit(solution)/shard_map/all_to_all | solution.py:59
  73.8 0.9 %shard_map.58 = bf16[128,1536]{1,0:T(8,128)(2,1)} custom-call(bf16[8,192,128]{2,1,0:T(8,128)(2,1)S(1)} %all_to_all.15.x_ref), custom_call_target="tpu_custom_call" | custom-call | flops 300000000 | bytes 2000000 | tf_op jit(solution)/shard_map/pallas_call | solution.py:47
  (20 shorter events, 1.4 us)
Async XLA Ops:
  2.9 5.4 %copy-start.1 = (bf16[8,1536]{1,0:T(8,128)(2,1)S(1)}, bf16[8,1536]{1,0:T(8,128)(2,1)}, u32[]{:S(2)}) copy-start(bf16[8,1536]{1,0:T(8,128)(2,1)} %get-tuple-element.18.ours_ref) | copy-start | bytes 73732
  2.9 21.6 %all-to-all-start.1 = ((bf16[8,576,128]{2,1,0:T(8,128)(2,1)}), bf16[8,576,128]{2,1,0:T(8,128)(2,1)S(1)}, u32[]{:S(2)}, u32[]{:S(2)}) async-start(bf16[8,576,128]{2,1,0:T(8,128)(2,1)} %get-tuple-element.19), calls=%async_computation.1 | async-start | bytes 2359296 | tf_op jit(solution)/shard_map/all_to_all | solution.py:59
  8.4 3.9 %collective-permute-start = (bf16[8,1536]{1,0:T(8,128)(2,1)S(1)}, bf16[8,1536]{1,0:T(8,128)(2,1)S(1)}, u32[]{:S(2)}, u32[]{:S(2)}) collective-permute-start(bf16[8,1536]{1,0:T(8,128)(2,1)S(1)} %copy-done.1), channel_id=1, source_target_pairs={{0,8},{8,0},{16,24},{24,16},{32,40},{40,32},{48,56},{56,48},{64,12... | collective-permute-start | bytes 73736 | tf_op jit(solution)/shard_map/ppermute | solution.py:418
  12.3 8.7 %collective-permute-start.3 = (bf16[8,1536]{1,0:T(8,128)(2,1)S(1)}, bf16[8,1536]{1,0:T(8,128)(2,1)S(1)}, u32[]{:S(2)}, u32[]{:S(2)}) collective-permute-start(bf16[8,1536]{1,0:T(8,128)(2,1)S(1)} %shard_map.47.refs_0_), channel_id=1, source_target_pairs={{0,48},{8,56},{16,0},{24,8},{32,16},{40,24},{48,32},{56,40},{64,11... | collective-permute-start | bytes 73736 | tf_op jit(solution)/shard_map/ppermute | solution.py:422
  12.4 8.6 %collective-permute-start.2 = (bf16[8,1536]{1,0:T(8,128)(2,1)S(1)}, bf16[8,1536]{1,0:T(8,128)(2,1)S(1)}, u32[]{:S(2)}, u32[]{:S(2)}) collective-permute-start(bf16[8,1536]{1,0:T(8,128)(2,1)S(1)} %shard_map.47.refs_0_), channel_id=1, source_target_pairs={{0,32},{8,40},{16,48},{24,56},{32,0},{40,8},{48,16},{56,24},{64,96... | collective-permute-start | bytes 73736 | tf_op jit(solution)/shard_map/ppermute | solution.py:422
  18.3 4.7 %collective-permute-start.1 = (bf16[8,1536]{1,0:T(8,128)(2,1)S(1)}, bf16[8,1536]{1,0:T(8,128)(2,1)S(1)}, u32[]{:S(2)}, u32[]{:S(2)}) collective-permute-start(bf16[8,1536]{1,0:T(8,128)(2,1)S(1)} %shard_map.47.refs_0_), channel_id=1, source_target_pairs={{0,16},{8,24},{16,32},{24,40},{32,48},{40,56},{48,0},{56,8},{64,80... | collective-permute-start | bytes 73736 | tf_op jit(solution)/shard_map/ppermute | solution.py:422
  24.6 11.5 %all-to-all-start = ((bf16[8,32,192]{2,1,0:T(8,128)(2,1)}), bf16[8,32,192]{2,1,0:T(8,128)(2,1)S(1)}, u32[]{:S(2)}, u32[]{:S(2)}) async-start(bf16[8,32,192]{2,1,0:T(8,128)(2,1)} %shard_map.48), calls=%async_computation | async-start | bytes 262144 | tf_op jit(solution)/shard_map/all_to_all | solution.py:59
  29.8 9.2 %collective-permute-start.5 = (bf16[192,256]{1,0:T(8,128)(2,1)S(1)}, bf16[192,256]{1,0:T(8,128)(2,1)S(1)}, u32[]{:S(2)}, u32[]{:S(2)}) collective-permute-start(bf16[192,256]{1,0:T(8,128)(2,1)S(1)} %get-tuple-element.25), channel_id=1, source_target_pairs={{0,64},{128,192},{64,0},{192,128},{1,65},{129,193},{65,1},{193,129... | collective-permute-start | bytes 294920 | tf_op jit(solution)/shard_map/ppermute | solution.py:432
  29.9 9.0 %copy-start = (f32[3,3,3,1536]{3,2,1,0:T(4,128)S(1)}, f32[3,3,3,1536]{3,2,1,0:T(4,128)}, u32[]{:S(2)}) copy-start(f32[3,3,3,1536]{3,2,1,0:T(4,128)} %w_ref.1) | copy-start | bytes 497668
  29.9 9.1 %collective-permute-start.6 = (bf16[192,256]{1,0:T(8,128)(2,1)S(1)}, bf16[192,256]{1,0:T(8,128)(2,1)S(1)}, u32[]{:S(2)}, u32[]{:S(2)}) collective-permute-start(bf16[192,256]{1,0:T(8,128)(2,1)S(1)} %get-tuple-element.26), channel_id=1, source_target_pairs={{64,128},{128,64},{65,129},{129,65},{66,130},{130,66},{67,131},{13... | collective-permute-start | bytes 294920 | tf_op jit(solution)/shard_map/ppermute | solution.py:434
  37.8 4.2 %collective-permute-start.4 = (bf16[208,128]{1,0:T(8,128)(2,1)S(1)}, bf16[208,128]{1,0:T(8,128)(2,1)S(1)}, u32[]{:S(2)}, u32[]{:S(2)}) collective-permute-start(bf16[208,128]{1,0:T(8,128)(2,1)S(1)} %get-tuple-element.24), channel_id=1, source_target_pairs={{0,8},{8,0},{16,24},{24,16},{32,40},{40,32},{48,56},{56,48},{64,12... | collective-permute-start | bytes 159752 | tf_op jit(solution)/shard_map/ppermute | solution.py:443
  42.0 12.6 %collective-permute-start.9 = (bf16[400,128]{1,0:T(8,128)(2,1)S(1)}, bf16[400,128]{1,0:T(8,128)(2,1)S(1)}, u32[]{:S(2)}, u32[]{:S(2)}) collective-permute-start(bf16[400,128]{1,0:T(8,128)(2,1)S(1)} %get-tuple-element.29), channel_id=1, source_target_pairs={{0,56},{8,48},{16,8},{24,0},{32,24},{40,16},{48,40},{56,32},{64,72... | collective-permute-start | bytes 307208 | tf_op jit(solution)/shard_map/ppermute | solution.py:458
  44.7 10.0 %collective-permute-start.7 = (bf16[400,128]{1,0:T(8,128)(2,1)S(1)}, bf16[400,128]{1,0:T(8,128)(2,1)S(1)}, u32[]{:S(2)}, u32[]{:S(2)}) collective-permute-start(bf16[400,128]{1,0:T(8,128)(2,1)S(1)} %get-tuple-element.29), channel_id=1, source_target_pairs={{0,24},{8,16},{16,40},{24,32},{32,56},{40,48},{48,8},{56,0},{64,10... | collective-permute-start | bytes 307208 | tf_op jit(solution)/shard_map/ppermute | solution.py:458
  45.7 9.0 %collective-permute-start.8 = (bf16[208,128]{1,0:T(8,128)(2,1)S(1)}, bf16[208,128]{1,0:T(8,128)(2,1)S(1)}, u32[]{:S(2)}, u32[]{:S(2)}) collective-permute-start(bf16[208,128]{1,0:T(8,128)(2,1)S(1)} %get-tuple-element.28.refs_0_), channel_id=1, source_target_pairs={{0,32},{8,40},{16,48},{24,56},{32,0},{40,8},{48,16},{56,24},{64,96... | collective-permute-start | bytes 159752 | tf_op jit(solution)/shard_map/ppermute | solution.py:458
  54.8 6.3 %collective-permute-start.10 = (bf16[384,128]{1,0:T(8,128)(2,1)S(1)}, bf16[384,128]{1,0:T(8,128)(2,1)S(1)}, u32[]{:S(2)}, u32[]{:S(2)}) collective-permute-start(bf16[384,128]{1,0:T(8,128)(2,1)S(1)} %shard_map.55.ours_ref), channel_id=1, source_target_pairs={{0,8},{8,0},{16,24},{24,16},{32,40},{40,32},{48,56},{56,48},{64,12... | collective-permute-start | bytes 294920 | tf_op jit(solution)/shard_map/ppermute | solution.py:464

commit v14 on v13

--- a/solution.py
+++ b/solution.py
@@ -173,8 +173,7 @@
 
 
 def comb_kernel(*refs):
-    parts, (kin_ref, out_ref) = refs[:PAIRS], refs[PAIRS:]
-    out_ref[GROUP:, :] = kin_ref[...]
+    parts, out_ref = refs[:PAIRS], refs[PAIRS]
     logs = [logs_of(part[GROUP : GROUP + STATS, :]) for part in parts]
     peak = logs[0]
     for log in logs[1:]:
@@ -318,15 +317,15 @@
         e_ref[h] = weights.astype(BF16)
 
 
-def mix_kernel(tm_ref, z_ref, e_ref, total_ref, ours_ref, theirs_ref, one_ref, three_ref, local_ref, out_ref):
+def mix_kernel(tm_ref, z_ref, e_ref, total_ref, ours_ref, theirs_ref, one_ref, three_ref, kin_ref, local_ref, out_ref):
     low, second = lax.rem(z_ref[0] // 2 + z_ref[0], 2) == 0, lax.rem(z_ref[0], 2) == 1
     odd = lax.rem(tm_ref[0], 2)
     first, last = z_ref[0] == (PLANES - 1) * odd, z_ref[0] == PLANES - 1 - odd
-    ours, theirs = ours_ref[:GROUP], theirs_ref[:GROUP]
+    ours, theirs = ours_ref[...], theirs_ref[...]
     values = jnp.concatenate(
         [jnp.where(low, ours, theirs), jnp.where(low, theirs, ours)], axis=1
     )
-    kin = theirs_ref[GROUP:].astype(F32)
+    kin = kin_ref[...].astype(F32)
     one, three = one_ref[GROUP + STATS :].astype(F32), three_ref[GROUP + STATS :].astype(F32)
     above, below = jnp.where(odd == 1, three, one), jnp.where(odd == 1, one, three)
     above = jnp.where(first, 0.0, jnp.where(second, kin, above))
@@ -457,10 +456,11 @@
         parts.append(
             lax.ppermute(moved, LINE, along(lambda at, odd: other_side(at, -n if odd else n)))
         )
+    kin = lax.ppermute(kin, LINE, along(pair_plane))
     local = call(
         conv_kernel, shape((TILES, GROUP, TOKENS), F32), 5.0, x, near, far, taps, scalars=where
     )
-    ours = call(comb_kernel, shape((2 * GROUP, HALF), BF16), 1.0, *parts, kin)
+    ours = call(comb_kernel, shape((GROUP, HALF), BF16), 1.0, *parts)
     theirs = lax.ppermute(ours, LINE, along(pair_plane))
     weights, totals = call(
         query_kernel,
@@ -479,6 +479,7 @@
         theirs,
         parts[1],
         parts[3],
+        kin,
         local,
         scalars=where,
     )

time: 76.1 us -> 78.3 us (1.029)
  the two profiles are of different devices: /device:TPU:96 before, /device:TPU:1 now
where the time goes in v14:
time: 78.3 us; the launch traced here: 77.9 us
  starting transfers between devices  40.5 us (52%)
  blocking collectives  14.6 us (19%)
  Pallas kernels  13.1 us (17%)
  waiting for transfers between devices  9.62 us (12%)
    all_to_all x1, blocking collectives, exchange(): return lax.all_to_all(x, axes, 0, 0)  14.6 us
    pallas_call x13, Pallas kernels, call(): pl.pallas_call(kernel, out_shape=out_shape, in_specs=[SMEM] * len(scalars...  13.1 us
    all_to_all x2, starting transfers between devices, exchange(): return lax.all_to_all(x, axes, 0, 0)  11.1 us
    ppermute x3, starting transfers between devices, body(): lax.ppermute(moved, LINE, along(lambda at, odd: other_side(at, -n if odd...  8.39 us
    ppermute x3, starting transfers between devices, body(): lax.ppermute(couple, LINE, along(lambda at, odd: same_side(at, n)))  6.15 us
    ppermute x1, starting transfers between devices, body(): met = lax.ppermute(pooled, LINE, along(pair_plane))  5.66 us
    ppermute x1, starting transfers between devices, body(): far = lax.ppermute(far, 'tm', pairs + [(b, a) for a, b in pairs])  4.4 us
    ppermute x1, starting transfers between devices, body(): near = lax.ppermute(near, 'tm', pairs + [(b, a) for a, b in pairs])  3.55 us
  transfers between devices with their start and end apart: 14, of which 7 were waited for; matrix products, arithmetic and copies ran while one was open for 0% of the time, Pallas kernels for 11%

profile of v14, /device:TPU:1, one launch (start us, length us, event | category | flops | bytes accessed | tf_op | source)
XLA Modules:
  0.0 77.9 jit_solution(6628504166322307449)
XLA Ops:
  0.0 2.9 %shard_map.46 = (bf16[8,576,128]{2,1,0:T(8,128)(2,1)}, bf16[8,1536]{1,0:T(8,128)(2,1)}) custom-call(bf16[128,1536]{1,0:T(8,128)(2,1)} %bitcast.9, bf16[128,1536]{1,0:T(8,128)(2,1)} %bitcast.10, bf16[128,1536]{1,0:T(8,128)(2,1)} %bitcast.11), custom_call_target="tpu_custom_call" | custom-call | flops 900000000 | bytes 6000000 | tf_op jit(solution)/shard_map/pallas_call | solution.py:47
  2.9 5.9 %all-to-all-start.1 = ((bf16[8,576,128]{2,1,0:T(8,128)(2,1)}), bf16[8,576,128]{2,1,0:T(8,128)(2,1)S(1)}, u32[]{:S(2)}, u32[]{:S(2)}) async-start(bf16[8,576,128]{2,1,0:T(8,128)(2,1)} %get-tuple-element.19), calls=%async_computation.1 | async-start | bytes 2359296 | tf_op jit(solution)/shard_map/all_to_all | solution.py:59
  8.9 5.7 %collective-permute-start = (bf16[8,1536]{1,0:T(8,128)(2,1)S(1)}, bf16[8,1536]{1,0:T(8,128)(2,1)S(1)}, u32[]{:S(2)}, u32[]{:S(2)}) collective-permute-start(bf16[8,1536]{1,0:T(8,128)(2,1)S(1)} %copy-done.1), channel_id=1, source_target_pairs={{0,8},{8,0},{16,24},{24,16},{32,40},{40,32},{48,56},{56,48},{64,12... | collective-permute-start | bytes 73736 | tf_op jit(solution)/shard_map/ppermute | solution.py:417
  14.6 1.5 %collective-permute-done.theirs_ref = bf16[8,1536]{1,0:T(8,128)(2,1)S(1)} collective-permute-done((bf16[8,1536]{1,0:T(8,128)(2,1)S(1)}, bf16[8,1536]{1,0:T(8,128)(2,1)S(1)}, u32[]{:S(2)}, u32[]{:S(2)}) %collective-permute-start) | collective-permute-done | bytes 24608 | tf_op jit(solution)/shard_map/ppermute | solution.py:417
  16.1 1.7 %collective-permute-start.3 = (bf16[8,1536]{1,0:T(8,128)(2,1)S(1)}, bf16[8,1536]{1,0:T(8,128)(2,1)S(1)}, u32[]{:S(2)}, u32[]{:S(2)}) collective-permute-start(bf16[8,1536]{1,0:T(8,128)(2,1)S(1)} %shard_map.47.refs_0_), channel_id=1, source_target_pairs={{0,48},{8,56},{16,0},{24,8},{32,16},{40,24},{48,32},{56,40},{64,11... | collective-permute-start | bytes 73736 | tf_op jit(solution)/shard_map/ppermute | solution.py:421
  17.8 2.2 %collective-permute-start.2 = (bf16[8,1536]{1,0:T(8,128)(2,1)S(1)}, bf16[8,1536]{1,0:T(8,128)(2,1)S(1)}, u32[]{:S(2)}, u32[]{:S(2)}) collective-permute-start(bf16[8,1536]{1,0:T(8,128)(2,1)S(1)} %shard_map.47.refs_0_), channel_id=1, source_target_pairs={{0,32},{8,40},{16,48},{24,56},{32,0},{40,8},{48,16},{56,24},{64,96... | collective-permute-start | bytes 73736 | tf_op jit(solution)/shard_map/ppermute | solution.py:421
  20.0 2.3 %collective-permute-start.1 = (bf16[8,1536]{1,0:T(8,128)(2,1)S(1)}, bf16[8,1536]{1,0:T(8,128)(2,1)S(1)}, u32[]{:S(2)}, u32[]{:S(2)}) collective-permute-start(bf16[8,1536]{1,0:T(8,128)(2,1)S(1)} %shard_map.47.refs_0_), channel_id=1, source_target_pairs={{0,16},{8,24},{16,32},{24,40},{32,48},{40,56},{48,0},{56,8},{64,80... | collective-permute-start | bytes 73736 | tf_op jit(solution)/shard_map/ppermute | solution.py:421
  22.2 2.1 %collective-permute-done.2.refs_2_ = bf16[8,1536]{1,0:T(8,128)(2,1)S(1)} collective-permute-done((bf16[8,1536]{1,0:T(8,128)(2,1)S(1)}, bf16[8,1536]{1,0:T(8,128)(2,1)S(1)}, u32[]{:S(2)}, u32[]{:S(2)}) %collective-permute-start.2) | collective-permute-done | bytes 24608 | tf_op jit(solution)/shard_map/ppermute | solution.py:421
  24.9 0.8 shard_map.48
  25.6 5.2 %all-to-all-start = ((bf16[8,32,192]{2,1,0:T(8,128)(2,1)}), bf16[8,32,192]{2,1,0:T(8,128)(2,1)S(1)}, u32[]{:S(2)}, u32[]{:S(2)}) async-start(bf16[8,32,192]{2,1,0:T(8,128)(2,1)} %shard_map.48), calls=%async_computation | async-start | bytes 262144 | tf_op jit(solution)/shard_map/all_to_all | solution.py:59
  31.2 3.5 %collective-permute-start.5 = (bf16[192,256]{1,0:T(8,128)(2,1)S(1)}, bf16[192,256]{1,0:T(8,128)(2,1)S(1)}, u32[]{:S(2)}, u32[]{:S(2)}) collective-permute-start(bf16[192,256]{1,0:T(8,128)(2,1)S(1)} %get-tuple-element.25), channel_id=1, source_target_pairs={{0,64},{128,192},{64,0},{192,128},{1,65},{129,193},{65,1},{193,129... | collective-permute-start | bytes 294920 | tf_op jit(solution)/shard_map/ppermute | solution.py:431
  34.7 4.4 %collective-permute-start.6 = (bf16[192,256]{1,0:T(8,128)(2,1)S(1)}, bf16[192,256]{1,0:T(8,128)(2,1)S(1)}, u32[]{:S(2)}, u32[]{:S(2)}) collective-permute-start(bf16[192,256]{1,0:T(8,128)(2,1)S(1)} %get-tuple-element.26), channel_id=1, source_target_pairs={{64,128},{128,64},{65,129},{129,65},{66,130},{130,66},{67,131},{13... | collective-permute-start | bytes 294920 | tf_op jit(solution)/shard_map/ppermute | solution.py:433
  39.2 1.8 %shard_map.51 = (f32[200,128]{1,0:T(8,128)S(1)}, bf16[208,128]{1,0:T(8,128)(2,1)S(1)}) custom-call(s32[1]{0:T(128)} %bitcast.tm_ref, s32[1]{0:T(128)} %bitcast.1.z_ref, bf16[8,32,192]{2,1,0:T(8,128)(2,1)S(1)} %all-to-all-done.a_ref, bf16[8,576,128]{2,1,0:T(8,128)(2,1)S(1)} %all-to-all-done.1.x_ref), custom_call_target="tpu_custom_call" | custom-call | flops 900000000 | bytes 6000000 | tf_op jit(solution)/shard_map/pallas_call | solution.py:47
  40.9 1.1 %collective-permute-start.4 = (bf16[208,128]{1,0:T(8,128)(2,1)S(1)}, bf16[208,128]{1,0:T(8,128)(2,1)S(1)}, u32[]{:S(2)}, u32[]{:S(2)}) collective-permute-start(bf16[208,128]{1,0:T(8,128)(2,1)S(1)} %get-tuple-element.24), channel_id=1, source_target_pairs={{0,8},{8,0},{16,24},{24,16},{32,40},{40,32},{48,56},{56,48},{64,12... | collective-permute-start | bytes 159752 | tf_op jit(solution)/shard_map/ppermute | solution.py:442
  42.3 0.9 %shard_map.53 = (bf16[192,128]{1,0:T(8,128)(2,1)S(1)}, bf16[192,128]{1,0:T(8,128)(2,1)S(1)}) custom-call(s32[1]{0:T(128)} %bitcast.tm_ref, s32[1]{0:T(128)} %bitcast.1.z_ref, bf16[8,576,128]{2,1,0:T(8,128)(2,1)S(1)} %all-to-all-done.1.x_ref, bf16[192,256]{1,0:T(8,128)(2,1)S(1)} %collective-permute-done.5.near_ref, ...), custom_call_target="tpu_custom_call" | custom-call | flops 300000000 | bytes 2000000 | tf_op jit(solution)/shard_map/pallas_call | solution.py:47
  43.2 2.0 %collective-permute-done.4.came_ref = bf16[208,128]{1,0:T(8,128)(2,1)S(1)} collective-permute-done((bf16[208,128]{1,0:T(8,128)(2,1)S(1)}, bf16[208,128]{1,0:T(8,128)(2,1)S(1)}, u32[]{:S(2)}, u32[]{:S(2)}) %collective-permute-start.4) | collective-permute-done | bytes 53280 | tf_op jit(solution)/shard_map/ppermute | solution.py:442
  45.3 4.5 %collective-permute-start.7 = (bf16[400,128]{1,0:T(8,128)(2,1)S(1)}, bf16[400,128]{1,0:T(8,128)(2,1)S(1)}, u32[]{:S(2)}, u32[]{:S(2)}) collective-permute-start(bf16[400,128]{1,0:T(8,128)(2,1)S(1)} %get-tuple-element.29), channel_id=1, source_target_pairs={{0,24},{8,16},{16,40},{24,32},{32,56},{40,48},{48,8},{56,0},{64,10... | collective-permute-start | bytes 307208 | tf_op jit(solution)/shard_map/ppermute | solution.py:457
  49.8 3.8 %collective-permute-start.8 = (bf16[208,128]{1,0:T(8,128)(2,1)S(1)}, bf16[208,128]{1,0:T(8,128)(2,1)S(1)}, u32[]{:S(2)}, u32[]{:S(2)}) collective-permute-start(bf16[208,128]{1,0:T(8,128)(2,1)S(1)} %get-tuple-element.28.refs_0_), channel_id=1, source_target_pairs={{0,32},{8,40},{16,48},{24,56},{32,0},{40,8},{48,16},{56,24},{64,96... | collective-permute-start | bytes 159752 | tf_op jit(solution)/shard_map/ppermute | solution.py:457
  53.7 1.2 %shard_map.50 = (bf16[3,256,1024]{2,1,0:T(8,128)(2,1)S(1)}, f32[8,1024]{1,0:T(8,128)S(1)}) custom-call(bf16[8,32,192]{2,1,0:T(8,128)(2,1)S(1)} %all-to-all-done.a_ref, bf16[192,1024]{1,0:T(8,128)(2,1)S(1)} %get-tuple-element.20.q_ref), custom_call_target="tpu_custom_call" | custom-call | flops 600000000 | bytes 4000000 | tf_op jit(solution)/shard_map/pallas_call | solution.py:47
  55.0 2.8 %collective-permute-done.8.refs_2_ = bf16[208,128]{1,0:T(8,128)(2,1)S(1)} collective-permute-done((bf16[208,128]{1,0:T(8,128)(2,1)S(1)}, bf16[208,128]{1,0:T(8,128)(2,1)S(1)}, u32[]{:S(2)}, u32[]{:S(2)}) %collective-permute-start.8) | collective-permute-done | bytes 53280 | tf_op jit(solution)/shard_map/ppermute | solution.py:457
  58.0 3.5 %shard_map.56.local_ref = f32[8,192,128]{2,1,0:T(8,128)S(1)} custom-call(s32[1]{0:T(128)} %bitcast.tm_ref, s32[1]{0:T(128)} %bitcast.1.z_ref, bf16[8,576,128]{2,1,0:T(8,128)(2,1)S(1)} %all-to-all-done.1.x_ref, bf16[192,256]{1,0:T(8,128)(2,1)S(1)} %collective-permute-done.5.near_ref, bf16[192,256]{1,0:T(8,128)(2,1)S(1)} %collective-permute-done.6.far_ref, ...), custom_call_target="tpu_custom_call" | custom-call | flops 1500000000 | bytes 10000000 | tf_op jit(solution)/shard_map/pallas_call | solution.py:47
  61.5 0.6 collective-permute-done.10.theirs_ref
  62.5 14.6 %all_to_all.15.x_ref = bf16[8,192,128]{2,1,0:T(8,128)(2,1)S(1)} all-to-all(bf16[8,192,128]{2,1,0:T(8,128)(2,1)S(1)} %shard_map.57), channel_id=1, replica_groups=mesh['tm'=4,'zh'=4,'zl'=2,'xy'=8] {'xy'}, dimensions={0} | all-to-all | bytes 786432 | tf_op jit(solution)/shard_map/all_to_all | solution.py:59
  77.1 0.9 %shard_map.58 = bf16[128,1536]{1,0:T(8,128)(2,1)} custom-call(bf16[8,192,128]{2,1,0:T(8,128)(2,1)S(1)} %all_to_all.15.x_ref), custom_call_target="tpu_custom_call" | custom-call | flops 300000000 | bytes 2000000 | tf_op jit(solution)/shard_map/pallas_call | solution.py:47
  (22 shorter events, 2.0 us)
Async XLA Ops:
  2.9 6.0 %copy-start.1 = (bf16[8,1536]{1,0:T(8,128)(2,1)S(1)}, bf16[8,1536]{1,0:T(8,128)(2,1)}, u32[]{:S(2)}) copy-start(bf16[8,1536]{1,0:T(8,128)(2,1)} %get-tuple-element.18.ours_ref) | copy-start | bytes 73732
  2.9 22.7 %all-to-all-start.1 = ((bf16[8,576,128]{2,1,0:T(8,128)(2,1)}), bf16[8,576,128]{2,1,0:T(8,128)(2,1)S(1)}, u32[]{:S(2)}, u32[]{:S(2)}) async-start(bf16[8,576,128]{2,1,0:T(8,128)(2,1)} %get-tuple-element.19), calls=%async_computation.1 | async-start | bytes 2359296 | tf_op jit(solution)/shard_map/all_to_all | solution.py:59
  8.9 7.2 %collective-permute-start = (bf16[8,1536]{1,0:T(8,128)(2,1)S(1)}, bf16[8,1536]{1,0:T(8,128)(2,1)S(1)}, u32[]{:S(2)}, u32[]{:S(2)}) collective-permute-start(bf16[8,1536]{1,0:T(8,128)(2,1)S(1)} %copy-done.1), channel_id=1, source_target_pairs={{0,8},{8,0},{16,24},{24,16},{32,40},{40,32},{48,56},{56,48},{64,12... | collective-permute-start | bytes 73736 | tf_op jit(solution)/shard_map/ppermute | solution.py:417
  16.1 6.2 %collective-permute-start.3 = (bf16[8,1536]{1,0:T(8,128)(2,1)S(1)}, bf16[8,1536]{1,0:T(8,128)(2,1)S(1)}, u32[]{:S(2)}, u32[]{:S(2)}) collective-permute-start(bf16[8,1536]{1,0:T(8,128)(2,1)S(1)} %shard_map.47.refs_0_), channel_id=1, source_target_pairs={{0,48},{8,56},{16,0},{24,8},{32,16},{40,24},{48,32},{56,40},{64,11... | collective-permute-start | bytes 73736 | tf_op jit(solution)/shard_map/ppermute | solution.py:421
  17.8 6.6 %collective-permute-start.2 = (bf16[8,1536]{1,0:T(8,128)(2,1)S(1)}, bf16[8,1536]{1,0:T(8,128)(2,1)S(1)}, u32[]{:S(2)}, u32[]{:S(2)}) collective-permute-start(bf16[8,1536]{1,0:T(8,128)(2,1)S(1)} %shard_map.47.refs_0_), channel_id=1, source_target_pairs={{0,32},{8,40},{16,48},{24,56},{32,0},{40,8},{48,16},{56,24},{64,96... | collective-permute-start | bytes 73736 | tf_op jit(solution)/shard_map/ppermute | solution.py:421
  20.0 4.9 %collective-permute-start.1 = (bf16[8,1536]{1,0:T(8,128)(2,1)S(1)}, bf16[8,1536]{1,0:T(8,128)(2,1)S(1)}, u32[]{:S(2)}, u32[]{:S(2)}) collective-permute-start(bf16[8,1536]{1,0:T(8,128)(2,1)S(1)} %shard_map.47.refs_0_), channel_id=1, source_target_pairs={{0,16},{8,24},{16,32},{24,40},{32,48},{40,56},{48,0},{56,8},{64,80... | collective-permute-start | bytes 73736 | tf_op jit(solution)/shard_map/ppermute | solution.py:421
  25.6 13.5 %all-to-all-start = ((bf16[8,32,192]{2,1,0:T(8,128)(2,1)}), bf16[8,32,192]{2,1,0:T(8,128)(2,1)S(1)}, u32[]{:S(2)}, u32[]{:S(2)}) async-start(bf16[8,32,192]{2,1,0:T(8,128)(2,1)} %shard_map.48), calls=%async_computation | async-start | bytes 262144 | tf_op jit(solution)/shard_map/all_to_all | solution.py:59
  31.2 11.0 %collective-permute-start.5 = (bf16[192,256]{1,0:T(8,128)(2,1)S(1)}, bf16[192,256]{1,0:T(8,128)(2,1)S(1)}, u32[]{:S(2)}, u32[]{:S(2)}) collective-permute-start(bf16[192,256]{1,0:T(8,128)(2,1)S(1)} %get-tuple-element.25), channel_id=1, source_target_pairs={{0,64},{128,192},{64,0},{192,128},{1,65},{129,193},{65,1},{193,129... | collective-permute-start | bytes 294920 | tf_op jit(solution)/shard_map/ppermute | solution.py:431
  34.7 7.3 %copy-start = (f32[3,3,3,1536]{3,2,1,0:T(4,128)S(1)}, f32[3,3,3,1536]{3,2,1,0:T(4,128)}, u32[]{:S(2)}) copy-start(f32[3,3,3,1536]{3,2,1,0:T(4,128)} %w_ref.1) | copy-start | bytes 497668
  34.7 7.6 %collective-permute-start.6 = (bf16[192,256]{1,0:T(8,128)(2,1)S(1)}, bf16[192,256]{1,0:T(8,128)(2,1)S(1)}, u32[]{:S(2)}, u32[]{:S(2)}) collective-permute-start(bf16[192,256]{1,0:T(8,128)(2,1)S(1)} %get-tuple-element.26), channel_id=1, source_target_pairs={{64,128},{128,64},{65,129},{129,65},{66,130},{130,66},{67,131},{13... | collective-permute-start | bytes 294920 | tf_op jit(solution)/shard_map/ppermute | solution.py:433
  40.9 4.3 %collective-permute-start.4 = (bf16[208,128]{1,0:T(8,128)(2,1)S(1)}, bf16[208,128]{1,0:T(8,128)(2,1)S(1)}, u32[]{:S(2)}, u32[]{:S(2)}) collective-permute-start(bf16[208,128]{1,0:T(8,128)(2,1)S(1)} %get-tuple-element.24), channel_id=1, source_target_pairs={{0,8},{8,0},{16,24},{24,16},{32,40},{40,32},{48,56},{56,48},{64,12... | collective-permute-start | bytes 159752 | tf_op jit(solution)/shard_map/ppermute | solution.py:442
  45.3 12.5 %collective-permute-start.9 = (bf16[400,128]{1,0:T(8,128)(2,1)S(1)}, bf16[400,128]{1,0:T(8,128)(2,1)S(1)}, u32[]{:S(2)}, u32[]{:S(2)}) collective-permute-start(bf16[400,128]{1,0:T(8,128)(2,1)S(1)} %get-tuple-element.29), channel_id=1, source_target_pairs={{0,56},{8,48},{16,8},{24,0},{32,24},{40,16},{48,40},{56,32},{64,72... | collective-permute-start | bytes 307208 | tf_op jit(solution)/shard_map/ppermute | solution.py:457
  45.3 12.4 %collective-permute-start.7 = (bf16[400,128]{1,0:T(8,128)(2,1)S(1)}, bf16[400,128]{1,0:T(8,128)(2,1)S(1)}, u32[]{:S(2)}, u32[]{:S(2)}) collective-permute-start(bf16[400,128]{1,0:T(8,128)(2,1)S(1)} %get-tuple-element.29), channel_id=1, source_target_pairs={{0,24},{8,16},{16,40},{24,32},{32,56},{40,48},{48,8},{56,0},{64,10... | collective-permute-start | bytes 307208 | tf_op jit(solution)/shard_map/ppermute | solution.py:457
  49.8 8.0 %collective-permute-start.8 = (bf16[208,128]{1,0:T(8,128)(2,1)S(1)}, bf16[208,128]{1,0:T(8,128)(2,1)S(1)}, u32[]{:S(2)}, u32[]{:S(2)}) collective-permute-start(bf16[208,128]{1,0:T(8,128)(2,1)S(1)} %get-tuple-element.28.refs_0_), channel_id=1, source_target_pairs={{0,32},{8,40},{16,48},{24,56},{32,0},{40,8},{48,16},{56,24},{64,96... | collective-permute-start | bytes 159752 | tf_op jit(solution)/shard_map/ppermute | solution.py:457
  54.9 6.6 %collective-permute-start.11 = (bf16[192,128]{1,0:T(8,128)(2,1)S(1)}, bf16[192,128]{1,0:T(8,128)(2,1)S(1)}, u32[]{:S(2)}, u32[]{:S(2)}) collective-permute-start(bf16[192,128]{1,0:T(8,128)(2,1)S(1)} %get-tuple-element.30), channel_id=1, source_target_pairs={{0,8},{8,0},{16,24},{24,16},{32,40},{40,32},{48,56},{56,48},{64,12... | collective-permute-start | bytes 147464 | tf_op jit(solution)/shard_map/ppermute | solution.py:459
  57.8 4.2 %collective-permute-start.10 = (bf16[192,128]{1,0:T(8,128)(2,1)S(1)}, bf16[192,128]{1,0:T(8,128)(2,1)S(1)}, u32[]{:S(2)}, u32[]{:S(2)}) collective-permute-start(bf16[192,128]{1,0:T(8,128)(2,1)S(1)} %shard_map.55.ours_ref), channel_id=1, source_target_pairs={{0,8},{8,0},{16,24},{24,16},{32,40},{40,32},{48,56},{56,48},{64,12... | collective-permute-start | bytes 147464 | tf_op jit(solution)/shard_map/ppermute | solution.py:464

commit v15 on v14

--- a/solution.py
+++ b/solution.py
@@ -19,7 +19,6 @@
 TILES = 8
 AGENTS = 256
 SLOT = 8
-HALF = AGENTS // 2
 GROUP_HEADS = HEADS // TILES
 GROUP = GROUP_HEADS * HEAD_DIM
 K_ROW = GROUP
@@ -108,8 +107,7 @@
         out_ref[tile] = agents[:, tile * GROUP : (tile + 1) * GROUP]
 
 
-def agent_kernel(tm_ref, z_ref, a_ref, x_ref, keep_ref, send_ref):
-    low = lax.rem(z_ref[0] // 2 + z_ref[0], 2) == 0
+def agent_kernel(a_ref, x_ref, keep_ref, send_ref):
     everyone = a_ref[...].reshape(AGENTS, GROUP)
     columns = []
     logs = []
@@ -131,11 +129,9 @@
     for h, log in enumerate(logs):
         stats = jnp.where(lane == h, log, stats)
     part = jnp.concatenate(columns + [stats], axis=1).T
-    near, far = part[:, :HALF], part[:, HALF:]
-    keep_ref[...] = jnp.where(low, near, far)[: GROUP + 8]
-    away = jnp.where(low, far, near)
-    send_ref[:GROUP] = away[:GROUP].astype(BF16)
-    send_ref[GROUP:] = pieces_of(away[GROUP : GROUP + GROUP_HEADS])
+    keep_ref[...] = part[: GROUP + 8]
+    send_ref[:GROUP] = part[:GROUP].astype(BF16)
+    send_ref[GROUP:] = pieces_of(part[GROUP : GROUP + GROUP_HEADS])
 
 
 def pieces_of(logs):
@@ -144,7 +140,7 @@
         short = logs.astype(BF16).astype(F32)
         logs = logs - short
         pieces.append(short)
-    pieces.append(jnp.zeros((STATS - 3 * GROUP_HEADS, HALF), F32))
+    pieces.append(jnp.zeros((STATS - 3 * GROUP_HEADS, AGENTS), F32))
     return jnp.concatenate(pieces, axis=0).astype(BF16)
 
 
@@ -169,7 +165,9 @@
         long_ref[rows, :] = part
     out_ref[GROUP:, :] = stats
     long_ref[GROUP : GROUP + STATS, :] = stats
-    long_ref[GROUP + STATS :, :] = cross_ref[...]
+    for n in range(2):
+        lanes = slice(n * TOKENS, (n + 1) * TOKENS)
+        long_ref[GROUP + STATS :, lanes] = cross_ref[n * GROUP // 2 : (n + 1) * GROUP // 2, :]
 
 
 def comb_kernel(*refs):
@@ -317,22 +315,23 @@
         e_ref[h] = weights.astype(BF16)
 
 
-def mix_kernel(tm_ref, z_ref, e_ref, total_ref, ours_ref, theirs_ref, one_ref, three_ref, kin_ref, local_ref, out_ref):
-    low, second = lax.rem(z_ref[0] // 2 + z_ref[0], 2) == 0, lax.rem(z_ref[0], 2) == 1
+def mix_kernel(tm_ref, z_ref, e_ref, total_ref, values_ref, one_ref, three_ref, kin_ref, local_ref, out_ref):
+    second = lax.rem(z_ref[0], 2) == 1
     odd = lax.rem(tm_ref[0], 2)
     first, last = z_ref[0] == (PLANES - 1) * odd, z_ref[0] == PLANES - 1 - odd
-    ours, theirs = ours_ref[...], theirs_ref[...]
-    values = jnp.concatenate(
-        [jnp.where(low, ours, theirs), jnp.where(low, theirs, ours)], axis=1
-    )
     kin = kin_ref[...].astype(F32)
-    one, three = one_ref[GROUP + STATS :].astype(F32), three_ref[GROUP + STATS :].astype(F32)
+    one, three = (
+        jnp.concatenate(
+            [ref[GROUP + STATS :, :TOKENS], ref[GROUP + STATS :, TOKENS:]], axis=0
+        ).astype(F32)
+        for ref in (one_ref, three_ref)
+    )
     above, below = jnp.where(odd == 1, three, one), jnp.where(odd == 1, one, three)
     above = jnp.where(first, 0.0, jnp.where(second, kin, above))
     below = jnp.where(last, 0.0, jnp.where(second, below, kin))
     for h in range(GROUP_HEADS):
         rows = slice(h * HEAD_DIM, (h + 1) * HEAD_DIM)
-        mixed = jnp.dot(values[rows], e_ref[h], preferred_element_type=F32)
+        mixed = jnp.dot(values_ref[rows, :], e_ref[h], preferred_element_type=F32)
         mixed = mixed / total_ref[h : h + 1, :]
         for s in range(TILES):
             cells = mixed[:, s * TOKENS : (s + 1) * TOKENS] + local_ref[s, rows, :]
@@ -433,18 +432,17 @@
     far = lax.ppermute(far, "tm", pairs + [(b, a) for a, b in pairs])
     keep, send = call(
         agent_kernel,
-        (shape((GROUP + 8, HALF), F32), shape((GROUP + STATS, HALF), BF16)),
+        (shape((GROUP + 8, AGENTS), F32), shape((GROUP + STATS, AGENTS), BF16)),
         3.0,
         agents,
         x,
-        scalars=where,
     )
     theirs = lax.ppermute(send, LINE, along(pair_plane))
     row = shape((GROUP, TOKENS), BF16)
     cross, kin = call(rim_kernel, (row, row), 1.0, x, near, far, taps, scalars=where)
     blended, longer = call(
         blend_kernel,
-        (shape((GROUP + STATS, HALF), BF16), shape((2 * GROUP + STATS, HALF), BF16)),
+        (shape((GROUP + STATS, AGENTS), BF16), shape((GROUP + STATS + GROUP // 2, AGENTS), BF16)),
         1.0,
         keep,
         theirs,
@@ -460,8 +458,7 @@
     local = call(
         conv_kernel, shape((TILES, GROUP, TOKENS), F32), 5.0, x, near, far, taps, scalars=where
     )
-    ours = call(comb_kernel, shape((GROUP, HALF), BF16), 1.0, *parts)
-    theirs = lax.ppermute(ours, LINE, along(pair_plane))
+    values = call(comb_kernel, shape((GROUP, AGENTS), BF16), 1.0, *parts)
     weights, totals = call(
         query_kernel,
         (shape((GROUP_HEADS, AGENTS, TILES * TOKENS), BF16), shape((8, TILES * TOKENS), F32)),
@@ -475,8 +472,7 @@
         1.0,
         weights,
         totals,
-        ours,
-        theirs,
+        values,
         parts[1],
         parts[3],
         kin,

time: 78.3 us -> 76.8 us (0.981)
  blocking collectives: 14.6 us -> 12.2 us
  waiting for transfers between devices: 9.62 us -> 10.5 us
    all_to_all x1, blocking collectives: 14.6 us -> 12.2 us  [exchange(): return lax.all_to_all(x, axes, 0, 0)]
    ppermute x3, waiting for transfers between devices: 2.81 us -> 3.64 us  [body(): lax.ppermute(moved, LINE, along(lambda at, odd: other_side(at, -n if odd...]
  transfers between devices with their start and end apart: 14 -> 13, of which waited for: 7 -> 6; matrix products, arithmetic and copies ran while one was open for 0% -> 0% of each run, Pallas kernels for 11% -> 12%
where the time goes in v15:
time: 76.8 us; the launch traced here: 76.5 us
  starting transfers between devices  40.5 us (53%)
  Pallas kernels  13.1 us (17%)
  blocking collectives  12.2 us (16%)
  waiting for transfers between devices  10.5 us (14%)
    pallas_call x13, Pallas kernels, call(): pl.pallas_call(kernel, out_shape=out_shape, in_specs=[SMEM] * len(scalars...  13.1 us
    all_to_all x1, blocking collectives, exchange(): return lax.all_to_all(x, axes, 0, 0)  12.2 us
    all_to_all x2, starting transfers between devices, exchange(): return lax.all_to_all(x, axes, 0, 0)  11.1 us
    ppermute x3, starting transfers between devices, body(): lax.ppermute(moved, LINE, along(lambda at, odd: other_side(at, -n if odd...  8.49 us
    ppermute x3, starting transfers between devices, body(): lax.ppermute(couple, LINE, along(lambda at, odd: same_side(at, n)))  6.15 us
    ppermute x1, starting transfers between devices, body(): met = lax.ppermute(pooled, LINE, along(pair_plane))  5.66 us
    ppermute x1, starting transfers between devices, body(): far = lax.ppermute(far, 'tm', pairs + [(b, a) for a, b in pairs])  4.4 us
    ppermute x3, waiting for transfers between devices, body(): lax.ppermute(moved, LINE, along(lambda at, odd: other_side(at, -n if odd...  3.64 us
  transfers between devices with their start and end apart: 13, of which 6 were waited for; matrix products, arithmetic and copies ran while one was open for 0% of the time, Pallas kernels for 12%

profile of v15, /device:TPU:1, one launch (start us, length us, event | category | flops | bytes accessed | tf_op | source)
XLA Modules:
  0.0 76.5 jit_solution(6951585144356622147)
XLA Ops:
  0.0 2.9 %shard_map.46 = (bf16[8,576,128]{2,1,0:T(8,128)(2,1)}, bf16[8,1536]{1,0:T(8,128)(2,1)}) custom-call(bf16[128,1536]{1,0:T(8,128)(2,1)} %bitcast.9, bf16[128,1536]{1,0:T(8,128)(2,1)} %bitcast.10, bf16[128,1536]{1,0:T(8,128)(2,1)} %bitcast.11), custom_call_target="tpu_custom_call" | custom-call | flops 900000000 | bytes 6000000 | tf_op jit(solution)/shard_map/pallas_call | solution.py:46
  2.9 5.9 %all-to-all-start.1 = ((bf16[8,576,128]{2,1,0:T(8,128)(2,1)}), bf16[8,576,128]{2,1,0:T(8,128)(2,1)S(1)}, u32[]{:S(2)}, u32[]{:S(2)}) async-start(bf16[8,576,128]{2,1,0:T(8,128)(2,1)} %get-tuple-element.19), calls=%async_computation.1 | async-start | bytes 2359296 | tf_op jit(solution)/shard_map/all_to_all | solution.py:58
  8.9 5.7 %collective-permute-start = (bf16[8,1536]{1,0:T(8,128)(2,1)S(1)}, bf16[8,1536]{1,0:T(8,128)(2,1)S(1)}, u32[]{:S(2)}, u32[]{:S(2)}) collective-permute-start(bf16[8,1536]{1,0:T(8,128)(2,1)S(1)} %copy-done.1), channel_id=1, source_target_pairs={{0,8},{8,0},{16,24},{24,16},{32,40},{40,32},{48,56},{56,48},{64,12... | collective-permute-start | bytes 73736 | tf_op jit(solution)/shard_map/ppermute | solution.py:416
  14.6 1.5 %collective-permute-done.theirs_ref = bf16[8,1536]{1,0:T(8,128)(2,1)S(1)} collective-permute-done((bf16[8,1536]{1,0:T(8,128)(2,1)S(1)}, bf16[8,1536]{1,0:T(8,128)(2,1)S(1)}, u32[]{:S(2)}, u32[]{:S(2)}) %collective-permute-start) | collective-permute-done | bytes 24608 | tf_op jit(solution)/shard_map/ppermute | solution.py:416
  16.1 1.7 %collective-permute-start.3 = (bf16[8,1536]{1,0:T(8,128)(2,1)S(1)}, bf16[8,1536]{1,0:T(8,128)(2,1)S(1)}, u32[]{:S(2)}, u32[]{:S(2)}) collective-permute-start(bf16[8,1536]{1,0:T(8,128)(2,1)S(1)} %shard_map.47.refs_0_), channel_id=1, source_target_pairs={{0,48},{8,56},{16,0},{24,8},{32,16},{40,24},{48,32},{56,40},{64,11... | collective-permute-start | bytes 73736 | tf_op jit(solution)/shard_map/ppermute | solution.py:420
  17.8 2.2 %collective-permute-start.2 = (bf16[8,1536]{1,0:T(8,128)(2,1)S(1)}, bf16[8,1536]{1,0:T(8,128)(2,1)S(1)}, u32[]{:S(2)}, u32[]{:S(2)}) collective-permute-start(bf16[8,1536]{1,0:T(8,128)(2,1)S(1)} %shard_map.47.refs_0_), channel_id=1, source_target_pairs={{0,32},{8,40},{16,48},{24,56},{32,0},{40,8},{48,16},{56,24},{64,96... | collective-permute-start | bytes 73736 | tf_op jit(solution)/shard_map/ppermute | solution.py:420
  20.0 2.3 %collective-permute-start.1 = (bf16[8,1536]{1,0:T(8,128)(2,1)S(1)}, bf16[8,1536]{1,0:T(8,128)(2,1)S(1)}, u32[]{:S(2)}, u32[]{:S(2)}) collective-permute-start(bf16[8,1536]{1,0:T(8,128)(2,1)S(1)} %shard_map.47.refs_0_), channel_id=1, source_target_pairs={{0,16},{8,24},{16,32},{24,40},{32,48},{40,56},{48,0},{56,8},{64,80... | collective-permute-start | bytes 73736 | tf_op jit(solution)/shard_map/ppermute | solution.py:420
  22.2 2.1 %collective-permute-done.2.refs_2_ = bf16[8,1536]{1,0:T(8,128)(2,1)S(1)} collective-permute-done((bf16[8,1536]{1,0:T(8,128)(2,1)S(1)}, bf16[8,1536]{1,0:T(8,128)(2,1)S(1)}, u32[]{:S(2)}, u32[]{:S(2)}) %collective-permute-start.2) | collective-permute-done | bytes 24608 | tf_op jit(solution)/shard_map/ppermute | solution.py:420
  24.4 0.5 collective-permute-done.1.refs_1_
  24.9 0.8 %shard_map.48 = bf16[8,32,192]{2,1,0:T(8,128)(2,1)} custom-call(s32[1]{0:T(128)} %bitcast.1.z_ref, bf16[8,1536]{1,0:T(8,128)(2,1)S(1)} %shard_map.47.refs_0_, bf16[8,1536]{1,0:T(8,128)(2,1)S(1)} %collective-permute-done.1.refs_1_, bf16[8,1536]{1,0:T(8,128)(2,1)S(1)} %collective-permute-done.2.refs_2_, bf16[8,1536]{1,0:T(8,128)(2,1)S(1)} %collective-permute-done.3.refs_3_), custom_call_target="tpu_custom_call" | custom-call | flops 300000000 | bytes 2000000 | tf_op jit(solution)/shard_map/pallas_call | solution.py:46
  25.6 5.2 %all-to-all-start = ((bf16[8,32,192]{2,1,0:T(8,128)(2,1)}), bf16[8,32,192]{2,1,0:T(8,128)(2,1)S(1)}, u32[]{:S(2)}, u32[]{:S(2)}) async-start(bf16[8,32,192]{2,1,0:T(8,128)(2,1)} %shard_map.48), calls=%async_computation | async-start | bytes 262144 | tf_op jit(solution)/shard_map/all_to_all | solution.py:58
  31.2 3.5 %collective-permute-start.5 = (bf16[192,256]{1,0:T(8,128)(2,1)S(1)}, bf16[192,256]{1,0:T(8,128)(2,1)S(1)}, u32[]{:S(2)}, u32[]{:S(2)}) collective-permute-start(bf16[192,256]{1,0:T(8,128)(2,1)S(1)} %get-tuple-element.25), channel_id=1, source_target_pairs={{0,64},{128,192},{64,0},{192,128},{1,65},{129,193},{65,1},{193,129... | collective-permute-start | bytes 294920 | tf_op jit(solution)/shard_map/ppermute | solution.py:430
  34.7 4.4 %collective-permute-start.6 = (bf16[192,256]{1,0:T(8,128)(2,1)S(1)}, bf16[192,256]{1,0:T(8,128)(2,1)S(1)}, u32[]{:S(2)}, u32[]{:S(2)}) collective-permute-start(bf16[192,256]{1,0:T(8,128)(2,1)S(1)} %get-tuple-element.26), channel_id=1, source_target_pairs={{64,128},{128,64},{65,129},{129,65},{66,130},{130,66},{67,131},{13... | collective-permute-start | bytes 294920 | tf_op jit(solution)/shard_map/ppermute | solution.py:432
  39.2 1.8 %shard_map.51 = (f32[200,256]{1,0:T(8,128)S(1)}, bf16[208,256]{1,0:T(8,128)(2,1)S(1)}) custom-call(bf16[8,32,192]{2,1,0:T(8,128)(2,1)S(1)} %all-to-all-done.a_ref, bf16[8,576,128]{2,1,0:T(8,128)(2,1)S(1)} %all-to-all-done.1.x_ref), custom_call_target="tpu_custom_call" | custom-call | flops 900000000 | bytes 6000000 | tf_op jit(solution)/shard_map/pallas_call | solution.py:46
  40.9 1.1 %collective-permute-start.4 = (bf16[208,256]{1,0:T(8,128)(2,1)S(1)}, bf16[208,256]{1,0:T(8,128)(2,1)S(1)}, u32[]{:S(2)}, u32[]{:S(2)}) collective-permute-start(bf16[208,256]{1,0:T(8,128)(2,1)S(1)} %get-tuple-element.24), channel_id=1, source_target_pairs={{0,8},{8,0},{16,24},{24,16},{32,40},{40,32},{48,56},{56,48},{64,12... | collective-permute-start | bytes 319496 | tf_op jit(solution)/shard_map/ppermute | solution.py:440
  42.3 0.9 %shard_map.53 = (bf16[192,128]{1,0:T(8,128)(2,1)S(1)}, bf16[192,128]{1,0:T(8,128)(2,1)S(1)}) custom-call(s32[1]{0:T(128)} %bitcast.tm_ref, s32[1]{0:T(128)} %bitcast.1.z_ref, bf16[8,576,128]{2,1,0:T(8,128)(2,1)S(1)} %all-to-all-done.1.x_ref, bf16[192,256]{1,0:T(8,128)(2,1)S(1)} %collective-permute-done.5.near_ref, ...), custom_call_target="tpu_custom_call" | custom-call | flops 300000000 | bytes 2000000 | tf_op jit(solution)/shard_map/pallas_call | solution.py:46
  43.3 2.5 %collective-permute-done.4.came_ref = bf16[208,256]{1,0:T(8,128)(2,1)S(1)} collective-permute-done((bf16[208,256]{1,0:T(8,128)(2,1)S(1)}, bf16[208,256]{1,0:T(8,128)(2,1)S(1)}, u32[]{:S(2)}, u32[]{:S(2)}) %collective-permute-start.4) | collective-permute-done | bytes 106528 | tf_op jit(solution)/shard_map/ppermute | solution.py:440
  45.9 4.5 %collective-permute-start.7 = (bf16[304,256]{1,0:T(8,128)(2,1)S(1)}, bf16[304,256]{1,0:T(8,128)(2,1)S(1)}, u32[]{:S(2)}, u32[]{:S(2)}) collective-permute-start(bf16[304,256]{1,0:T(8,128)(2,1)S(1)} %get-tuple-element.29), channel_id=1, source_target_pairs={{0,24},{8,16},{16,40},{24,32},{32,56},{40,48},{48,8},{56,0},{64,10... | collective-permute-start | bytes 466952 | tf_op jit(solution)/shard_map/ppermute | solution.py:455
  50.4 1.2 %shard_map.50 = (bf16[3,256,1024]{2,1,0:T(8,128)(2,1)S(1)}, f32[8,1024]{1,0:T(8,128)S(1)}) custom-call(bf16[8,32,192]{2,1,0:T(8,128)(2,1)S(1)} %all-to-all-done.a_ref, bf16[192,1024]{1,0:T(8,128)(2,1)S(1)} %get-tuple-element.20.q_ref), custom_call_target="tpu_custom_call" | custom-call | flops 600000000 | bytes 4000000 | tf_op jit(solution)/shard_map/pallas_call | solution.py:46
  51.7 3.9 %collective-permute-start.8 = (bf16[208,256]{1,0:T(8,128)(2,1)S(1)}, bf16[208,256]{1,0:T(8,128)(2,1)S(1)}, u32[]{:S(2)}, u32[]{:S(2)}) collective-permute-start(bf16[208,256]{1,0:T(8,128)(2,1)S(1)} %get-tuple-element.28.refs_0_), channel_id=1, source_target_pairs={{0,32},{8,40},{16,48},{24,56},{32,0},{40,8},{48,16},{56,24},{64,96... | collective-permute-start | bytes 319496 | tf_op jit(solution)/shard_map/ppermute | solution.py:455
  55.7 3.5 %shard_map.56.local_ref = f32[8,192,128]{2,1,0:T(8,128)S(1)} custom-call(s32[1]{0:T(128)} %bitcast.tm_ref, s32[1]{0:T(128)} %bitcast.1.z_ref, bf16[8,576,128]{2,1,0:T(8,128)(2,1)S(1)} %all-to-all-done.1.x_ref, bf16[192,256]{1,0:T(8,128)(2,1)S(1)} %collective-permute-done.5.near_ref, bf16[192,256]{1,0:T(8,128)(2,1)S(1)} %collective-permute-done.6.far_ref, ...), custom_call_target="tpu_custom_call" | custom-call | flops 1500000000 | bytes 10000000 | tf_op jit(solution)/shard_map/pallas_call | solution.py:46
  59.2 3.6 %collective-permute-done.8.refs_2_ = bf16[208,256]{1,0:T(8,128)(2,1)S(1)} collective-permute-done((bf16[208,256]{1,0:T(8,128)(2,1)S(1)}, bf16[208,256]{1,0:T(8,128)(2,1)S(1)}, u32[]{:S(2)}, u32[]{:S(2)}) %collective-permute-start.8) | collective-permute-done | bytes 106528 | tf_op jit(solution)/shard_map/ppermute | solution.py:455
  63.4 12.2 %all_to_all.15.x_ref = bf16[8,192,128]{2,1,0:T(8,128)(2,1)S(1)} all-to-all(bf16[8,192,128]{2,1,0:T(8,128)(2,1)S(1)} %shard_map.57), channel_id=1, replica_groups=mesh['tm'=4,'zh'=4,'zl'=2,'xy'=8] {'xy'}, dimensions={0} | all-to-all | bytes 786432 | tf_op jit(solution)/shard_map/all_to_all | solution.py:58
  75.6 0.9 %shard_map.58 = bf16[128,1536]{1,0:T(8,128)(2,1)} custom-call(bf16[8,192,128]{2,1,0:T(8,128)(2,1)S(1)} %all_to_all.15.x_ref), custom_call_target="tpu_custom_call" | custom-call | flops 300000000 | bytes 2000000 | tf_op jit(solution)/shard_map/pallas_call | solution.py:46
  (20 shorter events, 1.5 us)
Async XLA Ops:
  2.9 6.0 %copy-start.1 = (bf16[8,1536]{1,0:T(8,128)(2,1)S(1)}, bf16[8,1536]{1,0:T(8,128)(2,1)}, u32[]{:S(2)}) copy-start(bf16[8,1536]{1,0:T(8,128)(2,1)} %get-tuple-element.18.ours_ref) | copy-start | bytes 73732
  2.9 22.7 %all-to-all-start.1 = ((bf16[8,576,128]{2,1,0:T(8,128)(2,1)}), bf16[8,576,128]{2,1,0:T(8,128)(2,1)S(1)}, u32[]{:S(2)}, u32[]{:S(2)}) async-start(bf16[8,576,128]{2,1,0:T(8,128)(2,1)} %get-tuple-element.19), calls=%async_computation.1 | async-start | bytes 2359296 | tf_op jit(solution)/shard_map/all_to_all | solution.py:58
  8.9 7.2 %collective-permute-start = (bf16[8,1536]{1,0:T(8,128)(2,1)S(1)}, bf16[8,1536]{1,0:T(8,128)(2,1)S(1)}, u32[]{:S(2)}, u32[]{:S(2)}) collective-permute-start(bf16[8,1536]{1,0:T(8,128)(2,1)S(1)} %copy-done.1), channel_id=1, source_target_pairs={{0,8},{8,0},{16,24},{24,16},{32,40},{40,32},{48,56},{56,48},{64,12... | collective-permute-start | bytes 73736 | tf_op jit(solution)/shard_map/ppermute | solution.py:416
  16.1 6.2 %collective-permute-start.3 = (bf16[8,1536]{1,0:T(8,128)(2,1)S(1)}, bf16[8,1536]{1,0:T(8,128)(2,1)S(1)}, u32[]{:S(2)}, u32[]{:S(2)}) collective-permute-start(bf16[8,1536]{1,0:T(8,128)(2,1)S(1)} %shard_map.47.refs_0_), channel_id=1, source_target_pairs={{0,48},{8,56},{16,0},{24,8},{32,16},{40,24},{48,32},{56,40},{64,11... | collective-permute-start | bytes 73736 | tf_op jit(solution)/shard_map/ppermute | solution.py:420
  17.8 6.6 %collective-permute-start.2 = (bf16[8,1536]{1,0:T(8,128)(2,1)S(1)}, bf16[8,1536]{1,0:T(8,128)(2,1)S(1)}, u32[]{:S(2)}, u32[]{:S(2)}) collective-permute-start(bf16[8,1536]{1,0:T(8,128)(2,1)S(1)} %shard_map.47.refs_0_), channel_id=1, source_target_pairs={{0,32},{8,40},{16,48},{24,56},{32,0},{40,8},{48,16},{56,24},{64,96... | collective-permute-start | bytes 73736 | tf_op jit(solution)/shard_map/ppermute | solution.py:420
  20.0 4.9 %collective-permute-start.1 = (bf16[8,1536]{1,0:T(8,128)(2,1)S(1)}, bf16[8,1536]{1,0:T(8,128)(2,1)S(1)}, u32[]{:S(2)}, u32[]{:S(2)}) collective-permute-start(bf16[8,1536]{1,0:T(8,128)(2,1)S(1)} %shard_map.47.refs_0_), channel_id=1, source_target_pairs={{0,16},{8,24},{16,32},{24,40},{32,48},{40,56},{48,0},{56,8},{64,80... | collective-permute-start | bytes 73736 | tf_op jit(solution)/shard_map/ppermute | solution.py:420
  25.6 13.5 %all-to-all-start = ((bf16[8,32,192]{2,1,0:T(8,128)(2,1)}), bf16[8,32,192]{2,1,0:T(8,128)(2,1)S(1)}, u32[]{:S(2)}, u32[]{:S(2)}) async-start(bf16[8,32,192]{2,1,0:T(8,128)(2,1)} %shard_map.48), calls=%async_computation | async-start | bytes 262144 | tf_op jit(solution)/shard_map/all_to_all | solution.py:58
  31.2 11.0 %collective-permute-start.5 = (bf16[192,256]{1,0:T(8,128)(2,1)S(1)}, bf16[192,256]{1,0:T(8,128)(2,1)S(1)}, u32[]{:S(2)}, u32[]{:S(2)}) collective-permute-start(bf16[192,256]{1,0:T(8,128)(2,1)S(1)} %get-tuple-element.25), channel_id=1, source_target_pairs={{0,64},{128,192},{64,0},{192,128},{1,65},{129,193},{65,1},{193,129... | collective-permute-start | bytes 294920 | tf_op jit(solution)/shard_map/ppermute | solution.py:430
  34.7 7.2 %copy-start = (f32[3,3,3,1536]{3,2,1,0:T(4,128)S(1)}, f32[3,3,3,1536]{3,2,1,0:T(4,128)}, u32[]{:S(2)}) copy-start(f32[3,3,3,1536]{3,2,1,0:T(4,128)} %w_ref.1) | copy-start | bytes 497668
  34.7 7.6 %collective-permute-start.6 = (bf16[192,256]{1,0:T(8,128)(2,1)S(1)}, bf16[192,256]{1,0:T(8,128)(2,1)S(1)}, u32[]{:S(2)}, u32[]{:S(2)}) collective-permute-start(bf16[192,256]{1,0:T(8,128)(2,1)S(1)} %get-tuple-element.26), channel_id=1, source_target_pairs={{64,128},{128,64},{65,129},{129,65},{66,130},{130,66},{67,131},{13... | collective-permute-start | bytes 294920 | tf_op jit(solution)/shard_map/ppermute | solution.py:432
  40.9 4.9 %collective-permute-start.4 = (bf16[208,256]{1,0:T(8,128)(2,1)S(1)}, bf16[208,256]{1,0:T(8,128)(2,1)S(1)}, u32[]{:S(2)}, u32[]{:S(2)}) collective-permute-start(bf16[208,256]{1,0:T(8,128)(2,1)S(1)} %get-tuple-element.24), channel_id=1, source_target_pairs={{0,8},{8,0},{16,24},{24,16},{32,40},{40,32},{48,56},{56,48},{64,12... | collective-permute-start | bytes 319496 | tf_op jit(solution)/shard_map/ppermute | solution.py:440
  45.8 17.0 %collective-permute-start.9 = (bf16[304,256]{1,0:T(8,128)(2,1)S(1)}, bf16[304,256]{1,0:T(8,128)(2,1)S(1)}, u32[]{:S(2)}, u32[]{:S(2)}) collective-permute-start(bf16[304,256]{1,0:T(8,128)(2,1)S(1)} %get-tuple-element.29), channel_id=1, source_target_pairs={{0,56},{8,48},{16,8},{24,0},{32,24},{40,16},{48,40},{56,32},{64,72... | collective-permute-start | bytes 466952 | tf_op jit(solution)/shard_map/ppermute | solution.py:455
  45.9 16.9 %collective-permute-start.7 = (bf16[304,256]{1,0:T(8,128)(2,1)S(1)}, bf16[304,256]{1,0:T(8,128)(2,1)S(1)}, u32[]{:S(2)}, u32[]{:S(2)}) collective-permute-start(bf16[304,256]{1,0:T(8,128)(2,1)S(1)} %get-tuple-element.29), channel_id=1, source_target_pairs={{0,24},{8,16},{16,40},{24,32},{32,56},{40,48},{48,8},{56,0},{64,10... | collective-permute-start | bytes 466952 | tf_op jit(solution)/shard_map/ppermute | solution.py:455
  51.6 11.4 %collective-permute-start.10 = (bf16[192,128]{1,0:T(8,128)(2,1)S(1)}, bf16[192,128]{1,0:T(8,128)(2,1)S(1)}, u32[]{:S(2)}, u32[]{:S(2)}) collective-permute-start(bf16[192,128]{1,0:T(8,128)(2,1)S(1)} %get-tuple-element.30), channel_id=1, source_target_pairs={{0,8},{8,0},{16,24},{24,16},{32,40},{40,32},{48,56},{56,48},{64,12... | collective-permute-start | bytes 147464 | tf_op jit(solution)/shard_map/ppermute | solution.py:457
  51.7 11.1 %collective-permute-start.8 = (bf16[208,256]{1,0:T(8,128)(2,1)S(1)}, bf16[208,256]{1,0:T(8,128)(2,1)S(1)}, u32[]{:S(2)}, u32[]{:S(2)}) collective-permute-start(bf16[208,256]{1,0:T(8,128)(2,1)S(1)} %get-tuple-element.28.refs_0_), channel_id=1, source_target_pairs={{0,32},{8,40},{16,48},{24,56},{32,0},{40,8},{48,16},{56,24},{64,96... | collective-permute-start | bytes 319496 | tf_op jit(solution)/shard_map/ppermute | solution.py:455

commit v16 on v15

--- a/solution.py
+++ b/solution.py
@@ -150,7 +150,7 @@
     return pieces[:n] + pieces[n : 2 * n] + pieces[2 * n : 3 * n]
 
 
-def blend_kernel(keep_ref, came_ref, cross_ref, out_ref, long_ref):
+def blend_kernel(keep_ref, came_ref, out_ref):
     ours, theirs = keep_ref[GROUP : GROUP + GROUP_HEADS, :], logs_of(came_ref[GROUP:, :])
     peak = jnp.maximum(ours, theirs)
     left, right = jnp.exp(ours - peak), jnp.exp(theirs - peak)
@@ -162,12 +162,7 @@
         part = keep_ref[rows, :] * left[h : h + 1] + came_ref[rows, :].astype(F32) * right[h : h + 1]
         part = part.astype(BF16)
         out_ref[rows, :] = part
-        long_ref[rows, :] = part
     out_ref[GROUP:, :] = stats
-    long_ref[GROUP : GROUP + STATS, :] = stats
-    for n in range(2):
-        lanes = slice(n * TOKENS, (n + 1) * TOKENS)
-        long_ref[GROUP + STATS :, lanes] = cross_ref[n * GROUP // 2 : (n + 1) * GROUP // 2, :]
 
 
 def comb_kernel(*refs):
@@ -315,20 +310,14 @@
         e_ref[h] = weights.astype(BF16)
 
 
-def mix_kernel(tm_ref, z_ref, e_ref, total_ref, values_ref, one_ref, three_ref, kin_ref, local_ref, out_ref):
+def mix_kernel(tm_ref, z_ref, e_ref, total_ref, values_ref, cross_ref, kin_ref, local_ref, out_ref):
     second = lax.rem(z_ref[0], 2) == 1
     odd = lax.rem(tm_ref[0], 2)
     first, last = z_ref[0] == (PLANES - 1) * odd, z_ref[0] == PLANES - 1 - odd
     kin = kin_ref[...].astype(F32)
-    one, three = (
-        jnp.concatenate(
-            [ref[GROUP + STATS :, :TOKENS], ref[GROUP + STATS :, TOKENS:]], axis=0
-        ).astype(F32)
-        for ref in (one_ref, three_ref)
-    )
-    above, below = jnp.where(odd == 1, three, one), jnp.where(odd == 1, one, three)
-    above = jnp.where(first, 0.0, jnp.where(second, kin, above))
-    below = jnp.where(last, 0.0, jnp.where(second, below, kin))
+    across = cross_ref[...].astype(F32)
+    above = jnp.where(first, 0.0, jnp.where(second, kin, across))
+    below = jnp.where(last, 0.0, jnp.where(second, across, kin))
     for h in range(GROUP_HEADS):
         rows = slice(h * HEAD_DIM, (h + 1) * HEAD_DIM)
         mixed = jnp.dot(values_ref[rows, :], e_ref[h], preferred_element_type=F32)
@@ -375,8 +364,8 @@
     return 2 * ((at // 2 + n) % PAIRS) + at % 2
 
 
-def other_side(at, n):
-    return 2 * ((at // 2 + n) % PAIRS) + (at + n) % 2
+def plane_across(at, odd):
+    return (at + 1 if at % 2 else at - 1) % PLANES
 
 
 def scalar(x):
@@ -440,19 +429,12 @@
     theirs = lax.ppermute(send, LINE, along(pair_plane))
     row = shape((GROUP, TOKENS), BF16)
     cross, kin = call(rim_kernel, (row, row), 1.0, x, near, far, taps, scalars=where)
-    blended, longer = call(
-        blend_kernel,
-        (shape((GROUP + STATS, AGENTS), BF16), shape((GROUP + STATS + GROUP // 2, AGENTS), BF16)),
-        1.0,
-        keep,
-        theirs,
-        cross,
-    )
+    blended = call(blend_kernel, shape((GROUP + STATS, AGENTS), BF16), 1.0, keep, theirs)
+    cross = lax.ppermute(cross, LINE, along(plane_across))
     parts = [blended]
     for n in range(1, PAIRS):
-        moved = longer if n % 2 else blended
         parts.append(
-            lax.ppermute(moved, LINE, along(lambda at, odd: other_side(at, -n if odd else n)))
+            lax.ppermute(blended, LINE, along(lambda at, odd: same_side(at, -n if odd else n)))
         )
     kin = lax.ppermute(kin, LINE, along(pair_plane))
     local = call(
@@ -473,8 +455,7 @@
         weights,
         totals,
         values,
-        parts[1],
-        parts[3],
+        cross,
         kin,
         local,
         scalars=where,

time: 76.8 us -> 74.1 us (0.965)
  the two profiles are of different devices: /device:TPU:1 before, /device:TPU:4 now
where the time goes in v16:
time: 74.1 us; the launch traced here: 73.8 us
  starting transfers between devices  36 us (49%)
  Pallas kernels  13.1 us (18%)
  waiting for transfers between devices  12.6 us (17%)
  blocking collectives  11.9 us (16%)
    pallas_call x13, Pallas kernels, call(): pl.pallas_call(kernel, out_shape=out_shape, in_specs=[SMEM] * len(scalars...  13.1 us
    all_to_all x1, blocking collectives, exchange(): return lax.all_to_all(x, axes, 0, 0)  11.9 us
    all_to_all x2, starting transfers between devices, exchange(): return lax.all_to_all(x, axes, 0, 0)  10.7 us
    ppermute x3, starting transfers between devices, body(): lax.ppermute(couple, LINE, along(lambda at, odd: same_side(at, n)))  10.2 us
    ppermute x3, starting transfers between devices, body(): lax.ppermute(blended, LINE, along(lambda at, odd: same_side(at, -n if odd...  7.55 us
    ppermute x3, waiting for transfers between devices, body(): lax.ppermute(couple, LINE, along(lambda at, odd: same_side(at, n)))  3.92 us
    ppermute x3, waiting for transfers between devices, body(): lax.ppermute(blended, LINE, along(lambda at, odd: same_side(at, -n if odd...  3.59 us
    all_to_all x2, waiting for transfers between devices, exchange(): return lax.all_to_all(x, axes, 0, 0)  3.19 us
  transfers between devices with their start and end apart: 14, of which 5 were waited for; matrix products, arithmetic and copies ran while one was open for 0% of the time, Pallas kernels for 12%

profile of v16, /device:TPU:4, one launch (start us, length us, event | category | flops | bytes accessed | tf_op | source)
XLA Modules:
  0.0 73.8 jit_solution(10643962290877136736)
XLA Ops:
  0.0 2.9 %shard_map.46 = (bf16[8,576,128]{2,1,0:T(8,128)(2,1)}, bf16[8,1536]{1,0:T(8,128)(2,1)}) custom-call(bf16[128,1536]{1,0:T(8,128)(2,1)} %bitcast.9, bf16[128,1536]{1,0:T(8,128)(2,1)} %bitcast.10, bf16[128,1536]{1,0:T(8,128)(2,1)} %bitcast.11), custom_call_target="tpu_custom_call" | custom-call | flops 900000000 | bytes 6000000 | tf_op jit(solution)/shard_map/pallas_call | solution.py:46
  2.9 5.1 %all-to-all-start.1 = ((bf16[8,576,128]{2,1,0:T(8,128)(2,1)}), bf16[8,576,128]{2,1,0:T(8,128)(2,1)S(1)}, u32[]{:S(2)}, u32[]{:S(2)}) async-start(bf16[8,576,128]{2,1,0:T(8,128)(2,1)} %get-tuple-element.17), calls=%async_computation.1 | async-start | bytes 2359296 | tf_op jit(solution)/shard_map/all_to_all | solution.py:58
  8.1 2.0 %collective-permute-start = (bf16[8,1536]{1,0:T(8,128)(2,1)S(1)}, bf16[8,1536]{1,0:T(8,128)(2,1)S(1)}, u32[]{:S(2)}, u32[]{:S(2)}) collective-permute-start(bf16[8,1536]{1,0:T(8,128)(2,1)S(1)} %copy-done.1), channel_id=1, source_target_pairs={{0,8},{8,0},{16,24},{24,16},{32,40},{40,32},{48,56},{56,48},{64,12... | collective-permute-start | bytes 73736 | tf_op jit(solution)/shard_map/ppermute | solution.py:405
  10.1 1.9 %collective-permute-done.theirs_ref = bf16[8,1536]{1,0:T(8,128)(2,1)S(1)} collective-permute-done((bf16[8,1536]{1,0:T(8,128)(2,1)S(1)}, bf16[8,1536]{1,0:T(8,128)(2,1)S(1)}, u32[]{:S(2)}, u32[]{:S(2)}) %collective-permute-start) | collective-permute-done | bytes 24608 | tf_op jit(solution)/shard_map/ppermute | solution.py:405
  12.0 6.4 %collective-permute-start.3 = (bf16[8,1536]{1,0:T(8,128)(2,1)S(1)}, bf16[8,1536]{1,0:T(8,128)(2,1)S(1)}, u32[]{:S(2)}, u32[]{:S(2)}) collective-permute-start(bf16[8,1536]{1,0:T(8,128)(2,1)S(1)} %shard_map.47.refs_0_), channel_id=1, source_target_pairs={{0,48},{8,56},{16,0},{24,8},{32,16},{40,24},{48,32},{56,40},{64,11... | collective-permute-start | bytes 73736 | tf_op jit(solution)/shard_map/ppermute | solution.py:409
  18.4 1.0 %collective-permute-start.2 = (bf16[8,1536]{1,0:T(8,128)(2,1)S(1)}, bf16[8,1536]{1,0:T(8,128)(2,1)S(1)}, u32[]{:S(2)}, u32[]{:S(2)}) collective-permute-start(bf16[8,1536]{1,0:T(8,128)(2,1)S(1)} %shard_map.47.refs_0_), channel_id=1, source_target_pairs={{0,32},{8,40},{16,48},{24,56},{32,0},{40,8},{48,16},{56,24},{64,96... | collective-permute-start | bytes 73736 | tf_op jit(solution)/shard_map/ppermute | solution.py:409
  19.4 2.8 %collective-permute-start.1 = (bf16[8,1536]{1,0:T(8,128)(2,1)S(1)}, bf16[8,1536]{1,0:T(8,128)(2,1)S(1)}, u32[]{:S(2)}, u32[]{:S(2)}) collective-permute-start(bf16[8,1536]{1,0:T(8,128)(2,1)S(1)} %shard_map.47.refs_0_), channel_id=1, source_target_pairs={{0,16},{8,24},{16,32},{24,40},{32,48},{40,56},{48,0},{56,8},{64,80... | collective-permute-start | bytes 73736 | tf_op jit(solution)/shard_map/ppermute | solution.py:409
  22.2 3.9 %collective-permute-done.2.refs_2_ = bf16[8,1536]{1,0:T(8,128)(2,1)S(1)} collective-permute-done((bf16[8,1536]{1,0:T(8,128)(2,1)S(1)}, bf16[8,1536]{1,0:T(8,128)(2,1)S(1)}, u32[]{:S(2)}, u32[]{:S(2)}) %collective-permute-start.2) | collective-permute-done | bytes 24608 | tf_op jit(solution)/shard_map/ppermute | solution.py:409
  26.1 0.8 %shard_map.48 = bf16[8,32,192]{2,1,0:T(8,128)(2,1)} custom-call(s32[1]{0:T(128)} %bitcast.1.z_ref, bf16[8,1536]{1,0:T(8,128)(2,1)S(1)} %shard_map.47.refs_0_, bf16[8,1536]{1,0:T(8,128)(2,1)S(1)} %collective-permute-done.1.refs_1_, bf16[8,1536]{1,0:T(8,128)(2,1)S(1)} %collective-permute-done.2.refs_2_, bf16[8,1536]{1,0:T(8,128)(2,1)S(1)} %collective-permute-done.3.refs_3_), custom_call_target="tpu_custom_call" | custom-call | flops 300000000 | bytes 2000000 | tf_op jit(solution)/shard_map/pallas_call | solution.py:46
  26.9 5.6 %all-to-all-start = ((bf16[8,32,192]{2,1,0:T(8,128)(2,1)}), bf16[8,32,192]{2,1,0:T(8,128)(2,1)S(1)}, u32[]{:S(2)}, u32[]{:S(2)}) async-start(bf16[8,32,192]{2,1,0:T(8,128)(2,1)} %shard_map.48), calls=%async_computation | async-start | bytes 262144 | tf_op jit(solution)/shard_map/all_to_all | solution.py:58
  33.0 2.9 %collective-permute-start.9 = (bf16[192,256]{1,0:T(8,128)(2,1)S(1)}, bf16[192,256]{1,0:T(8,128)(2,1)S(1)}, u32[]{:S(2)}, u32[]{:S(2)}) collective-permute-start(bf16[192,256]{1,0:T(8,128)(2,1)S(1)} %get-tuple-element.24), channel_id=1, source_target_pairs={{64,128},{128,64},{65,129},{129,65},{66,130},{130,66},{67,131},{13... | collective-permute-start | bytes 294920 | tf_op jit(solution)/shard_map/ppermute | solution.py:421
  35.9 3.2 %all-to-all-done.a_ref = bf16[8,32,192]{2,1,0:T(8,128)(2,1)S(1)} async-done(((bf16[8,32,192]{2,1,0:T(8,128)(2,1)}), bf16[8,32,192]{2,1,0:T(8,128)(2,1)S(1)}, u32[]{:S(2)}, u32[]{:S(2)}) %all-to-all-start) | async-done | bytes 98336 | tf_op jit(solution)/shard_map/all_to_all | solution.py:58
  39.1 1.8 %shard_map.51 = (f32[200,256]{1,0:T(8,128)S(1)}, bf16[208,256]{1,0:T(8,128)(2,1)S(1)}) custom-call(bf16[8,32,192]{2,1,0:T(8,128)(2,1)S(1)} %all-to-all-done.a_ref, bf16[8,576,128]{2,1,0:T(8,128)(2,1)S(1)} %all-to-all-done.1.x_ref), custom_call_target="tpu_custom_call" | custom-call | flops 900000000 | bytes 6000000 | tf_op jit(solution)/shard_map/pallas_call | solution.py:46
  40.9 1.1 %collective-permute-start.4 = (bf16[208,256]{1,0:T(8,128)(2,1)S(1)}, bf16[208,256]{1,0:T(8,128)(2,1)S(1)}, u32[]{:S(2)}, u32[]{:S(2)}) collective-permute-start(bf16[208,256]{1,0:T(8,128)(2,1)S(1)} %get-tuple-element.22), channel_id=1, source_target_pairs={{0,8},{8,0},{16,24},{24,16},{32,40},{40,32},{48,56},{56,48},{64,12... | collective-permute-start | bytes 319496 | tf_op jit(solution)/shard_map/ppermute | solution.py:429
  42.1 1.2 %shard_map.50 = (bf16[3,256,1024]{2,1,0:T(8,128)(2,1)S(1)}, f32[8,1024]{1,0:T(8,128)S(1)}) custom-call(bf16[8,32,192]{2,1,0:T(8,128)(2,1)S(1)} %all-to-all-done.a_ref, bf16[192,1024]{1,0:T(8,128)(2,1)S(1)} %get-tuple-element.18.q_ref), custom_call_target="tpu_custom_call" | custom-call | flops 600000000 | bytes 4000000 | tf_op jit(solution)/shard_map/pallas_call | solution.py:46
  43.3 1.0 %shard_map.55 = (bf16[192,128]{1,0:T(8,128)(2,1)S(1)}, bf16[192,128]{1,0:T(8,128)(2,1)S(1)}) custom-call(s32[1]{0:T(128)} %bitcast.tm_ref, s32[1]{0:T(128)} %bitcast.1.z_ref, bf16[8,576,128]{2,1,0:T(8,128)(2,1)S(1)} %all-to-all-done.1.x_ref, bf16[192,256]{1,0:T(8,128)(2,1)S(1)} %collective-permute-done.8.near_ref, ...), custom_call_target="tpu_custom_call" | custom-call | flops 300000000 | bytes 2000000 | tf_op jit(solution)/shard_map/pallas_call | solution.py:46
  44.3 1.3 %collective-permute-start.10 = (bf16[192,128]{1,0:T(8,128)(2,1)S(1)}, bf16[192,128]{1,0:T(8,128)(2,1)S(1)}, u32[]{:S(2)}, u32[]{:S(2)}) collective-permute-start(bf16[192,128]{1,0:T(8,128)(2,1)S(1)} %get-tuple-element.25), channel_id=1, source_target_pairs={{0,56},{8,16},{16,8},{24,32},{32,24},{40,48},{48,40},{56,0},{64,72... | collective-permute-start | bytes 147464 | tf_op jit(solution)/shard_map/ppermute | solution.py:433
  45.8 3.4 %collective-permute-start.7 = (bf16[208,256]{1,0:T(8,128)(2,1)S(1)}, bf16[208,256]{1,0:T(8,128)(2,1)S(1)}, u32[]{:S(2)}, u32[]{:S(2)}) collective-permute-start(bf16[208,256]{1,0:T(8,128)(2,1)S(1)} %shard_map.52.refs_0_), channel_id=1, source_target_pairs={{0,48},{8,56},{16,0},{24,8},{32,16},{40,24},{48,32},{56,40},{64,80... | collective-permute-start | bytes 319496 | tf_op jit(solution)/shard_map/ppermute | solution.py:437
  49.2 4.1 %collective-permute-start.6 = (bf16[208,256]{1,0:T(8,128)(2,1)S(1)}, bf16[208,256]{1,0:T(8,128)(2,1)S(1)}, u32[]{:S(2)}, u32[]{:S(2)}) collective-permute-start(bf16[208,256]{1,0:T(8,128)(2,1)S(1)} %shard_map.52.refs_0_), channel_id=1, source_target_pairs={{0,32},{8,40},{16,48},{24,56},{32,0},{40,8},{48,16},{56,24},{64,96... | collective-permute-start | bytes 319496 | tf_op jit(solution)/shard_map/ppermute | solution.py:437
  53.4 3.5 %shard_map.56.local_ref = f32[8,192,128]{2,1,0:T(8,128)S(1)} custom-call(s32[1]{0:T(128)} %bitcast.tm_ref, s32[1]{0:T(128)} %bitcast.1.z_ref, bf16[8,576,128]{2,1,0:T(8,128)(2,1)S(1)} %all-to-all-done.1.x_ref, bf16[192,256]{1,0:T(8,128)(2,1)S(1)} %collective-permute-done.8.near_ref, bf16[192,256]{1,0:T(8,128)(2,1)S(1)} %collective-permute-done.9.far_ref, ...), custom_call_target="tpu_custom_call" | custom-call | flops 1500000000 | bytes 10000000 | tf_op jit(solution)/shard_map/pallas_call | solution.py:46
  56.9 2.9 %collective-permute-done.7.refs_3_ = bf16[208,256]{1,0:T(8,128)(2,1)S(1)} collective-permute-done((bf16[208,256]{1,0:T(8,128)(2,1)S(1)}, bf16[208,256]{1,0:T(8,128)(2,1)S(1)}, u32[]{:S(2)}, u32[]{:S(2)}) %collective-permute-start.7) | collective-permute-done | bytes 106528 | tf_op jit(solution)/shard_map/ppermute | solution.py:437
  59.8 0.7 collective-permute-done.5.refs_1_
  61.1 11.9 %all_to_all.15.x_ref = bf16[8,192,128]{2,1,0:T(8,128)(2,1)S(1)} all-to-all(bf16[8,192,128]{2,1,0:T(8,128)(2,1)S(1)} %shard_map.57), channel_id=1, replica_groups=mesh['tm'=4,'zh'=4,'zl'=2,'xy'=8] {'xy'}, dimensions={0} | all-to-all | bytes 786432 | tf_op jit(solution)/shard_map/all_to_all | solution.py:58
  72.9 0.9 %shard_map.58 = bf16[128,1536]{1,0:T(8,128)(2,1)} custom-call(bf16[8,192,128]{2,1,0:T(8,128)(2,1)S(1)} %all_to_all.15.x_ref), custom_call_target="tpu_custom_call" | custom-call | flops 300000000 | bytes 2000000 | tf_op jit(solution)/shard_map/pallas_call | solution.py:46
  (22 shorter events, 1.4 us)
Async XLA Ops:
  2.9 5.1 %copy-start.1 = (bf16[8,1536]{1,0:T(8,128)(2,1)S(1)}, bf16[8,1536]{1,0:T(8,128)(2,1)}, u32[]{:S(2)}) copy-start(bf16[8,1536]{1,0:T(8,128)(2,1)} %get-tuple-element.16.ours_ref) | copy-start | bytes 73732
  2.9 23.9 %all-to-all-start.1 = ((bf16[8,576,128]{2,1,0:T(8,128)(2,1)}), bf16[8,576,128]{2,1,0:T(8,128)(2,1)S(1)}, u32[]{:S(2)}, u32[]{:S(2)}) async-start(bf16[8,576,128]{2,1,0:T(8,128)(2,1)} %get-tuple-element.17), calls=%async_computation.1 | async-start | bytes 2359296 | tf_op jit(solution)/shard_map/all_to_all | solution.py:58
  8.1 3.9 %collective-permute-start = (bf16[8,1536]{1,0:T(8,128)(2,1)S(1)}, bf16[8,1536]{1,0:T(8,128)(2,1)S(1)}, u32[]{:S(2)}, u32[]{:S(2)}) collective-permute-start(bf16[8,1536]{1,0:T(8,128)(2,1)S(1)} %copy-done.1), channel_id=1, source_target_pairs={{0,8},{8,0},{16,24},{24,16},{32,40},{40,32},{48,56},{56,48},{64,12... | collective-permute-start | bytes 73736 | tf_op jit(solution)/shard_map/ppermute | solution.py:405
  12.0 10.2 %collective-permute-start.3 = (bf16[8,1536]{1,0:T(8,128)(2,1)S(1)}, bf16[8,1536]{1,0:T(8,128)(2,1)S(1)}, u32[]{:S(2)}, u32[]{:S(2)}) collective-permute-start(bf16[8,1536]{1,0:T(8,128)(2,1)S(1)} %shard_map.47.refs_0_), channel_id=1, source_target_pairs={{0,48},{8,56},{16,0},{24,8},{32,16},{40,24},{48,32},{56,40},{64,11... | collective-permute-start | bytes 73736 | tf_op jit(solution)/shard_map/ppermute | solution.py:409
  18.4 7.7 %collective-permute-start.2 = (bf16[8,1536]{1,0:T(8,128)(2,1)S(1)}, bf16[8,1536]{1,0:T(8,128)(2,1)S(1)}, u32[]{:S(2)}, u32[]{:S(2)}) collective-permute-start(bf16[8,1536]{1,0:T(8,128)(2,1)S(1)} %shard_map.47.refs_0_), channel_id=1, source_target_pairs={{0,32},{8,40},{16,48},{24,56},{32,0},{40,8},{48,16},{56,24},{64,96... | collective-permute-start | bytes 73736 | tf_op jit(solution)/shard_map/ppermute | solution.py:409
  19.4 6.7 %collective-permute-start.1 = (bf16[8,1536]{1,0:T(8,128)(2,1)S(1)}, bf16[8,1536]{1,0:T(8,128)(2,1)S(1)}, u32[]{:S(2)}, u32[]{:S(2)}) collective-permute-start(bf16[8,1536]{1,0:T(8,128)(2,1)S(1)} %shard_map.47.refs_0_), channel_id=1, source_target_pairs={{0,16},{8,24},{16,32},{24,40},{32,48},{40,56},{48,0},{56,8},{64,80... | collective-permute-start | bytes 73736 | tf_op jit(solution)/shard_map/ppermute | solution.py:409
  26.9 12.2 %all-to-all-start = ((bf16[8,32,192]{2,1,0:T(8,128)(2,1)}), bf16[8,32,192]{2,1,0:T(8,128)(2,1)S(1)}, u32[]{:S(2)}, u32[]{:S(2)}) async-start(bf16[8,32,192]{2,1,0:T(8,128)(2,1)} %shard_map.48), calls=%async_computation | async-start | bytes 262144 | tf_op jit(solution)/shard_map/all_to_all | solution.py:58
  32.9 10.5 %collective-permute-start.8 = (bf16[192,256]{1,0:T(8,128)(2,1)S(1)}, bf16[192,256]{1,0:T(8,128)(2,1)S(1)}, u32[]{:S(2)}, u32[]{:S(2)}) collective-permute-start(bf16[192,256]{1,0:T(8,128)(2,1)S(1)} %get-tuple-element.23), channel_id=1, source_target_pairs={{0,64},{128,192},{64,0},{192,128},{1,65},{129,193},{65,1},{193,129... | collective-permute-start | bytes 294920 | tf_op jit(solution)/shard_map/ppermute | solution.py:419
  33.0 9.0 %copy-start = (f32[3,3,3,1536]{3,2,1,0:T(4,128)S(1)}, f32[3,3,3,1536]{3,2,1,0:T(4,128)}, u32[]{:S(2)}) copy-start(f32[3,3,3,1536]{3,2,1,0:T(4,128)} %w_ref.1) | copy-start | bytes 497668
  33.0 10.4 %collective-permute-start.9 = (bf16[192,256]{1,0:T(8,128)(2,1)S(1)}, bf16[192,256]{1,0:T(8,128)(2,1)S(1)}, u32[]{:S(2)}, u32[]{:S(2)}) collective-permute-start(bf16[192,256]{1,0:T(8,128)(2,1)S(1)} %get-tuple-element.24), channel_id=1, source_target_pairs={{64,128},{128,64},{65,129},{129,65},{66,130},{130,66},{67,131},{13... | collective-permute-start | bytes 294920 | tf_op jit(solution)/shard_map/ppermute | solution.py:421
  40.9 4.9 %collective-permute-start.4 = (bf16[208,256]{1,0:T(8,128)(2,1)S(1)}, bf16[208,256]{1,0:T(8,128)(2,1)S(1)}, u32[]{:S(2)}, u32[]{:S(2)}) collective-permute-start(bf16[208,256]{1,0:T(8,128)(2,1)S(1)} %get-tuple-element.22), channel_id=1, source_target_pairs={{0,8},{8,0},{16,24},{24,16},{32,40},{40,32},{48,56},{56,48},{64,12... | collective-permute-start | bytes 319496 | tf_op jit(solution)/shard_map/ppermute | solution.py:429
  44.3 16.3 %collective-permute-start.10 = (bf16[192,128]{1,0:T(8,128)(2,1)S(1)}, bf16[192,128]{1,0:T(8,128)(2,1)S(1)}, u32[]{:S(2)}, u32[]{:S(2)}) collective-permute-start(bf16[192,128]{1,0:T(8,128)(2,1)S(1)} %get-tuple-element.25), channel_id=1, source_target_pairs={{0,56},{8,16},{16,8},{24,32},{32,24},{40,48},{48,40},{56,0},{64,72... | collective-permute-start | bytes 147464 | tf_op jit(solution)/shard_map/ppermute | solution.py:433
  45.6 15.0 %collective-permute-start.11 = (bf16[192,128]{1,0:T(8,128)(2,1)S(1)}, bf16[192,128]{1,0:T(8,128)(2,1)S(1)}, u32[]{:S(2)}, u32[]{:S(2)}) collective-permute-start(bf16[192,128]{1,0:T(8,128)(2,1)S(1)} %get-tuple-element.26), channel_id=1, source_target_pairs={{0,8},{8,0},{16,24},{24,16},{32,40},{40,32},{48,56},{56,48},{64,12... | collective-permute-start | bytes 147464 | tf_op jit(solution)/shard_map/ppermute | solution.py:439
  45.8 14.0 %collective-permute-start.7 = (bf16[208,256]{1,0:T(8,128)(2,1)S(1)}, bf16[208,256]{1,0:T(8,128)(2,1)S(1)}, u32[]{:S(2)}, u32[]{:S(2)}) collective-permute-start(bf16[208,256]{1,0:T(8,128)(2,1)S(1)} %shard_map.52.refs_0_), channel_id=1, source_target_pairs={{0,48},{8,56},{16,0},{24,8},{32,16},{40,24},{48,32},{56,40},{64,80... | collective-permute-start | bytes 319496 | tf_op jit(solution)/shard_map/ppermute | solution.py:437
  49.2 10.6 %collective-permute-start.6 = (bf16[208,256]{1,0:T(8,128)(2,1)S(1)}, bf16[208,256]{1,0:T(8,128)(2,1)S(1)}, u32[]{:S(2)}, u32[]{:S(2)}) collective-permute-start(bf16[208,256]{1,0:T(8,128)(2,1)S(1)} %shard_map.52.refs_0_), channel_id=1, source_target_pairs={{0,32},{8,40},{16,48},{24,56},{32,0},{40,8},{48,16},{56,24},{64,96... | collective-permute-start | bytes 319496 | tf_op jit(solution)/shard_map/ppermute | solution.py:437
  53.4 7.1 %collective-permute-start.5 = (bf16[208,256]{1,0:T(8,128)(2,1)S(1)}, bf16[208,256]{1,0:T(8,128)(2,1)S(1)}, u32[]{:S(2)}, u32[]{:S(2)}) collective-permute-start(bf16[208,256]{1,0:T(8,128)(2,1)S(1)} %shard_map.52.refs_0_), channel_id=1, source_target_pairs={{0,16},{8,24},{16,32},{24,40},{32,48},{40,56},{48,0},{56,8},{64,11... | collective-permute-start | bytes 319496 | tf_op jit(solution)/shard_map/ppermute | solution.py:437
